TPU v7x, 256 devices: a whole 4x4x8 slice. The times are simulated.
256 devices in a mesh: dp: 2 (over core), ctx: 32 (over y, z), head: 4 (over x).
Axes of the slice: x: 4, y: 4, z: 8, core: 2. Of those that a mesh axis runs over, the one named last changes fastest.
Arguments:
- query_states: bfloat16 [32768, 4096], P(('dp', 'ctx'), 'head'), parts along dimension 0, may hold values from -72 to 72
- key_states: bfloat16 [32768, 4096], P(('dp', 'ctx'), 'head'), parts along dimension 0, may hold values from -18 to 18
- value_states: bfloat16 [32768, 4096], P(('dp', 'ctx'), 'head'), parts along dimension 0, may hold values from -6 to 6
- gate_logits: bfloat16 [32, 32768], P('head', ('dp', 'ctx')), parts along dimension 1, may hold values from -16 to 6
- selected_blocks: int32 [256, 8], P(('dp', 'ctx')), parts along dimension 0, may hold values from 0 to 127, as said below
Outputs:
- attn_output: bfloat16 [32768, 4096], P(('dp', 'ctx'), 'head'), parts along dimension 0
There are 2 independent parts, one for each index of `dp`. A program takes and returns all parts, laid end to end along the dimension named above; each array names one. Nothing has to cross between parts.
Inputs may be any that keep to these rules, and one draw needn't show every extreme that they name: `selected_blocks`: row b holds 8 block numbers: each is b itself, which selects nothing, or an earlier block, and the earlier ones of a row are distinct. Over the rows of the blocks inside one aligned span of 512 tokens, the earlier blocks selected that lie inside any other aligned span of 512 tokens are at most one distinct block.
All inputs are finite; a program needn't handle non-finite values.
Results may differ from a plain program's by a relative error of at most 0.012.
Values may be sent and summed in bfloat16 or wider, within the bound.
No kernel may reach another device: no remote copies, remote signals or barrier semaphores. Data moves between devices by JAX's collectives and lax.ppermute only.
A program may use at most 128 MiB of HBM per device.

v0:
```python
import jax
import jax.numpy as jnp
from jax import lax
from jax.sharding import PartitionSpec as P

BLOCK = 128


NEG_FILL = -1e30
ROPE_BASE = 10000.0


def entering(value, axis, join, neutral):
    count, mine = (lax.axis_size(axis), lax.axis_index(axis))
    pieces = lax.all_gather(value, axis)
    running = jnp.full_like(value, 0) + jnp.asarray(neutral, value.dtype)

    def turn(position, running):
        longer = join(running, pieces[position])
        return jnp.where(position < mine, longer, running)

    return lax.fori_loop(0, count - 1, turn, running)


def rotate(inputs, angles):
    row_count = inputs.shape[0]
    head_count = angles.shape[0]
    widened = inputs.astype(jnp.float32).reshape(row_count, head_count, -1)
    half_width = widened.shape[-1] // 2
    inv_freq = ROPE_BASE ** (-jnp.arange(half_width).astype(jnp.float32) / half_width)
    phases = angles.T[:, :, None] * inv_freq
    cos_part = jnp.cos(phases)
    sin_part = jnp.sin(phases)
    first_half = widened[..., :half_width]
    second_half = widened[..., half_width:]
    rotated = jnp.concatenate(
        [
            first_half * cos_part - second_half * sin_part,
            second_half * cos_part + first_half * sin_part,
        ],
        axis=-1,
    )
    return rotated.reshape(row_count, -1).astype(jnp.bfloat16)


def add_pair(earlier, later):
    return earlier + later


def shards(query_states, key_states, value_states, gate_logits, selected_blocks):
    tok_count, feat_width = query_states.shape
    head_count = gate_logits.shape[0]
    head_width = feat_width // head_count
    ctx_count = lax.axis_size("ctx")
    my_index = lax.axis_index("ctx")
    block_count = tok_count // BLOCK
    top_count = selected_blocks.shape[1]
    gate_values = jax.nn.sigmoid(gate_logits.astype(jnp.float32))
    local_sum = jnp.cumsum(gate_values, axis=1)
    device_total = local_sum[:, -1]
    carry_in = entering(device_total, "ctx", add_pair, jnp.zeros_like(device_total))
    angles = carry_in[:, None] + local_sum
    query_rot = rotate(query_states, angles)
    key_rot = rotate(key_states, angles)
    key_blocks = key_rot.reshape(block_count, BLOCK, feat_width)
    value_blocks = value_states.reshape(block_count, BLOCK, feat_width)
    source_dev = selected_blocks // block_count
    inside_idx = selected_blocks % block_count
    peer_ids = jnp.arange(ctx_count, dtype=jnp.int32)
    is_remote = source_dev != my_index
    matches = (source_dev.reshape(-1)[:, None] == peer_ids[None, :]) & is_remote.reshape(-1)[
        :, None
    ]
    wanted_blk = jnp.max(jnp.where(matches, inside_idx.reshape(-1)[:, None], -1), axis=0)
    asked_blk = lax.all_to_all(wanted_blk[:, None], "ctx", split_axis=0, concat_axis=0, tiled=True)
    pick_blk = jnp.maximum(asked_blk[:, 0], 0)
    send_values = jnp.take(value_blocks, pick_blk, axis=0)
    recv_keys, recv_values = (
        lax.all_to_all(
            jnp.take(key_blocks, pick_blk, axis=0), "ctx", split_axis=0, concat_axis=0, tiled=True
        ),
        lax.all_to_all(send_values, "ctx", split_axis=0, concat_axis=0, tiled=True),
    )
    pool_keys = jnp.concatenate([recv_keys, key_blocks], axis=0)
    pool_values = jnp.concatenate([recv_values, value_blocks], axis=0)
    group_size = min(block_count, 4)
    group_count = block_count // group_size
    score_scale = head_width ** (-0.5)
    causal_mask = jnp.tril(jnp.ones((BLOCK, BLOCK), dtype=bool))
    query_blocks = query_rot.reshape(block_count, BLOCK, head_count, head_width)
    own_key_blocks = key_rot.reshape(block_count, BLOCK, head_count, head_width)
    own_value_blocks = value_states.reshape(block_count, BLOCK, head_count, head_width)

    def attend(group_idx):
        first_blk = group_idx * group_size
        own_blk = my_index * block_count + first_blk + jnp.arange(group_size, dtype=jnp.int32)
        empty_slot = selected_blocks == own_blk[:, None]
        slot_dev = selected_blocks // block_count
        slot_idx = jnp.where(
            slot_dev == my_index, ctx_count + selected_blocks % block_count, slot_dev
        )
        sel_keys = jnp.take(pool_keys, slot_idx.reshape(-1), axis=0).reshape(
            group_size, top_count * BLOCK, head_count, head_width
        )
        sel_values = jnp.take(pool_values, slot_idx.reshape(-1), axis=0).reshape(
            group_size, top_count * BLOCK, head_count, head_width
        )
        sel_scores = (
            jnp.einsum(
                "gqhd,gkhd->ghqk", query_blocks, sel_keys, preferred_element_type=jnp.float32
            )
            * score_scale
        )
        keep_mask = jnp.repeat(jnp.logical_not(empty_slot), BLOCK, axis=1)
        sel_scores = jnp.where(keep_mask[:, None, None, :], sel_scores, NEG_FILL)
        own_scores = (
            jnp.einsum(
                "gqhd,gkhd->ghqk", query_blocks, own_key_blocks, preferred_element_type=jnp.float32
            )
            * score_scale
        )
        own_scores = jnp.where(causal_mask[None, None], own_scores, NEG_FILL)
        row_max = jnp.maximum(sel_scores.max(-1), own_scores.max(-1))
        sel_weight = jnp.exp(sel_scores - row_max[..., None])
        own_weight = jnp.exp(own_scores - row_max[..., None])
        weight_sum = sel_weight.sum(-1) + own_weight.sum(-1)
        mixed = jnp.einsum(
            "ghqk,gkhd->gqhd",
            sel_weight.astype(jnp.bfloat16),
            sel_values,
            preferred_element_type=jnp.float32,
        )
        mixed = mixed + jnp.einsum(
            "ghqk,gkhd->gqhd",
            own_weight.astype(jnp.bfloat16),
            own_value_blocks,
            preferred_element_type=jnp.float32,
        )
        mixed = mixed / jnp.moveaxis(weight_sum, 1, 2)[..., None]
        return mixed.astype(jnp.bfloat16).reshape(group_size * BLOCK, feat_width)

    blocks_out = lax.map(attend, jnp.arange(group_count, dtype=jnp.int32))
    return blocks_out.reshape(tok_count, feat_width)


def solution(mesh):
    placed = (
        P(("dp", "ctx"), "head"),
        P(("dp", "ctx"), "head"),
        P(("dp", "ctx"), "head"),
        P("head", ("dp", "ctx")),
        P(("dp", "ctx"), None),
    )
    return jax.shard_map(
        shards, mesh=mesh, in_specs=placed, out_specs=P(("dp", "ctx"), "head"), check_vma=False
    )
```

profile of v0, /device:TPU:2, one launch (start us, length us, event | category | flops | bytes accessed | tf_op | source)
XLA Modules:
  0.0 562.9 jit_solution(8150804027683653542)
XLA Ops:
  1.7 11.5 %all-to-all-start = ((s32[32,1,1]{2,1,0:T(1,128)}), s32[32,1,1]{2,1,0:T(1,128)S(1)}, u32[]{:S(2)}, u32[]{:S(2)}) async-start(s32[32,1,1]{2,1,0:T(1,128)} %copy.51), calls=%async_computation | async-start | bytes 32768 | tf_op jit(solution)/shard_map/all_to_all | solution.py:75
  17.8 74.8 %all-reduce = f32[256]{0:T(256)S(1)} all-reduce(f32[256]{0:T(256)S(1)} %dynamic-update-slice), channel_id=2, replica_groups=mesh['dp'=2,'ctx'=32,'head'=4] {'ctx'}, use_global_device_ids=true, to_apply=%add | all-reduce | flops 256 | bytes 2048
  94.1 1.5 convert_bitcast_fusion
  96.1 8.7 %fusion.24 = (bf16[512,8,64]{2,1,0:T(8,128)(2,1)S(1)}, bf16[512,8,64]{2,1,0:T(8,128)(2,1)S(1)}) fusion(f32[512,8,128]{2,1,0:T(8,128)S(1)} %bitcast.61, f32[64]{0:T(128)S(1)} %multiply_power_fusion, f32[512,8]{1,0:T(8,128)S(1)} %copy.52), kind=kLoop, calls=%fused_computation.39 | loop fusion | flops 2359296 | bytes 3162368 | tf_op jit(solution)/shard_map/sub | solution.py:38
  106.6 5.0 gather_fusion.2
  111.5 5.0 gather_fusion
  116.6 9.4 %broadcast_select_fusion.5 = (bf16[32,128,1024]{2,1,0:T(8,128)(2,1)}, bf16[32,128,1024]{2,1,0:T(8,128)(2,1)S(1)}) fusion(bf16[32,128,1024]{2,1,0:T(8,128)(2,1)} %gather_fusion, pred[32]{0:T(512)(128)(4,1)S(1)} %compare_and_fusion.1, bf16[32,128,1024]{2,1,0:T(8,128)(2,1)} %gather_fusion.2), kind=kLoop, calls=%fused_computation.23 | loop fusion | flops 8388608 | bytes 33554464 | tf_op jit(solution)/shard_map/jit(_take)/select_n | solution.py:77
  125.9 176.8 %all_to_all.19 = bf16[32,128,1024]{2,1,0:T(8,128)(2,1)} all-to-all(bf16[32,128,1024]{2,1,0:T(8,128)(2,1)S(1)} %get-tuple-element.150), channel_id=1, replica_groups=mesh['dp'=2,'ctx'=32,'head'=4] {'ctx'}, dimensions={0} | all-to-all | bytes 16777216 | tf_op jit(solution)/shard_map/all_to_all | solution.py:79
  302.7 14.0 %all-to-all-start.1 = ((bf16[32,128,1024]{2,1,0:T(8,128)(2,1)}), bf16[32,128,1024]{2,1,0:T(8,128)(2,1)}, u32[]{:S(2)}, u32[]{:S(2)}) async-start(bf16[32,128,1024]{2,1,0:T(8,128)(2,1)} %get-tuple-element.149), calls=%async_computation.1 | async-start | bytes 16777216 | tf_op jit(solution)/shard_map/all_to_all | solution.py:82
  317.0 1.8 copy.66
  319.0 1.3 copy.69
  320.3 10.7 %fusion.21 = (bf16[512,8,64]{2,1,0:T(8,128)(2,1)S(1)}, bf16[512,8,64]{2,1,0:T(8,128)(2,1)S(1)}) fusion(f32[512,8,128]{2,1,0:T(8,128)} %bitcast.60, f32[64]{0:T(128)S(1)} %multiply_power_fusion, f32[512,8]{1,0:T(8,128)S(1)} %copy.52), kind=kLoop, calls=%fused_computation.36 | loop fusion | flops 2359296 | bytes 3162368 | tf_op jit(solution)/shard_map/convert.2
  331.6 3.4 fusion.28
  335.0 4.0 pad_maximum_fusion.1
  339.0 8.7 %gather_fusion.3 = bf16[32,128,1024]{2,1,0:T(8,128)(2,1)} fusion(bf16[36,128,1024]{2,1,0:T(8,128)(2,1)} %pad_maximum_fusion.1, s32[1024]{0:T(1024)S(1)} %pad_clamp_fusion), kind=kCustom, calls=%fused_computation.3.clone | custom fusion | bytes 16777344 | tf_op jit(solution)/shard_map/while/body/eval_jaxpr/jit(_take)/gather | solution.py:102
  347.7 134.4 %all-to-all-done.1 = bf16[32,128,1024]{2,1,0:T(8,128)(2,1)} async-done(((bf16[32,128,1024]{2,1,0:T(8,128)(2,1)}), bf16[32,128,1024]{2,1,0:T(8,128)(2,1)}, u32[]{:S(2)}, u32[]{:S(2)}) %all-to-all-start.1) | async-done | bytes 8388640 | tf_op jit(solution)/shard_map/all_to_all | solution.py:82
  482.1 7.4 %pad_maximum_fusion = bf16[36,128,1024]{2,1,0:T(8,128)(2,1)} fusion(bf16[4,128,1024]{2,1,0:T(8,128)(2,1)S(1)} %bitcast.54, bf16[32,128,1024]{2,1,0:T(8,128)(2,1)} %all-to-all-done.1), kind=kLoop, calls=%fused_computation.11 | loop fusion | flops 4718592 | bytes 18874368 | tf_op jit(solution)/shard_map/concatenate | solution.py:85
  489.5 8.7 %gather_fusion.1 = bf16[32,128,1024]{2,1,0:T(8,128)(2,1)} fusion(bf16[36,128,1024]{2,1,0:T(8,128)(2,1)} %pad_maximum_fusion, s32[1024]{0:T(1024)S(1)} %pad_clamp_fusion), kind=kCustom, calls=%fused_computation.1.clone | custom fusion | bytes 16777344 | tf_op jit(solution)/shard_map/while/body/eval_jaxpr/jit(_take)/gather | solution.py:105
  498.3 11.7 %broadcast_select_fusion.3 = (bf16[32,128,1024]{2,1,0:T(8,128)(2,1)}, bf16[32,128,1024]{2,1,0:T(8,128)(2,1)}) fusion(bf16[32,128,1024]{2,1,0:T(8,128)(2,1)} %gather_fusion.1, pred[32]{0:T(512)(128)(4,1)S(1)} %compare_and_fusion, bf16[32,128,1024]{2,1,0:T(8,128)(2,1)} %gather_fusion.3), kind=kLoop, calls=%fused_computation.21 | loop fusion | flops 8388608 | bytes 33554464 | tf_op jit(solution)/shard_map/while/body/eval_jaxpr/jit(_take)/select_n | solution.py:105
  509.9 8.8 %copy.68 = bf16[512,8,8,128]{3,2,1,0:T(8,128)(2,1)} copy(bf16[512,8,8,128]{3,1,2,0:T(8,128)(2,1)} %bitcast.56) | data formatting | bytes 16777216
  518.7 12.6 %fusion = (f32[4,8,128]{2,1,0:T(8,128)S(1)}, f32[4,8,128,1024]{3,2,1,0:T(8,128)}) fusion(pred[4,1024]{1,0:T(4,128)(4,1)S(1)} %bitcast.68, bf16[4,1024,8,128]{3,2,1,0:T(8,128)(2,1)} %bitcast.59, bf16[4,128,8,128]{3,2,1,0:T(8,128)(2,1)S(1)} %bitcast.64), kind=kOutput, calls=%fused_computation.8 | convolution fusion | flops 1086320640 | bytes 26234880 | tf_op jit(solution)/shard_map/while/body/eval_jaxpr/gqhd,gkhd->ghqk/dot_general | solution.py:109
  531.9 8.2 %fusion.1 = f32[4,8,128]{2,1,0:T(8,128)S(1)} fusion(f32[4,8,128,1024]{3,2,1,0:T(8,128)} %get-tuple-element.152, f32[4,8,128]{2,1,0:T(8,128)S(1)} %max.20, pred[4,1024]{1,0:T(4,128)(4,1)S(1)} %bitcast.69), kind=kLoop, calls=%fused_computation.9 | loop fusion | flops 16773120 | bytes 16814080 | tf_op jit(solution)/shard_map/while/body/eval_jaxpr/reduce_sum | solution.py:126
  540.9 8.8 %copy.64 = bf16[512,8,8,128]{3,2,1,0:T(8,128)(2,1)} copy(bf16[512,8,8,128]{3,1,2,0:T(8,128)(2,1)} %bitcast.55) | data formatting | bytes 16777216
  549.7 11.2 %fusion.27 = bf16[4,128,8,128]{1,3,2,0:T(8,128)(2,1)S(1)} fusion(f32[4,8,128,128]{2,3,1,0:T(8,128)S(1)} %fusion.35, f32[4,8,128,1024]{3,2,1,0:T(8,128)} %get-tuple-element.152, f32[4,8,128]{2,1,0:T(8,128)S(1)} %max.20, pred[4,1024]{1,0:T(4,128)(4,1)S(1)} %bitcast.70, bf16[4,1024,8,128]{3,2,1,0:T(8,128)(2,1)} %bitcast.62, f32[4,128,8]{1,2,0:T(8,128)S(1)} %add_bitcast_fusion), kind=kOutput, calls=%fused_computation.44 | convolution fusion | flops 1092091904 | bytes 28348416 | tf_op jit(solution)/shard_map/while/body/eval_jaxpr/ghqk,gkhd->gqhd/dot_general | solution.py:127
  (96 shorter events, 14.2 us)
Async XLA Ops:
  1.7 104.1 %all-to-all-start = ((s32[32,1,1]{2,1,0:T(1,128)}), s32[32,1,1]{2,1,0:T(1,128)S(1)}, u32[]{:S(2)}, u32[]{:S(2)}) async-start(s32[32,1,1]{2,1,0:T(1,128)} %copy.51), calls=%async_computation | async-start | bytes 32768 | tf_op jit(solution)/shard_map/all_to_all | solution.py:75
  105.3 1.2 copy-start.2
  106.6 5.0 copy-start
  302.7 14.0 %copy-start.4 = (bf16[512,1024]{1,0:T(8,128)(2,1)S(1)}, bf16[512,1024]{1,0:T(8,128)(2,1)}, u32[]{:S(2)}) copy-start(bf16[512,1024]{1,0:T(8,128)(2,1)} %param.11) | copy-start | bytes 3145732
  302.7 16.1 %copy-start.5 = (s32[4,8]{1,0:T(4,128)S(1)}, s32[4,8]{1,0:T(4,128)}, u32[]{:S(2)}) copy-start(s32[4,8]{1,0:T(4,128)} %param.15) | copy-start | bytes 388
  302.7 179.4 %all-to-all-start.1 = ((bf16[32,128,1024]{2,1,0:T(8,128)(2,1)}), bf16[32,128,1024]{2,1,0:T(8,128)(2,1)}, u32[]{:S(2)}, u32[]{:S(2)}) async-start(bf16[32,128,1024]{2,1,0:T(8,128)(2,1)} %get-tuple-element.149), calls=%async_computation.1 | async-start | bytes 16777216 | tf_op jit(solution)/shard_map/all_to_all | solution.py:82
  318.8 16.2 %slice-start = ((s8[8388608]{0:T(1024)(128)(4,1)}), s8[4194304]{0:T(1024)(128)(4,1)S(1)}, s32[]{:S(2)}) async-start(s8[8388608]{0:T(1024)(128)(4,1)} %bitcast.57), calls=%async_computation.3 | async-start | bytes 8388608
  320.3 14.7 %slice-start.1 = ((s8[8388608]{0:T(1024)(128)(4,1)}), s8[4194304]{0:T(1024)(128)(4,1)S(1)}, s32[]{:S(2)}) async-start(s8[8388608]{0:T(1024)(128)(4,1)} %bitcast.57), calls=%async_computation.4 | async-start | bytes 8388608
  518.7 12.7 %copy-start.1 = (f32[4,8,128,128]{2,3,1,0:T(8,128)S(1)}, f32[4,8,128,128]{2,3,1,0:T(8,128)}, u32[]{:S(2)}) copy-start(f32[4,8,128,128]{2,3,1,0:T(8,128)} %get-tuple-element.154) | copy-start | bytes 6291460
  531.9 8.2 %copy-start.3 = (bf16[64,8,8,128]{3,2,1,0:T(8,128)(2,1)S(1)}, bf16[64,8,8,128]{3,2,1,0:T(8,128)(2,1)}, u32[]{:S(2)}) copy-start(bf16[64,8,8,128]{3,2,1,0:T(8,128)(2,1)} %copy.69) | copy-start | bytes 3145732
where the time goes:
time: 564 us; the launch traced here: 563 us
  blocking collectives  252 us (45%)
  waiting for transfers between devices  134 us (24%)
  other arithmetic  67.6 us (12%)
  local copies, waits for them, and re-layouts  54.3 us (10%)
  matrix products  28 us (5%)
  starting transfers between devices  25.4 us (5%)
    all_to_all x1, blocking collectives, shards(): lax.all_to_all(jnp.take(key_blocks, pick_blk, axis=0), 'ctx', split_axis=...  177 us
    all_to_all x1, waiting for transfers between devices, shards(): lax.all_to_all(send_values, 'ctx', split_axis=0, concat_axis=0, tiled=True)  134 us
    unnamed x1, blocking collectives  74.8 us
    unnamed x27, local copies, waits for them, and re-layouts  24.1 us
    all_to_all x1, starting transfers between devices, shards(): lax.all_to_all(send_values, 'ctx', split_axis=0, concat_axis=0, tiled=True)  14 us
    another operation x5, other arithmetic  12.7 us
    dot_general x1, matrix products, attend(): jnp.einsum('gqhd,gkhd->ghqk', query_blocks, sel_keys, preferred_element_t...  12.6 us
    select_n x2, other arithmetic, attend(): jnp.take(pool_values, slot_idx.reshape(-1), axis=0)  11.7 us
  transfers between devices with their start and end apart: 2, of which 1 were waited for; matrix products, arithmetic and copies ran while one was open for 8% of the time, Pallas kernels for 0%

commit v1 on v0

v1 whole, which is shorter than its diff:
```python
import functools
import math

import jax
import jax.numpy as jnp
from jax import lax
from jax.experimental import pallas as pl
from jax.experimental.pallas import tpu as pltpu
from jax.sharding import Mesh, PartitionSpec as P

BLOCK = 128
HEAD = 128
ROWS = 4
RING = 8
NEG_FILL = -1e30
ROPE_BASE = 10000.0
STAT = 48
CHUNKS = ((0, 6), (6, 2))
GROUPS = (((0, 1), (2,), (3,), (4,)), ((0, 1, 2), (3, 4)))


def rotate(inputs, angles):
    row_count = inputs.shape[0]
    head_count = angles.shape[0]
    widened = inputs.astype(jnp.float32).reshape(row_count, head_count, -1)
    half_width = widened.shape[-1] // 2
    inv_freq = ROPE_BASE ** (-jnp.arange(half_width).astype(jnp.float32) / half_width)
    phases = angles.T[:, :, None] * inv_freq
    cos_part = jnp.cos(phases)
    sin_part = jnp.sin(phases)
    first_half = widened[..., :half_width]
    second_half = widened[..., half_width:]
    rotated = jnp.concatenate(
        [
            first_half * cos_part - second_half * sin_part,
            second_half * cos_part + first_half * sin_part,
        ],
        axis=-1,
    )
    return rotated.reshape(row_count, -1).astype(jnp.bfloat16)


def attend_kernel(offsets, heads, first, last, meta, *refs):
    count = len(offsets)
    q_ref = refs[0]
    k_refs = refs[1 : 1 + count]
    v_refs = refs[1 + count : 1 + 2 * count]
    rest = list(refs[1 + 2 * count :])
    given = None
    if not first:
        given = rest[:3]
        rest = rest[3:]
    if last:
        acc0_ref, m0_ref, l0_ref, packed_ref, acc, m_run, l_run = rest
    else:
        acc, m_run, l_run = rest
    r = pl.program_id(0)
    my_y, my_z = meta[0], meta[1]
    scale = HEAD**-0.5 * math.log2(math.e)

    if first:
        acc[...] = jnp.zeros_like(acc)
        m_run[...] = jnp.full_like(m_run, NEG_FILL)
        l_run[...] = jnp.zeros_like(l_run)
    else:
        acc[...] = given[0][...]
        m_run[...] = given[1][...]
        l_run[...] = given[2][...]

    def pair(qb, kb, k_ref, v_ref, causal):
        q_rows = pl.ds(pl.multiple_of(qb * BLOCK, BLOCK), BLOCK)
        k_rows = pl.ds(pl.multiple_of(kb * BLOCK, BLOCK), BLOCK)
        for h in range(heads):
            cols = slice(h * HEAD, (h + 1) * HEAD)
            scores = lax.dot_general(
                k_ref[k_rows, cols],
                q_ref[0, q_rows, cols],
                (((1,), (1,)), ((), ())),
                preferred_element_type=jnp.float32,
            )
            if causal:
                key_pos = lax.broadcasted_iota(jnp.int32, scores.shape, 0)
                query_pos = lax.broadcasted_iota(jnp.int32, scores.shape, 1)
                scores = jnp.where(key_pos <= query_pos, scores, NEG_FILL)
            m_old = m_run[qb, h : h + 1, :]
            m_new = jnp.maximum(m_old, jnp.max(scores, axis=0, keepdims=True))
            weights = jnp.exp2((scores - m_new) * scale)
            fade = jnp.exp2((m_old - m_new) * scale)
            m_run[qb, h : h + 1, :] = m_new
            l_run[qb, h : h + 1, :] = l_run[qb, h : h + 1, :] * fade + jnp.sum(
                weights, axis=0, keepdims=True
            )
            mixed = jnp.dot(
                v_ref[kb, cols, :], weights.astype(jnp.bfloat16), preferred_element_type=jnp.float32
            )
            acc[qb, cols, :] = acc[qb, cols, :] * fade + mixed

    @pl.when(my_y + r < ROWS)
    def _():
        def per_block(qb, carry):
            own = ((my_y + r) * RING + my_z) * 4 + qb
            if 0 in offsets:
                at = offsets.index(0)

                @pl.when(r == 0)
                def _():
                    pair(qb, qb, k_refs[at], v_refs[at], True)

            def per_pick(j, inner):
                blk = meta[2 + (r * 4 + qb) * 8 + j]
                away = lax.rem((blk // 4) % RING - my_z + RING, RING)
                here = jnp.logical_and(blk // (4 * RING) == my_y, blk != own)
                for at, offset in enumerate(offsets):

                    @pl.when(jnp.logical_and(here, away == offset % RING))
                    def _(at=at):
                        pair(qb, blk % 4, k_refs[at], v_refs[at], False)

                return inner

            return lax.fori_loop(0, 8, per_pick, carry)

        lax.fori_loop(0, 4, per_block, 0)

    if last:

        @pl.when(r == 0)
        def _():
            acc0_ref[...] = acc[...]
            m0_ref[...] = m_run[...]
            l0_ref[...] = l_run[...]

        @pl.when(r > 0)
        def _():
            def pack(qb, carry):
                m_all, l_all = m_run[qb], l_run[qb]
                pieces = []
                for value in (m_all, l_all):
                    for _ in range(3):
                        piece = value.astype(jnp.bfloat16).astype(jnp.float32)
                        pieces.append(piece)
                        value = value - piece
                packed_ref[0, qb, heads * HEAD :, :] = jnp.concatenate(pieces, axis=0).astype(
                    jnp.bfloat16
                )
                for h in range(heads):
                    cols = slice(h * HEAD, (h + 1) * HEAD)
                    total = l_run[qb, h : h + 1, :]
                    inverse = 1.0 / jnp.where(total > 0, total, 1.0)
                    packed_ref[0, qb, cols, :] = (acc[qb, cols, :] * inverse).astype(jnp.bfloat16)
                return carry

            lax.fori_loop(0, 4, pack, 0)


def attend(meta, queries, chunk, offsets, keys, values, state, last):
    first_head, heads = chunk
    width = heads * HEAD
    first = state is None
    acc_spec = pl.BlockSpec((4, width, BLOCK), lambda r, meta: (r, 0, 0))
    run_spec = pl.BlockSpec((4, 8, BLOCK), lambda r, meta: (r, 0, 0))
    state_specs = [acc_spec, run_spec, run_spec]
    in_specs = [pl.BlockSpec((1, 512, width), lambda r, meta: (r, 0, first_head // heads))]
    in_specs += [pl.BlockSpec((512, width), lambda r, meta: (0, 0)) for _ in offsets]
    in_specs += [pl.BlockSpec((4, width, BLOCK), lambda r, meta: (0, 0, 0)) for _ in offsets]
    operands = [queries, *keys, *values]
    if not first:
        in_specs += state_specs
        operands += list(state)
    f32 = jnp.float32
    scratch = []
    if last:
        out_shape = [
            jax.ShapeDtypeStruct((4, width, BLOCK), f32),
            jax.ShapeDtypeStruct((4, 8, BLOCK), f32),
            jax.ShapeDtypeStruct((4, 8, BLOCK), f32),
            jax.ShapeDtypeStruct((3, 4, width + STAT, BLOCK), jnp.bfloat16),
        ]
        out_specs = [
            pl.BlockSpec((4, width, BLOCK), lambda r, meta: (0, 0, 0)),
            pl.BlockSpec((4, 8, BLOCK), lambda r, meta: (0, 0, 0)),
            pl.BlockSpec((4, 8, BLOCK), lambda r, meta: (0, 0, 0)),
            pl.BlockSpec((1, 4, width + STAT, BLOCK), lambda r, meta: (jnp.maximum(r - 1, 0), 0, 0, 0)),
        ]
        scratch = [
            pltpu.VMEM((4, width, BLOCK), f32),
            pltpu.VMEM((4, 8, BLOCK), f32),
            pltpu.VMEM((4, 8, BLOCK), f32),
        ]
    else:
        out_shape = [
            jax.ShapeDtypeStruct((16, width, BLOCK), f32),
            jax.ShapeDtypeStruct((16, 8, BLOCK), f32),
            jax.ShapeDtypeStruct((16, 8, BLOCK), f32),
        ]
        out_specs = state_specs
    pairs = 10 * len(offsets)
    return pl.pallas_call(
        functools.partial(attend_kernel, offsets, heads, first, last),
        out_shape=out_shape,
        grid_spec=pltpu.PrefetchScalarGridSpec(
            num_scalar_prefetch=1,
            grid=(ROWS,),
            in_specs=in_specs,
            out_specs=out_specs,
            scratch_shapes=scratch,
        ),
        compiler_params=pltpu.CompilerParams(vmem_limit_bytes=40 << 20),
        cost_estimate=pl.CostEstimate(
            flops=pairs * heads * 4 * BLOCK**3,
            bytes_accessed=(4 << 20) + 16 * width * BLOCK * 8,
            transcendentals=pairs * heads * BLOCK * BLOCK,
        ),
        name=f"attend_{first_head}_{'_'.join(str(o % RING) for o in offsets)}",
    )(meta, *operands)


def join_kernel(heads, acc_ref, m_ref, l_ref, one, two, three, *rest):
    out_ref = rest[-1]
    width = heads * HEAD
    tops, sums = [m_ref[0]], [l_ref[0]]
    for part in (one, two, three):
        stats = part[0, width:, :].astype(jnp.float32)
        top = (stats[16:24] + stats[8:16]) + stats[0:8]
        total = (stats[40:48] + stats[32:40]) + stats[24:32]
        tops.append(jnp.where(total > 0, top, NEG_FILL))
        sums.append(total)
    scale = HEAD**-0.5 * math.log2(math.e)
    highest = jnp.maximum(jnp.maximum(tops[0], tops[1]), jnp.maximum(tops[2], tops[3]))
    fades = [jnp.exp2((top - highest) * scale) for top in tops]
    shares = [fades[0]] + [fades[i] * sums[i] for i in (1, 2, 3)]
    whole = fades[0] * sums[0] + shares[1] + shares[2] + shares[3]
    inverse = 1.0 / whole
    for h in range(heads):
        cols = slice(h * HEAD, (h + 1) * HEAD)
        mixed = acc_ref[0, cols, :] * shares[0][h : h + 1, :]
        for i, part in enumerate((one, two, three)):
            mixed += part[0, cols, :].astype(jnp.float32) * shares[i + 1][h : h + 1, :]
        mixed = mixed * inverse[h : h + 1, :]
        out_ref[:, cols] = mixed.T.astype(jnp.bfloat16)


def join(chunk, state, parts, out):
    first_head, heads = chunk
    width = heads * HEAD
    in_specs = [
        pl.BlockSpec((1, width, BLOCK), lambda b: (b, 0, 0)),
        pl.BlockSpec((1, 8, BLOCK), lambda b: (b, 0, 0)),
        pl.BlockSpec((1, 8, BLOCK), lambda b: (b, 0, 0)),
    ] + [pl.BlockSpec((1, width + STAT, BLOCK), lambda b: (b, 0, 0))] * 3
    operands = [*state, *parts]
    aliases = {}
    if out is not None:
        aliases = {len(operands): 0}
        in_specs.append(pl.BlockSpec(memory_space=pl.ANY))
        operands.append(out)
    return pl.pallas_call(
        functools.partial(join_kernel, heads),
        out_shape=jax.ShapeDtypeStruct((512, 1024), jnp.bfloat16),
        grid=(4,),
        in_specs=in_specs,
        out_specs=pl.BlockSpec((BLOCK, width), lambda b: (b, first_head // heads)),
        input_output_aliases=aliases,
        compiler_params=pltpu.CompilerParams(vmem_limit_bytes=24 << 20),
        cost_estimate=pl.CostEstimate(
            flops=512 * width * 10, bytes_accessed=512 * width * 14, transcendentals=0
        ),
        name=f"join_{first_head}",
    )(*operands)


def shift(value, axis, step):
    size = lax.axis_size(axis)
    return lax.ppermute(value, axis, [(i, (i + step) % size) for i in range(size)])


def to_row(value, step):
    moves = [(i, i + step) for i in range(ROWS) if 0 <= i + step < ROWS]
    return lax.ppermute(value, "y", moves)


def swap(value, axis, bit):
    size = lax.axis_size(axis)
    return lax.ppermute(value, axis, [(i, i ^ bit) for i in range(size)])


def shards(query_states, key_states, value_states, gate_logits, selected_blocks):
    my_y, my_z = lax.axis_index("y"), lax.axis_index("z")
    gate_values = jax.nn.sigmoid(gate_logits.astype(jnp.float32))
    total = jnp.sum(gate_values, axis=1, keepdims=True)
    before = jnp.zeros_like(total)
    picks = [selected_blocks] + [to_row(selected_blocks, -s) for s in (1, 2, 3)]
    for bit in (1, 2, 4):
        other = swap(total, "z", bit)
        before = before + jnp.where((my_z & bit) != 0, other, 0.0)
        total = total + other
    value_states, total = lax.optimization_barrier((value_states, total))
    value_blocks = value_states.reshape(4, BLOCK, -1).transpose(0, 2, 1)
    for bit in (1, 2):
        other = swap(total, "y", bit)
        before = before + jnp.where((my_y & bit) != 0, other, 0.0)
        total = total + other
    angles = before + jnp.cumsum(gate_values, axis=1)
    key_rot = rotate(key_states, angles)
    query_rot = rotate(query_states, angles)
    meta = jnp.concatenate(
        [jnp.stack([my_y, my_z]).astype(jnp.int32)] + [p.reshape(-1) for p in picks]
    )
    queries = jnp.stack([query_rot] + [to_row(query_rot, -s) for s in (1, 2, 3)])

    rings = []
    for first_head, heads in CHUNKS:
        lo, hi = first_head * HEAD, (first_head + heads) * HEAD
        rings.append({0: (key_rot[:, lo:hi], value_blocks[:, lo:hi])})
    for chunk, ring in zip(CHUNKS, rings):
        for sign in (1, -1):
            key, value = ring[0]
            for step in (1, 2, 3):
                value = shift(value, "z", sign)
                key = shift(key, "z", sign)
                ring[-sign * step] = (key, value)
        half = chunk[1] // 2 * HEAD
        far = [
            (
                shift(ring[-sign * 3][0][:, part], "z", sign),
                shift(ring[-sign * 3][1][:, part], "z", sign),
            )
            for sign, part in ((1, slice(0, half)), (-1, slice(half, None)))
        ]
        ring[4] = tuple(jnp.concatenate([far[0][i], far[1][i]], axis=1) for i in (0, 1))

    out = None
    for chunk, ring, groups in zip(CHUNKS, rings, GROUPS):
        state = None
        for index, group in enumerate(groups):
            offsets = []
            for distance in group:
                offsets += [distance] if distance in (0, 4) else [-distance, distance]
            state = attend(
                meta,
                queries,
                chunk,
                tuple(offsets),
                [ring[o][0] for o in offsets],
                [ring[o][1] for o in offsets],
                state,
                index == len(groups) - 1,
            )
        packed = state[3]
        parts = [to_row(packed[s - 1], s) for s in (1, 2, 3)]
        out = join(chunk, state[:3], parts, out)
    return out


def solution(mesh):
    grid = Mesh(mesh.devices.reshape(2, ROWS, RING, 4), ("dp", "y", "z", "head"))
    tokens = ("dp", "y", "z")
    placed = (
        P(tokens, "head"),
        P(tokens, "head"),
        P(tokens, "head"),
        P("head", tokens),
        P(tokens, None),
    )
    return jax.shard_map(
        shards, mesh=grid, in_specs=placed, out_specs=P(tokens, "head"), check_vma=False
    )
```

time: 564 us -> 414 us (0.73); the launches traced: 563 us -> 407 us
  blocking collectives: 252 us -> 0 us
  Pallas kernels: 0 us -> 176 us
  starting transfers between devices: 25.4 us -> 103 us
  waiting for transfers between devices: 134 us -> 79.7 us
  other arithmetic: 67.6 us -> 26.7 us
  local copies, waits for them, and re-layouts: 54.3 us -> 20.2 us
  matrix products: 28 us -> 0 us
    all_to_all x1 -> x0, blocking collectives: 177 us -> none  [shards(): lax.all_to_all(jnp.take(key_blocks, pick_blk, axis=0), 'ctx', split_axis=...]
    pallas_call x0 -> x8, Pallas kernels: none -> 176 us  [the longest x6 172 us: attend(): pl.pallas_call(functools.partial(attend_kernel, offsets, heads, first, la...]
    all_to_all x2 -> x0, waiting for transfers between devices: 134 us -> none  [the longest x1 134 us: shards(): lax.all_to_all(send_values, 'ctx', split_axis=0, concat_axis=0, tiled=True)]
    ppermute x0 -> x49, starting transfers between devices: none -> 103 us  [the longest x32 71.5 us: shift(): lax.ppermute(value, axis, [(i, (i + step) % size) for i in range(size)])]
    ppermute x0 -> x49, waiting for transfers between devices: none -> 79.7 us  [the longest x12 48.3 us: to_row(): return lax.ppermute(value, 'y', moves)]
    unnamed x1 -> x0, blocking collectives: 74.8 us -> none
    dot_general x4 -> x0, matrix products: 28 us -> none  [the longest x1 12.6 us: attend(): jnp.einsum('gqhd,gkhd->ghqk', query_blocks, sel_keys, preferred_element_t...]
    gather x4 -> x0, local copies, waits for them, and re-layouts: 27.5 us -> none  [the longest x1 8.75 us: attend(): jnp.take(pool_keys, slot_idx.reshape(-1), axis=0)]
  transfers between devices with their start and end apart: 2 -> 49, of which waited for: 1 -> 15; matrix products, arithmetic and copies ran while one was open for 8% -> 9% of each run, Pallas kernels for 0% -> 43%
where the time goes in v1:
time: 414 us; the launch traced here: 407 us
  Pallas kernels  176 us (43%)
  starting transfers between devices  103 us (25%)
  waiting for transfers between devices  79.7 us (19%)
  other arithmetic  26.7 us (6%)
  local copies, waits for them, and re-layouts  20.2 us (5%)
    pallas_call x6, Pallas kernels, attend(): pl.pallas_call(functools.partial(attend_kernel, offsets, heads, first, la...  172 us
    ppermute x32, starting transfers between devices, shift(): lax.ppermute(value, axis, [(i, (i + step) % size) for i in range(size)])  71.5 us
    ppermute x12, waiting for transfers between devices, to_row(): return lax.ppermute(value, 'y', moves)  48.3 us
    ppermute x32, waiting for transfers between devices, shift(): lax.ppermute(value, axis, [(i, (i + step) % size) for i in range(size)])  24.6 us
    ppermute x5, starting transfers between devices, swap(): return lax.ppermute(value, axis, [(i, i ^ bit) for i in range(size)])  16.1 us
    ppermute x12, starting transfers between devices, to_row(): return lax.ppermute(value, 'y', moves)  15.6 us
    unnamed x60, local copies, waits for them, and re-layouts  11.9 us
    another operation x3, other arithmetic  11.8 us
  transfers between devices with their start and end apart: 49, of which 15 were waited for; matrix products, arithmetic and copies ran while one was open for 9% of the time, Pallas kernels for 43%

profile of v1, /device:TPU:2, one launch (start us, length us, event | category | flops | bytes accessed | tf_op | source)
XLA Modules:
  0.0 406.8 jit_solution(9647588833741107326)
XLA Ops:
  7.5 3.4 collective-permute-start.4
  12.3 5.9 %collective-permute-start.5 = (f32[8,1]{0,1:T(1,128)S(1)}, f32[8,1]{0,1:T(1,128)S(1)}, u32[]{:S(2)}, u32[]{:S(2)}) collective-permute-start(f32[8,1]{0,1:T(1,128)S(1)} %add.46), channel_id=1, source_target_pairs={{0,16},{4,20},{8,24},{12,28},{16,0},{20,4},{24,8},{28,12},{1,17},{... | collective-permute-start | bytes 104 | tf_op jit(solution)/shard_map/ppermute | solution.py:284
  22.6 3.7 collective-permute-start.42
  35.1 10.7 %fusion.11 = (bf16[512,8,64]{2,1,0:T(8,128)(2,1)S(1)}, bf16[512,8,64]{2,1,0:T(8,128)(2,1)S(1)}) fusion(f32[512,8,128]{2,1,0:T(8,128)} %bitcast.45, f32[64]{0:T(128)S(1)} %multiply_power_fusion, f32[512,8]{1,0:T(8,128)S(1)} %copy.7), kind=kLoop, calls=%fused_computation.14 | loop fusion | flops 2359296 | bytes 3162368 | tf_op jit(solution)/shard_map/convert.2
  56.3 4.2 %collective-permute-done = s32[4,8]{1,0:T(4,128)S(1)} collective-permute-done((s32[4,8]{1,0:T(4,128)S(1)}, s32[4,8]{1,0:T(4,128)S(1)}, u32[]{:S(2)}, u32[]{:S(2)}) %collective-permute-start) | collective-permute-done | bytes 160 | tf_op jit(solution)/shard_map/ppermute | solution.py:279
  61.8 5.7 %collective-permute-done.1 = s32[4,8]{1,0:T(4,128)S(1)} collective-permute-done((s32[4,8]{1,0:T(4,128)S(1)}, s32[4,8]{1,0:T(4,128)S(1)}, u32[]{:S(2)}, u32[]{:S(2)}) %collective-permute-start.1) | collective-permute-done | bytes 160 | tf_op jit(solution)/shard_map/ppermute | solution.py:279
  69.8 4.4 %collective-permute-done.2 = s32[4,8]{1,0:T(4,128)S(1)} collective-permute-done((s32[4,8]{1,0:T(4,128)S(1)}, s32[4,8]{1,0:T(4,128)S(1)}, u32[]{:S(2)}, u32[]{:S(2)}) %collective-permute-start.2) | collective-permute-done | bytes 160 | tf_op jit(solution)/shard_map/ppermute | solution.py:279
  74.3 3.5 collective-permute-start.35
  77.8 7.5 %collective-permute-done.39.refs_3_ = bf16[4,768,128]{2,1,0:T(8,128)(2,1)S(1)} collective-permute-done((bf16[4,768,128]{2,1,0:T(8,128)(2,1)S(1)}, bf16[4,768,128]{2,1,0:T(8,128)(2,1)S(1)}, u32[]{:S(2)}, u32[]{:S(2)}) %collective-permute-start.39) | collective-permute-done | bytes 786464 | tf_op jit(solution)/shard_map/ppermute | solution.py:274
  91.7 8.7 %fusion.8 = (bf16[512,8,64]{2,1,0:T(8,128)(2,1)S(1)}, bf16[512,8,64]{2,1,0:T(8,128)(2,1)S(1)}) fusion(f32[512,8,128]{2,1,0:T(8,128)S(1)} %bitcast.46, f32[64]{0:T(128)S(1)} %multiply_power_fusion, f32[512,8]{1,0:T(8,128)S(1)} %copy-done.23), kind=kLoop, calls=%fused_computation.11 | loop fusion | flops 2359296 | bytes 3162368 | tf_op jit(solution)/shard_map/sub | solution.py:35
  102.3 15.3 %collective-permute-done.22.refs_8_ = bf16[4,256,128]{2,1,0:T(8,128)(2,1)S(1)} collective-permute-done((bf16[4,256,128]{2,1,0:T(8,128)(2,1)S(1)}, bf16[4,256,128]{2,1,0:T(8,128)(2,1)S(1)}, u32[]{:S(2)}, u32[]{:S(2)}) %collective-permute-start.22) | collective-permute-done | bytes 262176 | tf_op jit(solution)/shard_map/ppermute | solution.py:274
  122.0 3.4 collective-permute-start.36
  129.2 9.5 %collective-permute-done.8 = bf16[512,1024]{1,0:T(8,128)(2,1)} collective-permute-done((bf16[512,1024]{1,0:T(8,128)(2,1)}, bf16[512,1024]{1,0:T(8,128)(2,1)}, u32[]{:S(2)}, u32[]{:S(2)}) %collective-permute-start.8) | collective-permute-done | bytes 1048608 | tf_op jit(solution)/shard_map/ppermute | solution.py:279
  141.9 3.7 collective-permute-start.14
  145.6 18.7 %collective-permute-done.10 = bf16[512,1024]{1,0:T(8,128)(2,1)} collective-permute-done((bf16[512,1024]{1,0:T(8,128)(2,1)}, bf16[512,1024]{1,0:T(8,128)(2,1)}, u32[]{:S(2)}, u32[]{:S(2)}) %collective-permute-start.10) | collective-permute-done | bytes 1048608 | tf_op jit(solution)/shard_map/ppermute | solution.py:279
  172.7 11.2 %collective-permute-start.33 = (bf16[512,384]{1,0:T(8,128)(2,1)S(1)}, bf16[512,384]{1,0:T(8,128)(2,1)S(1)}, u32[]{:S(2)}, u32[]{:S(2)}) collective-permute-start(bf16[512,384]{1,0:T(8,128)(2,1)S(1)} %slice.108), channel_id=1, source_target_pairs={{0,4},{4,8},{8,12},{12,16},{16,20},{20,24},{24,28},{28,0},{1,5},{5... | collective-permute-start | bytes 1179656 | tf_op jit(solution)/shard_map/ppermute | solution.py:274
  184.9 55.7 %attend_0_0_7_1.1 = (f32[16,768,128]{2,1,0:T(8,128)}, f32[16,8,128]{2,1,0:T(8,128)S(1)}, f32[16,8,128]{2,1,0:T(8,128)S(1)}) custom-call(s32[130]{0:T(256)S(1)} %concatenate.22.meta, bf16[4,512,1024]{2,1,0:T(8,128)(2,1)S(1)} %pad_maximum_fusion.refs_0_, bf16[512,768]{1,0:T(8,128)(2,1)S(1)} %slice.107.refs_1_, bf16[512,768]{1,0:T(8,128)(2,1)S(1)} %copy-done.7, ...), custom_call_target="tpu_custom_call" | custom-call | flops 1509949440 | bytes 16777216 | tf_op jit(solution)/shard_map/attend_0_0_7_1/pallas_call | solution.py:198
  243.9 28.0 %attend_0_6_2.1 = (f32[16,768,128]{2,1,0:T(8,128)S(1)}, f32[16,8,128]{2,1,0:T(8,128)S(1)}, f32[16,8,128]{2,1,0:T(8,128)S(1)}) custom-call(s32[130]{0:T(256)S(1)} %concatenate.22.meta, bf16[4,512,1024]{2,1,0:T(8,128)(2,1)S(1)} %pad_maximum_fusion.refs_0_, bf16[512,768]{1,0:T(8,128)(2,1)} %collective-permute-done.31.refs_1_, ...), custom_call_target="tpu_custom_call" | custom-call | flops 1006632960 | bytes 16777216 | tf_op jit(solution)/shard_map/attend_0_6_2/pallas_call | solution.py:198
  274.6 21.4 %attend_0_5_3.1 = (f32[16,768,128]{2,1,0:T(8,128)S(1)}, f32[16,8,128]{2,1,0:T(8,128)S(1)}, f32[16,8,128]{2,1,0:T(8,128)S(1)}) custom-call(s32[130]{0:T(256)S(1)} %concatenate.22.meta, bf16[4,512,1024]{2,1,0:T(8,128)(2,1)S(1)} %pad_maximum_fusion.refs_0_, bf16[512,768]{1,0:T(8,128)(2,1)} %collective-permute-done.32.refs_1_, ...), custom_call_target="tpu_custom_call" | custom-call | flops 1006632960 | bytes 16777216 | tf_op jit(solution)/shard_map/attend_0_5_3/pallas_call | solution.py:198
  298.8 12.3 %collective-permute-start.24 = (bf16[4,256,128]{2,1,0:T(8,128)(2,1)S(1)}, bf16[4,256,128]{2,1,0:T(8,128)(2,1)S(1)}, u32[]{:S(2)}, u32[]{:S(2)}) collective-permute-start(bf16[4,256,128]{2,1,0:T(8,128)(2,1)S(1)} %collective-permute-done.23.refs_10_), channel_id=1, source_target_pairs={{0,28},{4,0},{8,4},{12,8},{16,12},{20,16},{24,20},{28,24},{1,29},{... | collective-permute-start | bytes 786440 | tf_op jit(solution)/shard_map/ppermute | solution.py:274
  314.4 16.0 %attend_0_4.1 = (f32[4,768,128]{2,1,0:T(8,128)S(1)}, f32[4,8,128]{2,1,0:T(8,128)S(1)}, f32[4,8,128]{2,1,0:T(8,128)S(1)}, bf16[3,4,816,128]{3,2,1,0:T(8,128)(2,1)S(1)}) custom-call(s32[130]{0:T(256)S(1)} %concatenate.22.meta, bf16[4,512,1024]{2,1,0:T(8,128)(2,1)S(1)} %pad_maximum_fusion.refs_0_, bf16[512,768]{1,0:T(8,128)(2,1)S(1)} %pad_maximum_fusion.2.refs_1_, ...), custom_call_target="tpu_custom_call" | custom-call | flops 503316480 | bytes 16777216 | tf_op jit(solution)/shard_map/attend_0_4/pallas_call | solution.py:198
  332.5 5.9 %collective-permute-start.26 = (bf16[4,128,128]{2,1,0:T(8,128)(2,1)S(1)}, bf16[4,128,128]{2,1,0:T(8,128)(2,1)S(1)}, u32[]{:S(2)}, u32[]{:S(2)}) collective-permute-start(bf16[4,128,128]{2,1,0:T(8,128)(2,1)S(1)} %slice.106), channel_id=1, source_target_pairs={{0,28},{4,0},{8,4},{12,8},{16,12},{20,16},{24,20},{28,24},{1,29},{... | collective-permute-start | bytes 393224 | tf_op jit(solution)/shard_map/ppermute | solution.py:274
  344.7 35.2 %attend_6_0_7_1_6_2.1 = (f32[16,256,128]{2,1,0:T(8,128)S(1)}, f32[16,8,128]{2,1,0:T(8,128)S(1)}, f32[16,8,128]{2,1,0:T(8,128)S(1)}) custom-call(s32[130]{0:T(256)S(1)} %concatenate.22.meta, bf16[4,512,1024]{2,1,0:T(8,128)(2,1)S(1)} %pad_maximum_fusion.refs_0_, bf16[512,256]{1,0:T(8,128)(2,1)S(1)} %slice.101.refs_1_, ...), custom_call_target="tpu_custom_call" | custom-call | flops 838860800 | bytes 8388608 | tf_op jit(solution)/shard_map/attend_6_0_7_1_6_2/pallas_call | solution.py:198
  379.9 15.9 %attend_6_5_3_4.1 = (f32[4,256,128]{2,1,0:T(8,128)S(1)}, f32[4,8,128]{2,1,0:T(8,128)S(1)}, f32[4,8,128]{2,1,0:T(8,128)S(1)}, bf16[3,4,304,128]{3,2,1,0:T(8,128)(2,1)S(1)}) custom-call(s32[130]{0:T(256)S(1)} %concatenate.22.meta, bf16[4,512,1024]{2,1,0:T(8,128)(2,1)S(1)} %pad_maximum_fusion.refs_0_, bf16[512,256]{1,0:T(8,128)(2,1)S(1)} %collective-permute-done.13.refs_1_, ...), custom_call_target="tpu_custom_call" | custom-call | flops 503316480 | bytes 8388608 | tf_op jit(solution)/shard_map/attend_6_5_3_4/pallas_call | solution.py:198
  (188 shorter events, 96.2 us)
Async XLA Ops:
  50.0 35.3 %collective-permute-start.39 = (bf16[4,768,128]{2,1,0:T(8,128)(2,1)S(1)}, bf16[4,768,128]{2,1,0:T(8,128)(2,1)S(1)}, u32[]{:S(2)}, u32[]{:S(2)}) collective-permute-start(bf16[4,768,128]{2,1,0:T(8,128)(2,1)S(1)} %collective-permute-done.38.refs_5_), channel_id=1, source_target_pairs={{0,4},{4,8},{8,12},{12,16},{16,20},{20,24},{24,28},{28,0},{1,5},{5... | collective-permute-start | bytes 2359304 | tf_op jit(solution)/shard_map/ppermute | solution.py:274
  50.9 34.4 %collective-permute-start.43 = (bf16[4,768,128]{2,1,0:T(8,128)(2,1)S(1)}, bf16[4,768,128]{2,1,0:T(8,128)(2,1)S(1)}, u32[]{:S(2)}, u32[]{:S(2)}) collective-permute-start(bf16[4,768,128]{2,1,0:T(8,128)(2,1)S(1)} %collective-permute-done.42.refs_6_), channel_id=1, source_target_pairs={{0,28},{4,0},{8,4},{12,8},{16,12},{20,16},{24,20},{28,24},{1,29},{... | collective-permute-start | bytes 2359304 | tf_op jit(solution)/shard_map/ppermute | solution.py:274
  74.2 44.7 %collective-permute-start.31 = (bf16[512,768]{1,0:T(8,128)(2,1)S(1)}, bf16[512,768]{1,0:T(8,128)(2,1)}, u32[]{:S(2)}, u32[]{:S(2)}) collective-permute-start(bf16[512,768]{1,0:T(8,128)(2,1)S(1)} %collective-permute-done.30.refs_2_), channel_id=1, source_target_pairs={{0,4},{4,8},{8,12},{12,16},{16,20},{20,24},{24,28},{28,0},{1,5},{5... | collective-permute-start | bytes 2359304 | tf_op jit(solution)/shard_map/ppermute | solution.py:274
  74.3 45.9 %collective-permute-start.35 = (bf16[512,768]{1,0:T(8,128)(2,1)S(1)}, bf16[512,768]{1,0:T(8,128)(2,1)}, u32[]{:S(2)}, u32[]{:S(2)}) collective-permute-start(bf16[512,768]{1,0:T(8,128)(2,1)S(1)} %collective-permute-done.34.refs_3_), channel_id=1, source_target_pairs={{0,28},{4,0},{8,4},{12,8},{16,12},{20,16},{24,20},{28,24},{1,29},{... | collective-permute-start | bytes 2359304 | tf_op jit(solution)/shard_map/ppermute | solution.py:274
  85.3 36.1 %collective-permute-start.40 = (bf16[4,768,128]{2,1,0:T(8,128)(2,1)S(1)}, bf16[4,768,128]{2,1,0:T(8,128)(2,1)S(1)}, u32[]{:S(2)}, u32[]{:S(2)}) collective-permute-start(bf16[4,768,128]{2,1,0:T(8,128)(2,1)S(1)} %collective-permute-done.39.refs_3_), channel_id=1, source_target_pairs={{0,4},{4,8},{8,12},{12,16},{16,20},{20,24},{24,28},{28,0},{1,5},{5... | collective-permute-start | bytes 2359304 | tf_op jit(solution)/shard_map/ppermute | solution.py:274
  85.4 36.7 %collective-permute-start.44 = (bf16[4,768,128]{2,1,0:T(8,128)(2,1)S(1)}, bf16[4,768,128]{2,1,0:T(8,128)(2,1)S(1)}, u32[]{:S(2)}, u32[]{:S(2)}) collective-permute-start(bf16[4,768,128]{2,1,0:T(8,128)(2,1)S(1)} %collective-permute-done.43.refs_4_), channel_id=1, source_target_pairs={{0,28},{4,0},{8,4},{12,8},{16,12},{20,16},{24,20},{28,24},{1,29},{... | collective-permute-start | bytes 2359304 | tf_op jit(solution)/shard_map/ppermute | solution.py:274
  120.2 44.1 %collective-permute-start.10 = (bf16[512,1024]{1,0:T(8,128)(2,1)}, bf16[512,1024]{1,0:T(8,128)(2,1)}, u32[]{:S(2)}, u32[]{:S(2)}) collective-permute-start(bf16[512,1024]{1,0:T(8,128)(2,1)} %bitcast.44), channel_id=1, source_target_pairs={{96,0},{97,1},{98,2},{99,3},{100,4},{101,5},{102,6},{103,7},{104,8... | collective-permute-start | bytes 3145736 | tf_op jit(solution)/shard_map/ppermute | solution.py:279
  121.5 43.0 %collective-permute-start.32 = (bf16[512,768]{1,0:T(8,128)(2,1)}, bf16[512,768]{1,0:T(8,128)(2,1)}, u32[]{:S(2)}, u32[]{:S(2)}) collective-permute-start(bf16[512,768]{1,0:T(8,128)(2,1)} %collective-permute-done.31.refs_1_), channel_id=1, source_target_pairs={{0,4},{4,8},{8,12},{12,16},{16,20},{20,24},{24,28},{28,0},{1,5},{5... | collective-permute-start | bytes 2359304 | tf_op jit(solution)/shard_map/ppermute | solution.py:274
  122.0 45.7 %collective-permute-start.36 = (bf16[512,768]{1,0:T(8,128)(2,1)}, bf16[512,768]{1,0:T(8,128)(2,1)}, u32[]{:S(2)}, u32[]{:S(2)}) collective-permute-start(bf16[512,768]{1,0:T(8,128)(2,1)} %collective-permute-done.35.refs_2_), channel_id=1, source_target_pairs={{0,28},{4,0},{8,4},{12,8},{16,12},{20,16},{24,20},{28,24},{1,29},{... | collective-permute-start | bytes 2359304 | tf_op jit(solution)/shard_map/ppermute | solution.py:274
  138.7 33.9 %collective-permute-start.11 = (bf16[512,256]{1,0:T(8,128)(2,1)S(1)}, bf16[512,256]{1,0:T(8,128)(2,1)S(1)}, u32[]{:S(2)}, u32[]{:S(2)}) collective-permute-start(bf16[512,256]{1,0:T(8,128)(2,1)S(1)} %slice.101.refs_1_), channel_id=1, source_target_pairs={{0,4},{4,8},{8,12},{12,16},{16,20},{20,24},{24,28},{28,0},{1,5},{5... | collective-permute-start | bytes 786440 | tf_op jit(solution)/shard_map/ppermute | solution.py:274
  141.9 41.9 %collective-permute-start.14 = (bf16[512,256]{1,0:T(8,128)(2,1)S(1)}, bf16[512,256]{1,0:T(8,128)(2,1)S(1)}, u32[]{:S(2)}, u32[]{:S(2)}) collective-permute-start(bf16[512,256]{1,0:T(8,128)(2,1)S(1)} %slice.101.refs_1_), channel_id=1, source_target_pairs={{0,28},{4,0},{8,4},{12,8},{16,12},{20,16},{24,20},{28,24},{1,29},{... | collective-permute-start | bytes 786440 | tf_op jit(solution)/shard_map/ppermute | solution.py:274
  164.3 76.3 %collective-permute-start.20 = (bf16[4,256,128]{2,1,0:T(8,128)(2,1)S(1)}, bf16[4,256,128]{2,1,0:T(8,128)(2,1)S(1)}, u32[]{:S(2)}, u32[]{:S(2)}) collective-permute-start(bf16[4,256,128]{2,1,0:T(8,128)(2,1)S(1)} %copy-done.15), channel_id=1, source_target_pairs={{0,4},{4,8},{8,12},{12,16},{16,20},{20,24},{24,28},{28,0},{1,5},{5... | collective-permute-start | bytes 786440 | tf_op jit(solution)/shard_map/ppermute | solution.py:274
  164.4 76.2 %collective-permute-start.41 = (bf16[4,384,128]{2,1,0:T(8,128)(2,1)S(1)}, bf16[4,384,128]{2,1,0:T(8,128)(2,1)S(1)}, u32[]{:S(2)}, u32[]{:S(2)}) collective-permute-start(bf16[4,384,128]{2,1,0:T(8,128)(2,1)S(1)} %slice.111), channel_id=1, source_target_pairs={{0,4},{4,8},{8,12},{12,16},{16,20},{20,24},{24,28},{28,0},{1,5},{5... | collective-permute-start | bytes 1179656 | tf_op jit(solution)/shard_map/ppermute | solution.py:274
  167.7 74.9 %collective-permute-start.45 = (bf16[4,384,128]{2,1,0:T(8,128)(2,1)S(1)}, bf16[4,384,128]{2,1,0:T(8,128)(2,1)S(1)}, u32[]{:S(2)}, u32[]{:S(2)}) collective-permute-start(bf16[4,384,128]{2,1,0:T(8,128)(2,1)S(1)} %slice.112), channel_id=1, source_target_pairs={{0,28},{4,0},{8,4},{12,8},{16,12},{20,16},{24,20},{28,24},{1,29},{... | collective-permute-start | bytes 1179656 | tf_op jit(solution)/shard_map/ppermute | solution.py:274
  172.7 138.4 %collective-permute-start.33 = (bf16[512,384]{1,0:T(8,128)(2,1)S(1)}, bf16[512,384]{1,0:T(8,128)(2,1)S(1)}, u32[]{:S(2)}, u32[]{:S(2)}) collective-permute-start(bf16[512,384]{1,0:T(8,128)(2,1)S(1)} %slice.108), channel_id=1, source_target_pairs={{0,4},{4,8},{8,12},{12,16},{16,20},{20,24},{24,28},{28,0},{1,5},{5... | collective-permute-start | bytes 1179656 | tf_op jit(solution)/shard_map/ppermute | solution.py:274
  183.9 130.5 %collective-permute-start.37 = (bf16[512,384]{1,0:T(8,128)(2,1)S(1)}, bf16[512,384]{1,0:T(8,128)(2,1)S(1)}, u32[]{:S(2)}, u32[]{:S(2)}) collective-permute-start(bf16[512,384]{1,0:T(8,128)(2,1)S(1)} %slice.109), channel_id=1, source_target_pairs={{0,28},{4,0},{8,4},{12,8},{16,12},{20,16},{24,20},{28,24},{1,29},{... | collective-permute-start | bytes 1179656 | tf_op jit(solution)/shard_map/ppermute | solution.py:274
  240.6 58.1 %collective-permute-start.23 = (bf16[4,256,128]{2,1,0:T(8,128)(2,1)S(1)}, bf16[4,256,128]{2,1,0:T(8,128)(2,1)S(1)}, u32[]{:S(2)}, u32[]{:S(2)}) collective-permute-start(bf16[4,256,128]{2,1,0:T(8,128)(2,1)S(1)} %copy-done.17), channel_id=1, source_target_pairs={{0,28},{4,0},{8,4},{12,8},{16,12},{20,16},{24,20},{28,24},{1,29},{... | collective-permute-start | bytes 786440 | tf_op jit(solution)/shard_map/ppermute | solution.py:274
  240.6 58.2 %collective-permute-start.12 = (bf16[512,256]{1,0:T(8,128)(2,1)S(1)}, bf16[512,256]{1,0:T(8,128)(2,1)S(1)}, u32[]{:S(2)}, u32[]{:S(2)}) collective-permute-start(bf16[512,256]{1,0:T(8,128)(2,1)S(1)} %collective-permute-done.11.refs_2_), channel_id=1, source_target_pairs={{0,4},{4,8},{8,12},{12,16},{16,20},{20,24},{24,28},{28,0},{1,5},{5... | collective-permute-start | bytes 786440 | tf_op jit(solution)/shard_map/ppermute | solution.py:274
  242.6 68.5 %collective-permute-start.15 = (bf16[512,256]{1,0:T(8,128)(2,1)S(1)}, bf16[512,256]{1,0:T(8,128)(2,1)S(1)}, u32[]{:S(2)}, u32[]{:S(2)}) collective-permute-start(bf16[512,256]{1,0:T(8,128)(2,1)S(1)} %collective-permute-done.14.refs_3_), channel_id=1, source_target_pairs={{0,28},{4,0},{8,4},{12,8},{16,12},{20,16},{24,20},{28,24},{1,29},{... | collective-permute-start | bytes 786440 | tf_op jit(solution)/shard_map/ppermute | solution.py:274
  298.7 33.2 %collective-permute-start.21 = (bf16[4,256,128]{2,1,0:T(8,128)(2,1)S(1)}, bf16[4,256,128]{2,1,0:T(8,128)(2,1)S(1)}, u32[]{:S(2)}, u32[]{:S(2)}) collective-permute-start(bf16[4,256,128]{2,1,0:T(8,128)(2,1)S(1)} %collective-permute-done.20.refs_9_), channel_id=1, source_target_pairs={{0,4},{4,8},{8,12},{12,16},{16,20},{20,24},{24,28},{28,0},{1,5},{5... | collective-permute-start | bytes 786440 | tf_op jit(solution)/shard_map/ppermute | solution.py:274
  298.8 33.7 %collective-permute-start.24 = (bf16[4,256,128]{2,1,0:T(8,128)(2,1)S(1)}, bf16[4,256,128]{2,1,0:T(8,128)(2,1)S(1)}, u32[]{:S(2)}, u32[]{:S(2)}) collective-permute-start(bf16[4,256,128]{2,1,0:T(8,128)(2,1)S(1)} %collective-permute-done.23.refs_10_), channel_id=1, source_target_pairs={{0,28},{4,0},{8,4},{12,8},{16,12},{20,16},{24,20},{28,24},{1,29},{... | collective-permute-start | bytes 786440 | tf_op jit(solution)/shard_map/ppermute | solution.py:274
  330.6 68.0 %collective-permute-start.46 = (bf16[4,816,128]{2,1,0:T(8,128)(2,1)S(1)}, bf16[4,816,128]{2,1,0:T(8,128)(2,1)S(1)}, u32[]{:S(2)}, u32[]{:S(2)}) collective-permute-start(bf16[4,816,128]{2,1,0:T(8,128)(2,1)S(1)} %get-tuple-element.51), channel_id=1, source_target_pairs={{0,32},{32,64},{64,96},{1,33},{33,65},{65,97},{2,34},{34,66},{66,9... | collective-permute-start | bytes 2506760 | tf_op jit(solution)/shard_map/ppermute | solution.py:279
  341.9 58.0 %collective-permute-start.47 = (bf16[4,816,128]{2,1,0:T(8,128)(2,1)S(1)}, bf16[4,816,128]{2,1,0:T(8,128)(2,1)S(1)}, u32[]{:S(2)}, u32[]{:S(2)}) collective-permute-start(bf16[4,816,128]{2,1,0:T(8,128)(2,1)S(1)} %get-tuple-element.50), channel_id=1, source_target_pairs={{0,64},{32,96},{1,65},{33,97},{2,66},{34,98},{3,67},{35,99},{4,68}... | collective-permute-start | bytes 2506760 | tf_op jit(solution)/shard_map/ppermute | solution.py:279
  343.2 56.7 %collective-permute-start.48 = (bf16[4,816,128]{2,1,0:T(8,128)(2,1)S(1)}, bf16[4,816,128]{2,1,0:T(8,128)(2,1)S(1)}, u32[]{:S(2)}, u32[]{:S(2)}) collective-permute-start(bf16[4,816,128]{2,1,0:T(8,128)(2,1)S(1)} %get-tuple-element.49), channel_id=1, source_target_pairs={{0,96},{1,97},{2,98},{3,99},{4,100},{5,101},{6,102},{7,103},{8,104... | collective-permute-start | bytes 2506760 | tf_op jit(solution)/shard_map/ppermute | solution.py:279
  (54 other events, 935.6 us)

commit v2 on v1

v2 whole, which is shorter than its diff:
```python
import functools
import math

import jax
import jax.numpy as jnp
from jax import lax
from jax.experimental import pallas as pl
from jax.experimental.pallas import tpu as pltpu
from jax.sharding import Mesh, PartitionSpec as P

BLOCK = 128
HEAD = 128
ROWS = 4
RING = 8
NEG_FILL = -1e30
ROPE_BASE = 10000.0
STAT = 48
CHUNKS = ((0, 4), (4, 4))
GROUPS = (((0, 1), (2,), (3, 4)), ((0, 1), (2,), (3, 4)))


QUARTER = (1.5703125, 4.837512969970703e-4, 7.54978995489188216e-8)


def sin_cos(phase):
    turns = jnp.floor(phase * (2 / math.pi) + 0.5)
    x = phase
    for part in QUARTER:
        x = x - turns * part
    square = x * x
    sine = ((-1.9515295891e-4 * square + 8.3321608736e-3) * square - 1.6666654611e-1) * square
    sine = sine * x + x
    cosine = ((2.443315711809948e-5 * square - 1.388731625493765e-3) * square + 4.166664568298827e-2)
    cosine = cosine * square * square - 0.5 * square + 1.0
    quadrant = turns.astype(jnp.int32) & 3
    odd = (quadrant & 1) == 1
    sine, cosine = jnp.where(odd, cosine, sine), jnp.where(odd, sine, cosine)
    sine = jnp.where(quadrant >= 2, -sine, sine)
    cosine = jnp.where((quadrant == 1) | (quadrant == 2), -cosine, cosine)
    return sine, cosine


def rotate_kernel(angle_ref, freq_ref, q_ref, k_ref, v_ref, q_out, ka_out, *both_out):
    freq = freq_ref[...]
    lane = lax.broadcasted_iota(jnp.int32, (BLOCK, HEAD), 1)
    low = lane < HEAD // 2
    heads = q_ref.shape[1] // HEAD
    for pair in range(heads // 2):
        even = angle_ref[:, 2 * pair : 2 * pair + 1]
        odd = angle_ref[:, 2 * pair + 1 : 2 * pair + 2]
        sine, cosine = sin_cos(jnp.where(low, even, odd) * freq)
        sine_turned = pltpu.roll(sine, HEAD // 2, 1)
        cosine_turned = pltpu.roll(cosine, HEAD // 2, 1)
        for h in (2 * pair, 2 * pair + 1):
            first, second = (sine, sine_turned) if h % 2 == 0 else (sine_turned, sine)
            signed = jnp.where(low, -first, second)
            first, second = (cosine, cosine_turned) if h % 2 == 0 else (cosine_turned, cosine)
            plain = jnp.where(low, first, second)
            cols = slice(h * HEAD, (h + 1) * HEAD)

            def turn(x):
                x = x.astype(jnp.float32)
                return (x * plain + pltpu.roll(x, HEAD // 2, 1) * signed).astype(jnp.bfloat16)

            q_out[:, cols] = turn(q_ref[:, cols])
            key = turn(k_ref[:, cols])
            if h < 4:
                ka_out[0, h * HEAD : (h + 1) * HEAD, :] = key
            else:
                both_out[(h - 4) // 2][0, 0, h % 2 * HEAD : (h % 2 + 1) * HEAD, :] = key
    for i, out in enumerate(both_out):
        out[1, 0] = v_ref[0, (4 + 2 * i) * HEAD : (6 + 2 * i) * HEAD, :]


def rotate(angles, queries, keys, value_tiles):
    half = HEAD // 2
    inv_freq = ROPE_BASE ** (-jnp.arange(half).astype(jnp.float32) / half)
    inv_freq = jnp.concatenate([inv_freq, inv_freq])[None]
    heads = angles.shape[0]
    bf16 = jnp.bfloat16
    rows = pl.BlockSpec((BLOCK, heads * HEAD), lambda b: (b, 0))
    both = pl.BlockSpec((2, 1, 2 * HEAD, BLOCK), lambda b: (0, b, 0, 0))
    return pl.pallas_call(
        rotate_kernel,
        out_shape=[
            jax.ShapeDtypeStruct(queries.shape, bf16),
            jax.ShapeDtypeStruct((4, 4 * HEAD, BLOCK), bf16),
            jax.ShapeDtypeStruct((2, 4, 2 * HEAD, BLOCK), bf16),
            jax.ShapeDtypeStruct((2, 4, 2 * HEAD, BLOCK), bf16),
        ],
        grid=(4,),
        in_specs=[
            pl.BlockSpec((BLOCK, heads), lambda b: (b, 0)),
            pl.BlockSpec((1, HEAD), lambda b: (0, 0)),
            rows,
            rows,
            pl.BlockSpec((1, heads * HEAD, BLOCK), lambda b: (b, 0, 0)),
        ],
        out_specs=[rows, pl.BlockSpec((1, 4 * HEAD, BLOCK), lambda b: (b, 0, 0)), both, both],
        compiler_params=pltpu.CompilerParams(vmem_limit_bytes=24 << 20),
        cost_estimate=pl.CostEstimate(flops=5 * 10**9, bytes_accessed=6 << 20, transcendentals=0),
        name="rotate",
    )(angles.T, inv_freq, queries, keys, value_tiles)


def attend_kernel(offsets, heads, pieces, first, last, meta, *refs):
    count = len(offsets)
    q_refs, refs = refs[:ROWS], refs[ROWS:]
    flat_k = refs[: count * pieces]
    flat_v = refs[count * pieces : 2 * count * pieces]
    k_refs = [flat_k[i * pieces : (i + 1) * pieces] for i in range(count)]
    v_refs = [flat_v[i * pieces : (i + 1) * pieces] for i in range(count)]
    rest = list(refs[2 * count * pieces :])
    q_ref = rest.pop()
    given = None
    if not first:
        given = rest[:3]
        rest = rest[3:]
    if last:
        acc0_ref, m0_ref, l0_ref, packed_ref, acc, m_run, l_run = rest
    else:
        acc, m_run, l_run = rest
    r = pl.program_id(0)
    scale = HEAD**-0.5 * math.log2(math.e)

    for row in range(ROWS):

        @pl.when(r == row)
        def _(row=row):
            q_ref[...] = q_refs[row][...]

    if first:
        acc[...] = jnp.zeros_like(acc)
        m_run[...] = jnp.full_like(m_run, NEG_FILL)
        l_run[...] = jnp.zeros_like(l_run)
    else:
        acc[...] = given[0][...]
        m_run[...] = given[1][...]
        l_run[...] = given[2][...]

    def pair(qb, kb, k_ref, v_ref, causal):
        q_rows = pl.ds(pl.multiple_of(qb * BLOCK, BLOCK), BLOCK)
        span = range(heads)
        cols = [slice(h * HEAD, (h + 1) * HEAD) for h in span]
        each = heads // pieces
        part = [slice(h % each * HEAD, (h % each + 1) * HEAD) for h in span]
        m_all, l_all = m_run[qb], l_run[qb]
        scores = [
            lax.dot_general(
                k_ref[h // each][kb, part[h], :],
                q_ref[q_rows, cols[h]],
                (((1,), (1,)), ((), ())),
                preferred_element_type=jnp.float32,
            )
            for h in span
        ]
        if causal:
            key_pos = lax.broadcasted_iota(jnp.int32, scores[0].shape, 0)
            query_pos = lax.broadcasted_iota(jnp.int32, scores[0].shape, 1)
            scores = [jnp.where(key_pos <= query_pos, s, NEG_FILL) for s in scores]
        tops = [jnp.max(s, axis=0, keepdims=True) for s in scores]
        if heads < 8:
            tops.append(m_all[heads:])
        m_new = jnp.maximum(m_all, jnp.concatenate(tops, axis=0))
        fade = jnp.exp2((m_all - m_new) * scale)
        weights = [jnp.exp2((scores[h] - m_new[h : h + 1]) * scale) for h in span]
        sums = [jnp.sum(w, axis=0, keepdims=True) for w in weights]
        if heads < 8:
            sums.append(jnp.zeros((8 - heads, BLOCK), jnp.float32))
        mixed = [
            jnp.dot(
                v_ref[h // each][kb, part[h], :],
                weights[h].astype(jnp.bfloat16),
                preferred_element_type=jnp.float32,
            )
            for h in span
        ]
        whole = [acc[qb, cols[h], :] * fade[h : h + 1] + mixed[h] for h in span]
        m_run[qb] = m_new
        l_run[qb] = l_all * fade + jnp.concatenate(sums, axis=0)
        for h in span:
            acc[qb, cols[h], :] = whole[h]

    def per_block(qb, carry):
        base = (r * 4 + qb) * RING
        for at, offset in enumerate(offsets):
            code = meta[base + offset % RING]
            if offset == 0:

                @pl.when(r == 0)
                def _(at=at):
                    pair(qb, qb, k_refs[at], v_refs[at], True)

                def per_pick(kb, inner, at=at, code=code):
                    @pl.when((code >> kb) & 1 == 1)
                    def _():
                        pair(qb, kb, k_refs[at], v_refs[at], False)

                    return inner

                lax.fori_loop(0, 4, per_pick, 0)
            else:

                @pl.when(code > 0)
                def _(at=at, code=code):
                    pair(qb, code - 1, k_refs[at], v_refs[at], False)

        return carry

    lax.fori_loop(0, 4, per_block, 0)

    if last:

        @pl.when(r == 0)
        def _():
            acc0_ref[...] = acc[...]
            m0_ref[...] = m_run[...]
            l0_ref[...] = l_run[...]

        @pl.when(r > 0)
        def _():
            def pack(qb, carry):
                m_all, l_all = m_run[qb], l_run[qb]
                pieces = []
                for value in (m_all, l_all):
                    for _ in range(3):
                        piece = value.astype(jnp.bfloat16).astype(jnp.float32)
                        pieces.append(piece)
                        value = value - piece
                packed_ref[0, qb, heads * HEAD :, :] = jnp.concatenate(pieces, axis=0).astype(
                    jnp.bfloat16
                )
                for h in range(heads):
                    cols = slice(h * HEAD, (h + 1) * HEAD)
                    total = l_run[qb, h : h + 1, :]
                    inverse = 1.0 / jnp.where(total > 0, total, 1.0)
                    packed_ref[0, qb, cols, :] = (acc[qb, cols, :] * inverse).astype(jnp.bfloat16)
                return carry

            lax.fori_loop(0, 4, pack, 0)


def attend(meta, queries, chunk, offsets, keys, values, state, last):
    first_head, heads = chunk
    width = heads * HEAD
    first = state is None
    acc_spec = pl.BlockSpec((4, width, BLOCK), lambda r, meta: (r, 0, 0))
    run_spec = pl.BlockSpec((4, 8, BLOCK), lambda r, meta: (r, 0, 0))
    state_specs = [acc_spec, run_spec, run_spec]
    in_specs = [pl.BlockSpec((512, width), lambda r, meta: (0, first_head // heads))] * ROWS
    pieces = len(keys[0])
    for group, half in ((keys, 0), (values, 1)):
        for arrays in group:
            for array in arrays:
                if array.ndim == 3:
                    in_specs.append(
                        pl.BlockSpec((4, width // pieces, BLOCK), lambda r, meta: (0, 0, 0))
                    )
                else:
                    in_specs.append(
                        pl.BlockSpec(
                            (None, 4, width // pieces, BLOCK),
                            lambda r, meta, half=half: (half, 0, 0, 0),
                        )
                    )
    operands = list(queries) + [x for arrays in keys for x in arrays] + [x for arrays in values for x in arrays]
    if not first:
        in_specs += state_specs
        operands += list(state)
    f32 = jnp.float32
    scratch = []
    if last:
        out_shape = [
            jax.ShapeDtypeStruct((4, width, BLOCK), f32),
            jax.ShapeDtypeStruct((4, 8, BLOCK), f32),
            jax.ShapeDtypeStruct((4, 8, BLOCK), f32),
            jax.ShapeDtypeStruct((3, 4, width + STAT, BLOCK), jnp.bfloat16),
        ]
        out_specs = [
            pl.BlockSpec((4, width, BLOCK), lambda r, meta: (0, 0, 0)),
            pl.BlockSpec((4, 8, BLOCK), lambda r, meta: (0, 0, 0)),
            pl.BlockSpec((4, 8, BLOCK), lambda r, meta: (0, 0, 0)),
            pl.BlockSpec((1, 4, width + STAT, BLOCK), lambda r, meta: (jnp.maximum(r - 1, 0), 0, 0, 0)),
        ]
        scratch = [
            pltpu.VMEM((4, width, BLOCK), f32),
            pltpu.VMEM((4, 8, BLOCK), f32),
            pltpu.VMEM((4, 8, BLOCK), f32),
        ]
    else:
        out_shape = [
            jax.ShapeDtypeStruct((16, width, BLOCK), f32),
            jax.ShapeDtypeStruct((16, 8, BLOCK), f32),
            jax.ShapeDtypeStruct((16, 8, BLOCK), f32),
        ]
        out_specs = state_specs
    scratch.append(pltpu.VMEM((512, width), jnp.bfloat16))
    return pl.pallas_call(
        functools.partial(attend_kernel, offsets, heads, pieces, first, last),
        out_shape=out_shape,
        grid_spec=pltpu.PrefetchScalarGridSpec(
            num_scalar_prefetch=1,
            grid=(ROWS,),
            in_specs=in_specs,
            out_specs=out_specs,
            scratch_shapes=scratch,
        ),
        compiler_params=pltpu.CompilerParams(vmem_limit_bytes=40 << 20),
        cost_estimate=pl.CostEstimate(
            flops=int((3 + 4 * len(offsets)) * 1.1e9),
            bytes_accessed=1 << 20,
            transcendentals=0,
        ),
        name=f"attend_{first_head}_{'_'.join(str(o % RING) for o in offsets)}",
    )(meta, *operands)


def join_kernel(heads, acc_ref, m_ref, l_ref, one, two, three, *rest):
    out_ref = rest[-1]
    width = heads * HEAD
    tops, sums = [m_ref[0]], [l_ref[0]]
    for part in (one, two, three):
        stats = part[0, width:, :].astype(jnp.float32)
        top = (stats[16:24] + stats[8:16]) + stats[0:8]
        total = (stats[40:48] + stats[32:40]) + stats[24:32]
        tops.append(jnp.where(total > 0, top, NEG_FILL))
        sums.append(total)
    scale = HEAD**-0.5 * math.log2(math.e)
    highest = jnp.maximum(jnp.maximum(tops[0], tops[1]), jnp.maximum(tops[2], tops[3]))
    fades = [jnp.exp2((top - highest) * scale) for top in tops]
    shares = [fades[0]] + [fades[i] * sums[i] for i in (1, 2, 3)]
    whole = fades[0] * sums[0] + shares[1] + shares[2] + shares[3]
    inverse = 1.0 / whole
    for h in range(heads):
        cols = slice(h * HEAD, (h + 1) * HEAD)
        mixed = acc_ref[0, cols, :] * shares[0][h : h + 1, :]
        for i, part in enumerate((one, two, three)):
            mixed += part[0, cols, :].astype(jnp.float32) * shares[i + 1][h : h + 1, :]
        mixed = mixed * inverse[h : h + 1, :]
        out_ref[:, cols] = mixed.T.astype(jnp.bfloat16)


def join(chunk, state, parts, out):
    first_head, heads = chunk
    width = heads * HEAD
    in_specs = [
        pl.BlockSpec((1, width, BLOCK), lambda b: (b, 0, 0)),
        pl.BlockSpec((1, 8, BLOCK), lambda b: (b, 0, 0)),
        pl.BlockSpec((1, 8, BLOCK), lambda b: (b, 0, 0)),
    ] + [pl.BlockSpec((1, width + STAT, BLOCK), lambda b: (b, 0, 0))] * 3
    operands = [*state, *parts]
    aliases = {}
    if out is not None:
        aliases = {len(operands): 0}
        in_specs.append(pl.BlockSpec(memory_space=pl.ANY))
        operands.append(out)
    return pl.pallas_call(
        functools.partial(join_kernel, heads),
        out_shape=jax.ShapeDtypeStruct((512, 1024), jnp.bfloat16),
        grid=(4,),
        in_specs=in_specs,
        out_specs=pl.BlockSpec((BLOCK, width), lambda b: (b, first_head // heads)),
        input_output_aliases=aliases,
        compiler_params=pltpu.CompilerParams(vmem_limit_bytes=24 << 20),
        cost_estimate=pl.CostEstimate(
            flops=512 * width * 10, bytes_accessed=512 * width * 14, transcendentals=0
        ),
        name=f"join_{first_head}",
    )(*operands)


def shift(value, axis, step):
    size = lax.axis_size(axis)
    return lax.ppermute(value, axis, [(i, (i + step) % size) for i in range(size)])


def to_row(value, step):
    moves = [(i, i + step) for i in range(ROWS) if 0 <= i + step < ROWS]
    return lax.ppermute(value, "y", moves)


def swap(value, axis, bit):
    size = lax.axis_size(axis)
    return lax.ppermute(value, axis, [(i, i ^ bit) for i in range(size)])


def after(value, *others):
    return lax.optimization_barrier((value, *others))[0]


class Wire:
    def __init__(self, side, sign, depth=2):
        self.side, self.sign, self.depth = side, sign, depth
        self.sent = []

    def send(self, name, ring, distance, *others):
        source = ring[-self.sign * (distance - 1)]
        waits = list(others)
        if len(self.sent) >= self.depth:
            waits.append(self.sent[-self.depth])
        if waits:
            source = after(source, *waits)
        with jax.named_scope(f"{name}{distance}_{self.side}"):
            got = shift(source, "z", self.sign)
        self.sent.append(got)
        ring[-self.sign * distance if distance < 4 else 4] = got


def shards(query_states, key_states, value_states, gate_logits, selected_blocks):
    my_y, my_z = lax.axis_index("y"), lax.axis_index("z")
    gate_values = jax.nn.sigmoid(gate_logits.astype(jnp.float32))
    total = jnp.sum(gate_values, axis=1, keepdims=True)
    before = jnp.zeros_like(total)
    value_tiles = value_states.reshape(4, BLOCK, -1).transpose(0, 2, 1)
    values_a = {0: value_tiles[:, : 4 * HEAD]}
    right, left = Wire("right", 1), Wire("left", -1)
    for wire in (right, left):
        wire.send("va", values_a, 1)
    with jax.named_scope("prefix"):
        for bit in (1, 2, 4):
            other = swap(total, "z", bit)
            before = before + jnp.where((my_z & bit) != 0, other, 0.0)
            total = total + other
        total = after(total, values_a[1], values_a[-1])
        for bit in (1, 2):
            other = swap(total, "y", bit)
            before = before + jnp.where((my_y & bit) != 0, other, 0.0)
            total = total + other
    for wire in (right, left):
        wire.send("va", values_a, 2)
    angles = before + jnp.cumsum(gate_values, axis=1)
    query_rot, keys, kv_b, kv_c = rotate(angles, query_states, key_states, value_tiles)
    keys_a, both = {0: keys}, [{0: kv_b}, {0: kv_c}]
    with jax.named_scope("queries"):
        queries = [query_rot] + [to_row(query_rot, -s) for s in (1, 2, 3)]
    chosen = after(selected_blocks, total)
    with jax.named_scope("picks"):
        picks = [chosen] + [to_row(chosen, -s) for s in (1, 2, 3)]

    blocks = jnp.stack(picks).reshape(16, 1, 8)
    row = lax.broadcasted_iota(jnp.int32, (16, RING, 8), 0)
    distance = lax.broadcasted_iota(jnp.int32, (16, RING, 8), 1)
    own = ((my_y + row // 4) * RING + my_z) * 4 + row % 4
    hit = (blocks >> 5 == my_y) & (((blocks >> 2) - my_z) & 7 == distance)
    hit &= (blocks != own) & (my_y + row // 4 < ROWS)
    code = jnp.where(distance == 0, 1 << (blocks & 3), (blocks & 3) + 1)
    meta = jnp.sum(jnp.where(hit, code, 0), axis=2).reshape(-1)

    def call(part, group, state, last):
        offsets = []
        for distance in group:
            offsets += [distance] if distance in (0, 4) else [-distance, distance]
        if part == 0:
            keys = [(keys_a[o],) for o in offsets]
            values = [(values_a[o],) for o in offsets]
        else:
            keys = values = [tuple(b[o] for b in both) for o in offsets]
        return attend(meta, queries, CHUNKS[part], tuple(offsets), keys, values, state, last)

    def finish(part, state, out):
        packed = state[3]
        with jax.named_scope("partials"):
            parts = [to_row(packed[s - 1], s) for s in (1, 2, 3)]
        return join(CHUNKS[part], state[:3], parts, out)

    b, c = both
    for name, ring, distance in (("ka", keys_a, 1), ("va", values_a, 3)):
        for wire in (right, left):
            wire.send(name, ring, distance)
    for wire in (right, left):
        wire.send("ka", keys_a, 2)
    right.send("va", values_a, 4)
    left.send("kvb", b, 1)
    for wire in (right, left):
        wire.send("ka", keys_a, 3)
    right.send("kvb", b, 1)
    left.send("kvc", c, 1)
    state = call(0, GROUPS[0][0], None, False)
    right.send("ka", keys_a, 4, state[1])
    left.send("kvb", b, 2, state[1])
    right.send("kvc", c, 1)
    left.send("kvc", c, 2)
    state = call(0, GROUPS[0][1], state, False)
    right.send("kvb", b, 2, state[1])
    left.send("kvb", b, 3, state[1])
    right.send("kvc", c, 2)
    left.send("kvc", c, 3)
    state = call(0, GROUPS[0][2], state, True)
    right.send("kvb", b, 3, state[1])
    left.send("kvb", b, 4, state[1])
    right.send("kvc", c, 3)
    left.send("kvc", c, 4)
    out = finish(0, state, None)
    state = call(1, GROUPS[1][0], None, False)
    state = call(1, GROUPS[1][1], state, False)
    state = call(1, GROUPS[1][2], state, True)
    return finish(1, state, out)


def solution(mesh):
    grid = Mesh(mesh.devices.reshape(2, ROWS, RING, 4), ("dp", "y", "z", "head"))
    tokens = ("dp", "y", "z")
    placed = (
        P(tokens, "head"),
        P(tokens, "head"),
        P(tokens, "head"),
        P("head", tokens),
        P(tokens, None),
    )
    return jax.shard_map(
        shards, mesh=grid, in_specs=placed, out_specs=P(tokens, "head"), check_vma=False
    )
```

time: 414 us -> 256 us (0.62); the launches traced: 407 us -> 253 us
  Pallas kernels: 176 us -> 78.7 us
  starting transfers between devices: 103 us -> 73.6 us
  other arithmetic: 26.7 us -> 2.34 us
  local copies, waits for them, and re-layouts: 20.2 us -> 15.7 us
    pallas_call x6 -> x7, Pallas kernels: 172 us -> 74.8 us  [the longest x6 70.8 us: attend(): pl.pallas_call(functools.partial(attend_kernel, offsets, heads, pieces, f...]
    ppermute x32 -> x28, starting transfers between devices: 71.5 us -> 49.4 us  [shift(): lax.ppermute(value, axis, [(i, (i + step) % size) for i in range(size)])]
    ppermute x12, waiting for transfers between devices: 48.3 us -> 29.1 us  [to_row(): return lax.ppermute(value, 'y', moves)]
    another operation x4, other arithmetic: 14.1 us -> 1.26 us
    ppermute x5, waiting for transfers between devices: 6.85 us -> 18.8 us  [swap(): return lax.ppermute(value, axis, [(i, i ^ bit) for i in range(size)])]
    ppermute x32 -> x28, waiting for transfers between devices: 24.6 us -> 34.4 us  [shift(): lax.ppermute(value, axis, [(i, (i + step) % size) for i in range(size)])]
    sub x1 -> x0, other arithmetic: 8.66 us -> none  [rotate(): first_half * cos_part - second_half * sin_part]
    ppermute x5, starting transfers between devices: 16.1 us -> 8.57 us  [swap(): return lax.ppermute(value, axis, [(i, i ^ bit) for i in range(size)])]
  transfers between devices with their start and end apart: 49 -> 45, of which waited for: 15 -> 17; matrix products, arithmetic and copies ran while one was open for 9% -> 2% of each run, Pallas kernels for 43% -> 30%
where the time goes in v2:
time: 256 us; the launch traced here: 253 us
  waiting for transfers between devices  82.3 us (32%)
  Pallas kernels  78.7 us (31%)
  starting transfers between devices  73.6 us (29%)
  local copies, waits for them, and re-layouts  15.7 us (6%)
    pallas_call x6, Pallas kernels, attend(): pl.pallas_call(functools.partial(attend_kernel, offsets, heads, pieces, f...  70.8 us
    ppermute x28, starting transfers between devices, shift(): lax.ppermute(value, axis, [(i, (i + step) % size) for i in range(size)])  49.4 us
    ppermute x28, waiting for transfers between devices, shift(): lax.ppermute(value, axis, [(i, (i + step) % size) for i in range(size)])  34.4 us
    ppermute x12, waiting for transfers between devices, to_row(): return lax.ppermute(value, 'y', moves)  29.1 us
    ppermute x5, waiting for transfers between devices, swap(): return lax.ppermute(value, axis, [(i, i ^ bit) for i in range(size)])  18.8 us
    ppermute x12, starting transfers between devices, to_row(): return lax.ppermute(value, 'y', moves)  15.6 us
    unnamed x30, local copies, waits for them, and re-layouts  12.4 us
    ppermute x5, starting transfers between devices, swap(): return lax.ppermute(value, axis, [(i, i ^ bit) for i in range(size)])  8.57 us
  transfers between devices with their start and end apart: 45, of which 17 were waited for; matrix products, arithmetic and copies ran while one was open for 2% of the time, Pallas kernels for 30%

profile of v2, /device:TPU:2, one launch (start us, length us, event | category | flops | bytes accessed | tf_op | source)
XLA Modules:
  0.0 253.1 jit_solution(11316067921054661375)
XLA Ops:
  1.7 5.9 %collective-permute-start.6 = (bf16[4,512,128]{2,1,0:T(8,128)(2,1)S(1)}, bf16[4,512,128]{2,1,0:T(8,128)(2,1)S(1)}, u32[]{:S(2)}, u32[]{:S(2)}) collective-permute-start(bf16[4,512,128]{2,1,0:T(8,128)(2,1)S(1)} %slice.36.refs_7_), channel_id=1, source_target_pairs={{0,28},{4,0},{8,4},{12,8},{16,12},{20,16},{24,20},{28,24},{1,29},{... | collective-permute-start | bytes 1572872 | tf_op jit(solution)/shard_map/va1_left/ppermute | solution.py:374
  10.2 8.7 %collective-permute-done.3 = f32[8,1]{0,1:T(1,128)S(1)} collective-permute-done((f32[8,1]{0,1:T(1,128)S(1)}, f32[8,1]{0,1:T(1,128)S(1)}, u32[]{:S(2)}, u32[]{:S(2)}) %collective-permute-start.3) | collective-permute-done | bytes 64 | tf_op jit(solution)/shard_map/prefix/ppermute | solution.py:384
  18.9 4.4 %collective-permute-done.4 = f32[8,1]{0,1:T(1,128)S(1)} collective-permute-done((f32[8,1]{0,1:T(1,128)S(1)}, f32[8,1]{0,1:T(1,128)S(1)}, u32[]{:S(2)}, u32[]{:S(2)}) %collective-permute-start.4) | collective-permute-done | bytes 64 | tf_op jit(solution)/shard_map/prefix/ppermute | solution.py:384
  23.3 3.8 %collective-permute-start.5 = (f32[8,1]{0,1:T(1,128)S(1)}, f32[8,1]{0,1:T(1,128)S(1)}, u32[]{:S(2)}, u32[]{:S(2)}) collective-permute-start(f32[8,1]{0,1:T(1,128)S(1)} %add.82), channel_id=1, source_target_pairs={{0,16},{4,20},{8,24},{12,28},{16,0},{20,4},{24,8},{28,12},{1,17},{... | collective-permute-start | bytes 104 | tf_op jit(solution)/shard_map/prefix/ppermute | solution.py:384
  27.1 3.6 %collective-permute-done.5 = f32[8,1]{0,1:T(1,128)S(1)} collective-permute-done((f32[8,1]{0,1:T(1,128)S(1)}, f32[8,1]{0,1:T(1,128)S(1)}, u32[]{:S(2)}, u32[]{:S(2)}) %collective-permute-start.5) | collective-permute-done | bytes 64 | tf_op jit(solution)/shard_map/prefix/ppermute | solution.py:384
  43.2 4.1 %rotate.1 = (bf16[512,1024]{1,0:T(8,128)(2,1)S(1)}, bf16[4,512,128]{2,1,0:T(8,128)(2,1)S(1)}, bf16[2,4,256,128]{3,2,1,0:T(8,128)(2,1)S(1)}, bf16[2,4,256,128]{3,2,1,0:T(8,128)(2,1)S(1)}) custom-call(f32[512,8]{1,0:T(8,128)S(1)} %bitcast.32, f32[1,128]{1,0:T(1,128)S(1)} %maximum_bitcast_fusion.freq_ref, bf16[512,1024]{1,0:T(8,128)(2,1)S(1)} %copy-done, ...), custom_call_target="tpu_custom_call" | custom-call | flops 5000000000 | bytes 6291456 | tf_op jit(solution)/shard_map/rotate/pallas_call | solution.py:83
  69.4 10.6 %collective-permute-done.14.refs_7_ = bf16[4,512,128]{2,1,0:T(8,128)(2,1)S(1)} collective-permute-done((bf16[4,512,128]{2,1,0:T(8,128)(2,1)}, bf16[4,512,128]{2,1,0:T(8,128)(2,1)S(1)}, u32[]{:S(2)}, u32[]{:S(2)}) %collective-permute-start.14) | collective-permute-done | bytes 524320 | tf_op jit(solution)/shard_map/va3_right/ppermute | solution.py:374
  80.3 3.4 %collective-permute-start.20 = (bf16[4,512,128]{2,1,0:T(8,128)(2,1)}, bf16[4,512,128]{2,1,0:T(8,128)(2,1)}, u32[]{:S(2)}, u32[]{:S(2)}) collective-permute-start(bf16[4,512,128]{2,1,0:T(8,128)(2,1)} %copy-done.10), channel_id=1, source_target_pairs={{0,28},{4,0},{8,4},{12,8},{16,12},{20,16},{24,20},{28,24},{1,29},{... | collective-permute-start | bytes 1572872 | tf_op jit(solution)/shard_map/ka2_left/ppermute | solution.py:374
  84.0 11.2 %collective-permute-done.18.refs_4_ = bf16[4,512,128]{2,1,0:T(8,128)(2,1)} collective-permute-done((bf16[4,512,128]{2,1,0:T(8,128)(2,1)}, bf16[4,512,128]{2,1,0:T(8,128)(2,1)}, u32[]{:S(2)}, u32[]{:S(2)}) %collective-permute-start.18) | collective-permute-done | bytes 524320 | tf_op jit(solution)/shard_map/ka2_right/ppermute | solution.py:374
  95.2 3.7 %collective-permute-start.31 = (bf16[2,4,256,128]{3,2,1,0:T(8,128)(2,1)}, bf16[2,4,256,128]{3,2,1,0:T(8,128)(2,1)S(1)}, u32[]{:S(2)}, u32[]{:S(2)}) collective-permute-start(bf16[2,4,256,128]{3,2,1,0:T(8,128)(2,1)} %copy-done.2), channel_id=1, source_target_pairs={{0,28},{4,0},{8,4},{12,8},{16,12},{20,16},{24,20},{28,24},{1,29},{... | collective-permute-start | bytes 1572872 | tf_op jit(solution)/shard_map/kvb1_left/ppermute | solution.py:374
  98.9 3.2 %collective-permute-start.25 = (bf16[4,512,128]{2,1,0:T(8,128)(2,1)}, bf16[4,512,128]{2,1,0:T(8,128)(2,1)S(1)}, u32[]{:S(2)}, u32[]{:S(2)}) collective-permute-start(bf16[4,512,128]{2,1,0:T(8,128)(2,1)} %collective-permute-done.20.refs_5_), channel_id=1, source_target_pairs={{0,28},{4,0},{8,4},{12,8},{16,12},{20,16},{24,20},{28,24},{1,29},{... | collective-permute-start | bytes 1572872 | tf_op jit(solution)/shard_map/ka3_left/ppermute | solution.py:374
  102.1 3.5 %collective-permute-done.12.refs_3_ = bf16[512,1024]{1,0:T(8,128)(2,1)} collective-permute-done((bf16[512,1024]{1,0:T(8,128)(2,1)S(1)}, bf16[512,1024]{1,0:T(8,128)(2,1)}, u32[]{:S(2)}, u32[]{:S(2)}) %collective-permute-start.12) | collective-permute-done | bytes 1048608 | tf_op jit(solution)/shard_map/queries/ppermute | solution.py:379
  108.8 16.1 %attend_0_0_7_1.1 = (f32[16,512,128]{2,1,0:T(8,128)S(1)}, f32[16,8,128]{2,1,0:T(8,128)S(1)}, f32[16,8,128]{2,1,0:T(8,128)S(1)}) custom-call(s32[128]{0:T(128)S(1)} %reshape.55.meta, bf16[512,1024]{1,0:T(8,128)(2,1)S(1)} %get-tuple-element.55.refs_0_, bf16[512,1024]{1,0:T(8,128)(2,1)} %collective-permute-done.10.refs_1_, ...), custom_call_target="tpu_custom_call" | custom-call | flops 16499999744 | bytes 1048576 | tf_op jit(solution)/shard_map/attend_0_0_7_1/pallas_call | solution.py:298
  130.1 10.1 %attend_0_6_2.1 = (f32[16,512,128]{2,1,0:T(8,128)S(1)}, f32[16,8,128]{2,1,0:T(8,128)S(1)}, f32[16,8,128]{2,1,0:T(8,128)S(1)}) custom-call(s32[128]{0:T(128)S(1)} %reshape.55.meta, bf16[512,1024]{1,0:T(8,128)(2,1)S(1)} %get-tuple-element.55.refs_0_, bf16[512,1024]{1,0:T(8,128)(2,1)} %collective-permute-done.10.refs_1_, ...), custom_call_target="tpu_custom_call" | custom-call | flops 12099999744 | bytes 1048576 | tf_op jit(solution)/shard_map/attend_0_6_2/pallas_call | solution.py:298
  140.2 5.3 %collective-permute-start.32 = (bf16[2,4,256,128]{3,2,1,0:T(8,128)(2,1)S(1)}, bf16[2,4,256,128]{3,2,1,0:T(8,128)(2,1)S(1)}, u32[]{:S(2)}, u32[]{:S(2)}) collective-permute-start(bf16[2,4,256,128]{3,2,1,0:T(8,128)(2,1)S(1)} %collective-permute-done.31.refs_8_.refs_14_), channel_id=1, source_target_pairs={{0,28},{4,0},{8,4},{12,8},{16,12},{20,16},{24,20},{28,24},{1,29},{... | collective-permute-start | bytes 1572872 | tf_op jit(solution)/shard_map/kvb2_left/ppermute | solution.py:374
  145.5 3.2 %collective-permute-start.35 = (bf16[2,4,256,128]{3,2,1,0:T(8,128)(2,1)S(1)}, bf16[2,4,256,128]{3,2,1,0:T(8,128)(2,1)S(1)}, u32[]{:S(2)}, u32[]{:S(2)}) collective-permute-start(bf16[2,4,256,128]{3,2,1,0:T(8,128)(2,1)S(1)} %collective-permute-done.34.refs_9_.refs_15_), channel_id=1, source_target_pairs={{0,28},{4,0},{8,4},{12,8},{16,12},{20,16},{24,20},{28,24},{1,29},{... | collective-permute-start | bytes 1572872 | tf_op jit(solution)/shard_map/kvc2_left/ppermute | solution.py:374
  148.8 5.4 %collective-permute-done.23.refs_6_ = bf16[4,512,128]{2,1,0:T(8,128)(2,1)S(1)} collective-permute-done((bf16[4,512,128]{2,1,0:T(8,128)(2,1)S(1)}, bf16[4,512,128]{2,1,0:T(8,128)(2,1)S(1)}, u32[]{:S(2)}, u32[]{:S(2)}) %collective-permute-start.23) | collective-permute-done | bytes 524320 | tf_op jit(solution)/shard_map/ka4_right/ppermute | solution.py:374
  154.2 9.6 %attend_0_5_3_4.1 = (f32[4,512,128]{2,1,0:T(8,128)S(1)}, f32[4,8,128]{2,1,0:T(8,128)S(1)}, f32[4,8,128]{2,1,0:T(8,128)S(1)}, bf16[3,4,560,128]{3,2,1,0:T(8,128)(2,1)S(1)}) custom-call(s32[128]{0:T(128)S(1)} %reshape.55.meta, bf16[512,1024]{1,0:T(8,128)(2,1)S(1)} %get-tuple-element.55.refs_0_, bf16[512,1024]{1,0:T(8,128)(2,1)} %collective-permute-done.10.refs_1_, ...), custom_call_target="tpu_custom_call" | custom-call | flops 16499999744 | bytes 1048576 | tf_op jit(solution)/shard_map/attend_0_5_3_4/pallas_call | solution.py:298
  172.5 15.9 %attend_4_0_7_1.1 = (f32[16,512,128]{2,1,0:T(8,128)S(1)}, f32[16,8,128]{2,1,0:T(8,128)S(1)}, f32[16,8,128]{2,1,0:T(8,128)S(1)}) custom-call(s32[128]{0:T(128)S(1)} %reshape.55.meta, bf16[512,1024]{1,0:T(8,128)(2,1)S(1)} %get-tuple-element.55.refs_0_, bf16[512,1024]{1,0:T(8,128)(2,1)} %collective-permute-done.10.refs_1_, ...), custom_call_target="tpu_custom_call" | custom-call | flops 16499999744 | bytes 1048576 | tf_op jit(solution)/shard_map/attend_4_0_7_1/pallas_call | solution.py:298
  196.6 9.5 %attend_4_6_2.1 = (f32[16,512,128]{2,1,0:T(8,128)S(1)}, f32[16,8,128]{2,1,0:T(8,128)S(1)}, f32[16,8,128]{2,1,0:T(8,128)S(1)}) custom-call(s32[128]{0:T(128)S(1)} %reshape.55.meta, bf16[512,1024]{1,0:T(8,128)(2,1)S(1)} %get-tuple-element.55.refs_0_, bf16[512,1024]{1,0:T(8,128)(2,1)} %collective-permute-done.10.refs_1_, ...), custom_call_target="tpu_custom_call" | custom-call | flops 12099999744 | bytes 1048576 | tf_op jit(solution)/shard_map/attend_4_6_2/pallas_call | solution.py:298
  208.8 5.2 %collective-permute-done.30.refs_5_.refs_11_ = bf16[2,4,256,128]{3,2,1,0:T(8,128)(2,1)S(1)} collective-permute-done((bf16[2,4,256,128]{3,2,1,0:T(8,128)(2,1)S(1)}, bf16[2,4,256,128]{3,2,1,0:T(8,128)(2,1)S(1)}, u32[]{:S(2)}, u32[]{:S(2)}) %collective-permute-start.30) | collective-permute-done | bytes 524320 | tf_op jit(solution)/shard_map/kvc3_right/ppermute | solution.py:374
  215.0 9.6 %attend_4_5_3_4.1 = (f32[4,512,128]{2,1,0:T(8,128)S(1)}, f32[4,8,128]{2,1,0:T(8,128)S(1)}, f32[4,8,128]{2,1,0:T(8,128)S(1)}, bf16[3,4,560,128]{3,2,1,0:T(8,128)(2,1)S(1)}) custom-call(s32[128]{0:T(128)S(1)} %reshape.55.meta, bf16[512,1024]{1,0:T(8,128)(2,1)S(1)} %get-tuple-element.55.refs_0_, bf16[512,1024]{1,0:T(8,128)(2,1)} %collective-permute-done.10.refs_1_, ...), custom_call_target="tpu_custom_call" | custom-call | flops 16499999744 | bytes 1048576 | tf_op jit(solution)/shard_map/attend_4_5_3_4/pallas_call | solution.py:298
  230.7 8.6 %collective-permute-done.39.one = bf16[4,560,128]{2,1,0:T(8,128)(2,1)S(1)} collective-permute-done((bf16[4,560,128]{2,1,0:T(8,128)(2,1)S(1)}, bf16[4,560,128]{2,1,0:T(8,128)(2,1)S(1)}, u32[]{:S(2)}, u32[]{:S(2)}) %collective-permute-start.39) | collective-permute-done | bytes 573472 | tf_op jit(solution)/shard_map/partials/ppermute | solution.py:379
  239.3 11.9 %collective-permute-done.40.two = bf16[4,560,128]{2,1,0:T(8,128)(2,1)S(1)} collective-permute-done((bf16[4,560,128]{2,1,0:T(8,128)(2,1)S(1)}, bf16[4,560,128]{2,1,0:T(8,128)(2,1)S(1)}, u32[]{:S(2)}, u32[]{:S(2)}) %collective-permute-start.40) | collective-permute-done | bytes 573472 | tf_op jit(solution)/shard_map/partials/ppermute | solution.py:379
  (138 shorter events, 76.2 us)
Async XLA Ops:
  1.7 29.1 %collective-permute-start.6 = (bf16[4,512,128]{2,1,0:T(8,128)(2,1)S(1)}, bf16[4,512,128]{2,1,0:T(8,128)(2,1)S(1)}, u32[]{:S(2)}, u32[]{:S(2)}) collective-permute-start(bf16[4,512,128]{2,1,0:T(8,128)(2,1)S(1)} %slice.36.refs_7_), channel_id=1, source_target_pairs={{0,28},{4,0},{8,4},{12,8},{16,12},{20,16},{24,20},{28,24},{1,29},{... | collective-permute-start | bytes 1572872 | tf_op jit(solution)/shard_map/va1_left/ppermute | solution.py:374
  7.6 23.1 %collective-permute-start.7 = (bf16[4,512,128]{2,1,0:T(8,128)(2,1)S(1)}, bf16[4,512,128]{2,1,0:T(8,128)(2,1)}, u32[]{:S(2)}, u32[]{:S(2)}) collective-permute-start(bf16[4,512,128]{2,1,0:T(8,128)(2,1)S(1)} %slice.36.refs_7_), channel_id=1, source_target_pairs={{0,4},{4,8},{8,12},{12,16},{16,20},{20,24},{24,28},{28,0},{1,5},{5... | collective-permute-start | bytes 1572872 | tf_op jit(solution)/shard_map/va1_right/ppermute | solution.py:374
  32.4 21.8 %collective-permute-start.13 = (bf16[4,512,128]{2,1,0:T(8,128)(2,1)}, bf16[4,512,128]{2,1,0:T(8,128)(2,1)}, u32[]{:S(2)}, u32[]{:S(2)}) collective-permute-start(bf16[4,512,128]{2,1,0:T(8,128)(2,1)} %collective-permute-done.7.refs_8_), channel_id=1, source_target_pairs={{0,4},{4,8},{8,12},{12,16},{16,20},{20,24},{24,28},{28,0},{1,5},{5... | collective-permute-start | bytes 1572872 | tf_op jit(solution)/shard_map/va2_right/ppermute | solution.py:374
  58.5 40.4 %collective-permute-start.10 = (bf16[512,1024]{1,0:T(8,128)(2,1)S(1)}, bf16[512,1024]{1,0:T(8,128)(2,1)}, u32[]{:S(2)}, u32[]{:S(2)}) collective-permute-start(bf16[512,1024]{1,0:T(8,128)(2,1)S(1)} %get-tuple-element.55.refs_0_), channel_id=1, source_target_pairs={{32,0},{64,32},{96,64},{33,1},{65,33},{97,65},{34,2},{66,34},{98,6... | collective-permute-start | bytes 3145736 | tf_op jit(solution)/shard_map/queries/ppermute | solution.py:379
  61.2 37.7 %collective-permute-start.11 = (bf16[512,1024]{1,0:T(8,128)(2,1)S(1)}, bf16[512,1024]{1,0:T(8,128)(2,1)}, u32[]{:S(2)}, u32[]{:S(2)}) collective-permute-start(bf16[512,1024]{1,0:T(8,128)(2,1)S(1)} %get-tuple-element.55.refs_0_), channel_id=1, source_target_pairs={{64,0},{96,32},{65,1},{97,33},{66,2},{98,34},{67,3},{99,35},{68,4}... | collective-permute-start | bytes 3145736 | tf_op jit(solution)/shard_map/queries/ppermute | solution.py:379
  64.5 41.1 %collective-permute-start.12 = (bf16[512,1024]{1,0:T(8,128)(2,1)S(1)}, bf16[512,1024]{1,0:T(8,128)(2,1)}, u32[]{:S(2)}, u32[]{:S(2)}) collective-permute-start(bf16[512,1024]{1,0:T(8,128)(2,1)S(1)} %get-tuple-element.55.refs_0_), channel_id=1, source_target_pairs={{96,0},{97,1},{98,2},{99,3},{100,4},{101,5},{102,6},{103,7},{104,8... | collective-permute-start | bytes 3145736 | tf_op jit(solution)/shard_map/queries/ppermute | solution.py:379
  95.2 31.6 %collective-permute-start.15 = (bf16[4,512,128]{2,1,0:T(8,128)(2,1)S(1)}, bf16[4,512,128]{2,1,0:T(8,128)(2,1)S(1)}, u32[]{:S(2)}, u32[]{:S(2)}) collective-permute-start(bf16[4,512,128]{2,1,0:T(8,128)(2,1)S(1)} %collective-permute-done.14.refs_7_), channel_id=1, source_target_pairs={{0,4},{4,8},{8,12},{12,16},{16,20},{20,24},{24,28},{28,0},{1,5},{5... | collective-permute-start | bytes 1572872 | tf_op jit(solution)/shard_map/va4_right/ppermute | solution.py:374
  95.2 32.2 %collective-permute-start.31 = (bf16[2,4,256,128]{3,2,1,0:T(8,128)(2,1)}, bf16[2,4,256,128]{3,2,1,0:T(8,128)(2,1)S(1)}, u32[]{:S(2)}, u32[]{:S(2)}) collective-permute-start(bf16[2,4,256,128]{3,2,1,0:T(8,128)(2,1)} %copy-done.2), channel_id=1, source_target_pairs={{0,28},{4,0},{8,4},{12,8},{16,12},{20,16},{24,20},{28,24},{1,29},{... | collective-permute-start | bytes 1572872 | tf_op jit(solution)/shard_map/kvb1_left/ppermute | solution.py:374
  98.9 31.2 %collective-permute-start.22 = (bf16[4,512,128]{2,1,0:T(8,128)(2,1)}, bf16[4,512,128]{2,1,0:T(8,128)(2,1)S(1)}, u32[]{:S(2)}, u32[]{:S(2)}) collective-permute-start(bf16[4,512,128]{2,1,0:T(8,128)(2,1)} %collective-permute-done.18.refs_4_), channel_id=1, source_target_pairs={{0,4},{4,8},{8,12},{12,16},{16,20},{20,24},{24,28},{28,0},{1,5},{5... | collective-permute-start | bytes 1572872 | tf_op jit(solution)/shard_map/ka3_right/ppermute | solution.py:374
  98.9 41.3 %collective-permute-start.25 = (bf16[4,512,128]{2,1,0:T(8,128)(2,1)}, bf16[4,512,128]{2,1,0:T(8,128)(2,1)S(1)}, u32[]{:S(2)}, u32[]{:S(2)}) collective-permute-start(bf16[4,512,128]{2,1,0:T(8,128)(2,1)} %collective-permute-done.20.refs_5_), channel_id=1, source_target_pairs={{0,28},{4,0},{8,4},{12,8},{16,12},{20,16},{24,20},{28,24},{1,29},{... | collective-permute-start | bytes 1572872 | tf_op jit(solution)/shard_map/ka3_left/ppermute | solution.py:374
  130.1 24.1 %collective-permute-start.23 = (bf16[4,512,128]{2,1,0:T(8,128)(2,1)S(1)}, bf16[4,512,128]{2,1,0:T(8,128)(2,1)S(1)}, u32[]{:S(2)}, u32[]{:S(2)}) collective-permute-start(bf16[4,512,128]{2,1,0:T(8,128)(2,1)S(1)} %collective-permute-done.22.refs_4_), channel_id=1, source_target_pairs={{0,4},{4,8},{8,12},{12,16},{16,20},{20,24},{24,28},{28,0},{1,5},{5... | collective-permute-start | bytes 1572872 | tf_op jit(solution)/shard_map/ka4_right/ppermute | solution.py:374
  140.2 27.2 %collective-permute-start.32 = (bf16[2,4,256,128]{3,2,1,0:T(8,128)(2,1)S(1)}, bf16[2,4,256,128]{3,2,1,0:T(8,128)(2,1)S(1)}, u32[]{:S(2)}, u32[]{:S(2)}) collective-permute-start(bf16[2,4,256,128]{3,2,1,0:T(8,128)(2,1)S(1)} %collective-permute-done.31.refs_8_.refs_14_), channel_id=1, source_target_pairs={{0,28},{4,0},{8,4},{12,8},{16,12},{20,16},{24,20},{28,24},{1,29},{... | collective-permute-start | bytes 1572872 | tf_op jit(solution)/shard_map/kvb2_left/ppermute | solution.py:374
  145.5 23.8 %collective-permute-start.28 = (bf16[2,4,256,128]{3,2,1,0:T(8,128)(2,1)S(1)}, bf16[2,4,256,128]{3,2,1,0:T(8,128)(2,1)S(1)}, u32[]{:S(2)}, u32[]{:S(2)}) collective-permute-start(bf16[2,4,256,128]{3,2,1,0:T(8,128)(2,1)S(1)} %copy-done.5), channel_id=1, source_target_pairs={{0,4},{4,8},{8,12},{12,16},{16,20},{20,24},{24,28},{28,0},{1,5},{5... | collective-permute-start | bytes 1572872 | tf_op jit(solution)/shard_map/kvc1_right/ppermute | solution.py:374
  145.5 24.0 %collective-permute-start.35 = (bf16[2,4,256,128]{3,2,1,0:T(8,128)(2,1)S(1)}, bf16[2,4,256,128]{3,2,1,0:T(8,128)(2,1)S(1)}, u32[]{:S(2)}, u32[]{:S(2)}) collective-permute-start(bf16[2,4,256,128]{3,2,1,0:T(8,128)(2,1)S(1)} %collective-permute-done.34.refs_9_.refs_15_), channel_id=1, source_target_pairs={{0,28},{4,0},{8,4},{12,8},{16,12},{20,16},{24,20},{28,24},{1,29},{... | collective-permute-start | bytes 1572872 | tf_op jit(solution)/shard_map/kvc2_left/ppermute | solution.py:374
  164.7 62.8 %collective-permute-start.42 = (bf16[4,560,128]{2,1,0:T(8,128)(2,1)}, bf16[4,560,128]{2,1,0:T(8,128)(2,1)S(1)}, u32[]{:S(2)}, u32[]{:S(2)}) collective-permute-start(bf16[4,560,128]{2,1,0:T(8,128)(2,1)} %get-tuple-element.105), channel_id=1, source_target_pairs={{0,32},{32,64},{64,96},{1,33},{33,65},{65,97},{2,34},{34,66},{66,9... | collective-permute-start | bytes 1720328 | tf_op jit(solution)/shard_map/partials/ppermute | solution.py:379
  166.0 24.5 %collective-permute-start.24 = (bf16[2,4,256,128]{3,2,1,0:T(8,128)(2,1)S(1)}, bf16[2,4,256,128]{3,2,1,0:T(8,128)(2,1)S(1)}, u32[]{:S(2)}, u32[]{:S(2)}) collective-permute-start(bf16[2,4,256,128]{3,2,1,0:T(8,128)(2,1)S(1)} %collective-permute-done.16.refs_6_.refs_12_), channel_id=1, source_target_pairs={{0,4},{4,8},{8,12},{12,16},{16,20},{20,24},{24,28},{28,0},{1,5},{5... | collective-permute-start | bytes 1572872 | tf_op jit(solution)/shard_map/kvb2_right/ppermute | solution.py:374
  167.5 23.0 %collective-permute-start.33 = (bf16[2,4,256,128]{3,2,1,0:T(8,128)(2,1)S(1)}, bf16[2,4,256,128]{3,2,1,0:T(8,128)(2,1)S(1)}, u32[]{:S(2)}, u32[]{:S(2)}) collective-permute-start(bf16[2,4,256,128]{3,2,1,0:T(8,128)(2,1)S(1)} %collective-permute-done.32.refs_6_.refs_10_), channel_id=1, source_target_pairs={{0,28},{4,0},{8,4},{12,8},{16,12},{20,16},{24,20},{28,24},{1,29},{... | collective-permute-start | bytes 1572872 | tf_op jit(solution)/shard_map/kvb3_left/ppermute | solution.py:374
  169.3 23.2 %collective-permute-start.29 = (bf16[2,4,256,128]{3,2,1,0:T(8,128)(2,1)S(1)}, bf16[2,4,256,128]{3,2,1,0:T(8,128)(2,1)S(1)}, u32[]{:S(2)}, u32[]{:S(2)}) collective-permute-start(bf16[2,4,256,128]{3,2,1,0:T(8,128)(2,1)S(1)} %collective-permute-done.28.refs_7_.refs_13_), channel_id=1, source_target_pairs={{0,4},{4,8},{8,12},{12,16},{16,20},{20,24},{24,28},{28,0},{1,5},{5... | collective-permute-start | bytes 1572872 | tf_op jit(solution)/shard_map/kvc2_right/ppermute | solution.py:374
  169.5 24.0 %collective-permute-start.36 = (bf16[2,4,256,128]{3,2,1,0:T(8,128)(2,1)S(1)}, bf16[2,4,256,128]{3,2,1,0:T(8,128)(2,1)S(1)}, u32[]{:S(2)}, u32[]{:S(2)}) collective-permute-start(bf16[2,4,256,128]{3,2,1,0:T(8,128)(2,1)S(1)} %collective-permute-done.35.refs_7_.refs_11_), channel_id=1, source_target_pairs={{0,28},{4,0},{8,4},{12,8},{16,12},{20,16},{24,20},{28,24},{1,29},{... | collective-permute-start | bytes 1572872 | tf_op jit(solution)/shard_map/kvc3_left/ppermute | solution.py:374
  192.5 21.4 %collective-permute-start.30 = (bf16[2,4,256,128]{3,2,1,0:T(8,128)(2,1)S(1)}, bf16[2,4,256,128]{3,2,1,0:T(8,128)(2,1)S(1)}, u32[]{:S(2)}, u32[]{:S(2)}) collective-permute-start(bf16[2,4,256,128]{3,2,1,0:T(8,128)(2,1)S(1)} %collective-permute-done.29.refs_5_.refs_9_), channel_id=1, source_target_pairs={{0,4},{4,8},{8,12},{12,16},{16,20},{20,24},{24,28},{28,0},{1,5},{5... | collective-permute-start | bytes 1572872 | tf_op jit(solution)/shard_map/kvc3_right/ppermute | solution.py:374
  193.5 21.5 %collective-permute-start.38 = (bf16[2,4,256,128]{3,2,1,0:T(8,128)(2,1)S(1)}, bf16[2,4,256,128]{3,2,1,0:T(8,128)(2,1)S(1)}, u32[]{:S(2)}, u32[]{:S(2)}) collective-permute-start(bf16[2,4,256,128]{3,2,1,0:T(8,128)(2,1)S(1)} %collective-permute-done.36.refs_7_.refs_13_), channel_id=1, source_target_pairs={{0,28},{4,0},{8,4},{12,8},{16,12},{20,16},{24,20},{28,24},{1,29},{... | collective-permute-start | bytes 1572872 | tf_op jit(solution)/shard_map/kvc4_left/ppermute | solution.py:374
  206.1 22.7 %collective-permute-start.43 = (bf16[4,560,128]{2,1,0:T(8,128)(2,1)S(1)}, bf16[4,560,128]{2,1,0:T(8,128)(2,1)S(1)}, u32[]{:S(2)}, u32[]{:S(2)}) collective-permute-start(bf16[4,560,128]{2,1,0:T(8,128)(2,1)S(1)} %get-tuple-element.104), channel_id=1, source_target_pairs={{0,64},{32,96},{1,65},{33,97},{2,66},{34,98},{3,67},{35,99},{4,68}... | collective-permute-start | bytes 1720328 | tf_op jit(solution)/shard_map/partials/ppermute | solution.py:379
  226.1 25.1 %collective-permute-start.40 = (bf16[4,560,128]{2,1,0:T(8,128)(2,1)S(1)}, bf16[4,560,128]{2,1,0:T(8,128)(2,1)S(1)}, u32[]{:S(2)}, u32[]{:S(2)}) collective-permute-start(bf16[4,560,128]{2,1,0:T(8,128)(2,1)S(1)} %get-tuple-element.107), channel_id=1, source_target_pairs={{0,64},{32,96},{1,65},{33,97},{2,66},{34,98},{3,67},{35,99},{4,68}... | collective-permute-start | bytes 1720328 | tf_op jit(solution)/shard_map/partials/ppermute | solution.py:379
  227.4 23.8 %collective-permute-start.41 = (bf16[4,560,128]{2,1,0:T(8,128)(2,1)S(1)}, bf16[4,560,128]{2,1,0:T(8,128)(2,1)S(1)}, u32[]{:S(2)}, u32[]{:S(2)}) collective-permute-start(bf16[4,560,128]{2,1,0:T(8,128)(2,1)S(1)} %get-tuple-element.106), channel_id=1, source_target_pairs={{0,96},{1,97},{2,98},{3,99},{4,100},{5,101},{6,102},{7,103},{8,104... | collective-permute-start | bytes 1720328 | tf_op jit(solution)/shard_map/partials/ppermute | solution.py:379
  (36 other events, 381.8 us)

commit v3 on v2

v3 whole, which is shorter than its diff:
```python
import functools
import math

import jax
import jax.numpy as jnp
from jax import lax
from jax.experimental import pallas as pl
from jax.experimental.pallas import tpu as pltpu
from jax.sharding import Mesh, PartitionSpec as P

BLOCK = 128
HEAD = 128
ROWS = 4
RING = 8
NEG_FILL = -1e30
ROPE_BASE = 10000.0
VMEM_LIMIT = 24 << 20
IDLE = 4
STAT = 48
CHUNKS = ((0, 4), (4, 4))
GROUPS = (((0, 1, 2), (3, 4)), ((0, 1), (2, 3), (4,)))


QUARTER = (1.5703125, 4.837512969970703e-4, 7.54978995489188216e-8)


def sin_cos(phase):
    turns = jnp.floor(phase * (2 / math.pi) + 0.5)
    x = phase
    for part in QUARTER:
        x = x - turns * part
    square = x * x
    sine = ((-1.9515295891e-4 * square + 8.3321608736e-3) * square - 1.6666654611e-1) * square
    sine = sine * x + x
    cosine = ((2.443315711809948e-5 * square - 1.388731625493765e-3) * square + 4.166664568298827e-2)
    cosine = cosine * square * square - 0.5 * square + 1.0
    quadrant = turns.astype(jnp.int32) & 3
    odd = (quadrant & 1) == 1
    sine, cosine = jnp.where(odd, cosine, sine), jnp.where(odd, sine, cosine)
    sine = jnp.where(quadrant >= 2, -sine, sine)
    cosine = jnp.where((quadrant == 1) | (quadrant == 2), -cosine, cosine)
    return sine, cosine


def rotate_kernel(angle_ref, freq_ref, q_ref, k_ref, *outs):
    freq = freq_ref[...]
    lane = lax.broadcasted_iota(jnp.int32, (BLOCK, HEAD), 1)
    low = lane < HEAD // 2
    heads = q_ref.shape[1] // HEAD
    for pair in range(heads // 2):
        even = angle_ref[:, 2 * pair : 2 * pair + 1]
        odd = angle_ref[:, 2 * pair + 1 : 2 * pair + 2]
        sine, cosine = sin_cos(jnp.where(low, even, odd) * freq)
        sine_turned = pltpu.roll(sine, HEAD // 2, 1)
        cosine_turned = pltpu.roll(cosine, HEAD // 2, 1)
        for h in (2 * pair, 2 * pair + 1):
            first, second = (sine, sine_turned) if h % 2 == 0 else (sine_turned, sine)
            signed = jnp.where(low, -first, second)
            first, second = (cosine, cosine_turned) if h % 2 == 0 else (cosine_turned, cosine)
            plain = jnp.where(low, first, second)
            cols = slice(h * HEAD, (h + 1) * HEAD)

            def turn(x):
                x = x.astype(jnp.float32)
                return (x * plain + pltpu.roll(x, HEAD // 2, 1) * signed).astype(jnp.bfloat16)

            part = slice(h % 4 * HEAD, (h % 4 + 1) * HEAD)
            outs[0][:, cols] = turn(q_ref[:, cols])
            outs[1 + h // 4][0, part, :] = turn(k_ref[:, cols])


def rotate(angles, queries, keys):
    half = HEAD // 2
    inv_freq = ROPE_BASE ** (-jnp.arange(half).astype(jnp.float32) / half)
    inv_freq = jnp.concatenate([inv_freq, inv_freq])[None]
    heads = angles.shape[0]
    bf16 = jnp.bfloat16
    rows = pl.BlockSpec((BLOCK, heads * HEAD), lambda b: (b, 0))
    tiled = pl.BlockSpec((1, 4 * HEAD, BLOCK), lambda b: (b, 0, 0))
    return pl.pallas_call(
        rotate_kernel,
        out_shape=[
            jax.ShapeDtypeStruct(queries.shape, bf16),
            jax.ShapeDtypeStruct((4, 4 * HEAD, BLOCK), bf16),
            jax.ShapeDtypeStruct((4, 4 * HEAD, BLOCK), bf16),
        ],
        grid=(4,),
        in_specs=[
            pl.BlockSpec((BLOCK, heads), lambda b: (b, 0)),
            pl.BlockSpec((1, HEAD), lambda b: (0, 0)),
            rows,
            rows,
        ],
        out_specs=[rows, tiled, tiled],
        compiler_params=pltpu.CompilerParams(vmem_limit_bytes=VMEM_LIMIT),
        cost_estimate=pl.CostEstimate(flops=5 * 10**9, bytes_accessed=6 << 20, transcendentals=0),
        name="rotate",
    )(angles.T, inv_freq, queries, keys)


def attend_kernel(offsets, heads, first, last, meta, *refs):
    count = len(offsets)
    given_q, refs = refs[0], refs[1:]
    k_refs, v_refs = refs[:count], refs[count : 2 * count]
    rest = list(refs[2 * count :])
    acc, m_run, l_run, q_ref, k_all, v_all, todo = rest[-7:]
    rest = rest[:-7]
    given = None
    if not first:
        given, rest = rest[:3], rest[3:]
    r = pl.program_id(0)
    scale = HEAD**-0.5 * math.log2(math.e)

    @pl.when(r == 0)
    def _():
        for at in range(count):
            k_all[at] = k_refs[at][...]
            v_all[at] = v_refs[at][...]
        q_ref[IDLE * BLOCK :, :] = jnp.zeros((BLOCK, heads * HEAD), jnp.bfloat16)
        acc[IDLE] = jnp.zeros((heads * HEAD, BLOCK), jnp.float32)
        m_run[IDLE] = jnp.full((8, BLOCK), NEG_FILL)
        l_run[IDLE] = jnp.zeros((8, BLOCK), jnp.float32)

    q_ref[: IDLE * BLOCK, :] = given_q[0]
    if first:
        acc[:IDLE] = jnp.zeros((IDLE, heads * HEAD, BLOCK), jnp.float32)
        m_run[:IDLE] = jnp.full((IDLE, 8, BLOCK), NEG_FILL)
        l_run[:IDLE] = jnp.zeros((IDLE, 8, BLOCK), jnp.float32)
    else:
        acc[:IDLE] = given[0][...]
        m_run[:IDLE] = given[1][...]
        l_run[:IDLE] = given[2][...]

    span = range(heads)
    cols = [slice(h * HEAD, (h + 1) * HEAD) for h in span]

    def two(items, causal):
        olds, scores = [], []
        for qb, at, kb in items:
            q_rows = pl.ds(pl.multiple_of(qb * BLOCK, BLOCK), BLOCK)
            olds.append((m_run[qb], l_run[qb]))
            scores.append(
                [
                    lax.dot_general(
                        k_all[at, kb, cols[h], :],
                        q_ref[q_rows, cols[h]],
                        (((1,), (1,)), ((), ())),
                        preferred_element_type=jnp.float32,
                    )
                    for h in span
                ]
            )
        if causal:
            key_pos = lax.broadcasted_iota(jnp.int32, (BLOCK, BLOCK), 0)
            query_pos = lax.broadcasted_iota(jnp.int32, (BLOCK, BLOCK), 1)
            seen = key_pos <= query_pos
            scores = [[jnp.where(seen, s, NEG_FILL) for s in group] for group in scores]
        results = []
        for (qb, at, kb), (m_old, l_old), group in zip(items, olds, scores):
            tops = [jnp.max(s, axis=0, keepdims=True) for s in group]
            if heads < 8:
                tops.append(m_old[heads:])
            m_new = jnp.maximum(m_old, jnp.concatenate(tops, axis=0))
            fade = jnp.exp2((m_old - m_new) * scale)
            weights = [jnp.exp2((group[h] - m_new[h : h + 1]) * scale) for h in span]
            sums = [jnp.sum(w, axis=0, keepdims=True) for w in weights]
            if heads < 8:
                sums.append(jnp.zeros((8 - heads, BLOCK), jnp.float32))
            mixed = [
                jnp.dot(
                    v_all[at, kb, cols[h], :],
                    weights[h].astype(jnp.bfloat16),
                    preferred_element_type=jnp.float32,
                )
                for h in span
            ]
            results.append((m_new, l_old * fade + jnp.concatenate(sums, axis=0), fade, mixed))
        wholes = [
            [acc[qb, cols[h], :] * fade[h : h + 1] + mixed[h] for h in span]
            for (qb, _, _), (_, _, fade, mixed) in zip(items, results)
        ]
        for (qb, _, _), (m_new, l_new, _, _), whole in zip(items, results, wholes):
            m_run[qb] = m_new
            l_run[qb] = l_new
            for h in span:
                acc[qb, cols[h], :] = whole[h]

    if 0 in offsets:
        here = offsets.index(0)

        @pl.when(r == 0)
        def _():
            def own(i, carry):
                two([(2 * i, here, 2 * i), (2 * i + 1, here, 2 * i + 1)], True)
                return carry

            lax.fori_loop(0, 2, own, 0)

    length, newest = jnp.int32(0), jnp.int32(-1)
    for at, offset in enumerate(offsets):
        for choice in range(4 if offset == 0 else 1):
            for qb in range(4):
                code = meta[(r * 4 + qb) * RING + offset % RING]
                if offset == 0:
                    valid, kb = (code >> choice) & 1, choice
                else:
                    valid, kb = (code > 0).astype(jnp.int32), jnp.maximum(code - 1, 0)
                item = qb + at * 16 + kb * 256
                clash = valid & length & (newest == qb).astype(jnp.int32) & 1
                todo[length] = jnp.where(clash == 1, IDLE, item)
                todo[length + 1] = item
                length += valid * (1 + clash)
                newest = jnp.where(valid == 1, qb, newest)
    todo[length] = IDLE

    def step(i, carry):
        items = []
        for side in (0, 1):
            item = todo[2 * i + side]
            items.append((item & 15, (item >> 4) & 15, item >> 8))
        two(items, False)
        return carry

    lax.fori_loop(0, (length + 1) >> 1, step, 0)

    if not last:
        acc_out, m_out, l_out = rest
        acc_out[...] = acc[:IDLE]
        m_out[...] = m_run[:IDLE]
        l_out[...] = l_run[:IDLE]
    else:
        acc0_ref, m0_ref, l0_ref, packed_ref = rest

        @pl.when(r == 0)
        def _():
            acc0_ref[...] = acc[:IDLE]
            m0_ref[...] = m_run[:IDLE]
            l0_ref[...] = l_run[:IDLE]

        @pl.when(r > 0)
        def _():
            def pack(qb, carry):
                pieces = []
                for value in (m_run[qb], l_run[qb]):
                    for _ in range(3):
                        piece = value.astype(jnp.bfloat16).astype(jnp.float32)
                        pieces.append(piece)
                        value = value - piece
                packed_ref[0, qb, heads * HEAD :, :] = jnp.concatenate(pieces, axis=0).astype(
                    jnp.bfloat16
                )
                total = l_run[qb]
                inverse = 1.0 / jnp.where(total > 0, total, 1.0)
                for h in span:
                    packed_ref[0, qb, cols[h], :] = (
                        acc[qb, cols[h], :] * inverse[h : h + 1]
                    ).astype(jnp.bfloat16)
                return carry

            lax.fori_loop(0, 4, pack, 0)


def attend(meta, queries, chunk, offsets, keys, values, state, last):
    first_head, heads = chunk
    width = heads * HEAD
    first = state is None
    acc_spec = pl.BlockSpec((4, width, BLOCK), lambda r, meta: (r, 0, 0))
    run_spec = pl.BlockSpec((4, 8, BLOCK), lambda r, meta: (r, 0, 0))
    state_specs = [acc_spec, run_spec, run_spec]
    in_specs = [
        pl.BlockSpec(
            (1, 512, width),
            lambda r, meta: (jnp.minimum(meta[16 * RING] + r, ROWS - 1), 0, first_head // heads),
        )
    ]
    in_specs += [pl.BlockSpec((4, width, BLOCK), lambda r, meta: (0, 0, 0))] * (2 * len(offsets))
    operands = [queries, *keys, *values]
    if not first:
        in_specs += state_specs
        operands += list(state)
    f32 = jnp.float32
    if last:
        out_shape = [
            jax.ShapeDtypeStruct((4, width, BLOCK), f32),
            jax.ShapeDtypeStruct((4, 8, BLOCK), f32),
            jax.ShapeDtypeStruct((4, 8, BLOCK), f32),
            jax.ShapeDtypeStruct((3, 4, width + STAT, BLOCK), jnp.bfloat16),
        ]
        out_specs = [
            pl.BlockSpec((4, width, BLOCK), lambda r, meta: (0, 0, 0)),
            pl.BlockSpec((4, 8, BLOCK), lambda r, meta: (0, 0, 0)),
            pl.BlockSpec((4, 8, BLOCK), lambda r, meta: (0, 0, 0)),
            pl.BlockSpec((1, 4, width + STAT, BLOCK), lambda r, meta: (jnp.maximum(r - 1, 0), 0, 0, 0)),
        ]
    else:
        out_shape = [
            jax.ShapeDtypeStruct((16, width, BLOCK), f32),
            jax.ShapeDtypeStruct((16, 8, BLOCK), f32),
            jax.ShapeDtypeStruct((16, 8, BLOCK), f32),
        ]
        out_specs = state_specs
    count = len(offsets)
    scratch = [
        pltpu.VMEM((5, width, BLOCK), f32),
        pltpu.VMEM((5, 8, BLOCK), f32),
        pltpu.VMEM((5, 8, BLOCK), f32),
        pltpu.VMEM((5 * BLOCK, width), jnp.bfloat16),
        pltpu.VMEM((count, 4, width, BLOCK), jnp.bfloat16),
        pltpu.VMEM((count, 4, width, BLOCK), jnp.bfloat16),
        pltpu.SMEM((80,), jnp.int32),
    ]
    return list(pl.pallas_call(
        functools.partial(attend_kernel, offsets, heads, first, last),
        out_shape=out_shape,
        grid_spec=pltpu.PrefetchScalarGridSpec(
            num_scalar_prefetch=1,
            grid=(ROWS,),
            in_specs=in_specs,
            out_specs=out_specs,
            scratch_shapes=scratch,
        ),
        compiler_params=pltpu.CompilerParams(vmem_limit_bytes=VMEM_LIMIT),
        cost_estimate=pl.CostEstimate(
            flops=int((2 + 3 * len(offsets)) * 1.1e9),
            bytes_accessed=1 << 20,
            transcendentals=0,
        ),
        name=f"attend_{first_head}_{'_'.join(str(o % RING) for o in offsets)}",
    )(meta, *operands))


def join_kernel(heads, acc_ref, m_ref, l_ref, one, two, three, *rest):
    out_ref = rest[-1]
    width = heads * HEAD
    tops, sums = [m_ref[0]], [l_ref[0]]
    for part in (one, two, three):
        stats = part[0, width:, :].astype(jnp.float32)
        top = (stats[16:24] + stats[8:16]) + stats[0:8]
        total = (stats[40:48] + stats[32:40]) + stats[24:32]
        tops.append(jnp.where(total > 0, top, NEG_FILL))
        sums.append(total)
    scale = HEAD**-0.5 * math.log2(math.e)
    highest = jnp.maximum(jnp.maximum(tops[0], tops[1]), jnp.maximum(tops[2], tops[3]))
    fades = [jnp.exp2((top - highest) * scale) for top in tops]
    shares = [fades[0]] + [fades[i] * sums[i] for i in (1, 2, 3)]
    whole = fades[0] * sums[0] + shares[1] + shares[2] + shares[3]
    inverse = 1.0 / whole
    for h in range(heads):
        cols = slice(h * HEAD, (h + 1) * HEAD)
        mixed = acc_ref[0, cols, :] * shares[0][h : h + 1, :]
        for i, part in enumerate((one, two, three)):
            mixed += part[0, cols, :].astype(jnp.float32) * shares[i + 1][h : h + 1, :]
        mixed = mixed * inverse[h : h + 1, :]
        out_ref[:, cols] = mixed.T.astype(jnp.bfloat16)


def join(chunk, state, parts, out):
    first_head, heads = chunk
    width = heads * HEAD
    in_specs = [
        pl.BlockSpec((1, width, BLOCK), lambda b: (b, 0, 0)),
        pl.BlockSpec((1, 8, BLOCK), lambda b: (b, 0, 0)),
        pl.BlockSpec((1, 8, BLOCK), lambda b: (b, 0, 0)),
    ] + [pl.BlockSpec((1, width + STAT, BLOCK), lambda b: (b, 0, 0))] * 3
    operands = [*state, *parts]
    aliases = {}
    if out is not None:
        aliases = {len(operands): 0}
        in_specs.append(pl.BlockSpec(memory_space=pl.ANY))
        operands.append(out)
    return pl.pallas_call(
        functools.partial(join_kernel, heads),
        out_shape=jax.ShapeDtypeStruct((512, 1024), jnp.bfloat16),
        grid=(4,),
        in_specs=in_specs,
        out_specs=pl.BlockSpec((BLOCK, width), lambda b: (b, first_head // heads)),
        input_output_aliases=aliases,
        compiler_params=pltpu.CompilerParams(vmem_limit_bytes=VMEM_LIMIT),
        cost_estimate=pl.CostEstimate(
            flops=512 * width * 10, bytes_accessed=512 * width * 14, transcendentals=0
        ),
        name=f"join_{first_head}",
    )(*operands)


def shift(value, axis, step):
    size = lax.axis_size(axis)
    return lax.ppermute(value, axis, [(i, (i + step) % size) for i in range(size)])


def to_row(value, step):
    moves = [(i, i + step) for i in range(ROWS) if 0 <= i + step < ROWS]
    return lax.ppermute(value, "y", moves)


def swap(value, axis, bit):
    size = lax.axis_size(axis)
    return lax.ppermute(value, axis, [(i, i ^ bit) for i in range(size)])


def after(value, *others):
    return lax.optimization_barrier((value, *others))[0]


class Wire:
    def __init__(self, side, sign, depth=2):
        self.side, self.sign, self.depth = side, sign, depth
        self.sent = []

    def send(self, name, ring, distance, *others):
        source = ring[-self.sign * (distance - 1)]
        waits = list(others)
        if len(self.sent) >= self.depth:
            waits.append(self.sent[-self.depth])
        if waits:
            source = after(source, *waits)
        with jax.named_scope(f"{name}{distance}_{self.side}"):
            got = shift(source, "z", self.sign)
        self.sent.append(got)
        ring[-self.sign * distance if distance < 4 else 4] = got


def shards(query_states, key_states, value_states, gate_logits, selected_blocks):
    my_y, my_z = lax.axis_index("y"), lax.axis_index("z")
    gate_values = jax.nn.sigmoid(gate_logits.astype(jnp.float32))
    total = jnp.sum(gate_values, axis=1, keepdims=True)
    before = jnp.zeros_like(total)
    value_tiles = value_states.reshape(4, BLOCK, -1).transpose(0, 2, 1)
    va, vb = {0: value_tiles[:, : 4 * HEAD]}, {0: value_tiles[:, 4 * HEAD :]}
    right, left = Wire("right", 1), Wire("left", -1)
    for wire in (right, left):
        wire.send("va", va, 1)
    with jax.named_scope("prefix"):
        for bit in (1, 2, 4):
            other = swap(total, "z", bit)
            before = before + jnp.where((my_z & bit) != 0, other, 0.0)
            total = total + other
    for wire in (right, left):
        wire.send("vb", vb, 1, total)
    total = after(total, va[1], va[-1])
    for wire in (right, left):
        wire.send("va", va, 2)
    picks = selected_blocks.T.astype(jnp.float32)
    with jax.named_scope("prefix"):
        for bit in (1, 2):
            other = swap(jnp.concatenate([total, picks], axis=1), "y", bit)
            before = before + jnp.where((my_y & bit) != 0, other[:, :1], 0.0)
            total = total + other[:, :1]
            picks = jnp.concatenate([picks, other[:, 1:]], axis=1)
    for wire in (right, left):
        wire.send("vb", vb, 2)
    angles = before + jnp.cumsum(gate_values, axis=1)
    angles = after(angles, vb[1], vb[-1])
    query_rot, keys_a, keys_b = rotate(angles, query_states, key_states)
    ka, kb = {0: keys_a}, {0: keys_b}
    with jax.named_scope("queries"):
        queries = lax.all_gather(query_rot, "y")

    picks = picks.astype(jnp.int32).T.reshape(4, 1, 4, 8)
    wanted = (my_y + lax.broadcasted_iota(jnp.int32, (4, 4, 1, 1), 1)) ^ my_y
    turn = lax.broadcasted_iota(jnp.int32, (4, 4, 1, 1), 0)
    blocks = jnp.sum(jnp.where(wanted == turn, picks, 0), axis=0).reshape(16, 1, 8)
    row = lax.broadcasted_iota(jnp.int32, (16, RING, 8), 0)
    distance = lax.broadcasted_iota(jnp.int32, (16, RING, 8), 1)
    own = ((my_y + row // 4) * RING + my_z) * 4 + row % 4
    hit = (blocks >> 5 == my_y) & (((blocks >> 2) - my_z) & 7 == distance)
    hit &= (blocks != own) & (my_y + row // 4 < ROWS)
    code = jnp.where(distance == 0, 1 << (blocks & 3), (blocks & 3) + 1)
    meta = jnp.sum(jnp.where(hit, code, 0), axis=2).reshape(-1)
    meta = jnp.concatenate([meta, my_y.astype(jnp.int32)[None]])

    def call(part, group, state, last):
        offsets = []
        for distance in group:
            offsets += [distance] if distance in (0, 4) else [-distance, distance]
        keys, values = (ka, va) if part == 0 else (kb, vb)
        return attend(
            meta,
            queries,
            CHUNKS[part],
            tuple(offsets),
            [keys[o] for o in offsets],
            [values[o] for o in offsets],
            state,
            last,
        )

    def deliver(part, state, orders):
        parts = []
        for s in (1, 2, 3):
            packed = state[3][s - 1]
            if orders and parts:
                packed = after(packed, parts[-1])
            with jax.named_scope(f"partial{part}_{s}"):
                parts.append(to_row(packed, s))
        return parts

    for name, ring, distance in (("ka", ka, 1), ("va", va, 3), ("ka", ka, 2)):
        for wire in (right, left):
            wire.send(name, ring, distance)
    right.send("va", va, 4)
    left.send("kb", kb, 1)
    for wire in (right, left):
        wire.send("ka", ka, 3)
    state = call(0, GROUPS[0][0], None, False)
    right.send("kb", kb, 1, state[1])
    left.send("kb", kb, 2, state[1])
    right.send("ka", ka, 4, state[1])
    left.send("vb", vb, 3, state[1])
    right.send("kb", kb, 2)
    left.send("kb", kb, 3)
    state = call(0, GROUPS[0][1], state, True)
    right.send("vb", vb, 3, state[1])
    left.send("vb", vb, 4, state[1])
    right.send("kb", kb, 3, state[1])
    left.send("kb", kb, 4, state[1])
    mine_a, parts_a = state[:3], deliver(0, state, True)
    state = call(1, GROUPS[1][0], None, False)
    state[1] = after(state[1], parts_a[0])
    state = call(1, GROUPS[1][1], state, False)
    state[1] = after(state[1], parts_a[1])
    state = call(1, GROUPS[1][2], state, True)
    out = join(CHUNKS[0], mine_a, parts_a, None)
    return join(CHUNKS[1], state[:3], deliver(1, state, False), out)


def solution(mesh):
    grid = Mesh(mesh.devices.reshape(2, ROWS, RING, 4), ("dp", "y", "z", "head"))
    tokens = ("dp", "y", "z")
    placed = (
        P(tokens, "head"),
        P(tokens, "head"),
        P(tokens, "head"),
        P("head", tokens),
        P(tokens, None),
    )
    return jax.shard_map(
        shards, mesh=grid, in_specs=placed, out_specs=P(tokens, "head"), check_vma=False
    )
```

time: 256 us -> 249 us (0.973)
  waiting for transfers between devices: 82.3 us -> 101 us
  Pallas kernels: 78.7 us -> 61.2 us
  between operations: 0.42 us -> 13.8 us
  starting transfers between devices: 73.6 us -> 60.7 us
  local copies, waits for them, and re-layouts: 15.7 us -> 9.45 us
    ppermute x28, waiting for transfers between devices: 34.4 us -> 65 us  [shift(): lax.ppermute(value, axis, [(i, (i + step) % size) for i in range(size)])]
    pallas_call x6 -> x5, Pallas kernels: 70.8 us -> 52.7 us  [attend(): pl.pallas_call(functools.partial(attend_kernel, offsets, heads, first, la...]
    ppermute x12 -> x6, waiting for transfers between devices: 29.1 us -> 16.2 us  [to_row(): return lax.ppermute(value, 'y', moves)]
    ppermute x28, starting transfers between devices: 49.4 us -> 40.5 us  [shift(): lax.ppermute(value, axis, [(i, (i + step) % size) for i in range(size)])]
    unnamed x30 -> x20, local copies, waits for them, and re-layouts: 12.4 us -> 4.88 us
    ppermute x12 -> x6, starting transfers between devices: 15.6 us -> 11.4 us  [to_row(): return lax.ppermute(value, 'y', moves)]
  transfers between devices with their start and end apart: 45 -> 40, of which waited for: 17 -> 16; matrix products, arithmetic and copies ran while one was open for 2% -> 1% of each run, Pallas kernels for 30% -> 22%
where the time goes in v3:
time: 249 us; the launch traced here: 248 us
  waiting for transfers between devices  101 us (41%)
  Pallas kernels  61.2 us (25%)
  starting transfers between devices  60.7 us (24%)
  between operations  13.8 us (6%)
  local copies, waits for them, and re-layouts  9.45 us (4%)
    ppermute x28, waiting for transfers between devices, shift(): lax.ppermute(value, axis, [(i, (i + step) % size) for i in range(size)])  65 us
    pallas_call x5, Pallas kernels, attend(): pl.pallas_call(functools.partial(attend_kernel, offsets, heads, first, la...  52.7 us
    ppermute x28, starting transfers between devices, shift(): lax.ppermute(value, axis, [(i, (i + step) % size) for i in range(size)])  40.5 us
    ppermute x5, waiting for transfers between devices, swap(): return lax.ppermute(value, axis, [(i, i ^ bit) for i in range(size)])  19.5 us
    ppermute x6, waiting for transfers between devices, to_row(): return lax.ppermute(value, 'y', moves)  16.2 us
    ppermute x6, starting transfers between devices, to_row(): return lax.ppermute(value, 'y', moves)  11.4 us
    ppermute x5, starting transfers between devices, swap(): return lax.ppermute(value, axis, [(i, i ^ bit) for i in range(size)])  8.74 us
  transfers between devices with their start and end apart: 40, of which 16 were waited for; matrix products, arithmetic and copies ran while one was open for 1% of the time, Pallas kernels for 22%

profile of v3, /device:TPU:2, one launch (start us, length us, event | category | flops | bytes accessed | tf_op | source)
XLA Modules:
  0.0 247.5 jit_solution(9635251545572018942)
XLA Ops:
  10.3 5.9 %collective-permute-start.3 = (bf16[4,512,128]{2,1,0:T(8,128)(2,1)S(1)}, bf16[4,512,128]{2,1,0:T(8,128)(2,1)}, u32[]{:S(2)}, u32[]{:S(2)}) collective-permute-start(bf16[4,512,128]{2,1,0:T(8,128)(2,1)S(1)} %get-tuple-element.114.refs_6_), channel_id=1, source_target_pairs={{0,28},{4,0},{8,4},{12,8},{16,12},{20,16},{24,20},{28,24},{1,29},{... | collective-permute-start | bytes 1572872 | tf_op jit(solution)/shard_map/va1_left/ppermute | solution.py:388
  18.0 9.5 %collective-permute-done = f32[8,1]{0,1:T(1,128)S(1)} collective-permute-done((f32[8,1]{0,1:T(1,128)S(1)}, f32[8,1]{0,1:T(1,128)S(1)}, u32[]{:S(2)}, u32[]{:S(2)}) %collective-permute-start) | collective-permute-done | bytes 64 | tf_op jit(solution)/shard_map/prefix/ppermute | solution.py:398
  27.6 4.3 %collective-permute-done.1 = f32[8,1]{0,1:T(1,128)S(1)} collective-permute-done((f32[8,1]{0,1:T(1,128)S(1)}, f32[8,1]{0,1:T(1,128)S(1)}, u32[]{:S(2)}, u32[]{:S(2)}) %collective-permute-start.1) | collective-permute-done | bytes 64 | tf_op jit(solution)/shard_map/prefix/ppermute | solution.py:398
  31.9 3.9 %collective-permute-start.2 = (f32[8,1]{0,1:T(1,128)S(1)}, f32[8,1]{0,1:T(1,128)S(1)}, u32[]{:S(2)}, u32[]{:S(2)}) collective-permute-start(f32[8,1]{0,1:T(1,128)S(1)} %add.82), channel_id=1, source_target_pairs={{0,16},{4,20},{8,24},{12,28},{16,0},{20,4},{24,8},{28,12},{1,17},{... | collective-permute-start | bytes 104 | tf_op jit(solution)/shard_map/prefix/ppermute | solution.py:398
  35.8 3.6 %collective-permute-done.2 = f32[8,1]{0,1:T(1,128)S(1)} collective-permute-done((f32[8,1]{0,1:T(1,128)S(1)}, f32[8,1]{0,1:T(1,128)S(1)}, u32[]{:S(2)}, u32[]{:S(2)}) %collective-permute-start.2) | collective-permute-done | bytes 64 | tf_op jit(solution)/shard_map/prefix/ppermute | solution.py:398
  41.0 3.3 %collective-permute-start.7 = (bf16[4,512,128]{2,1,0:T(8,128)(2,1)S(1)}, bf16[4,512,128]{2,1,0:T(8,128)(2,1)}, u32[]{:S(2)}, u32[]{:S(2)}) collective-permute-start(bf16[4,512,128]{2,1,0:T(8,128)(2,1)S(1)} %get-tuple-element.57.refs_4_), channel_id=1, source_target_pairs={{0,28},{4,0},{8,4},{12,8},{16,12},{20,16},{24,20},{28,24},{1,29},{... | collective-permute-start | bytes 1572872 | tf_op jit(solution)/shard_map/vb1_left/ppermute | solution.py:388
  55.2 4.7 %rotate.1 = (bf16[512,1024]{1,0:T(8,128)(2,1)}, bf16[4,512,128]{2,1,0:T(8,128)(2,1)S(1)}, bf16[4,512,128]{2,1,0:T(8,128)(2,1)S(1)}) custom-call(f32[512,8]{1,0:T(8,128)S(1)} %bitcast.33, f32[1,128]{1,0:T(1,128)S(1)} %maximum_bitcast_fusion.freq_ref, bf16[512,1024]{1,0:T(8,128)(2,1)S(1)} %copy-done.2, bf16[512,1024]{1,0:T(8,128)(2,1)S(1)} %copy-done.3), custom_call_target="tpu_custom_call" | custom-call | flops 5000000000 | bytes 6291456 | tf_op jit(solution)/shard_map/rotate/pallas_call | solution.py:80
  63.8 3.2 %collective-permute-start.10 = (bf16[4,512,128]{2,1,0:T(8,128)(2,1)}, bf16[4,512,128]{2,1,0:T(8,128)(2,1)S(1)}, u32[]{:S(2)}, u32[]{:S(2)}) collective-permute-start(bf16[4,512,128]{2,1,0:T(8,128)(2,1)} %collective-permute-done.7.refs_6_), channel_id=1, source_target_pairs={{0,28},{4,0},{8,4},{12,8},{16,12},{20,16},{24,20},{28,24},{1,29},{... | collective-permute-start | bytes 1572872 | tf_op jit(solution)/shard_map/vb2_left/ppermute | solution.py:388
  67.0 9.7 %collective-permute-done.9.refs_10_ = bf16[4,512,128]{2,1,0:T(8,128)(2,1)S(1)} collective-permute-done((bf16[4,512,128]{2,1,0:T(8,128)(2,1)}, bf16[4,512,128]{2,1,0:T(8,128)(2,1)S(1)}, u32[]{:S(2)}, u32[]{:S(2)}) %collective-permute-start.9) | collective-permute-done | bytes 524320 | tf_op jit(solution)/shard_map/va2_left/ppermute | solution.py:388
  78.9 10.6 %collective-permute-done.23.refs_5_ = bf16[4,512,128]{2,1,0:T(8,128)(2,1)S(1)} collective-permute-done((bf16[4,512,128]{2,1,0:T(8,128)(2,1)}, bf16[4,512,128]{2,1,0:T(8,128)(2,1)S(1)}, u32[]{:S(2)}, u32[]{:S(2)}) %collective-permute-start.23) | collective-permute-done | bytes 524320 | tf_op jit(solution)/shard_map/vb2_right/ppermute | solution.py:388
  92.7 6.6 %collective-permute-done.15.refs_3_ = bf16[4,512,128]{2,1,0:T(8,128)(2,1)} collective-permute-done((bf16[4,512,128]{2,1,0:T(8,128)(2,1)}, bf16[4,512,128]{2,1,0:T(8,128)(2,1)}, u32[]{:S(2)}, u32[]{:S(2)}) %collective-permute-start.15) | collective-permute-done | bytes 524320 | tf_op jit(solution)/shard_map/ka1_left/ppermute | solution.py:388
  101.9 10.2 %collective-permute-done.24.refs_4_ = bf16[4,512,128]{2,1,0:T(8,128)(2,1)} collective-permute-done((bf16[4,512,128]{2,1,0:T(8,128)(2,1)S(1)}, bf16[4,512,128]{2,1,0:T(8,128)(2,1)}, u32[]{:S(2)}, u32[]{:S(2)}) %collective-permute-start.24) | collective-permute-done | bytes 524320 | tf_op jit(solution)/shard_map/va3_right/ppermute | solution.py:388
  115.3 8.0 %collective-permute-done.16.refs_4_ = bf16[4,512,128]{2,1,0:T(8,128)(2,1)} collective-permute-done((bf16[4,512,128]{2,1,0:T(8,128)(2,1)}, bf16[4,512,128]{2,1,0:T(8,128)(2,1)}, u32[]{:S(2)}, u32[]{:S(2)}) %collective-permute-start.16) | collective-permute-done | bytes 524320 | tf_op jit(solution)/shard_map/ka2_right/ppermute | solution.py:388
  129.8 18.0 %attend_0_0_7_1_6_2.1 = (f32[16,512,128]{2,1,0:T(8,128)S(1)}, f32[16,8,128]{2,1,0:T(8,128)S(1)}, f32[16,8,128]{2,1,0:T(8,128)S(1)}) custom-call(s32[129]{0:T(256)S(1)} %pad_add_fusion.meta, bf16[4,512,1024]{2,1,0:T(8,128)(2,1)S(1)} %bitcast.34, bf16[4,512,128]{2,1,0:T(8,128)(2,1)S(1)} %copy-done.7, bf16[4,512,128]{2,1,0:T(8,128)(2,1)} %collective-permute-done.14.refs_2_, ...), custom_call_target="tpu_custom_call" | custom-call | flops 18699999232 | bytes 1048576 | tf_op jit(solution)/shard_map/attend_0_0_7_1_6_2/pallas_call | solution.py:312
  148.0 3.2 %collective-permute-start.27 = (bf16[4,512,128]{2,1,0:T(8,128)(2,1)S(1)}, bf16[4,512,128]{2,1,0:T(8,128)(2,1)S(1)}, u32[]{:S(2)}, u32[]{:S(2)}) collective-permute-start(bf16[4,512,128]{2,1,0:T(8,128)(2,1)S(1)} %collective-permute-done.10.refs_6_), channel_id=1, source_target_pairs={{0,28},{4,0},{8,4},{12,8},{16,12},{20,16},{24,20},{28,24},{1,29},{... | collective-permute-start | bytes 1572872 | tf_op jit(solution)/shard_map/vb3_left/ppermute | solution.py:388
  153.1 8.8 %collective-permute-done.29.refs_2_ = bf16[4,512,128]{2,1,0:T(8,128)(2,1)S(1)} collective-permute-done((bf16[4,512,128]{2,1,0:T(8,128)(2,1)S(1)}, bf16[4,512,128]{2,1,0:T(8,128)(2,1)S(1)}, u32[]{:S(2)}, u32[]{:S(2)}) %collective-permute-start.29) | collective-permute-done | bytes 524320 | tf_op jit(solution)/shard_map/kb1_right/ppermute | solution.py:388
  162.2 5.4 %collective-permute-done.22.refs_3_ = bf16[4,512,128]{2,1,0:T(8,128)(2,1)S(1)} collective-permute-done((bf16[4,512,128]{2,1,0:T(8,128)(2,1)}, bf16[4,512,128]{2,1,0:T(8,128)(2,1)S(1)}, u32[]{:S(2)}, u32[]{:S(2)}) %collective-permute-start.22) | collective-permute-done | bytes 524320 | tf_op jit(solution)/shard_map/ka4_right/ppermute | solution.py:388
  167.6 8.3 %attend_0_5_3_4.1 = (f32[4,512,128]{2,1,0:T(8,128)S(1)}, f32[4,8,128]{2,1,0:T(8,128)S(1)}, f32[4,8,128]{2,1,0:T(8,128)S(1)}, bf16[3,4,560,128]{3,2,1,0:T(8,128)(2,1)S(1)}) custom-call(s32[129]{0:T(256)S(1)} %pad_add_fusion.meta, bf16[4,512,1024]{2,1,0:T(8,128)(2,1)S(1)} %bitcast.35, bf16[4,512,128]{2,1,0:T(8,128)(2,1)} %collective-permute-done.20.refs_1_, ...), custom_call_target="tpu_custom_call" | custom-call | flops 12099999744 | bytes 1048576 | tf_op jit(solution)/shard_map/attend_0_5_3_4/pallas_call | solution.py:312
  182.8 13.1 %attend_4_0_7_1.1 = (f32[16,512,128]{2,1,0:T(8,128)S(1)}, f32[16,8,128]{2,1,0:T(8,128)S(1)}, f32[16,8,128]{2,1,0:T(8,128)S(1)}) custom-call(s32[129]{0:T(256)S(1)} %pad_add_fusion.meta, bf16[4,512,1024]{2,1,0:T(8,128)(2,1)S(1)} %bitcast.36, bf16[4,512,128]{2,1,0:T(8,128)(2,1)S(1)} %copy-done.5, bf16[4,512,128]{2,1,0:T(8,128)(2,1)S(1)} %collective-permute-done.29.refs_2_, ...), custom_call_target="tpu_custom_call" | custom-call | flops 12099999744 | bytes 1048576 | tf_op jit(solution)/shard_map/attend_4_0_7_1/pallas_call | solution.py:312
  198.5 9.9 %attend_4_6_2_5_3.1 = (f32[16,512,128]{2,1,0:T(8,128)S(1)}, f32[16,8,128]{2,1,0:T(8,128)S(1)}, f32[16,8,128]{2,1,0:T(8,128)S(1)}) custom-call(s32[129]{0:T(256)S(1)} %pad_add_fusion.meta, bf16[4,512,1024]{2,1,0:T(8,128)(2,1)S(1)} %bitcast.37, bf16[4,512,128]{2,1,0:T(8,128)(2,1)S(1)} %collective-permute-done.30.refs_1_, ...), custom_call_target="tpu_custom_call" | custom-call | flops 15399999488 | bytes 1048576 | tf_op jit(solution)/shard_map/attend_4_6_2_5_3/pallas_call | solution.py:312
  211.7 3.3 %attend_4_4.1 = (f32[4,512,128]{2,1,0:T(8,128)S(1)}, f32[4,8,128]{2,1,0:T(8,128)S(1)}, f32[4,8,128]{2,1,0:T(8,128)S(1)}, bf16[3,4,560,128]{3,2,1,0:T(8,128)(2,1)S(1)}) custom-call(s32[129]{0:T(256)S(1)} %pad_add_fusion.meta, bf16[4,512,1024]{2,1,0:T(8,128)(2,1)S(1)} %bitcast.38, bf16[4,512,128]{2,1,0:T(8,128)(2,1)S(1)} %collective-permute-done.26.refs_1_, ...), custom_call_target="tpu_custom_call" | custom-call | flops 5500000256 | bytes 1048576 | tf_op jit(solution)/shard_map/attend_4_4/pallas_call | solution.py:312
  216.5 3.9 %collective-permute-start.36 = (bf16[4,560,128]{2,1,0:T(8,128)(2,1)S(1)}, bf16[4,560,128]{2,1,0:T(8,128)(2,1)S(1)}, u32[]{:S(2)}, u32[]{:S(2)}) collective-permute-start(bf16[4,560,128]{2,1,0:T(8,128)(2,1)S(1)} %get-tuple-element.111), channel_id=1, source_target_pairs={{0,64},{32,96},{1,65},{33,97},{2,66},{34,98},{3,67},{35,99},{4,68}... | collective-permute-start | bytes 1720328 | tf_op jit(solution)/shard_map/partial1_2/ppermute | solution.py:393
  221.8 9.4 %collective-permute-done.38.three = bf16[4,560,128]{2,1,0:T(8,128)(2,1)S(1)} collective-permute-done((bf16[4,560,128]{2,1,0:T(8,128)(2,1)S(1)}, bf16[4,560,128]{2,1,0:T(8,128)(2,1)S(1)}, u32[]{:S(2)}, u32[]{:S(2)}) %collective-permute-start.38) | collective-permute-done | bytes 573472 | tf_op jit(solution)/shard_map/partial0_3/ppermute | solution.py:393
  233.2 5.6 %collective-permute-done.37.three = bf16[4,560,128]{2,1,0:T(8,128)(2,1)S(1)} collective-permute-done((bf16[4,560,128]{2,1,0:T(8,128)(2,1)S(1)}, bf16[4,560,128]{2,1,0:T(8,128)(2,1)S(1)}, u32[]{:S(2)}, u32[]{:S(2)}) %collective-permute-start.37) | collective-permute-done | bytes 573472 | tf_op jit(solution)/shard_map/partial1_3/ppermute | solution.py:393
  (127 shorter events, 61.2 us)
Async XLA Ops:
  6.5 120.0 %all-gather.3.cloned.1.call-start = ((), (), s32[]{:S(2)}) async-start(), calls=%async_computation | async-start | bytes 5242880 | tf_op jit(solution)/shard_map/queries/all_gather | solution.py:457
  10.3 29.1 %collective-permute-start.3 = (bf16[4,512,128]{2,1,0:T(8,128)(2,1)S(1)}, bf16[4,512,128]{2,1,0:T(8,128)(2,1)}, u32[]{:S(2)}, u32[]{:S(2)}) collective-permute-start(bf16[4,512,128]{2,1,0:T(8,128)(2,1)S(1)} %get-tuple-element.114.refs_6_), channel_id=1, source_target_pairs={{0,28},{4,0},{8,4},{12,8},{16,12},{20,16},{24,20},{28,24},{1,29},{... | collective-permute-start | bytes 1572872 | tf_op jit(solution)/shard_map/va1_left/ppermute | solution.py:388
  16.2 23.1 %collective-permute-start.4 = (bf16[4,512,128]{2,1,0:T(8,128)(2,1)S(1)}, bf16[4,512,128]{2,1,0:T(8,128)(2,1)}, u32[]{:S(2)}, u32[]{:S(2)}) collective-permute-start(bf16[4,512,128]{2,1,0:T(8,128)(2,1)S(1)} %get-tuple-element.114.refs_6_), channel_id=1, source_target_pairs={{0,4},{4,8},{8,12},{12,16},{16,20},{20,24},{24,28},{28,0},{1,5},{5... | collective-permute-start | bytes 1572872 | tf_op jit(solution)/shard_map/va1_right/ppermute | solution.py:388
  63.7 25.8 %collective-permute-start.23 = (bf16[4,512,128]{2,1,0:T(8,128)(2,1)}, bf16[4,512,128]{2,1,0:T(8,128)(2,1)S(1)}, u32[]{:S(2)}, u32[]{:S(2)}) collective-permute-start(bf16[4,512,128]{2,1,0:T(8,128)(2,1)} %collective-permute-done.8.refs_5_), channel_id=1, source_target_pairs={{0,4},{4,8},{8,12},{12,16},{16,20},{20,24},{24,28},{28,0},{1,5},{5... | collective-permute-start | bytes 1572872 | tf_op jit(solution)/shard_map/vb2_right/ppermute | solution.py:388
  63.8 26.2 %collective-permute-start.10 = (bf16[4,512,128]{2,1,0:T(8,128)(2,1)}, bf16[4,512,128]{2,1,0:T(8,128)(2,1)S(1)}, u32[]{:S(2)}, u32[]{:S(2)}) collective-permute-start(bf16[4,512,128]{2,1,0:T(8,128)(2,1)} %collective-permute-done.7.refs_6_), channel_id=1, source_target_pairs={{0,28},{4,0},{8,4},{12,8},{16,12},{20,16},{24,20},{28,24},{1,29},{... | collective-permute-start | bytes 1572872 | tf_op jit(solution)/shard_map/vb2_left/ppermute | solution.py:388
  76.7 22.6 %collective-permute-start.15 = (bf16[4,512,128]{2,1,0:T(8,128)(2,1)}, bf16[4,512,128]{2,1,0:T(8,128)(2,1)}, u32[]{:S(2)}, u32[]{:S(2)}) collective-permute-start(bf16[4,512,128]{2,1,0:T(8,128)(2,1)} %copy-done.6), channel_id=1, source_target_pairs={{0,28},{4,0},{8,4},{12,8},{16,12},{20,16},{24,20},{28,24},{1,29},{... | collective-permute-start | bytes 1572872 | tf_op jit(solution)/shard_map/ka1_left/ppermute | solution.py:388
  78.3 22.6 %collective-permute-start.14 = (bf16[4,512,128]{2,1,0:T(8,128)(2,1)}, bf16[4,512,128]{2,1,0:T(8,128)(2,1)}, u32[]{:S(2)}, u32[]{:S(2)}) collective-permute-start(bf16[4,512,128]{2,1,0:T(8,128)(2,1)} %copy-done.6), channel_id=1, source_target_pairs={{0,4},{4,8},{8,12},{12,16},{16,20},{20,24},{24,28},{28,0},{1,5},{5... | collective-permute-start | bytes 1572872 | tf_op jit(solution)/shard_map/ka1_right/ppermute | solution.py:388
  89.5 22.6 %collective-permute-start.24 = (bf16[4,512,128]{2,1,0:T(8,128)(2,1)S(1)}, bf16[4,512,128]{2,1,0:T(8,128)(2,1)}, u32[]{:S(2)}, u32[]{:S(2)}) collective-permute-start(bf16[4,512,128]{2,1,0:T(8,128)(2,1)S(1)} %collective-permute-done.13.refs_9_), channel_id=1, source_target_pairs={{0,4},{4,8},{8,12},{12,16},{16,20},{20,24},{24,28},{28,0},{1,5},{5... | collective-permute-start | bytes 1572872 | tf_op jit(solution)/shard_map/va3_right/ppermute | solution.py:388
  90.0 22.6 %collective-permute-start.11 = (bf16[4,512,128]{2,1,0:T(8,128)(2,1)S(1)}, bf16[4,512,128]{2,1,0:T(8,128)(2,1)}, u32[]{:S(2)}, u32[]{:S(2)}) collective-permute-start(bf16[4,512,128]{2,1,0:T(8,128)(2,1)S(1)} %collective-permute-done.9.refs_10_), channel_id=1, source_target_pairs={{0,28},{4,0},{8,4},{12,8},{16,12},{20,16},{24,20},{28,24},{1,29},{... | collective-permute-start | bytes 1572872 | tf_op jit(solution)/shard_map/va3_left/ppermute | solution.py:388
  99.3 24.5 %collective-permute-start.17 = (bf16[4,512,128]{2,1,0:T(8,128)(2,1)}, bf16[4,512,128]{2,1,0:T(8,128)(2,1)}, u32[]{:S(2)}, u32[]{:S(2)}) collective-permute-start(bf16[4,512,128]{2,1,0:T(8,128)(2,1)} %collective-permute-done.15.refs_3_), channel_id=1, source_target_pairs={{0,28},{4,0},{8,4},{12,8},{16,12},{20,16},{24,20},{28,24},{1,29},{... | collective-permute-start | bytes 1572872 | tf_op jit(solution)/shard_map/ka2_left/ppermute | solution.py:388
  100.8 22.5 %collective-permute-start.16 = (bf16[4,512,128]{2,1,0:T(8,128)(2,1)}, bf16[4,512,128]{2,1,0:T(8,128)(2,1)}, u32[]{:S(2)}, u32[]{:S(2)}) collective-permute-start(bf16[4,512,128]{2,1,0:T(8,128)(2,1)} %collective-permute-done.14.refs_2_), channel_id=1, source_target_pairs={{0,4},{4,8},{8,12},{12,16},{16,20},{20,24},{24,28},{28,0},{1,5},{5... | collective-permute-start | bytes 1572872 | tf_op jit(solution)/shard_map/ka2_right/ppermute | solution.py:388
  112.1 35.7 %collective-permute-start.25 = (bf16[4,512,128]{2,1,0:T(8,128)(2,1)}, bf16[4,512,128]{2,1,0:T(8,128)(2,1)}, u32[]{:S(2)}, u32[]{:S(2)}) collective-permute-start(bf16[4,512,128]{2,1,0:T(8,128)(2,1)} %collective-permute-done.24.refs_4_), channel_id=1, source_target_pairs={{0,4},{4,8},{8,12},{12,16},{16,20},{20,24},{24,28},{28,0},{1,5},{5... | collective-permute-start | bytes 1572872 | tf_op jit(solution)/shard_map/va4_right/ppermute | solution.py:388
  112.6 38.6 %collective-permute-start.12 = (bf16[4,512,128]{2,1,0:T(8,128)(2,1)}, bf16[4,512,128]{2,1,0:T(8,128)(2,1)}, u32[]{:S(2)}, u32[]{:S(2)}) collective-permute-start(bf16[4,512,128]{2,1,0:T(8,128)(2,1)} %copy-done.4), channel_id=1, source_target_pairs={{0,28},{4,0},{8,4},{12,8},{16,12},{20,16},{24,20},{28,24},{1,29},{... | collective-permute-start | bytes 1572872 | tf_op jit(solution)/shard_map/kb1_left/ppermute | solution.py:388
  123.3 24.6 %collective-permute-start.20 = (bf16[4,512,128]{2,1,0:T(8,128)(2,1)}, bf16[4,512,128]{2,1,0:T(8,128)(2,1)}, u32[]{:S(2)}, u32[]{:S(2)}) collective-permute-start(bf16[4,512,128]{2,1,0:T(8,128)(2,1)} %collective-permute-done.16.refs_4_), channel_id=1, source_target_pairs={{0,4},{4,8},{8,12},{12,16},{16,20},{20,24},{24,28},{28,0},{1,5},{5... | collective-permute-start | bytes 1572872 | tf_op jit(solution)/shard_map/ka3_right/ppermute | solution.py:388
  123.8 24.1 %collective-permute-start.21 = (bf16[4,512,128]{2,1,0:T(8,128)(2,1)}, bf16[4,512,128]{2,1,0:T(8,128)(2,1)}, u32[]{:S(2)}, u32[]{:S(2)}) collective-permute-start(bf16[4,512,128]{2,1,0:T(8,128)(2,1)} %collective-permute-done.17.refs_5_), channel_id=1, source_target_pairs={{0,28},{4,0},{8,4},{12,8},{16,12},{20,16},{24,20},{28,24},{1,29},{... | collective-permute-start | bytes 1572872 | tf_op jit(solution)/shard_map/ka3_left/ppermute | solution.py:388
  147.9 19.7 %collective-permute-start.22 = (bf16[4,512,128]{2,1,0:T(8,128)(2,1)}, bf16[4,512,128]{2,1,0:T(8,128)(2,1)S(1)}, u32[]{:S(2)}, u32[]{:S(2)}) collective-permute-start(bf16[4,512,128]{2,1,0:T(8,128)(2,1)} %collective-permute-done.20.refs_1_), channel_id=1, source_target_pairs={{0,4},{4,8},{8,12},{12,16},{16,20},{20,24},{24,28},{28,0},{1,5},{5... | collective-permute-start | bytes 1572872 | tf_op jit(solution)/shard_map/ka4_right/ppermute | solution.py:388
  148.0 32.7 %collective-permute-start.27 = (bf16[4,512,128]{2,1,0:T(8,128)(2,1)S(1)}, bf16[4,512,128]{2,1,0:T(8,128)(2,1)S(1)}, u32[]{:S(2)}, u32[]{:S(2)}) collective-permute-start(bf16[4,512,128]{2,1,0:T(8,128)(2,1)S(1)} %collective-permute-done.10.refs_6_), channel_id=1, source_target_pairs={{0,28},{4,0},{8,4},{12,8},{16,12},{20,16},{24,20},{28,24},{1,29},{... | collective-permute-start | bytes 1572872 | tf_op jit(solution)/shard_map/vb3_left/ppermute | solution.py:388
  151.2 26.3 %collective-permute-start.18 = (bf16[4,512,128]{2,1,0:T(8,128)(2,1)}, bf16[4,512,128]{2,1,0:T(8,128)(2,1)S(1)}, u32[]{:S(2)}, u32[]{:S(2)}) collective-permute-start(bf16[4,512,128]{2,1,0:T(8,128)(2,1)} %collective-permute-done.12.refs_3_), channel_id=1, source_target_pairs={{0,28},{4,0},{8,4},{12,8},{16,12},{20,16},{24,20},{28,24},{1,29},{... | collective-permute-start | bytes 1572872 | tf_op jit(solution)/shard_map/kb2_left/ppermute | solution.py:388
  162.0 19.8 %collective-permute-start.30 = (bf16[4,512,128]{2,1,0:T(8,128)(2,1)S(1)}, bf16[4,512,128]{2,1,0:T(8,128)(2,1)S(1)}, u32[]{:S(2)}, u32[]{:S(2)}) collective-permute-start(bf16[4,512,128]{2,1,0:T(8,128)(2,1)S(1)} %collective-permute-done.29.refs_2_), channel_id=1, source_target_pairs={{0,4},{4,8},{8,12},{12,16},{16,20},{20,24},{24,28},{28,0},{1,5},{5... | collective-permute-start | bytes 1572872 | tf_op jit(solution)/shard_map/kb2_right/ppermute | solution.py:388
  176.1 21.1 %collective-permute-start.33 = (bf16[4,560,128]{2,1,0:T(8,128)(2,1)S(1)}, bf16[4,560,128]{2,1,0:T(8,128)(2,1)S(1)}, u32[]{:S(2)}, u32[]{:S(2)}) collective-permute-start(bf16[4,560,128]{2,1,0:T(8,128)(2,1)S(1)} %get-tuple-element.109), channel_id=1, source_target_pairs={{0,32},{32,64},{64,96},{1,33},{33,65},{65,97},{2,34},{34,66},{66,9... | collective-permute-start | bytes 1720328 | tf_op jit(solution)/shard_map/partial0_1/ppermute | solution.py:393
  177.4 21.1 %collective-permute-start.32 = (bf16[4,512,128]{2,1,0:T(8,128)(2,1)S(1)}, bf16[4,512,128]{2,1,0:T(8,128)(2,1)S(1)}, u32[]{:S(2)}, u32[]{:S(2)}) collective-permute-start(bf16[4,512,128]{2,1,0:T(8,128)(2,1)S(1)} %collective-permute-done.23.refs_5_), channel_id=1, source_target_pairs={{0,4},{4,8},{8,12},{12,16},{16,20},{20,24},{24,28},{28,0},{1,5},{5... | collective-permute-start | bytes 1572872 | tf_op jit(solution)/shard_map/vb3_right/ppermute | solution.py:388
  177.5 18.4 %collective-permute-start.19 = (bf16[4,512,128]{2,1,0:T(8,128)(2,1)S(1)}, bf16[4,512,128]{2,1,0:T(8,128)(2,1)S(1)}, u32[]{:S(2)}, u32[]{:S(2)}) collective-permute-start(bf16[4,512,128]{2,1,0:T(8,128)(2,1)S(1)} %collective-permute-done.18.refs_2_), channel_id=1, source_target_pairs={{0,28},{4,0},{8,4},{12,8},{16,12},{20,16},{24,20},{28,24},{1,29},{... | collective-permute-start | bytes 1572872 | tf_op jit(solution)/shard_map/kb3_left/ppermute | solution.py:388
  180.7 31.0 %collective-permute-start.28 = (bf16[4,512,128]{2,1,0:T(8,128)(2,1)S(1)}, bf16[4,512,128]{2,1,0:T(8,128)(2,1)S(1)}, u32[]{:S(2)}, u32[]{:S(2)}) collective-permute-start(bf16[4,512,128]{2,1,0:T(8,128)(2,1)S(1)} %collective-permute-done.27.refs_8_), channel_id=1, source_target_pairs={{0,28},{4,0},{8,4},{12,8},{16,12},{20,16},{24,20},{28,24},{1,29},{... | collective-permute-start | bytes 1572872 | tf_op jit(solution)/shard_map/vb4_left/ppermute | solution.py:388
  209.6 21.7 %collective-permute-start.38 = (bf16[4,560,128]{2,1,0:T(8,128)(2,1)S(1)}, bf16[4,560,128]{2,1,0:T(8,128)(2,1)S(1)}, u32[]{:S(2)}, u32[]{:S(2)}) collective-permute-start(bf16[4,560,128]{2,1,0:T(8,128)(2,1)S(1)} %get-tuple-element.106), channel_id=1, source_target_pairs={{0,96},{1,97},{2,98},{3,99},{4,100},{5,101},{6,102},{7,103},{8,104... | collective-permute-start | bytes 1720328 | tf_op jit(solution)/shard_map/partial0_3/ppermute | solution.py:393
  (26 other events, 376.3 us)
Sparse Core Ops, SparseCore 0:
  61.7 48.2 all-gather.2

commit v4 on v3

--- a/solution.py
+++ b/solution.py
@@ -15,6 +15,7 @@
 NEG_FILL = -1e30
 ROPE_BASE = 10000.0
 VMEM_LIMIT = 24 << 20
+ATTEND_VMEM = 60 << 20
 IDLE = 4
 STAT = 48
 CHUNKS = ((0, 4), (4, 4))
@@ -113,23 +114,32 @@
 
     @pl.when(r == 0)
     def _():
-        for at in range(count):
-            k_all[at] = k_refs[at][...]
-            v_all[at] = v_refs[at][...]
+        def hold(kb, carry):
+            for at in range(count):
+                k_all[at, kb] = k_refs[at][kb]
+                v_all[at, kb] = v_refs[at][kb]
+            return carry
+
+        lax.fori_loop(0, 4, hold, 0)
         q_ref[IDLE * BLOCK :, :] = jnp.zeros((BLOCK, heads * HEAD), jnp.bfloat16)
         acc[IDLE] = jnp.zeros((heads * HEAD, BLOCK), jnp.float32)
         m_run[IDLE] = jnp.full((8, BLOCK), NEG_FILL)
         l_run[IDLE] = jnp.zeros((8, BLOCK), jnp.float32)
 
-    q_ref[: IDLE * BLOCK, :] = given_q[0]
-    if first:
-        acc[:IDLE] = jnp.zeros((IDLE, heads * HEAD, BLOCK), jnp.float32)
-        m_run[:IDLE] = jnp.full((IDLE, 8, BLOCK), NEG_FILL)
-        l_run[:IDLE] = jnp.zeros((IDLE, 8, BLOCK), jnp.float32)
-    else:
-        acc[:IDLE] = given[0][...]
-        m_run[:IDLE] = given[1][...]
-        l_run[:IDLE] = given[2][...]
+    def enter(qb, carry):
+        q_rows = pl.ds(pl.multiple_of(qb * BLOCK, BLOCK), BLOCK)
+        q_ref[q_rows, :] = given_q[0, q_rows, :]
+        if first:
+            acc[qb] = jnp.zeros((heads * HEAD, BLOCK), jnp.float32)
+            m_run[qb] = jnp.full((8, BLOCK), NEG_FILL)
+            l_run[qb] = jnp.zeros((8, BLOCK), jnp.float32)
+        else:
+            acc[qb] = given[0][qb]
+            m_run[qb] = given[1][qb]
+            l_run[qb] = given[2][qb]
+        return carry
+
+    lax.fori_loop(0, 4, enter, 0)
 
     span = range(heads)
     cols = [slice(h * HEAD, (h + 1) * HEAD) for h in span]
@@ -196,21 +206,29 @@
 
             lax.fori_loop(0, 2, own, 0)
 
-    length, newest = jnp.int32(0), jnp.int32(-1)
+    def note(at, choice, offset, qb, length, newest):
+        code = meta[(r * 4 + qb) * RING + offset % RING]
+        if offset == 0:
+            valid, kb = (code >> choice) & 1, choice
+        else:
+            valid, kb = (code > 0).astype(jnp.int32), jnp.maximum(code - 1, 0)
+        item = qb + at * 16 + kb * 256
+        clash = valid & length & (newest == qb).astype(jnp.int32)
+        todo[length] = jnp.where(clash == 1, IDLE, item)
+        todo[length + 1] = item
+        return length + valid * (1 + clash), jnp.where(valid == 1, qb, newest)
+
+    found = (jnp.int32(0), jnp.int32(-1))
     for at, offset in enumerate(offsets):
-        for choice in range(4 if offset == 0 else 1):
-            for qb in range(4):
-                code = meta[(r * 4 + qb) * RING + offset % RING]
-                if offset == 0:
-                    valid, kb = (code >> choice) & 1, choice
-                else:
-                    valid, kb = (code > 0).astype(jnp.int32), jnp.maximum(code - 1, 0)
-                item = qb + at * 16 + kb * 256
-                clash = valid & length & (newest == qb).astype(jnp.int32) & 1
-                todo[length] = jnp.where(clash == 1, IDLE, item)
-                todo[length + 1] = item
-                length += valid * (1 + clash)
-                newest = jnp.where(valid == 1, qb, newest)
+        if offset == 0:
+            found = lax.fori_loop(
+                0, 16, lambda i, f, at=at: note(at, i >> 2, 0, i & 3, *f), found
+            )
+        else:
+            found = lax.fori_loop(
+                0, 4, lambda i, f, at=at, offset=offset: note(at, 0, offset, i, *f), found
+            )
+    length = found[0]
     todo[length] = IDLE
 
     def step(i, carry):
@@ -223,19 +241,23 @@
 
     lax.fori_loop(0, (length + 1) >> 1, step, 0)
 
+    def leave(acc_out, m_out, l_out):
+        def copy(qb, carry):
+            acc_out[qb] = acc[qb]
+            m_out[qb] = m_run[qb]
+            l_out[qb] = l_run[qb]
+            return carry
+
+        lax.fori_loop(0, 4, copy, 0)
+
     if not last:
-        acc_out, m_out, l_out = rest
-        acc_out[...] = acc[:IDLE]
-        m_out[...] = m_run[:IDLE]
-        l_out[...] = l_run[:IDLE]
+        leave(*rest)
     else:
-        acc0_ref, m0_ref, l0_ref, packed_ref = rest
+        packed_ref = rest[3]
 
         @pl.when(r == 0)
         def _():
-            acc0_ref[...] = acc[:IDLE]
-            m0_ref[...] = m_run[:IDLE]
-            l0_ref[...] = l_run[:IDLE]
+            leave(*rest[:3])
 
         @pl.when(r > 0)
         def _():
@@ -284,13 +306,13 @@
             jax.ShapeDtypeStruct((4, width, BLOCK), f32),
             jax.ShapeDtypeStruct((4, 8, BLOCK), f32),
             jax.ShapeDtypeStruct((4, 8, BLOCK), f32),
-            jax.ShapeDtypeStruct((3, 4, width + STAT, BLOCK), jnp.bfloat16),
+            jax.ShapeDtypeStruct((ROWS, 4, width + STAT, BLOCK), jnp.bfloat16),
         ]
         out_specs = [
             pl.BlockSpec((4, width, BLOCK), lambda r, meta: (0, 0, 0)),
             pl.BlockSpec((4, 8, BLOCK), lambda r, meta: (0, 0, 0)),
             pl.BlockSpec((4, 8, BLOCK), lambda r, meta: (0, 0, 0)),
-            pl.BlockSpec((1, 4, width + STAT, BLOCK), lambda r, meta: (jnp.maximum(r - 1, 0), 0, 0, 0)),
+            pl.BlockSpec((1, 4, width + STAT, BLOCK), lambda r, meta: ((meta[16 * RING] + jnp.maximum(r, 1)) & 3, 0, 0, 0)),
         ]
     else:
         out_shape = [
@@ -319,7 +341,7 @@
             out_specs=out_specs,
             scratch_shapes=scratch,
         ),
-        compiler_params=pltpu.CompilerParams(vmem_limit_bytes=VMEM_LIMIT),
+        compiler_params=pltpu.CompilerParams(vmem_limit_bytes=ATTEND_VMEM),
         cost_estimate=pl.CostEstimate(
             flops=int((2 + 3 * len(offsets)) * 1.1e9),
             bytes_accessed=1 << 20,
@@ -410,8 +432,7 @@
     def send(self, name, ring, distance, *others):
         source = ring[-self.sign * (distance - 1)]
         waits = list(others)
-        if len(self.sent) >= self.depth:
-            waits.append(self.sent[-self.depth])
+        waits += self.sent[-self.depth - 1 : -self.depth + 1] if self.sent[1:] else []
         if waits:
             source = after(source, *waits)
         with jax.named_scope(f"{name}{distance}_{self.side}"):
@@ -427,34 +448,27 @@
     before = jnp.zeros_like(total)
     value_tiles = value_states.reshape(4, BLOCK, -1).transpose(0, 2, 1)
     va, vb = {0: value_tiles[:, : 4 * HEAD]}, {0: value_tiles[:, 4 * HEAD :]}
-    right, left = Wire("right", 1), Wire("left", -1)
-    for wire in (right, left):
-        wire.send("va", va, 1)
-    with jax.named_scope("prefix"):
-        for bit in (1, 2, 4):
-            other = swap(total, "z", bit)
-            before = before + jnp.where((my_z & bit) != 0, other, 0.0)
-            total = total + other
-    for wire in (right, left):
-        wire.send("vb", vb, 1, total)
-    total = after(total, va[1], va[-1])
-    for wire in (right, left):
-        wire.send("va", va, 2)
     picks = selected_blocks.T.astype(jnp.float32)
     with jax.named_scope("prefix"):
+        rows_before = before
         for bit in (1, 2):
-            other = swap(jnp.concatenate([total, picks], axis=1), "y", bit)
-            before = before + jnp.where((my_y & bit) != 0, other[:, :1], 0.0)
+            other = swap(jnp.concatenate([total, rows_before, picks], axis=1), "y", bit)
+            if bit == 1:
+                own_total = total
+            rows_before = rows_before + jnp.where((my_y & bit) != 0, other[:, :1], 0.0)
             total = total + other[:, :1]
-            picks = jnp.concatenate([picks, other[:, 1:]], axis=1)
-    for wire in (right, left):
-        wire.send("vb", vb, 2)
-    angles = before + jnp.cumsum(gate_values, axis=1)
-    angles = after(angles, vb[1], vb[-1])
+            picks = jnp.concatenate([picks, other[:, 2:]], axis=1)
+        for bit in (1, 2, 4):
+            other = swap(jnp.concatenate([own_total, rows_before], axis=1), "z", bit)
+            before = before + jnp.where((my_z & bit) != 0, other[:, :1], 0.0)
+            own_total = own_total + other[:, :1]
+            rows_before = rows_before + other[:, 1:]
+    angles = before + rows_before + jnp.cumsum(gate_values, axis=1)
     query_rot, keys_a, keys_b = rotate(angles, query_states, key_states)
     ka, kb = {0: keys_a}, {0: keys_b}
     with jax.named_scope("queries"):
-        queries = lax.all_gather(query_rot, "y")
+        copies = jnp.broadcast_to(query_rot[None], (ROWS, *query_rot.shape))
+        queries = lax.all_to_all(copies, "y", 0, 0, tiled=True)
 
     picks = picks.astype(jnp.int32).T.reshape(4, 1, 4, 8)
     wanted = (my_y + lax.broadcasted_iota(jnp.int32, (4, 4, 1, 1), 1)) ^ my_y
@@ -485,43 +499,49 @@
             last,
         )
 
-    def deliver(part, state, orders):
-        parts = []
-        for s in (1, 2, 3):
-            packed = state[3][s - 1]
-            if orders and parts:
-                packed = after(packed, parts[-1])
-            with jax.named_scope(f"partial{part}_{s}"):
-                parts.append(to_row(packed, s))
-        return parts
-
-    for name, ring, distance in (("ka", ka, 1), ("va", va, 3), ("ka", ka, 2)):
-        for wire in (right, left):
-            wire.send(name, ring, distance)
-    right.send("va", va, 4)
-    left.send("kb", kb, 1)
+    def pick(rows, step):
+        return lax.dynamic_index_in_dim(rows, (my_y + step) & 3, 0, keepdims=False)
+
+    right, left = Wire("right", 1), Wire("left", -1)
+    for distance in (1, 2):
+        for name, ring in (("va", va), ("ka", ka)):
+            for wire in (right, left):
+                wire.send(name, ring, distance)
     for wire in (right, left):
+        wire.send("va", va, 3)
         wire.send("ka", ka, 3)
     state = call(0, GROUPS[0][0], None, False)
-    right.send("kb", kb, 1, state[1])
-    left.send("kb", kb, 2, state[1])
+    right.send("va", va, 4)
+    left.send("vb", vb, 1)
     right.send("ka", ka, 4, state[1])
-    left.send("vb", vb, 3, state[1])
-    right.send("kb", kb, 2)
-    left.send("kb", kb, 3)
+    left.send("kb", kb, 1, state[1])
+    right.send("vb", vb, 1)
+    left.send("vb", vb, 2)
+    right.send("kb", kb, 1)
+    left.send("kb", kb, 2)
     state = call(0, GROUPS[0][1], state, True)
-    right.send("vb", vb, 3, state[1])
-    left.send("vb", vb, 4, state[1])
-    right.send("kb", kb, 3, state[1])
-    left.send("kb", kb, 4, state[1])
-    mine_a, parts_a = state[:3], deliver(0, state, True)
-    state = call(1, GROUPS[1][0], None, False)
-    state[1] = after(state[1], parts_a[0])
-    state = call(1, GROUPS[1][1], state, False)
-    state[1] = after(state[1], parts_a[1])
+    right.send("vb", vb, 2)
+    left.send("vb", vb, 3)
+    right.send("kb", kb, 2, state[1])
+    left.send("kb", kb, 3, state[1])
+    first_b = call(1, GROUPS[1][0], None, False)
+    right.send("vb", vb, 3)
+    left.send("vb", vb, 4)
+    right.send("kb", kb, 3, first_b[1])
+    left.send("kb", kb, 4, first_b[1])
+    mine_a = state[:3]
+    with jax.named_scope("partials_a"):
+        parts_a = lax.all_to_all(state[3], "y", 0, 0, tiled=True)
+    first_b[1] = after(first_b[1], parts_a)
+    state = call(1, GROUPS[1][1], first_b, False)
     state = call(1, GROUPS[1][2], state, True)
-    out = join(CHUNKS[0], mine_a, parts_a, None)
-    return join(CHUNKS[1], state[:3], deliver(1, state, False), out)
+    parts_b = []
+    for s in (1, 2, 3):
+        with jax.named_scope(f"partial_b{s}"):
+            parts_b.append(to_row(pick(state[3], s), s))
+    parts_a = after(parts_a, state[1])
+    out = join(CHUNKS[0], mine_a, [pick(parts_a, -s) for s in (1, 2, 3)], None)
+    return join(CHUNKS[1], state[:3], parts_b, out)
 
 
 def solution(mesh):

time: 249 us -> 256 us (1.028)
  Pallas kernels: 61.2 us -> 80.1 us
  waiting for transfers between devices: 101 us -> 86.9 us
  between operations: 13.8 us -> 0.42 us
  starting transfers between devices: 60.7 us -> 72.8 us
    pallas_call x5, Pallas kernels: 52.7 us -> 70.6 us  [attend(): pl.pallas_call(functools.partial(attend_kernel, offsets, heads, first, la...]
    ppermute x5, waiting for transfers between devices: 19.5 us -> 7.13 us  [swap(): return lax.ppermute(value, axis, [(i, i ^ bit) for i in range(size)])]
    ppermute x6 -> x3, waiting for transfers between devices: 16.2 us -> 6.67 us  [to_row(): return lax.ppermute(value, 'y', moves)]
    all_to_all x0 -> x2, starting transfers between devices: none -> 8.64 us  [the longest x1 5.02 us: shards(): queries = lax.all_to_all(copies, 'y', 0, 0, tiled=True)]
    ppermute x5, starting transfers between devices: 8.74 us -> 17.2 us  [swap(): return lax.ppermute(value, axis, [(i, i ^ bit) for i in range(size)])]
    ppermute x28, waiting for transfers between devices: 65 us -> 73 us  [shift(): lax.ppermute(value, axis, [(i, (i + step) % size) for i in range(size)])]
    ppermute x6 -> x3, starting transfers between devices: 11.4 us -> 4.93 us  [to_row(): return lax.ppermute(value, 'y', moves)]
    squeeze x2, local copies, waits for them, and re-layouts: 0.23 us -> 4.25 us  [pick(): return lax.dynamic_index_in_dim(rows, my_y + step & 3, 0, keepdims=False)]
  transfers between devices with their start and end apart: 40 -> 38, of which waited for: 16 -> 16; matrix products, arithmetic and copies ran while one was open for 1% -> 2% of each run, Pallas kernels for 22% -> 25%
where the time goes in v4:
time: 256 us; the launch traced here: 255 us
  waiting for transfers between devices  86.9 us (34%)
  Pallas kernels  80.1 us (31%)
  starting transfers between devices  72.8 us (28%)
  local copies, waits for them, and re-layouts  10.8 us (4%)
  other arithmetic  3.75 us (1%)
    ppermute x28, waiting for transfers between devices, shift(): lax.ppermute(value, axis, [(i, (i + step) % size) for i in range(size)])  73 us
    pallas_call x5, Pallas kernels, attend(): pl.pallas_call(functools.partial(attend_kernel, offsets, heads, first, la...  70.6 us
    ppermute x28, starting transfers between devices, shift(): lax.ppermute(value, axis, [(i, (i + step) % size) for i in range(size)])  42 us
    ppermute x5, starting transfers between devices, swap(): return lax.ppermute(value, axis, [(i, i ^ bit) for i in range(size)])  17.2 us
    ppermute x5, waiting for transfers between devices, swap(): return lax.ppermute(value, axis, [(i, i ^ bit) for i in range(size)])  7.13 us
    ppermute x3, waiting for transfers between devices, to_row(): return lax.ppermute(value, 'y', moves)  6.67 us
    pallas_call x2, Pallas kernels, join(): pl.pallas_call(functools.partial(join_kernel, heads), out_shape=jax.Shape...  5.48 us
  transfers between devices with their start and end apart: 38, of which 16 were waited for; matrix products, arithmetic and copies ran while one was open for 2% of the time, Pallas kernels for 25%

profile of v4, /device:TPU:2, one launch (start us, length us, event | category | flops | bytes accessed | tf_op | source)
XLA Modules:
  0.0 254.7 jit_solution(15562859797218817483)
XLA Ops:
  5.3 3.3 %collective-permute-start.1 = (f32[8,10]{0,1:T(8,128)S(1)}, f32[8,10]{0,1:T(8,128)S(1)}, u32[]{:S(2)}, u32[]{:S(2)}) collective-permute-start(f32[8,10]{0,1:T(8,128)S(1)} %pad_maximum_fusion), channel_id=1, source_target_pairs={{0,64},{32,96},{64,0},{96,32},{1,65},{33,97},{65,1},{97,33},{2,66}... | collective-permute-start | bytes 968 | tf_op jit(solution)/shard_map/prefix/ppermute | solution.py:420
  14.2 3.4 %collective-permute-start.3 = (f32[8,2]{0,1:T(2,128)S(1)}, f32[8,2]{0,1:T(2,128)S(1)}, u32[]{:S(2)}, u32[]{:S(2)}) collective-permute-start(f32[8,2]{0,1:T(2,128)S(1)} %pad_maximum_fusion.3), channel_id=1, source_target_pairs={{0,8},{4,12},{8,0},{12,4},{16,24},{20,28},{24,16},{28,20},{1,9},{5... | collective-permute-start | bytes 200 | tf_op jit(solution)/shard_map/prefix/ppermute | solution.py:420
  19.1 6.9 %collective-permute-start.4 = (f32[8,2]{0,1:T(2,128)S(1)}, f32[8,2]{0,1:T(2,128)S(1)}, u32[]{:S(2)}, u32[]{:S(2)}) collective-permute-start(f32[8,2]{0,1:T(2,128)S(1)} %pad_maximum_fusion.4), channel_id=1, source_target_pairs={{0,16},{4,20},{8,24},{12,28},{16,0},{20,4},{24,8},{28,12},{1,17},{... | collective-permute-start | bytes 200 | tf_op jit(solution)/shard_map/prefix/ppermute | solution.py:420
  30.1 4.0 %rotate.1 = (bf16[512,1024]{1,0:T(8,128)(2,1)S(1)}, bf16[4,512,128]{2,1,0:T(8,128)(2,1)S(1)}, bf16[4,512,128]{2,1,0:T(8,128)(2,1)S(1)}) custom-call(f32[512,8]{1,0:T(8,128)S(1)} %bitcast.33, f32[1,128]{1,0:T(1,128)S(1)} %maximum_bitcast_fusion.freq_ref, bf16[512,1024]{1,0:T(8,128)(2,1)S(1)} %copy-done.6, bf16[512,1024]{1,0:T(8,128)(2,1)S(1)} %copy-done.7), custom_call_target="tpu_custom_call" | custom-call | flops 5000000000 | bytes 6291456 | tf_op jit(solution)/shard_map/rotate/pallas_call | solution.py:81
  36.8 5.0 %all-to-all-start = ((bf16[4,512,1024]{2,1,0:T(8,128)(2,1)}), bf16[4,512,1024]{2,1,0:T(8,128)(2,1)}, u32[]{:S(2)}, u32[]{:S(2)}) async-start(bf16[4,512,1024]{2,1,0:T(8,128)(2,1)} %broadcast_in_dim.70), calls=%async_computation | async-start | bytes 8388608 | tf_op jit(solution)/shard_map/queries/all_to_all | solution.py:471
  42.6 4.7 %collective-permute-start.9 = (bf16[4,512,128]{2,1,0:T(8,128)(2,1)S(1)}, bf16[4,512,128]{2,1,0:T(8,128)(2,1)S(1)}, u32[]{:S(2)}, u32[]{:S(2)}) collective-permute-start(bf16[4,512,128]{2,1,0:T(8,128)(2,1)S(1)} %get-tuple-element.104.refs_6_), channel_id=1, source_target_pairs={{0,28},{4,0},{8,4},{12,8},{16,12},{20,16},{24,20},{28,24},{1,29},{... | collective-permute-start | bytes 1572872 | tf_op jit(solution)/shard_map/va1_left/ppermute | solution.py:410
  47.3 3.3 %collective-permute-start.6 = (bf16[4,512,128]{2,1,0:T(8,128)(2,1)S(1)}, bf16[4,512,128]{2,1,0:T(8,128)(2,1)}, u32[]{:S(2)}, u32[]{:S(2)}) collective-permute-start(bf16[4,512,128]{2,1,0:T(8,128)(2,1)S(1)} %get-tuple-element.53.refs_1_), channel_id=1, source_target_pairs={{0,28},{4,0},{8,4},{12,8},{16,12},{20,16},{24,20},{28,24},{1,29},{... | collective-permute-start | bytes 1572872 | tf_op jit(solution)/shard_map/ka1_left/ppermute | solution.py:410
  50.6 12.7 %collective-permute-done.7.refs_7_ = bf16[4,512,128]{2,1,0:T(8,128)(2,1)S(1)} collective-permute-done((bf16[4,512,128]{2,1,0:T(8,128)(2,1)S(1)}, bf16[4,512,128]{2,1,0:T(8,128)(2,1)S(1)}, u32[]{:S(2)}, u32[]{:S(2)}) %collective-permute-start.7) | collective-permute-done | bytes 524320 | tf_op jit(solution)/shard_map/va1_right/ppermute | solution.py:410
  66.7 4.2 %collective-permute-done.6.refs_3_ = bf16[4,512,128]{2,1,0:T(8,128)(2,1)} collective-permute-done((bf16[4,512,128]{2,1,0:T(8,128)(2,1)S(1)}, bf16[4,512,128]{2,1,0:T(8,128)(2,1)}, u32[]{:S(2)}, u32[]{:S(2)}) %collective-permute-start.6) | collective-permute-done | bytes 524320 | tf_op jit(solution)/shard_map/ka1_left/ppermute | solution.py:410
  70.8 3.8 %collective-permute-start.10 = (bf16[4,512,128]{2,1,0:T(8,128)(2,1)}, bf16[4,512,128]{2,1,0:T(8,128)(2,1)}, u32[]{:S(2)}, u32[]{:S(2)}) collective-permute-start(bf16[4,512,128]{2,1,0:T(8,128)(2,1)} %collective-permute-done.6.refs_3_), channel_id=1, source_target_pairs={{0,28},{4,0},{8,4},{12,8},{16,12},{20,16},{24,20},{28,24},{1,29},{... | collective-permute-start | bytes 1572872 | tf_op jit(solution)/shard_map/ka2_left/ppermute | solution.py:410
  74.6 11.2 %collective-permute-done.11.refs_9_ = bf16[4,512,128]{2,1,0:T(8,128)(2,1)} collective-permute-done((bf16[4,512,128]{2,1,0:T(8,128)(2,1)S(1)}, bf16[4,512,128]{2,1,0:T(8,128)(2,1)}, u32[]{:S(2)}, u32[]{:S(2)}) %collective-permute-start.11) | collective-permute-done | bytes 524320 | tf_op jit(solution)/shard_map/va2_right/ppermute | solution.py:410
  90.2 6.9 %collective-permute-done.8.refs_4_ = bf16[4,512,128]{2,1,0:T(8,128)(2,1)} collective-permute-done((bf16[4,512,128]{2,1,0:T(8,128)(2,1)}, bf16[4,512,128]{2,1,0:T(8,128)(2,1)}, u32[]{:S(2)}, u32[]{:S(2)}) %collective-permute-start.8) | collective-permute-done | bytes 524320 | tf_op jit(solution)/shard_map/ka2_right/ppermute | solution.py:410
  100.3 7.9 %collective-permute-done.19.refs_4_ = bf16[4,512,128]{2,1,0:T(8,128)(2,1)S(1)} collective-permute-done((bf16[4,512,128]{2,1,0:T(8,128)(2,1)}, bf16[4,512,128]{2,1,0:T(8,128)(2,1)S(1)}, u32[]{:S(2)}, u32[]{:S(2)}) %collective-permute-start.19) | collective-permute-done | bytes 524320 | tf_op jit(solution)/shard_map/va3_right/ppermute | solution.py:410
  111.5 20.0 %attend_0_0_7_1_6_2.1 = (f32[16,512,128]{2,1,0:T(8,128)}, f32[16,8,128]{2,1,0:T(8,128)}, f32[16,8,128]{2,1,0:T(8,128)}) custom-call(s32[129]{0:T(256)} %pad_add_fusion.meta, bf16[4,512,1024]{2,1,0:T(8,128)(2,1)} %all-to-all-done.refs_0_, bf16[4,512,128]{2,1,0:T(8,128)(2,1)} %copy-done.9, bf16[4,512,128]{2,1,0:T(8,128)(2,1)} %collective-permute-done.5.refs_2_, ...), custom_call_target="tpu_custom_call" | custom-call | flops 18699999232 | bytes 1048576 | tf_op jit(solution)/shard_map/attend_0_0_7_1_6_2/pallas_call | solution.py:334
  136.9 11.0 %collective-permute-done.20.refs_3_ = bf16[4,512,128]{2,1,0:T(8,128)(2,1)S(1)} collective-permute-done((bf16[4,512,128]{2,1,0:T(8,128)(2,1)}, bf16[4,512,128]{2,1,0:T(8,128)(2,1)S(1)}, u32[]{:S(2)}, u32[]{:S(2)}) %collective-permute-start.20) | collective-permute-done | bytes 524320 | tf_op jit(solution)/shard_map/ka4_right/ppermute | solution.py:410
  147.9 9.7 %collective-permute-done.25.refs_5_ = bf16[4,512,128]{2,1,0:T(8,128)(2,1)} collective-permute-done((bf16[4,512,128]{2,1,0:T(8,128)(2,1)S(1)}, bf16[4,512,128]{2,1,0:T(8,128)(2,1)}, u32[]{:S(2)}, u32[]{:S(2)}) %collective-permute-start.25) | collective-permute-done | bytes 524320 | tf_op jit(solution)/shard_map/vb1_right/ppermute | solution.py:410
  160.9 13.1 %attend_0_5_3_4.1 = (f32[4,512,128]{2,1,0:T(8,128)}, f32[4,8,128]{2,1,0:T(8,128)}, f32[4,8,128]{2,1,0:T(8,128)}, bf16[4,4,560,128]{3,2,1,0:T(8,128)(2,1)}) custom-call(s32[129]{0:T(256)} %pad_add_fusion.meta, bf16[4,512,1024]{2,1,0:T(8,128)(2,1)} %all-to-all-done.refs_0_, bf16[4,512,128]{2,1,0:T(8,128)(2,1)} %collective-permute-done.18.refs_1_, ...), custom_call_target="tpu_custom_call" | custom-call | flops 12099999744 | bytes 1048576 | tf_op jit(solution)/shard_map/attend_0_5_3_4/pallas_call | solution.py:334
  173.9 3.6 %all-to-all-start.1 = ((bf16[4,4,560,128]{3,2,1,0:T(8,128)(2,1)}), bf16[4,4,560,128]{3,2,1,0:T(8,128)(2,1)S(1)}, u32[]{:S(2)}, u32[]{:S(2)}) async-start(bf16[4,4,560,128]{3,2,1,0:T(8,128)(2,1)} %get-tuple-element.84), calls=%async_computation.1 | async-start | bytes 4587520 | tf_op jit(solution)/shard_map/partials_a/all_to_all | solution.py:534
  183.0 14.5 %attend_4_0_7_1.1 = (f32[16,512,128]{2,1,0:T(8,128)}, f32[16,8,128]{2,1,0:T(8,128)}, f32[16,8,128]{2,1,0:T(8,128)}) custom-call(s32[129]{0:T(256)} %pad_add_fusion.meta, bf16[4,512,1024]{2,1,0:T(8,128)(2,1)} %all-to-all-done.refs_0_, bf16[4,512,128]{2,1,0:T(8,128)(2,1)} %copy-done.8, bf16[4,512,128]{2,1,0:T(8,128)(2,1)} %collective-permute-done.24.refs_2_, ...), custom_call_target="tpu_custom_call" | custom-call | flops 12099999744 | bytes 1048576 | tf_op jit(solution)/shard_map/attend_4_0_7_1/pallas_call | solution.py:334
  202.9 7.4 %collective-permute-done.31.refs_3_ = bf16[4,512,128]{2,1,0:T(8,128)(2,1)} collective-permute-done((bf16[4,512,128]{2,1,0:T(8,128)(2,1)}, bf16[4,512,128]{2,1,0:T(8,128)(2,1)}, u32[]{:S(2)}, u32[]{:S(2)}) %collective-permute-start.31) | collective-permute-done | bytes 524320 | tf_op jit(solution)/shard_map/kb3_right/ppermute | solution.py:410
  210.2 14.9 %attend_4_6_2_5_3.1 = (f32[16,512,128]{2,1,0:T(8,128)}, f32[16,8,128]{2,1,0:T(8,128)}, f32[16,8,128]{2,1,0:T(8,128)}) custom-call(s32[129]{0:T(256)} %pad_add_fusion.meta, bf16[4,512,1024]{2,1,0:T(8,128)(2,1)} %all-to-all-done.refs_0_, bf16[4,512,128]{2,1,0:T(8,128)(2,1)} %collective-permute-done.29.refs_1_, ...), custom_call_target="tpu_custom_call" | custom-call | flops 15399999488 | bytes 1048576 | tf_op jit(solution)/shard_map/attend_4_6_2_5_3/pallas_call | solution.py:334
  225.2 8.1 %attend_4_4.1 = (f32[4,512,128]{2,1,0:T(8,128)}, f32[4,8,128]{2,1,0:T(8,128)}, f32[4,8,128]{2,1,0:T(8,128)}, bf16[4,4,560,128]{3,2,1,0:T(8,128)(2,1)}) custom-call(s32[129]{0:T(256)} %pad_add_fusion.meta, bf16[4,512,1024]{2,1,0:T(8,128)(2,1)} %all-to-all-done.refs_0_, bf16[4,512,128]{2,1,0:T(8,128)(2,1)} %collective-permute-done.27.refs_1_, ...), custom_call_target="tpu_custom_call" | custom-call | flops 5500000256 | bytes 1048576 | tf_op jit(solution)/shard_map/attend_4_4/pallas_call | solution.py:334
  245.0 6.1 %collective-permute-done.34.two = bf16[4,560,128]{2,1,0:T(8,128)(2,1)S(1)} collective-permute-done((bf16[4,560,128]{2,1,0:T(8,128)(2,1)}, bf16[4,560,128]{2,1,0:T(8,128)(2,1)S(1)}, u32[]{:S(2)}, u32[]{:S(2)}) %collective-permute-start.34) | collective-permute-done | bytes 573472 | tf_op jit(solution)/shard_map/partial_b2/ppermute | solution.py:415
  251.2 3.5 %join_4.1 = bf16[512,1024]{1,0:T(8,128)(2,1)} custom-call(f32[4,512,128]{2,1,0:T(8,128)S(1)} %copy-done, f32[4,8,128]{2,1,0:T(8,128)S(1)} %copy-done.4, f32[4,8,128]{2,1,0:T(8,128)S(1)} %copy-done.5, bf16[4,560,128]{2,1,0:T(8,128)(2,1)S(1)} %collective-permute-done.33.one, ...), custom_call_target="tpu_custom_call", output_to_operand_aliasing={{}: (6, {})} | custom-call | flops 2621440 | bytes 3670016 | tf_op jit(solution)/shard_map/join_4/pallas_call | solution.py:393
  (147 shorter events, 65.0 us)
Async XLA Ops:
  36.8 74.7 %all-to-all-start = ((bf16[4,512,1024]{2,1,0:T(8,128)(2,1)}), bf16[4,512,1024]{2,1,0:T(8,128)(2,1)}, u32[]{:S(2)}, u32[]{:S(2)}) async-start(bf16[4,512,1024]{2,1,0:T(8,128)(2,1)} %broadcast_in_dim.70), calls=%async_computation | async-start | bytes 8388608 | tf_op jit(solution)/shard_map/queries/all_to_all | solution.py:471
  47.3 23.6 %collective-permute-start.6 = (bf16[4,512,128]{2,1,0:T(8,128)(2,1)S(1)}, bf16[4,512,128]{2,1,0:T(8,128)(2,1)}, u32[]{:S(2)}, u32[]{:S(2)}) collective-permute-start(bf16[4,512,128]{2,1,0:T(8,128)(2,1)S(1)} %get-tuple-element.53.refs_1_), channel_id=1, source_target_pairs={{0,28},{4,0},{8,4},{12,8},{16,12},{20,16},{24,20},{28,24},{1,29},{... | collective-permute-start | bytes 1572872 | tf_op jit(solution)/shard_map/ka1_left/ppermute | solution.py:410
  50.6 24.1 %collective-permute-start.5 = (bf16[4,512,128]{2,1,0:T(8,128)(2,1)S(1)}, bf16[4,512,128]{2,1,0:T(8,128)(2,1)}, u32[]{:S(2)}, u32[]{:S(2)}) collective-permute-start(bf16[4,512,128]{2,1,0:T(8,128)(2,1)S(1)} %get-tuple-element.53.refs_1_), channel_id=1, source_target_pairs={{0,4},{4,8},{8,12},{12,16},{16,20},{20,24},{24,28},{28,0},{1,5},{5... | collective-permute-start | bytes 1572872 | tf_op jit(solution)/shard_map/ka1_right/ppermute | solution.py:410
  63.3 22.6 %collective-permute-start.11 = (bf16[4,512,128]{2,1,0:T(8,128)(2,1)S(1)}, bf16[4,512,128]{2,1,0:T(8,128)(2,1)}, u32[]{:S(2)}, u32[]{:S(2)}) collective-permute-start(bf16[4,512,128]{2,1,0:T(8,128)(2,1)S(1)} %collective-permute-done.7.refs_7_), channel_id=1, source_target_pairs={{0,4},{4,8},{8,12},{12,16},{16,20},{20,24},{24,28},{28,0},{1,5},{5... | collective-permute-start | bytes 1572872 | tf_op jit(solution)/shard_map/va2_right/ppermute | solution.py:410
  63.3 22.6 %collective-permute-start.12 = (bf16[4,512,128]{2,1,0:T(8,128)(2,1)S(1)}, bf16[4,512,128]{2,1,0:T(8,128)(2,1)}, u32[]{:S(2)}, u32[]{:S(2)}) collective-permute-start(bf16[4,512,128]{2,1,0:T(8,128)(2,1)S(1)} %collective-permute-done.9.refs_8_), channel_id=1, source_target_pairs={{0,28},{4,0},{8,4},{12,8},{16,12},{20,16},{24,20},{28,24},{1,29},{... | collective-permute-start | bytes 1572872 | tf_op jit(solution)/shard_map/va2_left/ppermute | solution.py:410
  70.8 26.3 %collective-permute-start.10 = (bf16[4,512,128]{2,1,0:T(8,128)(2,1)}, bf16[4,512,128]{2,1,0:T(8,128)(2,1)}, u32[]{:S(2)}, u32[]{:S(2)}) collective-permute-start(bf16[4,512,128]{2,1,0:T(8,128)(2,1)} %collective-permute-done.6.refs_3_), channel_id=1, source_target_pairs={{0,28},{4,0},{8,4},{12,8},{16,12},{20,16},{24,20},{28,24},{1,29},{... | collective-permute-start | bytes 1572872 | tf_op jit(solution)/shard_map/ka2_left/ppermute | solution.py:410
  74.6 22.5 %collective-permute-start.8 = (bf16[4,512,128]{2,1,0:T(8,128)(2,1)}, bf16[4,512,128]{2,1,0:T(8,128)(2,1)}, u32[]{:S(2)}, u32[]{:S(2)}) collective-permute-start(bf16[4,512,128]{2,1,0:T(8,128)(2,1)} %collective-permute-done.5.refs_2_), channel_id=1, source_target_pairs={{0,4},{4,8},{8,12},{12,16},{16,20},{20,24},{24,28},{28,0},{1,5},{5... | collective-permute-start | bytes 1572872 | tf_op jit(solution)/shard_map/ka2_right/ppermute | solution.py:410
  85.9 22.4 %collective-permute-start.19 = (bf16[4,512,128]{2,1,0:T(8,128)(2,1)}, bf16[4,512,128]{2,1,0:T(8,128)(2,1)S(1)}, u32[]{:S(2)}, u32[]{:S(2)}) collective-permute-start(bf16[4,512,128]{2,1,0:T(8,128)(2,1)} %collective-permute-done.11.refs_9_), channel_id=1, source_target_pairs={{0,4},{4,8},{8,12},{12,16},{16,20},{20,24},{24,28},{28,0},{1,5},{5... | collective-permute-start | bytes 1572872 | tf_op jit(solution)/shard_map/va3_right/ppermute | solution.py:410
  85.9 22.4 %collective-permute-start.13 = (bf16[4,512,128]{2,1,0:T(8,128)(2,1)}, bf16[4,512,128]{2,1,0:T(8,128)(2,1)}, u32[]{:S(2)}, u32[]{:S(2)}) collective-permute-start(bf16[4,512,128]{2,1,0:T(8,128)(2,1)} %collective-permute-done.12.refs_10_), channel_id=1, source_target_pairs={{0,28},{4,0},{8,4},{12,8},{16,12},{20,16},{24,20},{28,24},{1,29},{... | collective-permute-start | bytes 1572872 | tf_op jit(solution)/shard_map/va3_left/ppermute | solution.py:410
  97.1 34.4 %collective-permute-start.18 = (bf16[4,512,128]{2,1,0:T(8,128)(2,1)}, bf16[4,512,128]{2,1,0:T(8,128)(2,1)}, u32[]{:S(2)}, u32[]{:S(2)}) collective-permute-start(bf16[4,512,128]{2,1,0:T(8,128)(2,1)} %collective-permute-done.8.refs_4_), channel_id=1, source_target_pairs={{0,4},{4,8},{8,12},{12,16},{16,20},{20,24},{24,28},{28,0},{1,5},{5... | collective-permute-start | bytes 1572872 | tf_op jit(solution)/shard_map/ka3_right/ppermute | solution.py:410
  97.1 34.6 %collective-permute-start.14 = (bf16[4,512,128]{2,1,0:T(8,128)(2,1)}, bf16[4,512,128]{2,1,0:T(8,128)(2,1)}, u32[]{:S(2)}, u32[]{:S(2)}) collective-permute-start(bf16[4,512,128]{2,1,0:T(8,128)(2,1)} %collective-permute-done.10.refs_5_), channel_id=1, source_target_pairs={{0,28},{4,0},{8,4},{12,8},{16,12},{20,16},{24,20},{28,24},{1,29},{... | collective-permute-start | bytes 1572872 | tf_op jit(solution)/shard_map/ka3_left/ppermute | solution.py:410
  108.2 23.4 %collective-permute-start.21 = (bf16[4,512,128]{2,1,0:T(8,128)(2,1)S(1)}, bf16[4,512,128]{2,1,0:T(8,128)(2,1)}, u32[]{:S(2)}, u32[]{:S(2)}) collective-permute-start(bf16[4,512,128]{2,1,0:T(8,128)(2,1)S(1)} %collective-permute-done.19.refs_4_), channel_id=1, source_target_pairs={{0,4},{4,8},{8,12},{12,16},{16,20},{20,24},{24,28},{28,0},{1,5},{5... | collective-permute-start | bytes 1572872 | tf_op jit(solution)/shard_map/va4_right/ppermute | solution.py:410
  108.2 26.7 %collective-permute-start.16 = (bf16[4,512,128]{2,1,0:T(8,128)(2,1)S(1)}, bf16[4,512,128]{2,1,0:T(8,128)(2,1)}, u32[]{:S(2)}, u32[]{:S(2)}) collective-permute-start(bf16[4,512,128]{2,1,0:T(8,128)(2,1)S(1)} %get-tuple-element.74.refs_4_), channel_id=1, source_target_pairs={{0,28},{4,0},{8,4},{12,8},{16,12},{20,16},{24,20},{28,24},{1,29},{... | collective-permute-start | bytes 1572872 | tf_op jit(solution)/shard_map/vb1_left/ppermute | solution.py:410
  131.6 26.0 %collective-permute-start.25 = (bf16[4,512,128]{2,1,0:T(8,128)(2,1)S(1)}, bf16[4,512,128]{2,1,0:T(8,128)(2,1)}, u32[]{:S(2)}, u32[]{:S(2)}) collective-permute-start(bf16[4,512,128]{2,1,0:T(8,128)(2,1)S(1)} %get-tuple-element.74.refs_4_), channel_id=1, source_target_pairs={{0,4},{4,8},{8,12},{12,16},{16,20},{20,24},{24,28},{28,0},{1,5},{5... | collective-permute-start | bytes 1572872 | tf_op jit(solution)/shard_map/vb1_right/ppermute | solution.py:410
  131.7 25.9 %collective-permute-start.15 = (bf16[4,512,128]{2,1,0:T(8,128)(2,1)S(1)}, bf16[4,512,128]{2,1,0:T(8,128)(2,1)}, u32[]{:S(2)}, u32[]{:S(2)}) collective-permute-start(bf16[4,512,128]{2,1,0:T(8,128)(2,1)S(1)} %get-tuple-element.73.refs_1_), channel_id=1, source_target_pairs={{0,28},{4,0},{8,4},{12,8},{16,12},{20,16},{24,20},{28,24},{1,29},{... | collective-permute-start | bytes 1572872 | tf_op jit(solution)/shard_map/kb1_left/ppermute | solution.py:410
  135.0 42.6 %collective-permute-start.22 = (bf16[4,512,128]{2,1,0:T(8,128)(2,1)}, bf16[4,512,128]{2,1,0:T(8,128)(2,1)}, u32[]{:S(2)}, u32[]{:S(2)}) collective-permute-start(bf16[4,512,128]{2,1,0:T(8,128)(2,1)} %collective-permute-done.16.refs_6_), channel_id=1, source_target_pairs={{0,28},{4,0},{8,4},{12,8},{16,12},{20,16},{24,20},{28,24},{1,29},{... | collective-permute-start | bytes 1572872 | tf_op jit(solution)/shard_map/vb2_left/ppermute | solution.py:410
  147.9 29.8 %collective-permute-start.24 = (bf16[4,512,128]{2,1,0:T(8,128)(2,1)S(1)}, bf16[4,512,128]{2,1,0:T(8,128)(2,1)}, u32[]{:S(2)}, u32[]{:S(2)}) collective-permute-start(bf16[4,512,128]{2,1,0:T(8,128)(2,1)S(1)} %get-tuple-element.73.refs_1_), channel_id=1, source_target_pairs={{0,4},{4,8},{8,12},{12,16},{16,20},{20,24},{24,28},{28,0},{1,5},{5... | collective-permute-start | bytes 1572872 | tf_op jit(solution)/shard_map/kb1_right/ppermute | solution.py:410
  157.6 22.4 %collective-permute-start.17 = (bf16[4,512,128]{2,1,0:T(8,128)(2,1)}, bf16[4,512,128]{2,1,0:T(8,128)(2,1)}, u32[]{:S(2)}, u32[]{:S(2)}) collective-permute-start(bf16[4,512,128]{2,1,0:T(8,128)(2,1)} %collective-permute-done.15.refs_3_), channel_id=1, source_target_pairs={{0,28},{4,0},{8,4},{12,8},{16,12},{20,16},{24,20},{28,24},{1,29},{... | collective-permute-start | bytes 1572872 | tf_op jit(solution)/shard_map/kb2_left/ppermute | solution.py:410
  173.9 28.9 %all-to-all-start.1 = ((bf16[4,4,560,128]{3,2,1,0:T(8,128)(2,1)}), bf16[4,4,560,128]{3,2,1,0:T(8,128)(2,1)S(1)}, u32[]{:S(2)}, u32[]{:S(2)}) async-start(bf16[4,4,560,128]{3,2,1,0:T(8,128)(2,1)} %get-tuple-element.84), calls=%async_computation.1 | async-start | bytes 4587520 | tf_op jit(solution)/shard_map/partials_a/all_to_all | solution.py:534
  177.6 22.4 %collective-permute-start.26 = (bf16[4,512,128]{2,1,0:T(8,128)(2,1)}, bf16[4,512,128]{2,1,0:T(8,128)(2,1)}, u32[]{:S(2)}, u32[]{:S(2)}) collective-permute-start(bf16[4,512,128]{2,1,0:T(8,128)(2,1)} %collective-permute-done.22.refs_6_), channel_id=1, source_target_pairs={{0,28},{4,0},{8,4},{12,8},{16,12},{20,16},{24,20},{28,24},{1,29},{... | collective-permute-start | bytes 1572872 | tf_op jit(solution)/shard_map/vb3_left/ppermute | solution.py:410
  177.7 25.1 %collective-permute-start.32 = (bf16[4,512,128]{2,1,0:T(8,128)(2,1)S(1)}, bf16[4,512,128]{2,1,0:T(8,128)(2,1)S(1)}, u32[]{:S(2)}, u32[]{:S(2)}) collective-permute-start(bf16[4,512,128]{2,1,0:T(8,128)(2,1)S(1)} %collective-permute-done.30.refs_5_), channel_id=1, source_target_pairs={{0,4},{4,8},{8,12},{12,16},{16,20},{20,24},{24,28},{28,0},{1,5},{5... | collective-permute-start | bytes 1572872 | tf_op jit(solution)/shard_map/vb3_right/ppermute | solution.py:410
  180.1 22.7 %collective-permute-start.23 = (bf16[4,512,128]{2,1,0:T(8,128)(2,1)}, bf16[4,512,128]{2,1,0:T(8,128)(2,1)}, u32[]{:S(2)}, u32[]{:S(2)}) collective-permute-start(bf16[4,512,128]{2,1,0:T(8,128)(2,1)} %collective-permute-done.17.refs_2_), channel_id=1, source_target_pairs={{0,28},{4,0},{8,4},{12,8},{16,12},{20,16},{24,20},{28,24},{1,29},{... | collective-permute-start | bytes 1572872 | tf_op jit(solution)/shard_map/kb3_left/ppermute | solution.py:410
  200.0 25.2 %collective-permute-start.28 = (bf16[4,512,128]{2,1,0:T(8,128)(2,1)}, bf16[4,512,128]{2,1,0:T(8,128)(2,1)}, u32[]{:S(2)}, u32[]{:S(2)}) collective-permute-start(bf16[4,512,128]{2,1,0:T(8,128)(2,1)} %collective-permute-done.26.refs_8_), channel_id=1, source_target_pairs={{0,28},{4,0},{8,4},{12,8},{16,12},{20,16},{24,20},{28,24},{1,29},{... | collective-permute-start | bytes 1572872 | tf_op jit(solution)/shard_map/vb4_left/ppermute | solution.py:410
  202.8 22.4 %collective-permute-start.27 = (bf16[4,512,128]{2,1,0:T(8,128)(2,1)}, bf16[4,512,128]{2,1,0:T(8,128)(2,1)}, u32[]{:S(2)}, u32[]{:S(2)}) collective-permute-start(bf16[4,512,128]{2,1,0:T(8,128)(2,1)} %collective-permute-done.23.refs_4_), channel_id=1, source_target_pairs={{0,28},{4,0},{8,4},{12,8},{16,12},{20,16},{24,20},{28,24},{1,29},{... | collective-permute-start | bytes 1572872 | tf_op jit(solution)/shard_map/kb4_left/ppermute | solution.py:410
  (34 other events, 715.5 us)

commit v5 on v4

--- a/solution.py
+++ b/solution.py
@@ -15,7 +15,6 @@
 NEG_FILL = -1e30
 ROPE_BASE = 10000.0
 VMEM_LIMIT = 24 << 20
-ATTEND_VMEM = 60 << 20
 IDLE = 4
 STAT = 48
 CHUNKS = ((0, 4), (4, 4))
@@ -66,7 +65,9 @@
                 return (x * plain + pltpu.roll(x, HEAD // 2, 1) * signed).astype(jnp.bfloat16)
 
             part = slice(h % 4 * HEAD, (h % 4 + 1) * HEAD)
-            outs[0][:, cols] = turn(q_ref[:, cols])
+            query = turn(q_ref[:, cols])
+            for row in range(ROWS):
+                outs[0][row, :, cols] = query
             outs[1 + h // 4][0, part, :] = turn(k_ref[:, cols])
 
 
@@ -77,11 +78,12 @@
     heads = angles.shape[0]
     bf16 = jnp.bfloat16
     rows = pl.BlockSpec((BLOCK, heads * HEAD), lambda b: (b, 0))
+    copies = pl.BlockSpec((ROWS, BLOCK, heads * HEAD), lambda b: (0, b, 0))
     tiled = pl.BlockSpec((1, 4 * HEAD, BLOCK), lambda b: (b, 0, 0))
     return pl.pallas_call(
         rotate_kernel,
         out_shape=[
-            jax.ShapeDtypeStruct(queries.shape, bf16),
+            jax.ShapeDtypeStruct((ROWS, *queries.shape), bf16),
             jax.ShapeDtypeStruct((4, 4 * HEAD, BLOCK), bf16),
             jax.ShapeDtypeStruct((4, 4 * HEAD, BLOCK), bf16),
         ],
@@ -92,7 +94,7 @@
             rows,
             rows,
         ],
-        out_specs=[rows, tiled, tiled],
+        out_specs=[copies, tiled, tiled],
         compiler_params=pltpu.CompilerParams(vmem_limit_bytes=VMEM_LIMIT),
         cost_estimate=pl.CostEstimate(flops=5 * 10**9, bytes_accessed=6 << 20, transcendentals=0),
         name="rotate",
@@ -253,14 +255,13 @@
     if not last:
         leave(*rest)
     else:
-        packed_ref = rest[3]
+        packed_refs = rest[3:]
 
         @pl.when(r == 0)
         def _():
             leave(*rest[:3])
 
-        @pl.when(r > 0)
-        def _():
+        def send(packed_ref, lead):
             def pack(qb, carry):
                 pieces = []
                 for value in (m_run[qb], l_run[qb]):
@@ -268,22 +269,29 @@
                         piece = value.astype(jnp.bfloat16).astype(jnp.float32)
                         pieces.append(piece)
                         value = value - piece
-                packed_ref[0, qb, heads * HEAD :, :] = jnp.concatenate(pieces, axis=0).astype(
+                packed_ref[(*lead, qb, slice(heads * HEAD, None), slice(None))] = jnp.concatenate(pieces, axis=0).astype(
                     jnp.bfloat16
                 )
                 total = l_run[qb]
                 inverse = 1.0 / jnp.where(total > 0, total, 1.0)
                 for h in span:
-                    packed_ref[0, qb, cols[h], :] = (
+                    packed_ref[(*lead, qb, cols[h], slice(None))] = (
                         acc[qb, cols[h], :] * inverse[h : h + 1]
                     ).astype(jnp.bfloat16)
                 return carry
 
             lax.fori_loop(0, 4, pack, 0)
 
+        if len(packed_refs) == 1:
+            pl.when(r > 0)(lambda: send(packed_refs[0], (0,)))
+        else:
+            for row, packed_ref in enumerate(packed_refs):
+                pl.when(r == row + 1)(functools.partial(send, packed_ref, ()))
+
 
 def attend(meta, queries, chunk, offsets, keys, values, state, last):
     first_head, heads = chunk
+    apart = first_head > 0
     width = heads * HEAD
     first = state is None
     acc_spec = pl.BlockSpec((4, width, BLOCK), lambda r, meta: (r, 0, 0))
@@ -306,13 +314,21 @@
             jax.ShapeDtypeStruct((4, width, BLOCK), f32),
             jax.ShapeDtypeStruct((4, 8, BLOCK), f32),
             jax.ShapeDtypeStruct((4, 8, BLOCK), f32),
-            jax.ShapeDtypeStruct((ROWS, 4, width + STAT, BLOCK), jnp.bfloat16),
+            *(
+                [jax.ShapeDtypeStruct((4, width + STAT, BLOCK), jnp.bfloat16)] * 3
+                if apart
+                else [jax.ShapeDtypeStruct((ROWS, 4, width + STAT, BLOCK), jnp.bfloat16)]
+            ),
         ]
         out_specs = [
             pl.BlockSpec((4, width, BLOCK), lambda r, meta: (0, 0, 0)),
             pl.BlockSpec((4, 8, BLOCK), lambda r, meta: (0, 0, 0)),
             pl.BlockSpec((4, 8, BLOCK), lambda r, meta: (0, 0, 0)),
-            pl.BlockSpec((1, 4, width + STAT, BLOCK), lambda r, meta: ((meta[16 * RING] + jnp.maximum(r, 1)) & 3, 0, 0, 0)),
+            *(
+                [pl.BlockSpec((4, width + STAT, BLOCK), lambda r, meta: (0, 0, 0))] * 3
+                if apart
+                else [            pl.BlockSpec((1, 4, width + STAT, BLOCK), lambda r, meta: ((meta[16 * RING] + jnp.maximum(r, 1)) & 3, 0, 0, 0))]
+            ),
         ]
     else:
         out_shape = [
@@ -341,7 +357,7 @@
             out_specs=out_specs,
             scratch_shapes=scratch,
         ),
-        compiler_params=pltpu.CompilerParams(vmem_limit_bytes=ATTEND_VMEM),
+        compiler_params=pltpu.CompilerParams(vmem_limit_bytes=VMEM_LIMIT),
         cost_estimate=pl.CostEstimate(
             flops=int((2 + 3 * len(offsets)) * 1.1e9),
             bytes_accessed=1 << 20,
@@ -448,6 +464,10 @@
     before = jnp.zeros_like(total)
     value_tiles = value_states.reshape(4, BLOCK, -1).transpose(0, 2, 1)
     va, vb = {0: value_tiles[:, : 4 * HEAD]}, {0: value_tiles[:, 4 * HEAD :]}
+    right, left = Wire("right", 1), Wire("left", -1)
+    for name, ring in (("va", va), ("vb", vb)):
+        for wire in (right, left):
+            wire.send(name, ring, 1)
     picks = selected_blocks.T.astype(jnp.float32)
     with jax.named_scope("prefix"):
         rows_before = before
@@ -458,6 +478,7 @@
             rows_before = rows_before + jnp.where((my_y & bit) != 0, other[:, :1], 0.0)
             total = total + other[:, :1]
             picks = jnp.concatenate([picks, other[:, 2:]], axis=1)
+        own_total = after(own_total, va[1], va[-1], vb[1], vb[-1])
         for bit in (1, 2, 4):
             other = swap(jnp.concatenate([own_total, rows_before], axis=1), "z", bit)
             before = before + jnp.where((my_z & bit) != 0, other[:, :1], 0.0)
@@ -467,8 +488,7 @@
     query_rot, keys_a, keys_b = rotate(angles, query_states, key_states)
     ka, kb = {0: keys_a}, {0: keys_b}
     with jax.named_scope("queries"):
-        copies = jnp.broadcast_to(query_rot[None], (ROWS, *query_rot.shape))
-        queries = lax.all_to_all(copies, "y", 0, 0, tiled=True)
+        queries = lax.all_to_all(query_rot, "y", 0, 0, tiled=True)
 
     picks = picks.astype(jnp.int32).T.reshape(4, 1, 4, 8)
     wanted = (my_y + lax.broadcasted_iota(jnp.int32, (4, 4, 1, 1), 1)) ^ my_y
@@ -502,33 +522,32 @@
     def pick(rows, step):
         return lax.dynamic_index_in_dim(rows, (my_y + step) & 3, 0, keepdims=False)
 
-    right, left = Wire("right", 1), Wire("left", -1)
-    for distance in (1, 2):
-        for name, ring in (("va", va), ("ka", ka)):
-            for wire in (right, left):
-                wire.send(name, ring, distance)
-    for wire in (right, left):
-        wire.send("va", va, 3)
-        wire.send("ka", ka, 3)
+    for name, ring, distance in (
+        ("ka", ka, 1),
+        ("va", va, 2),
+        ("ka", ka, 2),
+        ("va", va, 3),
+        ("ka", ka, 3),
+    ):
+        for wire in (right, left):
+            wire.send(name, ring, distance)
+    right.send("va", va, 4)
+    right.send("ka", ka, 4)
+    left.send("kb", kb, 1)
     state = call(0, GROUPS[0][0], None, False)
-    right.send("va", va, 4)
-    left.send("vb", vb, 1)
-    right.send("ka", ka, 4, state[1])
-    left.send("kb", kb, 1, state[1])
-    right.send("vb", vb, 1)
+    right.send("kb", kb, 1)
     left.send("vb", vb, 2)
-    right.send("kb", kb, 1)
+    right.send("vb", vb, 2)
     left.send("kb", kb, 2)
     state = call(0, GROUPS[0][1], state, True)
-    right.send("vb", vb, 2)
-    left.send("vb", vb, 3)
     right.send("kb", kb, 2, state[1])
-    left.send("kb", kb, 3, state[1])
+    left.send("vb", vb, 3, state[1])
+    right.send("vb", vb, 3)
+    left.send("kb", kb, 3)
     first_b = call(1, GROUPS[1][0], None, False)
-    right.send("vb", vb, 3)
-    left.send("vb", vb, 4)
     right.send("kb", kb, 3, first_b[1])
-    left.send("kb", kb, 4, first_b[1])
+    left.send("vb", vb, 4, first_b[1])
+    left.send("kb", kb, 4)
     mine_a = state[:3]
     with jax.named_scope("partials_a"):
         parts_a = lax.all_to_all(state[3], "y", 0, 0, tiled=True)
@@ -538,7 +557,7 @@
     parts_b = []
     for s in (1, 2, 3):
         with jax.named_scope(f"partial_b{s}"):
-            parts_b.append(to_row(pick(state[3], s), s))
+            parts_b.append(to_row(state[2 + s], s))
     parts_a = after(parts_a, state[1])
     out = join(CHUNKS[0], mine_a, [pick(parts_a, -s) for s in (1, 2, 3)], None)
     return join(CHUNKS[1], state[:3], parts_b, out)

time: 256 us -> 265 us (1.035)
  waiting for transfers between devices: 86.9 us -> 107 us
  local copies, waits for them, and re-layouts: 10.8 us -> 21.7 us
  Pallas kernels: 80.1 us -> 70 us
  starting transfers between devices: 72.8 us -> 63.6 us
    unnamed x40 -> x42, local copies, waits for them, and re-layouts: 2.52 us -> 15.9 us
    pallas_call x5, Pallas kernels: 70.6 us -> 59.8 us  [attend(): pl.pallas_call(functools.partial(attend_kernel, offsets, heads, first, la...]
    ppermute x5, starting transfers between devices: 17.2 us -> 6.91 us  [swap(): return lax.ppermute(value, axis, [(i, i ^ bit) for i in range(size)])]
    ppermute x5, waiting for transfers between devices: 7.13 us -> 16.1 us  [swap(): return lax.ppermute(value, axis, [(i, i ^ bit) for i in range(size)])]
    ppermute x28, waiting for transfers between devices: 73 us -> 81.8 us  [shift(): lax.ppermute(value, axis, [(i, (i + step) % size) for i in range(size)])]
    squeeze x2 -> x1, local copies, waits for them, and re-layouts: 4.25 us -> 1.51 us  [pick(): return lax.dynamic_index_in_dim(rows, my_y + step & 3, 0, keepdims=False)]
  transfers between devices with their start and end apart: 38 -> 38, of which waited for: 16 -> 19; matrix products, arithmetic and copies ran while one was open for 2% -> 1% of each run, Pallas kernels for 25% -> 21%
where the time goes in v5:
time: 265 us; the launch traced here: 264 us
  waiting for transfers between devices  107 us (40%)
  Pallas kernels  70 us (26%)
  starting transfers between devices  63.6 us (24%)
  local copies, waits for them, and re-layouts  21.7 us (8%)
    ppermute x28, waiting for transfers between devices, shift(): lax.ppermute(value, axis, [(i, (i + step) % size) for i in range(size)])  81.8 us
    pallas_call x5, Pallas kernels, attend(): pl.pallas_call(functools.partial(attend_kernel, offsets, heads, first, la...  59.8 us
    ppermute x28, starting transfers between devices, shift(): lax.ppermute(value, axis, [(i, (i + step) % size) for i in range(size)])  42.4 us
    ppermute x5, waiting for transfers between devices, swap(): return lax.ppermute(value, axis, [(i, i ^ bit) for i in range(size)])  16.1 us
    unnamed x42, local copies, waits for them, and re-layouts  15.9 us
    ppermute x3, waiting for transfers between devices, to_row(): return lax.ppermute(value, 'y', moves)  8.6 us
    ppermute x5, starting transfers between devices, swap(): return lax.ppermute(value, axis, [(i, i ^ bit) for i in range(size)])  6.91 us
    pallas_call x2, Pallas kernels, join(): pl.pallas_call(functools.partial(join_kernel, heads), out_shape=jax.Shape...  5.47 us
  transfers between devices with their start and end apart: 38, of which 19 were waited for; matrix products, arithmetic and copies ran while one was open for 1% of the time, Pallas kernels for 21%

profile of v5, /device:TPU:2, one launch (start us, length us, event | category | flops | bytes accessed | tf_op | source)
XLA Modules:
  0.0 264.1 jit_solution(7106738033966216476)
XLA Ops:
  3.7 5.9 %collective-permute-start.2 = (bf16[4,512,128]{2,1,0:T(8,128)(2,1)S(1)}, bf16[4,512,128]{2,1,0:T(8,128)(2,1)}, u32[]{:S(2)}, u32[]{:S(2)}) collective-permute-start(bf16[4,512,128]{2,1,0:T(8,128)(2,1)S(1)} %get-tuple-element.107.refs_6_), channel_id=1, source_target_pairs={{0,28},{4,0},{8,4},{12,8},{16,12},{20,16},{24,20},{28,24},{1,29},{... | collective-permute-start | bytes 1572872 | tf_op jit(solution)/shard_map/va1_left/ppermute | solution.py:426
  22.0 3.8 %collective-permute-done.3.refs_7_ = bf16[4,512,128]{2,1,0:T(8,128)(2,1)} collective-permute-done((bf16[4,512,128]{2,1,0:T(8,128)(2,1)S(1)}, bf16[4,512,128]{2,1,0:T(8,128)(2,1)}, u32[]{:S(2)}, u32[]{:S(2)}) %collective-permute-start.3) | collective-permute-done | bytes 524320 | tf_op jit(solution)/shard_map/va1_right/ppermute | solution.py:426
  25.8 6.3 %collective-permute-done.4.refs_6_ = bf16[4,512,128]{2,1,0:T(8,128)(2,1)} collective-permute-done((bf16[4,512,128]{2,1,0:T(8,128)(2,1)S(1)}, bf16[4,512,128]{2,1,0:T(8,128)(2,1)}, u32[]{:S(2)}, u32[]{:S(2)}) %collective-permute-start.4) | collective-permute-done | bytes 524320 | tf_op jit(solution)/shard_map/vb1_left/ppermute | solution.py:426
  35.7 3.5 %collective-permute-done.6 = f32[8,2]{0,1:T(2,128)S(1)} collective-permute-done((f32[8,2]{0,1:T(2,128)S(1)}, f32[8,2]{0,1:T(2,128)S(1)}, u32[]{:S(2)}, u32[]{:S(2)}) %collective-permute-start.6) | collective-permute-done | bytes 96 | tf_op jit(solution)/shard_map/prefix/ppermute | solution.py:436
  39.4 4.4 %collective-permute-done.7 = f32[8,2]{0,1:T(2,128)S(1)} collective-permute-done((f32[8,2]{0,1:T(2,128)S(1)}, f32[8,2]{0,1:T(2,128)S(1)}, u32[]{:S(2)}, u32[]{:S(2)}) %collective-permute-start.7) | collective-permute-done | bytes 96 | tf_op jit(solution)/shard_map/prefix/ppermute | solution.py:436
  45.6 5.8 %collective-permute-done.8 = f32[8,2]{0,1:T(2,128)S(1)} collective-permute-done((f32[8,2]{0,1:T(2,128)S(1)}, f32[8,2]{0,1:T(2,128)S(1)}, u32[]{:S(2)}, u32[]{:S(2)}) %collective-permute-start.8) | collective-permute-done | bytes 96 | tf_op jit(solution)/shard_map/prefix/ppermute | solution.py:436
  51.4 4.8 %rotate.1 = (bf16[4,512,1024]{2,1,0:T(8,128)(2,1)S(1)}, bf16[4,512,128]{2,1,0:T(8,128)(2,1)S(1)}, bf16[4,512,128]{2,1,0:T(8,128)(2,1)S(1)}) custom-call(f32[512,8]{1,0:T(8,128)S(1)} %bitcast.26, f32[1,128]{1,0:T(1,128)S(1)} %maximum_bitcast_fusion.freq_ref, bf16[512,1024]{1,0:T(8,128)(2,1)S(1)} %copy-done.1, bf16[512,1024]{1,0:T(8,128)(2,1)S(1)} %copy-done.2), custom_call_target="tpu_custom_call" | custom-call | flops 5000000000 | bytes 6291456 | tf_op jit(solution)/shard_map/rotate/pallas_call | solution.py:83
  59.8 5.0 %all-to-all-start = ((bf16[4,512,1024]{2,1,0:T(8,128)(2,1)}), bf16[4,512,1024]{2,1,0:T(8,128)(2,1)}, u32[]{:S(2)}, u32[]{:S(2)}) async-start(bf16[4,512,1024]{2,1,0:T(8,128)(2,1)} %copy-done), calls=%async_computation | async-start | bytes 8388608 | tf_op jit(solution)/shard_map/queries/all_to_all | solution.py:491
  71.4 9.6 %collective-permute-done.18.refs_2_ = bf16[4,512,128]{2,1,0:T(8,128)(2,1)S(1)} collective-permute-done((bf16[4,512,128]{2,1,0:T(8,128)(2,1)S(1)}, bf16[4,512,128]{2,1,0:T(8,128)(2,1)S(1)}, u32[]{:S(2)}, u32[]{:S(2)}) %collective-permute-start.18) | collective-permute-done | bytes 524320 | tf_op jit(solution)/shard_map/ka1_right/ppermute | solution.py:426
  81.0 7.4 %collective-permute-done.9.refs_3_ = bf16[4,512,128]{2,1,0:T(8,128)(2,1)S(1)} collective-permute-done((bf16[4,512,128]{2,1,0:T(8,128)(2,1)S(1)}, bf16[4,512,128]{2,1,0:T(8,128)(2,1)S(1)}, u32[]{:S(2)}, u32[]{:S(2)}) %collective-permute-start.9) | collective-permute-done | bytes 524320 | tf_op jit(solution)/shard_map/ka1_left/ppermute | solution.py:426
  95.2 8.2 %collective-permute-done.19.refs_4_ = bf16[4,512,128]{2,1,0:T(8,128)(2,1)S(1)} collective-permute-done((bf16[4,512,128]{2,1,0:T(8,128)(2,1)S(1)}, bf16[4,512,128]{2,1,0:T(8,128)(2,1)S(1)}, u32[]{:S(2)}, u32[]{:S(2)}) %collective-permute-start.19) | collective-permute-done | bytes 524320 | tf_op jit(solution)/shard_map/ka2_right/ppermute | solution.py:426
  104.4 6.5 %collective-permute-done.12.refs_5_ = bf16[4,512,128]{2,1,0:T(8,128)(2,1)S(1)} collective-permute-done((bf16[4,512,128]{2,1,0:T(8,128)(2,1)S(1)}, bf16[4,512,128]{2,1,0:T(8,128)(2,1)S(1)}, u32[]{:S(2)}, u32[]{:S(2)}) %collective-permute-start.12) | collective-permute-done | bytes 524320 | tf_op jit(solution)/shard_map/va3_left/ppermute | solution.py:426
  116.8 9.2 %collective-permute-done.21.refs_1_ = bf16[4,512,128]{2,1,0:T(8,128)(2,1)} collective-permute-done((bf16[4,512,128]{2,1,0:T(8,128)(2,1)S(1)}, bf16[4,512,128]{2,1,0:T(8,128)(2,1)}, u32[]{:S(2)}, u32[]{:S(2)}) %collective-permute-start.21) | collective-permute-done | bytes 524320 | tf_op jit(solution)/shard_map/ka3_right/ppermute | solution.py:426
  126.6 8.1 %collective-permute-done.14.refs_2_ = bf16[4,512,128]{2,1,0:T(8,128)(2,1)} collective-permute-done((bf16[4,512,128]{2,1,0:T(8,128)(2,1)}, bf16[4,512,128]{2,1,0:T(8,128)(2,1)}, u32[]{:S(2)}, u32[]{:S(2)}) %collective-permute-start.14) | collective-permute-done | bytes 524320 | tf_op jit(solution)/shard_map/ka3_left/ppermute | solution.py:426
  139.9 8.6 %collective-permute-done.23.refs_3_ = bf16[4,512,128]{2,1,0:T(8,128)(2,1)} collective-permute-done((bf16[4,512,128]{2,1,0:T(8,128)(2,1)}, bf16[4,512,128]{2,1,0:T(8,128)(2,1)}, u32[]{:S(2)}, u32[]{:S(2)}) %collective-permute-start.23) | collective-permute-done | bytes 524320 | tf_op jit(solution)/shard_map/ka4_right/ppermute | solution.py:426
  151.6 17.7 %attend_0_0_7_1_6_2.1 = (f32[16,512,128]{2,1,0:T(8,128)S(1)}, f32[16,8,128]{2,1,0:T(8,128)S(1)}, f32[16,8,128]{2,1,0:T(8,128)S(1)}) custom-call(s32[129]{0:T(256)S(1)} %pad_add_fusion.meta, bf16[4,512,1024]{2,1,0:T(8,128)(2,1)} %all-to-all-done.refs_0_, bf16[4,512,128]{2,1,0:T(8,128)(2,1)S(1)} %copy-done.6, ...), custom_call_target="tpu_custom_call" | custom-call | flops 18699999232 | bytes 1048576 | tf_op jit(solution)/shard_map/attend_0_0_7_1_6_2/pallas_call | solution.py:350
  169.3 10.5 %attend_0_5_3_4.1 = (f32[4,512,128]{2,1,0:T(8,128)S(1)}, f32[4,8,128]{2,1,0:T(8,128)S(1)}, f32[4,8,128]{2,1,0:T(8,128)S(1)}, bf16[4,4,560,128]{3,2,1,0:T(8,128)(2,1)}) custom-call(s32[129]{0:T(256)S(1)} %pad_add_fusion.meta, bf16[4,512,1024]{2,1,0:T(8,128)(2,1)} %all-to-all-done.refs_0_, bf16[4,512,128]{2,1,0:T(8,128)(2,1)} %collective-permute-done.21.refs_1_, ...), custom_call_target="tpu_custom_call" | custom-call | flops 12099999744 | bytes 1048576 | tf_op jit(solution)/shard_map/attend_0_5_3_4/pallas_call | solution.py:350
  179.8 4.5 %all-to-all-start.1 = ((bf16[4,4,560,128]{3,2,1,0:T(8,128)(2,1)}), bf16[4,4,560,128]{3,2,1,0:T(8,128)(2,1)}, u32[]{:S(2)}, u32[]{:S(2)}) async-start(bf16[4,4,560,128]{3,2,1,0:T(8,128)(2,1)} %get-tuple-element.88), calls=%async_computation.1 | async-start | bytes 4587520 | tf_op jit(solution)/shard_map/partials_a/all_to_all | solution.py:553
  184.4 4.6 %collective-permute-start.17 = (bf16[4,512,128]{2,1,0:T(8,128)(2,1)}, bf16[4,512,128]{2,1,0:T(8,128)(2,1)S(1)}, u32[]{:S(2)}, u32[]{:S(2)}) collective-permute-start(bf16[4,512,128]{2,1,0:T(8,128)(2,1)} %collective-permute-done.15.refs_2_), channel_id=1, source_target_pairs={{0,28},{4,0},{8,4},{12,8},{16,12},{20,16},{24,20},{28,24},{1,29},{... | collective-permute-start | bytes 1572872 | tf_op jit(solution)/shard_map/kb3_left/ppermute | solution.py:426
  192.2 13.5 %attend_4_0_7_1.1 = (f32[16,512,128]{2,1,0:T(8,128)S(1)}, f32[16,8,128]{2,1,0:T(8,128)S(1)}, f32[16,8,128]{2,1,0:T(8,128)S(1)}) custom-call(s32[129]{0:T(256)S(1)} %pad_add_fusion.meta, bf16[4,512,1024]{2,1,0:T(8,128)(2,1)} %all-to-all-done.refs_0_, bf16[4,512,128]{2,1,0:T(8,128)(2,1)S(1)} %copy-done.4, ...), custom_call_target="tpu_custom_call" | custom-call | flops 12099999744 | bytes 1048576 | tf_op jit(solution)/shard_map/attend_4_0_7_1/pallas_call | solution.py:350
  214.2 7.4 %collective-permute-done.31.refs_3_ = bf16[4,512,128]{2,1,0:T(8,128)(2,1)} collective-permute-done((bf16[4,512,128]{2,1,0:T(8,128)(2,1)}, bf16[4,512,128]{2,1,0:T(8,128)(2,1)}, u32[]{:S(2)}, u32[]{:S(2)}) %collective-permute-start.31) | collective-permute-done | bytes 524320 | tf_op jit(solution)/shard_map/kb3_right/ppermute | solution.py:426
  223.8 12.1 %attend_4_6_2_5_3.1 = (f32[16,512,128]{2,1,0:T(8,128)S(1)}, f32[16,8,128]{2,1,0:T(8,128)S(1)}, f32[16,8,128]{2,1,0:T(8,128)S(1)}) custom-call(s32[129]{0:T(256)S(1)} %pad_add_fusion.meta, bf16[4,512,1024]{2,1,0:T(8,128)(2,1)} %all-to-all-done.refs_0_, bf16[4,512,128]{2,1,0:T(8,128)(2,1)} %collective-permute-done.29.refs_1_, ...), custom_call_target="tpu_custom_call" | custom-call | flops 15399999488 | bytes 1048576 | tf_op jit(solution)/shard_map/attend_4_6_2_5_3/pallas_call | solution.py:350
  237.8 6.0 %attend_4_4.1 = (f32[4,512,128]{2,1,0:T(8,128)S(1)}, f32[4,8,128]{2,1,0:T(8,128)S(1)}, f32[4,8,128]{2,1,0:T(8,128)S(1)}, bf16[4,560,128]{2,1,0:T(8,128)(2,1)}, b...) custom-call(s32[129]{0:T(256)S(1)} %pad_add_fusion.meta, bf16[4,512,1024]{2,1,0:T(8,128)(2,1)} %all-to-all-done.refs_0_, ...), custom_call_target="tpu_custom_call" | custom-call | flops 5500000256 | bytes 1048576 | tf_op jit(solution)/shard_map/attend_4_4/pallas_call | solution.py:350
  254.4 6.1 %collective-permute-done.34.two = bf16[4,560,128]{2,1,0:T(8,128)(2,1)S(1)} collective-permute-done((bf16[4,560,128]{2,1,0:T(8,128)(2,1)}, bf16[4,560,128]{2,1,0:T(8,128)(2,1)S(1)}, u32[]{:S(2)}, u32[]{:S(2)}) %collective-permute-start.34) | collective-permute-done | bytes 573472 | tf_op jit(solution)/shard_map/partial_b2/ppermute | solution.py:431
  (147 shorter events, 84.2 us)
Async XLA Ops:
  9.6 22.4 %collective-permute-start.4 = (bf16[4,512,128]{2,1,0:T(8,128)(2,1)S(1)}, bf16[4,512,128]{2,1,0:T(8,128)(2,1)}, u32[]{:S(2)}, u32[]{:S(2)}) collective-permute-start(bf16[4,512,128]{2,1,0:T(8,128)(2,1)S(1)} %get-tuple-element.106.refs_4_), channel_id=1, source_target_pairs={{0,28},{4,0},{8,4},{12,8},{16,12},{20,16},{24,20},{28,24},{1,29},{... | collective-permute-start | bytes 1572872 | tf_op jit(solution)/shard_map/vb1_left/ppermute | solution.py:426
  12.9 22.7 %collective-permute-start.5 = (bf16[4,512,128]{2,1,0:T(8,128)(2,1)S(1)}, bf16[4,512,128]{2,1,0:T(8,128)(2,1)}, u32[]{:S(2)}, u32[]{:S(2)}) collective-permute-start(bf16[4,512,128]{2,1,0:T(8,128)(2,1)S(1)} %get-tuple-element.106.refs_4_), channel_id=1, source_target_pairs={{0,4},{4,8},{8,12},{12,16},{16,20},{20,24},{24,28},{28,0},{1,5},{5... | collective-permute-start | bytes 1572872 | tf_op jit(solution)/shard_map/vb1_right/ppermute | solution.py:426
  59.8 88.7 %all-to-all-start = ((bf16[4,512,1024]{2,1,0:T(8,128)(2,1)}), bf16[4,512,1024]{2,1,0:T(8,128)(2,1)}, u32[]{:S(2)}, u32[]{:S(2)}) async-start(bf16[4,512,1024]{2,1,0:T(8,128)(2,1)} %copy-done), calls=%async_computation | async-start | bytes 8388608 | tf_op jit(solution)/shard_map/queries/all_to_all | solution.py:491
  64.9 27.5 %collective-permute-start.11 = (bf16[4,512,128]{2,1,0:T(8,128)(2,1)}, bf16[4,512,128]{2,1,0:T(8,128)(2,1)S(1)}, u32[]{:S(2)}, u32[]{:S(2)}) collective-permute-start(bf16[4,512,128]{2,1,0:T(8,128)(2,1)} %collective-permute-done.2.refs_8_), channel_id=1, source_target_pairs={{0,28},{4,0},{8,4},{12,8},{16,12},{20,16},{24,20},{28,24},{1,29},{... | collective-permute-start | bytes 1572872 | tf_op jit(solution)/shard_map/va2_left/ppermute | solution.py:426
  68.2 24.2 %collective-permute-start.20 = (bf16[4,512,128]{2,1,0:T(8,128)(2,1)}, bf16[4,512,128]{2,1,0:T(8,128)(2,1)S(1)}, u32[]{:S(2)}, u32[]{:S(2)}) collective-permute-start(bf16[4,512,128]{2,1,0:T(8,128)(2,1)} %collective-permute-done.3.refs_7_), channel_id=1, source_target_pairs={{0,4},{4,8},{8,12},{12,16},{16,20},{20,24},{24,28},{28,0},{1,5},{5... | collective-permute-start | bytes 1572872 | tf_op jit(solution)/shard_map/va2_right/ppermute | solution.py:426
  68.2 20.3 %collective-permute-start.9 = (bf16[4,512,128]{2,1,0:T(8,128)(2,1)S(1)}, bf16[4,512,128]{2,1,0:T(8,128)(2,1)S(1)}, u32[]{:S(2)}, u32[]{:S(2)}) collective-permute-start(bf16[4,512,128]{2,1,0:T(8,128)(2,1)S(1)} %copy-done.6), channel_id=1, source_target_pairs={{0,28},{4,0},{8,4},{12,8},{16,12},{20,16},{24,20},{28,24},{1,29},{... | collective-permute-start | bytes 1572872 | tf_op jit(solution)/shard_map/ka1_left/ppermute | solution.py:426
  81.0 22.5 %collective-permute-start.19 = (bf16[4,512,128]{2,1,0:T(8,128)(2,1)S(1)}, bf16[4,512,128]{2,1,0:T(8,128)(2,1)S(1)}, u32[]{:S(2)}, u32[]{:S(2)}) collective-permute-start(bf16[4,512,128]{2,1,0:T(8,128)(2,1)S(1)} %collective-permute-done.18.refs_2_), channel_id=1, source_target_pairs={{0,4},{4,8},{8,12},{12,16},{16,20},{20,24},{24,28},{28,0},{1,5},{5... | collective-permute-start | bytes 1572872 | tf_op jit(solution)/shard_map/ka2_right/ppermute | solution.py:426
  92.4 18.5 %collective-permute-start.12 = (bf16[4,512,128]{2,1,0:T(8,128)(2,1)S(1)}, bf16[4,512,128]{2,1,0:T(8,128)(2,1)S(1)}, u32[]{:S(2)}, u32[]{:S(2)}) collective-permute-start(bf16[4,512,128]{2,1,0:T(8,128)(2,1)S(1)} %collective-permute-done.11.refs_10_), channel_id=1, source_target_pairs={{0,28},{4,0},{8,4},{12,8},{16,12},{20,16},{24,20},{28,24},{1,29},{... | collective-permute-start | bytes 1572872 | tf_op jit(solution)/shard_map/va3_left/ppermute | solution.py:426
  92.4 22.4 %collective-permute-start.22 = (bf16[4,512,128]{2,1,0:T(8,128)(2,1)S(1)}, bf16[4,512,128]{2,1,0:T(8,128)(2,1)}, u32[]{:S(2)}, u32[]{:S(2)}) collective-permute-start(bf16[4,512,128]{2,1,0:T(8,128)(2,1)S(1)} %collective-permute-done.20.refs_9_), channel_id=1, source_target_pairs={{0,4},{4,8},{8,12},{12,16},{16,20},{20,24},{24,28},{28,0},{1,5},{5... | collective-permute-start | bytes 1572872 | tf_op jit(solution)/shard_map/va3_right/ppermute | solution.py:426
  103.5 22.6 %collective-permute-start.21 = (bf16[4,512,128]{2,1,0:T(8,128)(2,1)S(1)}, bf16[4,512,128]{2,1,0:T(8,128)(2,1)}, u32[]{:S(2)}, u32[]{:S(2)}) collective-permute-start(bf16[4,512,128]{2,1,0:T(8,128)(2,1)S(1)} %collective-permute-done.19.refs_4_), channel_id=1, source_target_pairs={{0,4},{4,8},{8,12},{12,16},{16,20},{20,24},{24,28},{28,0},{1,5},{5... | collective-permute-start | bytes 1572872 | tf_op jit(solution)/shard_map/ka3_right/ppermute | solution.py:426
  114.8 19.9 %collective-permute-start.14 = (bf16[4,512,128]{2,1,0:T(8,128)(2,1)}, bf16[4,512,128]{2,1,0:T(8,128)(2,1)}, u32[]{:S(2)}, u32[]{:S(2)}) collective-permute-start(bf16[4,512,128]{2,1,0:T(8,128)(2,1)} %collective-permute-done.10.refs_5_), channel_id=1, source_target_pairs={{0,28},{4,0},{8,4},{12,8},{16,12},{20,16},{24,20},{28,24},{1,29},{... | collective-permute-start | bytes 1572872 | tf_op jit(solution)/shard_map/ka3_left/ppermute | solution.py:426
  114.8 23.1 %collective-permute-start.24 = (bf16[4,512,128]{2,1,0:T(8,128)(2,1)}, bf16[4,512,128]{2,1,0:T(8,128)(2,1)}, u32[]{:S(2)}, u32[]{:S(2)}) collective-permute-start(bf16[4,512,128]{2,1,0:T(8,128)(2,1)} %collective-permute-done.22.refs_4_), channel_id=1, source_target_pairs={{0,4},{4,8},{8,12},{12,16},{16,20},{20,24},{24,28},{28,0},{1,5},{5... | collective-permute-start | bytes 1572872 | tf_op jit(solution)/shard_map/va4_right/ppermute | solution.py:426
  126.0 22.5 %collective-permute-start.23 = (bf16[4,512,128]{2,1,0:T(8,128)(2,1)}, bf16[4,512,128]{2,1,0:T(8,128)(2,1)}, u32[]{:S(2)}, u32[]{:S(2)}) collective-permute-start(bf16[4,512,128]{2,1,0:T(8,128)(2,1)} %collective-permute-done.21.refs_1_), channel_id=1, source_target_pairs={{0,4},{4,8},{8,12},{12,16},{16,20},{20,24},{24,28},{28,0},{1,5},{5... | collective-permute-start | bytes 1572872 | tf_op jit(solution)/shard_map/ka4_right/ppermute | solution.py:426
  134.7 49.7 %collective-permute-start.15 = (bf16[4,512,128]{2,1,0:T(8,128)(2,1)}, bf16[4,512,128]{2,1,0:T(8,128)(2,1)}, u32[]{:S(2)}, u32[]{:S(2)}) collective-permute-start(bf16[4,512,128]{2,1,0:T(8,128)(2,1)} %collective-permute-done.13.refs_3_), channel_id=1, source_target_pairs={{0,28},{4,0},{8,4},{12,8},{16,12},{20,16},{24,20},{28,24},{1,29},{... | collective-permute-start | bytes 1572872 | tf_op jit(solution)/shard_map/kb2_left/ppermute | solution.py:426
  137.9 46.4 %collective-permute-start.16 = (bf16[4,512,128]{2,1,0:T(8,128)(2,1)}, bf16[4,512,128]{2,1,0:T(8,128)(2,1)}, u32[]{:S(2)}, u32[]{:S(2)}) collective-permute-start(bf16[4,512,128]{2,1,0:T(8,128)(2,1)} %collective-permute-done.4.refs_6_), channel_id=1, source_target_pairs={{0,28},{4,0},{8,4},{12,8},{16,12},{20,16},{24,20},{28,24},{1,29},{... | collective-permute-start | bytes 1572872 | tf_op jit(solution)/shard_map/vb2_left/ppermute | solution.py:426
  138.0 51.0 %collective-permute-start.27 = (bf16[4,512,128]{2,1,0:T(8,128)(2,1)S(1)}, bf16[4,512,128]{2,1,0:T(8,128)(2,1)}, u32[]{:S(2)}, u32[]{:S(2)}) collective-permute-start(bf16[4,512,128]{2,1,0:T(8,128)(2,1)S(1)} %copy-done.4), channel_id=1, source_target_pairs={{0,4},{4,8},{8,12},{12,16},{16,20},{20,24},{24,28},{28,0},{1,5},{5... | collective-permute-start | bytes 1572872 | tf_op jit(solution)/shard_map/kb1_right/ppermute | solution.py:426
  148.5 40.4 %collective-permute-start.30 = (bf16[4,512,128]{2,1,0:T(8,128)(2,1)}, bf16[4,512,128]{2,1,0:T(8,128)(2,1)}, u32[]{:S(2)}, u32[]{:S(2)}) collective-permute-start(bf16[4,512,128]{2,1,0:T(8,128)(2,1)} %collective-permute-done.5.refs_5_), channel_id=1, source_target_pairs={{0,4},{4,8},{8,12},{12,16},{16,20},{20,24},{24,28},{28,0},{1,5},{5... | collective-permute-start | bytes 1572872 | tf_op jit(solution)/shard_map/vb2_right/ppermute | solution.py:426
  179.8 34.4 %all-to-all-start.1 = ((bf16[4,4,560,128]{3,2,1,0:T(8,128)(2,1)}), bf16[4,4,560,128]{3,2,1,0:T(8,128)(2,1)}, u32[]{:S(2)}, u32[]{:S(2)}) async-start(bf16[4,4,560,128]{3,2,1,0:T(8,128)(2,1)} %get-tuple-element.88), calls=%async_computation.1 | async-start | bytes 4587520 | tf_op jit(solution)/shard_map/partials_a/all_to_all | solution.py:553
  184.4 26.5 %collective-permute-start.17 = (bf16[4,512,128]{2,1,0:T(8,128)(2,1)}, bf16[4,512,128]{2,1,0:T(8,128)(2,1)S(1)}, u32[]{:S(2)}, u32[]{:S(2)}) collective-permute-start(bf16[4,512,128]{2,1,0:T(8,128)(2,1)} %collective-permute-done.15.refs_2_), channel_id=1, source_target_pairs={{0,28},{4,0},{8,4},{12,8},{16,12},{20,16},{24,20},{28,24},{1,29},{... | collective-permute-start | bytes 1572872 | tf_op jit(solution)/shard_map/kb3_left/ppermute | solution.py:426
  188.9 25.3 %collective-permute-start.32 = (bf16[4,512,128]{2,1,0:T(8,128)(2,1)}, bf16[4,512,128]{2,1,0:T(8,128)(2,1)}, u32[]{:S(2)}, u32[]{:S(2)}) collective-permute-start(bf16[4,512,128]{2,1,0:T(8,128)(2,1)} %collective-permute-done.30.refs_5_), channel_id=1, source_target_pairs={{0,4},{4,8},{8,12},{12,16},{16,20},{20,24},{24,28},{28,0},{1,5},{5... | collective-permute-start | bytes 1572872 | tf_op jit(solution)/shard_map/vb3_right/ppermute | solution.py:426
  188.9 21.9 %collective-permute-start.25 = (bf16[4,512,128]{2,1,0:T(8,128)(2,1)}, bf16[4,512,128]{2,1,0:T(8,128)(2,1)S(1)}, u32[]{:S(2)}, u32[]{:S(2)}) collective-permute-start(bf16[4,512,128]{2,1,0:T(8,128)(2,1)} %collective-permute-done.16.refs_6_), channel_id=1, source_target_pairs={{0,28},{4,0},{8,4},{12,8},{16,12},{20,16},{24,20},{28,24},{1,29},{... | collective-permute-start | bytes 1572872 | tf_op jit(solution)/shard_map/vb3_left/ppermute | solution.py:426
  192.2 18.7 %collective-permute-start.29 = (bf16[4,512,128]{2,1,0:T(8,128)(2,1)}, bf16[4,512,128]{2,1,0:T(8,128)(2,1)}, u32[]{:S(2)}, u32[]{:S(2)}) collective-permute-start(bf16[4,512,128]{2,1,0:T(8,128)(2,1)} %collective-permute-done.27.refs_2_), channel_id=1, source_target_pairs={{0,4},{4,8},{8,12},{12,16},{16,20},{20,24},{24,28},{28,0},{1,5},{5... | collective-permute-start | bytes 1572872 | tf_op jit(solution)/shard_map/kb2_right/ppermute | solution.py:426
  210.9 25.0 %collective-permute-start.26 = (bf16[4,512,128]{2,1,0:T(8,128)(2,1)S(1)}, bf16[4,512,128]{2,1,0:T(8,128)(2,1)S(1)}, u32[]{:S(2)}, u32[]{:S(2)}) collective-permute-start(bf16[4,512,128]{2,1,0:T(8,128)(2,1)S(1)} %collective-permute-done.17.refs_4_), channel_id=1, source_target_pairs={{0,28},{4,0},{8,4},{12,8},{16,12},{20,16},{24,20},{28,24},{1,29},{... | collective-permute-start | bytes 1572872 | tf_op jit(solution)/shard_map/kb4_left/ppermute | solution.py:426
  214.1 21.8 %collective-permute-start.28 = (bf16[4,512,128]{2,1,0:T(8,128)(2,1)S(1)}, bf16[4,512,128]{2,1,0:T(8,128)(2,1)S(1)}, u32[]{:S(2)}, u32[]{:S(2)}) collective-permute-start(bf16[4,512,128]{2,1,0:T(8,128)(2,1)S(1)} %collective-permute-done.25.refs_8_), channel_id=1, source_target_pairs={{0,28},{4,0},{8,4},{12,8},{16,12},{20,16},{24,20},{28,24},{1,29},{... | collective-permute-start | bytes 1572872 | tf_op jit(solution)/shard_map/vb4_left/ppermute | solution.py:426
  (35 other events, 376.3 us)

commit v6 on v5

--- a/solution.py
+++ b/solution.py
@@ -465,9 +465,8 @@
     value_tiles = value_states.reshape(4, BLOCK, -1).transpose(0, 2, 1)
     va, vb = {0: value_tiles[:, : 4 * HEAD]}, {0: value_tiles[:, 4 * HEAD :]}
     right, left = Wire("right", 1), Wire("left", -1)
-    for name, ring in (("va", va), ("vb", vb)):
-        for wire in (right, left):
-            wire.send(name, ring, 1)
+    for wire in (right, left):
+        wire.send("va", va, 1)
     picks = selected_blocks.T.astype(jnp.float32)
     with jax.named_scope("prefix"):
         rows_before = before
@@ -478,7 +477,7 @@
             rows_before = rows_before + jnp.where((my_y & bit) != 0, other[:, :1], 0.0)
             total = total + other[:, :1]
             picks = jnp.concatenate([picks, other[:, 2:]], axis=1)
-        own_total = after(own_total, va[1], va[-1], vb[1], vb[-1])
+        own_total = after(own_total, va[1], va[-1])
         for bit in (1, 2, 4):
             other = swap(jnp.concatenate([own_total, rows_before], axis=1), "z", bit)
             before = before + jnp.where((my_z & bit) != 0, other[:, :1], 0.0)
@@ -522,6 +521,8 @@
     def pick(rows, step):
         return lax.dynamic_index_in_dim(rows, (my_y + step) & 3, 0, keepdims=False)
 
+    for wire in (right, left):
+        wire.send("vb", vb, 1, own_total)
     for name, ring, distance in (
         ("ka", ka, 1),
         ("va", va, 2),
@@ -532,22 +533,22 @@
         for wire in (right, left):
             wire.send(name, ring, distance)
     right.send("va", va, 4)
-    right.send("ka", ka, 4)
     left.send("kb", kb, 1)
-    state = call(0, GROUPS[0][0], None, False)
     right.send("kb", kb, 1)
     left.send("vb", vb, 2)
-    right.send("vb", vb, 2)
-    left.send("kb", kb, 2)
+    state = call(0, GROUPS[0][0], None, False)
+    right.send("ka", ka, 4, state[1])
+    left.send("kb", kb, 2, state[1])
+    right.send("vb", vb, 2, state[1])
+    left.send("vb", vb, 3, state[1])
     state = call(0, GROUPS[0][1], state, True)
     right.send("kb", kb, 2, state[1])
-    left.send("vb", vb, 3, state[1])
-    right.send("vb", vb, 3)
-    left.send("kb", kb, 3)
+    left.send("kb", kb, 3, state[1])
+    right.send("vb", vb, 3, state[1])
+    left.send("vb", vb, 4, state[1])
     first_b = call(1, GROUPS[1][0], None, False)
     right.send("kb", kb, 3, first_b[1])
-    left.send("vb", vb, 4, first_b[1])
-    left.send("kb", kb, 4)
+    left.send("kb", kb, 4, first_b[1])
     mine_a = state[:3]
     with jax.named_scope("partials_a"):
         parts_a = lax.all_to_all(state[3], "y", 0, 0, tiled=True)

time: 265 us -> 248 us (0.936)
  waiting for transfers between devices: 107 us -> 93.5 us
  local copies, waits for them, and re-layouts: 21.7 us -> 15.5 us
    ppermute x28, waiting for transfers between devices: 81.8 us -> 69.3 us  [shift(): lax.ppermute(value, axis, [(i, (i + step) % size) for i in range(size)])]
    unnamed x42 -> x26, local copies, waits for them, and re-layouts: 15.9 us -> 9.65 us
  transfers between devices with their start and end apart: 38 -> 38, of which waited for: 19 -> 18; matrix products, arithmetic and copies ran while one was open for 1% -> 2% of each run, Pallas kernels for 21% -> 23%
where the time goes in v6:
time: 248 us; the launch traced here: 246 us
  waiting for transfers between devices  93.5 us (38%)
  Pallas kernels  70.8 us (29%)
  starting transfers between devices  64.5 us (26%)
  local copies, waits for them, and re-layouts  15.5 us (6%)
    ppermute x28, waiting for transfers between devices, shift(): lax.ppermute(value, axis, [(i, (i + step) % size) for i in range(size)])  69.3 us
    pallas_call x5, Pallas kernels, attend(): pl.pallas_call(functools.partial(attend_kernel, offsets, heads, first, la...  60.5 us
    ppermute x28, starting transfers between devices, shift(): lax.ppermute(value, axis, [(i, (i + step) % size) for i in range(size)])  43.4 us
    ppermute x5, waiting for transfers between devices, swap(): return lax.ppermute(value, axis, [(i, i ^ bit) for i in range(size)])  16.1 us
    unnamed x26, local copies, waits for them, and re-layouts  9.65 us
    ppermute x3, waiting for transfers between devices, to_row(): return lax.ppermute(value, 'y', moves)  8.05 us
    ppermute x5, starting transfers between devices, swap(): return lax.ppermute(value, axis, [(i, i ^ bit) for i in range(size)])  6.91 us
    pallas_call x2, Pallas kernels, join(): pl.pallas_call(functools.partial(join_kernel, heads), out_shape=jax.Shape...  5.47 us
  transfers between devices with their start and end apart: 38, of which 18 were waited for; matrix products, arithmetic and copies ran while one was open for 2% of the time, Pallas kernels for 23%

profile of v6, /device:TPU:2, one launch (start us, length us, event | category | flops | bytes accessed | tf_op | source)
XLA Modules:
  0.0 246.5 jit_solution(11644567149179410586)
XLA Ops:
  3.7 5.9 %collective-permute-start.2 = (bf16[4,512,128]{2,1,0:T(8,128)(2,1)S(1)}, bf16[4,512,128]{2,1,0:T(8,128)(2,1)}, u32[]{:S(2)}, u32[]{:S(2)}) collective-permute-start(bf16[4,512,128]{2,1,0:T(8,128)(2,1)S(1)} %get-tuple-element.107.refs_6_), channel_id=1, source_target_pairs={{0,28},{4,0},{8,4},{12,8},{16,12},{20,16},{24,20},{28,24},{1,29},{... | collective-permute-start | bytes 1572872 | tf_op jit(solution)/shard_map/va1_left/ppermute | solution.py:426
  13.5 3.3 %collective-permute-start.1 = (f32[8,10]{0,1:T(8,128)S(1)}, f32[8,10]{0,1:T(8,128)S(1)}, u32[]{:S(2)}, u32[]{:S(2)}) collective-permute-start(f32[8,10]{0,1:T(8,128)S(1)} %pad_maximum_fusion), channel_id=1, source_target_pairs={{0,64},{32,96},{64,0},{96,32},{1,65},{33,97},{65,1},{97,33},{2,66}... | collective-permute-start | bytes 968 | tf_op jit(solution)/shard_map/prefix/ppermute | solution.py:436
  20.8 3.5 %collective-permute-done.3.refs_7_ = bf16[4,512,128]{2,1,0:T(8,128)(2,1)} collective-permute-done((bf16[4,512,128]{2,1,0:T(8,128)(2,1)S(1)}, bf16[4,512,128]{2,1,0:T(8,128)(2,1)}, u32[]{:S(2)}, u32[]{:S(2)}) %collective-permute-start.3) | collective-permute-done | bytes 524320 | tf_op jit(solution)/shard_map/va1_right/ppermute | solution.py:426
  24.5 3.5 %collective-permute-done.4 = f32[8,2]{0,1:T(2,128)S(1)} collective-permute-done((f32[8,2]{0,1:T(2,128)S(1)}, f32[8,2]{0,1:T(2,128)S(1)}, u32[]{:S(2)}, u32[]{:S(2)}) %collective-permute-start.4) | collective-permute-done | bytes 96 | tf_op jit(solution)/shard_map/prefix/ppermute | solution.py:436
  28.1 4.4 %collective-permute-done.5 = f32[8,2]{0,1:T(2,128)S(1)} collective-permute-done((f32[8,2]{0,1:T(2,128)S(1)}, f32[8,2]{0,1:T(2,128)S(1)}, u32[]{:S(2)}, u32[]{:S(2)}) %collective-permute-start.5) | collective-permute-done | bytes 96 | tf_op jit(solution)/shard_map/prefix/ppermute | solution.py:436
  34.4 5.8 %collective-permute-done.6 = f32[8,2]{0,1:T(2,128)S(1)} collective-permute-done((f32[8,2]{0,1:T(2,128)S(1)}, f32[8,2]{0,1:T(2,128)S(1)}, u32[]{:S(2)}, u32[]{:S(2)}) %collective-permute-start.6) | collective-permute-done | bytes 96 | tf_op jit(solution)/shard_map/prefix/ppermute | solution.py:436
  40.2 4.8 %rotate.1 = (bf16[4,512,1024]{2,1,0:T(8,128)(2,1)S(1)}, bf16[4,512,128]{2,1,0:T(8,128)(2,1)S(1)}, bf16[4,512,128]{2,1,0:T(8,128)(2,1)S(1)}) custom-call(f32[512,8]{1,0:T(8,128)S(1)} %bitcast.26, f32[1,128]{1,0:T(1,128)S(1)} %maximum_bitcast_fusion.freq_ref, bf16[512,1024]{1,0:T(8,128)(2,1)S(1)} %copy-done.1, bf16[512,1024]{1,0:T(8,128)(2,1)S(1)} %copy-done.2), custom_call_target="tpu_custom_call" | custom-call | flops 5000000000 | bytes 6291456 | tf_op jit(solution)/shard_map/rotate/pallas_call | solution.py:83
  48.6 5.0 %all-to-all-start = ((bf16[4,512,1024]{2,1,0:T(8,128)(2,1)}), bf16[4,512,1024]{2,1,0:T(8,128)(2,1)}, u32[]{:S(2)}, u32[]{:S(2)}) async-start(bf16[4,512,1024]{2,1,0:T(8,128)(2,1)} %copy-done), calls=%async_computation | async-start | bytes 8388608 | tf_op jit(solution)/shard_map/queries/all_to_all | solution.py:490
  55.8 10.0 %collective-permute-done.14.refs_5_ = bf16[4,512,128]{2,1,0:T(8,128)(2,1)S(1)} collective-permute-done((bf16[4,512,128]{2,1,0:T(8,128)(2,1)S(1)}, bf16[4,512,128]{2,1,0:T(8,128)(2,1)S(1)}, u32[]{:S(2)}, u32[]{:S(2)}) %collective-permute-start.14) | collective-permute-done | bytes 524320 | tf_op jit(solution)/shard_map/vb1_right/ppermute | solution.py:426
  72.5 10.3 %collective-permute-done.7.refs_3_ = bf16[4,512,128]{2,1,0:T(8,128)(2,1)} collective-permute-done((bf16[4,512,128]{2,1,0:T(8,128)(2,1)S(1)}, bf16[4,512,128]{2,1,0:T(8,128)(2,1)}, u32[]{:S(2)}, u32[]{:S(2)}) %collective-permute-start.7) | collective-permute-done | bytes 524320 | tf_op jit(solution)/shard_map/ka1_left/ppermute | solution.py:426
  85.2 3.9 %collective-permute-done.13.refs_2_ = bf16[4,512,128]{2,1,0:T(8,128)(2,1)} collective-permute-done((bf16[4,512,128]{2,1,0:T(8,128)(2,1)S(1)}, bf16[4,512,128]{2,1,0:T(8,128)(2,1)}, u32[]{:S(2)}, u32[]{:S(2)}) %collective-permute-start.13) | collective-permute-done | bytes 524320 | tf_op jit(solution)/shard_map/ka1_right/ppermute | solution.py:426
  96.5 8.8 %collective-permute-done.9.refs_5_ = bf16[4,512,128]{2,1,0:T(8,128)(2,1)} collective-permute-done((bf16[4,512,128]{2,1,0:T(8,128)(2,1)}, bf16[4,512,128]{2,1,0:T(8,128)(2,1)}, u32[]{:S(2)}, u32[]{:S(2)}) %collective-permute-start.9) | collective-permute-done | bytes 524320 | tf_op jit(solution)/shard_map/ka2_left/ppermute | solution.py:426
  107.7 9.0 %collective-permute-done.20.refs_4_ = bf16[4,512,128]{2,1,0:T(8,128)(2,1)} collective-permute-done((bf16[4,512,128]{2,1,0:T(8,128)(2,1)S(1)}, bf16[4,512,128]{2,1,0:T(8,128)(2,1)}, u32[]{:S(2)}, u32[]{:S(2)}) %collective-permute-start.20) | collective-permute-done | bytes 524320 | tf_op jit(solution)/shard_map/va3_right/ppermute | solution.py:426
  117.5 18.2 %attend_0_0_7_1_6_2.1 = (f32[16,512,128]{2,1,0:T(8,128)S(1)}, f32[16,8,128]{2,1,0:T(8,128)S(1)}, f32[16,8,128]{2,1,0:T(8,128)S(1)}) custom-call(s32[129]{0:T(256)S(1)} %pad_add_fusion.meta, bf16[4,512,1024]{2,1,0:T(8,128)(2,1)} %all-to-all-done.refs_0_, bf16[4,512,128]{2,1,0:T(8,128)(2,1)S(1)} %copy-done.6, ...), custom_call_target="tpu_custom_call" | custom-call | flops 18699999232 | bytes 1048576 | tf_op jit(solution)/shard_map/attend_0_0_7_1_6_2/pallas_call | solution.py:350
  141.2 7.5 %collective-permute-done.22.refs_3_ = bf16[4,512,128]{2,1,0:T(8,128)(2,1)S(1)} collective-permute-done((bf16[4,512,128]{2,1,0:T(8,128)(2,1)}, bf16[4,512,128]{2,1,0:T(8,128)(2,1)S(1)}, u32[]{:S(2)}, u32[]{:S(2)}) %collective-permute-start.22) | collective-permute-done | bytes 524320 | tf_op jit(solution)/shard_map/ka4_right/ppermute | solution.py:426
  148.6 10.0 %attend_0_5_3_4.1 = (f32[4,512,128]{2,1,0:T(8,128)S(1)}, f32[4,8,128]{2,1,0:T(8,128)S(1)}, f32[4,8,128]{2,1,0:T(8,128)S(1)}, bf16[4,4,560,128]{3,2,1,0:T(8,128)(2,1)}) custom-call(s32[129]{0:T(256)S(1)} %pad_add_fusion.meta, bf16[4,512,1024]{2,1,0:T(8,128)(2,1)} %all-to-all-done.refs_0_, bf16[4,512,128]{2,1,0:T(8,128)(2,1)} %collective-permute-done.19.refs_1_, ...), custom_call_target="tpu_custom_call" | custom-call | flops 12099999744 | bytes 1048576 | tf_op jit(solution)/shard_map/attend_0_5_3_4/pallas_call | solution.py:350
  158.6 4.5 %all-to-all-start.1 = ((bf16[4,4,560,128]{3,2,1,0:T(8,128)(2,1)}), bf16[4,4,560,128]{3,2,1,0:T(8,128)(2,1)}, u32[]{:S(2)}, u32[]{:S(2)}) async-start(bf16[4,4,560,128]{3,2,1,0:T(8,128)(2,1)} %get-tuple-element.88), calls=%async_computation.1 | async-start | bytes 4587520 | tf_op jit(solution)/shard_map/partials_a/all_to_all | solution.py:554
  167.5 12.8 %attend_4_0_7_1.1 = (f32[16,512,128]{2,1,0:T(8,128)S(1)}, f32[16,8,128]{2,1,0:T(8,128)S(1)}, f32[16,8,128]{2,1,0:T(8,128)S(1)}) custom-call(s32[129]{0:T(256)S(1)} %pad_add_fusion.meta, bf16[4,512,1024]{2,1,0:T(8,128)(2,1)} %all-to-all-done.refs_0_, bf16[4,512,128]{2,1,0:T(8,128)(2,1)S(1)} %copy-done.4, ...), custom_call_target="tpu_custom_call" | custom-call | flops 12099999744 | bytes 1048576 | tf_op jit(solution)/shard_map/attend_4_0_7_1/pallas_call | solution.py:350
  189.8 8.8 %collective-permute-done.24.refs_4_ = bf16[4,512,128]{2,1,0:T(8,128)(2,1)S(1)} collective-permute-done((bf16[4,512,128]{2,1,0:T(8,128)(2,1)S(1)}, bf16[4,512,128]{2,1,0:T(8,128)(2,1)S(1)}, u32[]{:S(2)}, u32[]{:S(2)}) %collective-permute-start.24) | collective-permute-done | bytes 524320 | tf_op jit(solution)/shard_map/kb3_left/ppermute | solution.py:426
  200.8 3.1 %collective-permute-done.31.refs_3_ = bf16[4,512,128]{2,1,0:T(8,128)(2,1)} collective-permute-done((bf16[4,512,128]{2,1,0:T(8,128)(2,1)}, bf16[4,512,128]{2,1,0:T(8,128)(2,1)}, u32[]{:S(2)}, u32[]{:S(2)}) %collective-permute-start.31) | collective-permute-done | bytes 524320 | tf_op jit(solution)/shard_map/kb3_right/ppermute | solution.py:426
  207.1 12.9 %attend_4_6_2_5_3.1 = (f32[16,512,128]{2,1,0:T(8,128)S(1)}, f32[16,8,128]{2,1,0:T(8,128)S(1)}, f32[16,8,128]{2,1,0:T(8,128)S(1)}) custom-call(s32[129]{0:T(256)S(1)} %pad_add_fusion.meta, bf16[4,512,1024]{2,1,0:T(8,128)(2,1)} %all-to-all-done.refs_0_, bf16[4,512,128]{2,1,0:T(8,128)(2,1)} %collective-permute-done.29.refs_1_, ...), custom_call_target="tpu_custom_call" | custom-call | flops 15399999488 | bytes 1048576 | tf_op jit(solution)/shard_map/attend_4_6_2_5_3/pallas_call | solution.py:350
  220.0 6.6 %attend_4_4.1 = (f32[4,512,128]{2,1,0:T(8,128)S(1)}, f32[4,8,128]{2,1,0:T(8,128)S(1)}, f32[4,8,128]{2,1,0:T(8,128)S(1)}, bf16[4,560,128]{2,1,0:T(8,128)(2,1)}, b...) custom-call(s32[129]{0:T(256)S(1)} %pad_add_fusion.meta, bf16[4,512,1024]{2,1,0:T(8,128)(2,1)} %all-to-all-done.refs_0_, ...), custom_call_target="tpu_custom_call" | custom-call | flops 5500000256 | bytes 1048576 | tf_op jit(solution)/shard_map/attend_4_4/pallas_call | solution.py:350
  236.8 6.1 %collective-permute-done.34.two = bf16[4,560,128]{2,1,0:T(8,128)(2,1)S(1)} collective-permute-done((bf16[4,560,128]{2,1,0:T(8,128)(2,1)}, bf16[4,560,128]{2,1,0:T(8,128)(2,1)S(1)}, u32[]{:S(2)}, u32[]{:S(2)}) %collective-permute-start.34) | collective-permute-done | bytes 573472 | tf_op jit(solution)/shard_map/partial_b2/ppermute | solution.py:431
  243.0 3.5 %join_4.1 = bf16[512,1024]{1,0:T(8,128)(2,1)} custom-call(f32[4,512,128]{2,1,0:T(8,128)S(1)} %get-tuple-element.94.acc_ref, f32[4,8,128]{2,1,0:T(8,128)S(1)} %get-tuple-element.95.m_ref, f32[4,8,128]{2,1,0:T(8,128)S(1)} %get-tuple-element.96.l_ref, bf16[4,560,128]{2,1,0:T(8,128)(2,1)S(1)} %collective-permute-done.33.one, ...), custom_call_target="tpu_custom_call", output_to_operand_aliasing={{}: (6, {})} | custom-call | flops 2621440 | bytes 3670016 | tf_op jit(solution)/shard_map/join_4/pallas_call | solution.py:409
  (131 shorter events, 73.8 us)
Async XLA Ops:
  3.7 17.1 %collective-permute-start.2 = (bf16[4,512,128]{2,1,0:T(8,128)(2,1)S(1)}, bf16[4,512,128]{2,1,0:T(8,128)(2,1)}, u32[]{:S(2)}, u32[]{:S(2)}) collective-permute-start(bf16[4,512,128]{2,1,0:T(8,128)(2,1)S(1)} %get-tuple-element.107.refs_6_), channel_id=1, source_target_pairs={{0,28},{4,0},{8,4},{12,8},{16,12},{20,16},{24,20},{28,24},{1,29},{... | collective-permute-start | bytes 1572872 | tf_op jit(solution)/shard_map/va1_left/ppermute | solution.py:426
  48.6 68.9 %all-to-all-start = ((bf16[4,512,1024]{2,1,0:T(8,128)(2,1)}), bf16[4,512,1024]{2,1,0:T(8,128)(2,1)}, u32[]{:S(2)}, u32[]{:S(2)}) async-start(bf16[4,512,1024]{2,1,0:T(8,128)(2,1)} %copy-done), calls=%async_computation | async-start | bytes 8388608 | tf_op jit(solution)/shard_map/queries/all_to_all | solution.py:490
  53.6 16.3 %collective-permute-start.8 = (bf16[4,512,128]{2,1,0:T(8,128)(2,1)S(1)}, bf16[4,512,128]{2,1,0:T(8,128)(2,1)}, u32[]{:S(2)}, u32[]{:S(2)}) collective-permute-start(bf16[4,512,128]{2,1,0:T(8,128)(2,1)S(1)} %get-tuple-element.106.refs_4_), channel_id=1, source_target_pairs={{0,28},{4,0},{8,4},{12,8},{16,12},{20,16},{24,20},{28,24},{1,29},{... | collective-permute-start | bytes 1572872 | tf_op jit(solution)/shard_map/vb1_left/ppermute | solution.py:426
  65.8 25.3 %collective-permute-start.16 = (bf16[4,512,128]{2,1,0:T(8,128)(2,1)}, bf16[4,512,128]{2,1,0:T(8,128)(2,1)S(1)}, u32[]{:S(2)}, u32[]{:S(2)}) collective-permute-start(bf16[4,512,128]{2,1,0:T(8,128)(2,1)} %collective-permute-done.3.refs_7_), channel_id=1, source_target_pairs={{0,4},{4,8},{8,12},{12,16},{16,20},{20,24},{24,28},{28,0},{1,5},{5... | collective-permute-start | bytes 1572872 | tf_op jit(solution)/shard_map/va2_right/ppermute | solution.py:426
  69.0 20.1 %collective-permute-start.13 = (bf16[4,512,128]{2,1,0:T(8,128)(2,1)S(1)}, bf16[4,512,128]{2,1,0:T(8,128)(2,1)}, u32[]{:S(2)}, u32[]{:S(2)}) collective-permute-start(bf16[4,512,128]{2,1,0:T(8,128)(2,1)S(1)} %copy-done.6), channel_id=1, source_target_pairs={{0,4},{4,8},{8,12},{12,16},{16,20},{20,24},{24,28},{28,0},{1,5},{5... | collective-permute-start | bytes 1572872 | tf_op jit(solution)/shard_map/ka1_right/ppermute | solution.py:426
  70.0 24.0 %collective-permute-start.10 = (bf16[4,512,128]{2,1,0:T(8,128)(2,1)}, bf16[4,512,128]{2,1,0:T(8,128)(2,1)}, u32[]{:S(2)}, u32[]{:S(2)}) collective-permute-start(bf16[4,512,128]{2,1,0:T(8,128)(2,1)} %collective-permute-done.2.refs_8_), channel_id=1, source_target_pairs={{0,28},{4,0},{8,4},{12,8},{16,12},{20,16},{24,20},{28,24},{1,29},{... | collective-permute-start | bytes 1572872 | tf_op jit(solution)/shard_map/va2_left/ppermute | solution.py:426
  82.8 22.5 %collective-permute-start.9 = (bf16[4,512,128]{2,1,0:T(8,128)(2,1)}, bf16[4,512,128]{2,1,0:T(8,128)(2,1)}, u32[]{:S(2)}, u32[]{:S(2)}) collective-permute-start(bf16[4,512,128]{2,1,0:T(8,128)(2,1)} %collective-permute-done.7.refs_3_), channel_id=1, source_target_pairs={{0,28},{4,0},{8,4},{12,8},{16,12},{20,16},{24,20},{28,24},{1,29},{... | collective-permute-start | bytes 1572872 | tf_op jit(solution)/shard_map/ka2_left/ppermute | solution.py:426
  89.1 18.6 %collective-permute-start.15 = (bf16[4,512,128]{2,1,0:T(8,128)(2,1)}, bf16[4,512,128]{2,1,0:T(8,128)(2,1)}, u32[]{:S(2)}, u32[]{:S(2)}) collective-permute-start(bf16[4,512,128]{2,1,0:T(8,128)(2,1)} %collective-permute-done.13.refs_2_), channel_id=1, source_target_pairs={{0,4},{4,8},{8,12},{12,16},{16,20},{20,24},{24,28},{28,0},{1,5},{5... | collective-permute-start | bytes 1572872 | tf_op jit(solution)/shard_map/ka2_right/ppermute | solution.py:426
  91.1 25.6 %collective-permute-start.20 = (bf16[4,512,128]{2,1,0:T(8,128)(2,1)S(1)}, bf16[4,512,128]{2,1,0:T(8,128)(2,1)}, u32[]{:S(2)}, u32[]{:S(2)}) collective-permute-start(bf16[4,512,128]{2,1,0:T(8,128)(2,1)S(1)} %collective-permute-done.16.refs_9_), channel_id=1, source_target_pairs={{0,4},{4,8},{8,12},{12,16},{16,20},{20,24},{24,28},{28,0},{1,5},{5... | collective-permute-start | bytes 1572872 | tf_op jit(solution)/shard_map/va3_right/ppermute | solution.py:426
  94.0 42.9 %collective-permute-start.11 = (bf16[4,512,128]{2,1,0:T(8,128)(2,1)}, bf16[4,512,128]{2,1,0:T(8,128)(2,1)}, u32[]{:S(2)}, u32[]{:S(2)}) collective-permute-start(bf16[4,512,128]{2,1,0:T(8,128)(2,1)} %collective-permute-done.10.refs_10_), channel_id=1, source_target_pairs={{0,28},{4,0},{8,4},{12,8},{16,12},{20,16},{24,20},{28,24},{1,29},{... | collective-permute-start | bytes 1572872 | tf_op jit(solution)/shard_map/va3_left/ppermute | solution.py:426
  105.2 33.9 %collective-permute-start.17 = (bf16[4,512,128]{2,1,0:T(8,128)(2,1)}, bf16[4,512,128]{2,1,0:T(8,128)(2,1)}, u32[]{:S(2)}, u32[]{:S(2)}) collective-permute-start(bf16[4,512,128]{2,1,0:T(8,128)(2,1)} %collective-permute-done.9.refs_5_), channel_id=1, source_target_pairs={{0,28},{4,0},{8,4},{12,8},{16,12},{20,16},{24,20},{28,24},{1,29},{... | collective-permute-start | bytes 1572872 | tf_op jit(solution)/shard_map/ka3_left/ppermute | solution.py:426
  107.7 28.1 %collective-permute-start.19 = (bf16[4,512,128]{2,1,0:T(8,128)(2,1)}, bf16[4,512,128]{2,1,0:T(8,128)(2,1)}, u32[]{:S(2)}, u32[]{:S(2)}) collective-permute-start(bf16[4,512,128]{2,1,0:T(8,128)(2,1)} %collective-permute-done.15.refs_4_), channel_id=1, source_target_pairs={{0,4},{4,8},{8,12},{12,16},{16,20},{20,24},{24,28},{28,0},{1,5},{5... | collective-permute-start | bytes 1572872 | tf_op jit(solution)/shard_map/ka3_right/ppermute | solution.py:426
  116.7 19.0 %collective-permute-start.21 = (bf16[4,512,128]{2,1,0:T(8,128)(2,1)}, bf16[4,512,128]{2,1,0:T(8,128)(2,1)}, u32[]{:S(2)}, u32[]{:S(2)}) collective-permute-start(bf16[4,512,128]{2,1,0:T(8,128)(2,1)} %collective-permute-done.20.refs_4_), channel_id=1, source_target_pairs={{0,4},{4,8},{8,12},{12,16},{16,20},{20,24},{24,28},{28,0},{1,5},{5... | collective-permute-start | bytes 1572872 | tf_op jit(solution)/shard_map/va4_right/ppermute | solution.py:426
  136.9 26.2 %collective-permute-start.12 = (bf16[4,512,128]{2,1,0:T(8,128)(2,1)S(1)}, bf16[4,512,128]{2,1,0:T(8,128)(2,1)}, u32[]{:S(2)}, u32[]{:S(2)}) collective-permute-start(bf16[4,512,128]{2,1,0:T(8,128)(2,1)S(1)} %copy-done.4), channel_id=1, source_target_pairs={{0,28},{4,0},{8,4},{12,8},{16,12},{20,16},{24,20},{28,24},{1,29},{... | collective-permute-start | bytes 1572872 | tf_op jit(solution)/shard_map/kb1_left/ppermute | solution.py:426
  139.1 26.1 %collective-permute-start.23 = (bf16[4,512,128]{2,1,0:T(8,128)(2,1)}, bf16[4,512,128]{2,1,0:T(8,128)(2,1)S(1)}, u32[]{:S(2)}, u32[]{:S(2)}) collective-permute-start(bf16[4,512,128]{2,1,0:T(8,128)(2,1)} %collective-permute-done.8.refs_6_), channel_id=1, source_target_pairs={{0,28},{4,0},{8,4},{12,8},{16,12},{20,16},{24,20},{28,24},{1,29},{... | collective-permute-start | bytes 1572872 | tf_op jit(solution)/shard_map/vb2_left/ppermute | solution.py:426
  140.4 24.9 %collective-permute-start.25 = (bf16[4,512,128]{2,1,0:T(8,128)(2,1)S(1)}, bf16[4,512,128]{2,1,0:T(8,128)(2,1)}, u32[]{:S(2)}, u32[]{:S(2)}) collective-permute-start(bf16[4,512,128]{2,1,0:T(8,128)(2,1)S(1)} %copy-done.4), channel_id=1, source_target_pairs={{0,4},{4,8},{8,12},{12,16},{16,20},{20,24},{24,28},{28,0},{1,5},{5... | collective-permute-start | bytes 1572872 | tf_op jit(solution)/shard_map/kb1_right/ppermute | solution.py:426
  158.6 42.2 %all-to-all-start.1 = ((bf16[4,4,560,128]{3,2,1,0:T(8,128)(2,1)}), bf16[4,4,560,128]{3,2,1,0:T(8,128)(2,1)}, u32[]{:S(2)}, u32[]{:S(2)}) async-start(bf16[4,4,560,128]{3,2,1,0:T(8,128)(2,1)} %get-tuple-element.88), calls=%async_computation.1 | async-start | bytes 4587520 | tf_op jit(solution)/shard_map/partials_a/all_to_all | solution.py:554
  163.2 19.1 %collective-permute-start.18 = (bf16[4,512,128]{2,1,0:T(8,128)(2,1)}, bf16[4,512,128]{2,1,0:T(8,128)(2,1)S(1)}, u32[]{:S(2)}, u32[]{:S(2)}) collective-permute-start(bf16[4,512,128]{2,1,0:T(8,128)(2,1)} %collective-permute-done.12.refs_3_), channel_id=1, source_target_pairs={{0,28},{4,0},{8,4},{12,8},{16,12},{20,16},{24,20},{28,24},{1,29},{... | collective-permute-start | bytes 1572872 | tf_op jit(solution)/shard_map/kb2_left/ppermute | solution.py:426
  165.2 23.4 %collective-permute-start.26 = (bf16[4,512,128]{2,1,0:T(8,128)(2,1)S(1)}, bf16[4,512,128]{2,1,0:T(8,128)(2,1)}, u32[]{:S(2)}, u32[]{:S(2)}) collective-permute-start(bf16[4,512,128]{2,1,0:T(8,128)(2,1)S(1)} %collective-permute-done.23.refs_6_), channel_id=1, source_target_pairs={{0,28},{4,0},{8,4},{12,8},{16,12},{20,16},{24,20},{28,24},{1,29},{... | collective-permute-start | bytes 1572872 | tf_op jit(solution)/shard_map/vb3_left/ppermute | solution.py:426
  165.3 20.2 %collective-permute-start.30 = (bf16[4,512,128]{2,1,0:T(8,128)(2,1)S(1)}, bf16[4,512,128]{2,1,0:T(8,128)(2,1)}, u32[]{:S(2)}, u32[]{:S(2)}) collective-permute-start(bf16[4,512,128]{2,1,0:T(8,128)(2,1)S(1)} %collective-permute-done.14.refs_5_), channel_id=1, source_target_pairs={{0,4},{4,8},{8,12},{12,16},{16,20},{20,24},{24,28},{28,0},{1,5},{5... | collective-permute-start | bytes 1572872 | tf_op jit(solution)/shard_map/vb2_right/ppermute | solution.py:426
  167.2 19.3 %collective-permute-start.29 = (bf16[4,512,128]{2,1,0:T(8,128)(2,1)}, bf16[4,512,128]{2,1,0:T(8,128)(2,1)}, u32[]{:S(2)}, u32[]{:S(2)}) collective-permute-start(bf16[4,512,128]{2,1,0:T(8,128)(2,1)} %collective-permute-done.25.refs_2_), channel_id=1, source_target_pairs={{0,4},{4,8},{8,12},{12,16},{16,20},{20,24},{24,28},{28,0},{1,5},{5... | collective-permute-start | bytes 1572872 | tf_op jit(solution)/shard_map/kb2_right/ppermute | solution.py:426
  186.6 17.3 %collective-permute-start.31 = (bf16[4,512,128]{2,1,0:T(8,128)(2,1)}, bf16[4,512,128]{2,1,0:T(8,128)(2,1)}, u32[]{:S(2)}, u32[]{:S(2)}) collective-permute-start(bf16[4,512,128]{2,1,0:T(8,128)(2,1)} %collective-permute-done.29.refs_1_), channel_id=1, source_target_pairs={{0,4},{4,8},{8,12},{12,16},{16,20},{20,24},{24,28},{28,0},{1,5},{5... | collective-permute-start | bytes 1572872 | tf_op jit(solution)/shard_map/kb3_right/ppermute | solution.py:426
  188.6 31.4 %collective-permute-start.28 = (bf16[4,512,128]{2,1,0:T(8,128)(2,1)}, bf16[4,512,128]{2,1,0:T(8,128)(2,1)S(1)}, u32[]{:S(2)}, u32[]{:S(2)}) collective-permute-start(bf16[4,512,128]{2,1,0:T(8,128)(2,1)} %collective-permute-done.26.refs_8_), channel_id=1, source_target_pairs={{0,28},{4,0},{8,4},{12,8},{16,12},{20,16},{24,20},{28,24},{1,29},{... | collective-permute-start | bytes 1572872 | tf_op jit(solution)/shard_map/vb4_left/ppermute | solution.py:426
  198.6 21.4 %collective-permute-start.27 = (bf16[4,512,128]{2,1,0:T(8,128)(2,1)S(1)}, bf16[4,512,128]{2,1,0:T(8,128)(2,1)}, u32[]{:S(2)}, u32[]{:S(2)}) collective-permute-start(bf16[4,512,128]{2,1,0:T(8,128)(2,1)S(1)} %collective-permute-done.24.refs_4_), channel_id=1, source_target_pairs={{0,28},{4,0},{8,4},{12,8},{16,12},{20,16},{24,20},{28,24},{1,29},{... | collective-permute-start | bytes 1572872 | tf_op jit(solution)/shard_map/kb4_left/ppermute | solution.py:426
  (27 other events, 323.1 us)

commit v7 on v6

--- a/solution.py
+++ b/solution.py
@@ -18,7 +18,7 @@
 IDLE = 4
 STAT = 48
 CHUNKS = ((0, 4), (4, 4))
-GROUPS = (((0, 1, 2), (3, 4)), ((0, 1), (2, 3), (4,)))
+GROUPS = (((0, 1, 2), (3, 4)), ((0, 1), (2,), (3, 4)))
 
 
 QUARTER = (1.5703125, 4.837512969970703e-4, 7.54978995489188216e-8)
@@ -95,7 +95,7 @@
             rows,
         ],
         out_specs=[copies, tiled, tiled],
-        compiler_params=pltpu.CompilerParams(vmem_limit_bytes=VMEM_LIMIT),
+        compiler_params=pltpu.CompilerParams(vmem_limit_bytes=60 << 20),
         cost_estimate=pl.CostEstimate(flops=5 * 10**9, bytes_accessed=6 << 20, transcendentals=0),
         name="rotate",
     )(angles.T, inv_freq, queries, keys)
@@ -521,8 +521,6 @@
     def pick(rows, step):
         return lax.dynamic_index_in_dim(rows, (my_y + step) & 3, 0, keepdims=False)
 
-    for wire in (right, left):
-        wire.send("vb", vb, 1, own_total)
     for name, ring, distance in (
         ("ka", ka, 1),
         ("va", va, 2),
@@ -533,28 +531,30 @@
         for wire in (right, left):
             wire.send(name, ring, distance)
     right.send("va", va, 4)
-    left.send("kb", kb, 1)
-    right.send("kb", kb, 1)
-    left.send("vb", vb, 2)
+    left.send("vb", vb, 1)
     state = call(0, GROUPS[0][0], None, False)
     right.send("ka", ka, 4, state[1])
-    left.send("kb", kb, 2, state[1])
+    left.send("kb", kb, 1, state[1])
+    right.send("vb", vb, 1)
+    left.send("vb", vb, 2)
+    right.send("kb", kb, 1)
+    left.send("kb", kb, 2)
+    state = call(0, GROUPS[0][1], state, True)
     right.send("vb", vb, 2, state[1])
     left.send("vb", vb, 3, state[1])
-    state = call(0, GROUPS[0][1], state, True)
     right.send("kb", kb, 2, state[1])
     left.send("kb", kb, 3, state[1])
-    right.send("vb", vb, 3, state[1])
-    left.send("vb", vb, 4, state[1])
     first_b = call(1, GROUPS[1][0], None, False)
-    right.send("kb", kb, 3, first_b[1])
-    left.send("kb", kb, 4, first_b[1])
+    right.send("vb", vb, 3, first_b[1])
+    left.send("vb", vb, 4, first_b[1])
+    right.send("kb", kb, 3)
+    second_b = call(1, GROUPS[1][1], first_b, False)
+    left.send("kb", kb, 4, second_b[1])
     mine_a = state[:3]
     with jax.named_scope("partials_a"):
         parts_a = lax.all_to_all(state[3], "y", 0, 0, tiled=True)
-    first_b[1] = after(first_b[1], parts_a)
-    state = call(1, GROUPS[1][1], first_b, False)
-    state = call(1, GROUPS[1][2], state, True)
+    second_b[1] = after(second_b[1], parts_a)
+    state = call(1, GROUPS[1][2], second_b, True)
     parts_b = []
     for s in (1, 2, 3):
         with jax.named_scope(f"partial_b{s}"):

time: 248 us -> 241 us (0.972)
  waiting for transfers between devices: 93.5 us -> 80.9 us
  starting transfers between devices: 64.5 us -> 68.2 us
  Pallas kernels: 70.8 us -> 73.8 us
  local copies, waits for them, and re-layouts: 15.5 us -> 12.6 us
    ppermute x28, waiting for transfers between devices: 69.3 us -> 58.5 us  [shift(): lax.ppermute(value, axis, [(i, (i + step) % size) for i in range(size)])]
    ppermute x28, starting transfers between devices: 43.4 us -> 47.1 us  [shift(): lax.ppermute(value, axis, [(i, (i + step) % size) for i in range(size)])]
    unnamed x26 -> x24, local copies, waits for them, and re-layouts: 9.65 us -> 8.67 us
  transfers between devices with their start and end apart: 38 -> 38, of which waited for: 18 -> 15; matrix products, arithmetic and copies ran while one was open for 2% -> 2% of each run, Pallas kernels for 23% -> 21%
where the time goes in v7:
time: 241 us; the launch traced here: 239 us
  waiting for transfers between devices  80.9 us (34%)
  Pallas kernels  73.8 us (31%)
  starting transfers between devices  68.2 us (28%)
  local copies, waits for them, and re-layouts  12.6 us (5%)
  other arithmetic  3.08 us (1%)
    pallas_call x5, Pallas kernels, attend(): pl.pallas_call(functools.partial(attend_kernel, offsets, heads, first, la...  61.4 us
    ppermute x28, waiting for transfers between devices, shift(): lax.ppermute(value, axis, [(i, (i + step) % size) for i in range(size)])  58.5 us
    ppermute x28, starting transfers between devices, shift(): lax.ppermute(value, axis, [(i, (i + step) % size) for i in range(size)])  47.1 us
    ppermute x5, waiting for transfers between devices, swap(): return lax.ppermute(value, axis, [(i, i ^ bit) for i in range(size)])  15.6 us
    unnamed x24, local copies, waits for them, and re-layouts  8.67 us
    pallas_call x1, Pallas kernels, rotate(): pl.pallas_call(rotate_kernel, out_shape=[jax.ShapeDtypeStruct((ROWS, *que...  7.02 us
    ppermute x5, starting transfers between devices, swap(): return lax.ppermute(value, axis, [(i, i ^ bit) for i in range(size)])  6.87 us
    ppermute x3, waiting for transfers between devices, to_row(): return lax.ppermute(value, 'y', moves)  6.72 us
  transfers between devices with their start and end apart: 38, of which 15 were waited for; matrix products, arithmetic and copies ran while one was open for 2% of the time, Pallas kernels for 21%

profile of v7, /device:TPU:2, one launch (start us, length us, event | category | flops | bytes accessed | tf_op | source)
XLA Modules:
  0.0 238.9 jit_solution(10408631932621847780)
XLA Ops:
  1.7 5.9 %collective-permute-start.2 = (bf16[4,512,128]{2,1,0:T(8,128)(2,1)S(1)}, bf16[4,512,128]{2,1,0:T(8,128)(2,1)S(1)}, u32[]{:S(2)}, u32[]{:S(2)}) collective-permute-start(bf16[4,512,128]{2,1,0:T(8,128)(2,1)S(1)} %get-tuple-element.107.refs_6_), channel_id=1, source_target_pairs={{0,28},{4,0},{8,4},{12,8},{16,12},{20,16},{24,20},{28,24},{1,29},{... | collective-permute-start | bytes 1572872 | tf_op jit(solution)/shard_map/va1_left/ppermute | solution.py:426
  11.6 3.2 %collective-permute-start.1 = (f32[8,10]{0,1:T(8,128)S(1)}, f32[8,10]{0,1:T(8,128)S(1)}, u32[]{:S(2)}, u32[]{:S(2)}) collective-permute-start(f32[8,10]{0,1:T(8,128)S(1)} %pad_maximum_fusion), channel_id=1, source_target_pairs={{0,64},{32,96},{64,0},{96,32},{1,65},{33,97},{65,1},{97,33},{2,66}... | collective-permute-start | bytes 968 | tf_op jit(solution)/shard_map/prefix/ppermute | solution.py:436
  18.8 3.4 %collective-permute-done.3.refs_7_ = bf16[4,512,128]{2,1,0:T(8,128)(2,1)S(1)} collective-permute-done((bf16[4,512,128]{2,1,0:T(8,128)(2,1)S(1)}, bf16[4,512,128]{2,1,0:T(8,128)(2,1)S(1)}, u32[]{:S(2)}, u32[]{:S(2)}) %collective-permute-start.3) | collective-permute-done | bytes 524320 | tf_op jit(solution)/shard_map/va1_right/ppermute | solution.py:426
  22.4 3.5 %collective-permute-done.4 = f32[8,2]{0,1:T(2,128)S(1)} collective-permute-done((f32[8,2]{0,1:T(2,128)S(1)}, f32[8,2]{0,1:T(2,128)S(1)}, u32[]{:S(2)}, u32[]{:S(2)}) %collective-permute-start.4) | collective-permute-done | bytes 96 | tf_op jit(solution)/shard_map/prefix/ppermute | solution.py:436
  26.0 4.4 %collective-permute-done.5 = f32[8,2]{0,1:T(2,128)S(1)} collective-permute-done((f32[8,2]{0,1:T(2,128)S(1)}, f32[8,2]{0,1:T(2,128)S(1)}, u32[]{:S(2)}, u32[]{:S(2)}) %collective-permute-start.5) | collective-permute-done | bytes 96 | tf_op jit(solution)/shard_map/prefix/ppermute | solution.py:436
  32.3 5.8 %collective-permute-done.6 = f32[8,2]{0,1:T(2,128)S(1)} collective-permute-done((f32[8,2]{0,1:T(2,128)S(1)}, f32[8,2]{0,1:T(2,128)S(1)}, u32[]{:S(2)}, u32[]{:S(2)}) %collective-permute-start.6) | collective-permute-done | bytes 96 | tf_op jit(solution)/shard_map/prefix/ppermute | solution.py:436
  38.8 7.0 %rotate.1 = (bf16[4,512,1024]{2,1,0:T(8,128)(2,1)}, bf16[4,512,128]{2,1,0:T(8,128)(2,1)}, bf16[4,512,128]{2,1,0:T(8,128)(2,1)}) custom-call(f32[512,8]{1,0:T(8,128)} %bitcast.28, f32[1,128]{1,0:T(1,128)} %maximum_bitcast_fusion.freq_ref, bf16[512,1024]{1,0:T(8,128)(2,1)} %q_ref.1, bf16[512,1024]{1,0:T(8,128)(2,1)} %k_ref.1), custom_call_target="tpu_custom_call" | custom-call | flops 5000000000 | bytes 6291456 | tf_op jit(solution)/shard_map/rotate/pallas_call | solution.py:83
  45.8 5.0 %all-to-all-start = ((bf16[4,512,1024]{2,1,0:T(8,128)(2,1)}), bf16[4,512,1024]{2,1,0:T(8,128)(2,1)}, u32[]{:S(2)}, u32[]{:S(2)}) async-start(bf16[4,512,1024]{2,1,0:T(8,128)(2,1)} %get-tuple-element.55), calls=%async_computation | async-start | bytes 8388608 | tf_op jit(solution)/shard_map/queries/all_to_all | solution.py:490
  54.2 3.2 %collective-permute-start.13 = (bf16[4,512,128]{2,1,0:T(8,128)(2,1)S(1)}, bf16[4,512,128]{2,1,0:T(8,128)(2,1)}, u32[]{:S(2)}, u32[]{:S(2)}) collective-permute-start(bf16[4,512,128]{2,1,0:T(8,128)(2,1)S(1)} %copy-done.1), channel_id=1, source_target_pairs={{0,28},{4,0},{8,4},{12,8},{16,12},{20,16},{24,20},{28,24},{1,29},{... | collective-permute-start | bytes 1572872 | tf_op jit(solution)/shard_map/ka1_left/ppermute | solution.py:426
  57.6 9.3 %collective-permute-done.7.refs_9_ = bf16[4,512,128]{2,1,0:T(8,128)(2,1)} collective-permute-done((bf16[4,512,128]{2,1,0:T(8,128)(2,1)S(1)}, bf16[4,512,128]{2,1,0:T(8,128)(2,1)}, u32[]{:S(2)}, u32[]{:S(2)}) %collective-permute-start.7) | collective-permute-done | bytes 524320 | tf_op jit(solution)/shard_map/va2_right/ppermute | solution.py:426
  66.9 7.2 %collective-permute-done.8.refs_2_ = bf16[4,512,128]{2,1,0:T(8,128)(2,1)} collective-permute-done((bf16[4,512,128]{2,1,0:T(8,128)(2,1)S(1)}, bf16[4,512,128]{2,1,0:T(8,128)(2,1)}, u32[]{:S(2)}, u32[]{:S(2)}) %collective-permute-start.8) | collective-permute-done | bytes 524320 | tf_op jit(solution)/shard_map/ka1_right/ppermute | solution.py:426
  79.9 9.5 %collective-permute-done.9.refs_4_ = bf16[4,512,128]{2,1,0:T(8,128)(2,1)} collective-permute-done((bf16[4,512,128]{2,1,0:T(8,128)(2,1)}, bf16[4,512,128]{2,1,0:T(8,128)(2,1)}, u32[]{:S(2)}, u32[]{:S(2)}) %collective-permute-start.9) | collective-permute-done | bytes 524320 | tf_op jit(solution)/shard_map/va3_right/ppermute | solution.py:426
  89.4 8.0 %collective-permute-done.10.refs_4_ = bf16[4,512,128]{2,1,0:T(8,128)(2,1)} collective-permute-done((bf16[4,512,128]{2,1,0:T(8,128)(2,1)}, bf16[4,512,128]{2,1,0:T(8,128)(2,1)}, u32[]{:S(2)}, u32[]{:S(2)}) %collective-permute-start.10) | collective-permute-done | bytes 524320 | tf_op jit(solution)/shard_map/ka2_right/ppermute | solution.py:426
  103.5 17.1 %attend_0_0_7_1_6_2.1 = (f32[16,512,128]{2,1,0:T(8,128)S(1)}, f32[16,8,128]{2,1,0:T(8,128)S(1)}, f32[16,8,128]{2,1,0:T(8,128)S(1)}) custom-call(s32[129]{0:T(256)S(1)} %pad_add_fusion.meta, bf16[4,512,1024]{2,1,0:T(8,128)(2,1)} %all-to-all-done.refs_0_, bf16[4,512,128]{2,1,0:T(8,128)(2,1)S(1)} %copy-done.1, ...), custom_call_target="tpu_custom_call" | custom-call | flops 18699999232 | bytes 1048576 | tf_op jit(solution)/shard_map/attend_0_0_7_1_6_2/pallas_call | solution.py:350
  127.1 9.8 %collective-permute-done.16.refs_3_ = bf16[4,512,128]{2,1,0:T(8,128)(2,1)S(1)} collective-permute-done((bf16[4,512,128]{2,1,0:T(8,128)(2,1)}, bf16[4,512,128]{2,1,0:T(8,128)(2,1)S(1)}, u32[]{:S(2)}, u32[]{:S(2)}) %collective-permute-start.16) | collective-permute-done | bytes 524320 | tf_op jit(solution)/shard_map/ka4_right/ppermute | solution.py:426
  140.2 11.9 %attend_0_5_3_4.1 = (f32[4,512,128]{2,1,0:T(8,128)S(1)}, f32[4,8,128]{2,1,0:T(8,128)S(1)}, f32[4,8,128]{2,1,0:T(8,128)S(1)}, bf16[4,4,560,128]{3,2,1,0:T(8,128)(2,1)}) custom-call(s32[129]{0:T(256)S(1)} %pad_add_fusion.meta, bf16[4,512,1024]{2,1,0:T(8,128)(2,1)} %all-to-all-done.refs_0_, bf16[4,512,128]{2,1,0:T(8,128)(2,1)} %collective-permute-done.12.refs_1_, ...), custom_call_target="tpu_custom_call" | custom-call | flops 12099999744 | bytes 1048576 | tf_op jit(solution)/shard_map/attend_0_5_3_4/pallas_call | solution.py:350
  155.4 4.5 %all-to-all-start.1 = ((bf16[4,4,560,128]{3,2,1,0:T(8,128)(2,1)}), bf16[4,4,560,128]{3,2,1,0:T(8,128)(2,1)}, u32[]{:S(2)}, u32[]{:S(2)}) async-start(bf16[4,4,560,128]{3,2,1,0:T(8,128)(2,1)} %get-tuple-element.91), calls=%async_computation.1 | async-start | bytes 4587520 | tf_op jit(solution)/shard_map/partials_a/all_to_all | solution.py:555
  163.2 12.4 %attend_4_0_7_1.1 = (f32[16,512,128]{2,1,0:T(8,128)S(1)}, f32[16,8,128]{2,1,0:T(8,128)S(1)}, f32[16,8,128]{2,1,0:T(8,128)S(1)}) custom-call(s32[129]{0:T(256)S(1)} %pad_add_fusion.meta, bf16[4,512,1024]{2,1,0:T(8,128)(2,1)} %all-to-all-done.refs_0_, bf16[4,512,128]{2,1,0:T(8,128)(2,1)S(1)} %copy-done, bf16[4,512,128]{2,1,0:T(8,128)(2,1)} %collective-permute-done.17.refs_2_, ...), custom_call_target="tpu_custom_call" | custom-call | flops 12099999744 | bytes 1048576 | tf_op jit(solution)/shard_map/attend_4_0_7_1/pallas_call | solution.py:350
  182.0 7.9 %attend_4_6_2.1 = (f32[16,512,128]{2,1,0:T(8,128)S(1)}, f32[16,8,128]{2,1,0:T(8,128)S(1)}, f32[16,8,128]{2,1,0:T(8,128)S(1)}) custom-call(s32[129]{0:T(256)S(1)} %pad_add_fusion.meta, bf16[4,512,1024]{2,1,0:T(8,128)(2,1)} %all-to-all-done.refs_0_, bf16[4,512,128]{2,1,0:T(8,128)(2,1)} %collective-permute-done.21.refs_1_, ...), custom_call_target="tpu_custom_call" | custom-call | flops 8800000000 | bytes 1048576 | tf_op jit(solution)/shard_map/attend_4_6_2/pallas_call | solution.py:350
  191.9 4.4 %collective-permute-start.30 = (bf16[4,512,128]{2,1,0:T(8,128)(2,1)}, bf16[4,512,128]{2,1,0:T(8,128)(2,1)S(1)}, u32[]{:S(2)}, u32[]{:S(2)}) collective-permute-start(bf16[4,512,128]{2,1,0:T(8,128)(2,1)} %collective-permute-done.28.refs_2_), channel_id=1, source_target_pairs={{0,28},{4,0},{8,4},{12,8},{16,12},{20,16},{24,20},{28,24},{1,29},{... | collective-permute-start | bytes 1572872 | tf_op jit(solution)/shard_map/kb4_left/ppermute | solution.py:426
  197.1 6.2 %collective-permute-done.30.refs_3_ = bf16[4,512,128]{2,1,0:T(8,128)(2,1)S(1)} collective-permute-done((bf16[4,512,128]{2,1,0:T(8,128)(2,1)}, bf16[4,512,128]{2,1,0:T(8,128)(2,1)S(1)}, u32[]{:S(2)}, u32[]{:S(2)}) %collective-permute-start.30) | collective-permute-done | bytes 524320 | tf_op jit(solution)/shard_map/kb4_left/ppermute | solution.py:426
  208.4 12.0 %attend_4_5_3_4.1 = (f32[4,512,128]{2,1,0:T(8,128)S(1)}, f32[4,8,128]{2,1,0:T(8,128)S(1)}, f32[4,8,128]{2,1,0:T(8,128)S(1)}, bf16[4,560,128]{2,1,0:T(8,128)(2,1)...) custom-call(s32[129]{0:T(256)S(1)} %pad_add_fusion.meta, bf16[4,512,1024]{2,1,0:T(8,128)(2,1)} %all-to-all-done.refs_0_, ...), custom_call_target="tpu_custom_call" | custom-call | flops 12099999744 | bytes 1048576 | tf_op jit(solution)/shard_map/attend_4_5_3_4/pallas_call | solution.py:350
  229.2 6.1 %collective-permute-done.34.two = bf16[4,560,128]{2,1,0:T(8,128)(2,1)S(1)} collective-permute-done((bf16[4,560,128]{2,1,0:T(8,128)(2,1)}, bf16[4,560,128]{2,1,0:T(8,128)(2,1)S(1)}, u32[]{:S(2)}, u32[]{:S(2)}) %collective-permute-start.34) | collective-permute-done | bytes 573472 | tf_op jit(solution)/shard_map/partial_b2/ppermute | solution.py:431
  235.4 3.5 %join_4.1 = bf16[512,1024]{1,0:T(8,128)(2,1)} custom-call(f32[4,512,128]{2,1,0:T(8,128)S(1)} %get-tuple-element.94.acc_ref, f32[4,8,128]{2,1,0:T(8,128)S(1)} %get-tuple-element.95.m_ref, f32[4,8,128]{2,1,0:T(8,128)S(1)} %get-tuple-element.96.l_ref, bf16[4,560,128]{2,1,0:T(8,128)(2,1)S(1)} %collective-permute-done.33.one, ...), custom_call_target="tpu_custom_call", output_to_operand_aliasing={{}: (6, {})} | custom-call | flops 2621440 | bytes 3670016 | tf_op jit(solution)/shard_map/join_4/pallas_call | solution.py:409
  (129 shorter events, 66.9 us)
Async XLA Ops:
  1.7 17.1 %collective-permute-start.2 = (bf16[4,512,128]{2,1,0:T(8,128)(2,1)S(1)}, bf16[4,512,128]{2,1,0:T(8,128)(2,1)S(1)}, u32[]{:S(2)}, u32[]{:S(2)}) collective-permute-start(bf16[4,512,128]{2,1,0:T(8,128)(2,1)S(1)} %get-tuple-element.107.refs_6_), channel_id=1, source_target_pairs={{0,28},{4,0},{8,4},{12,8},{16,12},{20,16},{24,20},{28,24},{1,29},{... | collective-permute-start | bytes 1572872 | tf_op jit(solution)/shard_map/va1_left/ppermute | solution.py:426
  45.8 57.7 %all-to-all-start = ((bf16[4,512,1024]{2,1,0:T(8,128)(2,1)}), bf16[4,512,1024]{2,1,0:T(8,128)(2,1)}, u32[]{:S(2)}, u32[]{:S(2)}) async-start(bf16[4,512,1024]{2,1,0:T(8,128)(2,1)} %get-tuple-element.55), calls=%async_computation | async-start | bytes 8388608 | tf_op jit(solution)/shard_map/queries/all_to_all | solution.py:490
  51.0 26.4 %collective-permute-start.15 = (bf16[4,512,128]{2,1,0:T(8,128)(2,1)S(1)}, bf16[4,512,128]{2,1,0:T(8,128)(2,1)}, u32[]{:S(2)}, u32[]{:S(2)}) collective-permute-start(bf16[4,512,128]{2,1,0:T(8,128)(2,1)S(1)} %collective-permute-done.2.refs_8_), channel_id=1, source_target_pairs={{0,28},{4,0},{8,4},{12,8},{16,12},{20,16},{24,20},{28,24},{1,29},{... | collective-permute-start | bytes 1572872 | tf_op jit(solution)/shard_map/va2_left/ppermute | solution.py:426
  54.2 19.9 %collective-permute-start.8 = (bf16[4,512,128]{2,1,0:T(8,128)(2,1)S(1)}, bf16[4,512,128]{2,1,0:T(8,128)(2,1)}, u32[]{:S(2)}, u32[]{:S(2)}) collective-permute-start(bf16[4,512,128]{2,1,0:T(8,128)(2,1)S(1)} %copy-done.1), channel_id=1, source_target_pairs={{0,4},{4,8},{8,12},{12,16},{16,20},{20,24},{24,28},{28,0},{1,5},{5... | collective-permute-start | bytes 1572872 | tf_op jit(solution)/shard_map/ka1_right/ppermute | solution.py:426
  54.2 20.4 %collective-permute-start.13 = (bf16[4,512,128]{2,1,0:T(8,128)(2,1)S(1)}, bf16[4,512,128]{2,1,0:T(8,128)(2,1)}, u32[]{:S(2)}, u32[]{:S(2)}) collective-permute-start(bf16[4,512,128]{2,1,0:T(8,128)(2,1)S(1)} %copy-done.1), channel_id=1, source_target_pairs={{0,28},{4,0},{8,4},{12,8},{16,12},{20,16},{24,20},{28,24},{1,29},{... | collective-permute-start | bytes 1572872 | tf_op jit(solution)/shard_map/ka1_left/ppermute | solution.py:426
  74.1 23.3 %collective-permute-start.10 = (bf16[4,512,128]{2,1,0:T(8,128)(2,1)}, bf16[4,512,128]{2,1,0:T(8,128)(2,1)}, u32[]{:S(2)}, u32[]{:S(2)}) collective-permute-start(bf16[4,512,128]{2,1,0:T(8,128)(2,1)} %collective-permute-done.8.refs_2_), channel_id=1, source_target_pairs={{0,4},{4,8},{8,12},{12,16},{16,20},{20,24},{24,28},{28,0},{1,5},{5... | collective-permute-start | bytes 1572872 | tf_op jit(solution)/shard_map/ka2_right/ppermute | solution.py:426
  74.7 23.3 %collective-permute-start.14 = (bf16[4,512,128]{2,1,0:T(8,128)(2,1)}, bf16[4,512,128]{2,1,0:T(8,128)(2,1)}, u32[]{:S(2)}, u32[]{:S(2)}) collective-permute-start(bf16[4,512,128]{2,1,0:T(8,128)(2,1)} %collective-permute-done.13.refs_3_), channel_id=1, source_target_pairs={{0,28},{4,0},{8,4},{12,8},{16,12},{20,16},{24,20},{28,24},{1,29},{... | collective-permute-start | bytes 1572872 | tf_op jit(solution)/shard_map/ka2_left/ppermute | solution.py:426
  77.4 23.3 %collective-permute-start.19 = (bf16[4,512,128]{2,1,0:T(8,128)(2,1)}, bf16[4,512,128]{2,1,0:T(8,128)(2,1)S(1)}, u32[]{:S(2)}, u32[]{:S(2)}) collective-permute-start(bf16[4,512,128]{2,1,0:T(8,128)(2,1)} %collective-permute-done.15.refs_10_), channel_id=1, source_target_pairs={{0,28},{4,0},{8,4},{12,8},{16,12},{20,16},{24,20},{28,24},{1,29},{... | collective-permute-start | bytes 1572872 | tf_op jit(solution)/shard_map/va3_left/ppermute | solution.py:426
  97.4 26.5 %collective-permute-start.11 = (bf16[4,512,128]{2,1,0:T(8,128)(2,1)}, bf16[4,512,128]{2,1,0:T(8,128)(2,1)}, u32[]{:S(2)}, u32[]{:S(2)}) collective-permute-start(bf16[4,512,128]{2,1,0:T(8,128)(2,1)} %collective-permute-done.9.refs_4_), channel_id=1, source_target_pairs={{0,4},{4,8},{8,12},{12,16},{16,20},{20,24},{24,28},{28,0},{1,5},{5... | collective-permute-start | bytes 1572872 | tf_op jit(solution)/shard_map/va4_right/ppermute | solution.py:426
  97.4 23.2 %collective-permute-start.12 = (bf16[4,512,128]{2,1,0:T(8,128)(2,1)}, bf16[4,512,128]{2,1,0:T(8,128)(2,1)}, u32[]{:S(2)}, u32[]{:S(2)}) collective-permute-start(bf16[4,512,128]{2,1,0:T(8,128)(2,1)} %collective-permute-done.10.refs_4_), channel_id=1, source_target_pairs={{0,4},{4,8},{8,12},{12,16},{16,20},{20,24},{24,28},{28,0},{1,5},{5... | collective-permute-start | bytes 1572872 | tf_op jit(solution)/shard_map/ka3_right/ppermute | solution.py:426
  98.0 25.3 %collective-permute-start.18 = (bf16[4,512,128]{2,1,0:T(8,128)(2,1)}, bf16[4,512,128]{2,1,0:T(8,128)(2,1)}, u32[]{:S(2)}, u32[]{:S(2)}) collective-permute-start(bf16[4,512,128]{2,1,0:T(8,128)(2,1)} %collective-permute-done.14.refs_5_), channel_id=1, source_target_pairs={{0,28},{4,0},{8,4},{12,8},{16,12},{20,16},{24,20},{28,24},{1,29},{... | collective-permute-start | bytes 1572872 | tf_op jit(solution)/shard_map/ka3_left/ppermute | solution.py:426
  101.5 23.9 %collective-permute-start.25 = (bf16[4,512,128]{2,1,0:T(8,128)(2,1)S(1)}, bf16[4,512,128]{2,1,0:T(8,128)(2,1)}, u32[]{:S(2)}, u32[]{:S(2)}) collective-permute-start(bf16[4,512,128]{2,1,0:T(8,128)(2,1)S(1)} %get-tuple-element.78.refs_4_), channel_id=1, source_target_pairs={{0,28},{4,0},{8,4},{12,8},{16,12},{20,16},{24,20},{28,24},{1,29},{... | collective-permute-start | bytes 1572872 | tf_op jit(solution)/shard_map/vb1_left/ppermute | solution.py:426
  120.6 16.4 %collective-permute-start.16 = (bf16[4,512,128]{2,1,0:T(8,128)(2,1)}, bf16[4,512,128]{2,1,0:T(8,128)(2,1)S(1)}, u32[]{:S(2)}, u32[]{:S(2)}) collective-permute-start(bf16[4,512,128]{2,1,0:T(8,128)(2,1)} %collective-permute-done.12.refs_1_), channel_id=1, source_target_pairs={{0,4},{4,8},{8,12},{12,16},{16,20},{20,24},{24,28},{28,0},{1,5},{5... | collective-permute-start | bytes 1572872 | tf_op jit(solution)/shard_map/ka4_right/ppermute | solution.py:426
  123.9 28.2 %collective-permute-start.20 = (bf16[4,512,128]{2,1,0:T(8,128)(2,1)S(1)}, bf16[4,512,128]{2,1,0:T(8,128)(2,1)}, u32[]{:S(2)}, u32[]{:S(2)}) collective-permute-start(bf16[4,512,128]{2,1,0:T(8,128)(2,1)S(1)} %get-tuple-element.78.refs_4_), channel_id=1, source_target_pairs={{0,4},{4,8},{8,12},{12,16},{16,20},{20,24},{24,28},{28,0},{1,5},{5... | collective-permute-start | bytes 1572872 | tf_op jit(solution)/shard_map/vb1_right/ppermute | solution.py:426
  125.3 26.8 %collective-permute-start.27 = (bf16[4,512,128]{2,1,0:T(8,128)(2,1)}, bf16[4,512,128]{2,1,0:T(8,128)(2,1)S(1)}, u32[]{:S(2)}, u32[]{:S(2)}) collective-permute-start(bf16[4,512,128]{2,1,0:T(8,128)(2,1)} %collective-permute-done.25.refs_6_), channel_id=1, source_target_pairs={{0,28},{4,0},{8,4},{12,8},{16,12},{20,16},{24,20},{28,24},{1,29},{... | collective-permute-start | bytes 1572872 | tf_op jit(solution)/shard_map/vb2_left/ppermute | solution.py:426
  136.9 23.0 %collective-permute-start.17 = (bf16[4,512,128]{2,1,0:T(8,128)(2,1)S(1)}, bf16[4,512,128]{2,1,0:T(8,128)(2,1)}, u32[]{:S(2)}, u32[]{:S(2)}) collective-permute-start(bf16[4,512,128]{2,1,0:T(8,128)(2,1)S(1)} %copy-done), channel_id=1, source_target_pairs={{0,4},{4,8},{8,12},{12,16},{16,20},{20,24},{24,28},{28,0},{1,5},{5... | collective-permute-start | bytes 1572872 | tf_op jit(solution)/shard_map/kb1_right/ppermute | solution.py:426
  138.4 22.4 %collective-permute-start.26 = (bf16[4,512,128]{2,1,0:T(8,128)(2,1)}, bf16[4,512,128]{2,1,0:T(8,128)(2,1)}, u32[]{:S(2)}, u32[]{:S(2)}) collective-permute-start(bf16[4,512,128]{2,1,0:T(8,128)(2,1)} %collective-permute-done.24.refs_3_), channel_id=1, source_target_pairs={{0,28},{4,0},{8,4},{12,8},{16,12},{20,16},{24,20},{28,24},{1,29},{... | collective-permute-start | bytes 1572872 | tf_op jit(solution)/shard_map/kb2_left/ppermute | solution.py:426
  152.1 23.5 %collective-permute-start.22 = (bf16[4,512,128]{2,1,0:T(8,128)(2,1)}, bf16[4,512,128]{2,1,0:T(8,128)(2,1)}, u32[]{:S(2)}, u32[]{:S(2)}) collective-permute-start(bf16[4,512,128]{2,1,0:T(8,128)(2,1)} %collective-permute-done.20.refs_5_), channel_id=1, source_target_pairs={{0,4},{4,8},{8,12},{12,16},{16,20},{20,24},{24,28},{28,0},{1,5},{5... | collective-permute-start | bytes 1572872 | tf_op jit(solution)/shard_map/vb2_right/ppermute | solution.py:426
  152.1 25.8 %collective-permute-start.29 = (bf16[4,512,128]{2,1,0:T(8,128)(2,1)S(1)}, bf16[4,512,128]{2,1,0:T(8,128)(2,1)S(1)}, u32[]{:S(2)}, u32[]{:S(2)}) collective-permute-start(bf16[4,512,128]{2,1,0:T(8,128)(2,1)S(1)} %collective-permute-done.27.refs_4_), channel_id=1, source_target_pairs={{0,28},{4,0},{8,4},{12,8},{16,12},{20,16},{24,20},{28,24},{1,29},{... | collective-permute-start | bytes 1572872 | tf_op jit(solution)/shard_map/vb3_left/ppermute | solution.py:426
  155.4 40.9 %all-to-all-start.1 = ((bf16[4,4,560,128]{3,2,1,0:T(8,128)(2,1)}), bf16[4,4,560,128]{3,2,1,0:T(8,128)(2,1)}, u32[]{:S(2)}, u32[]{:S(2)}) async-start(bf16[4,4,560,128]{3,2,1,0:T(8,128)(2,1)} %get-tuple-element.91), calls=%async_computation.1 | async-start | bytes 4587520 | tf_op jit(solution)/shard_map/partials_a/all_to_all | solution.py:555
  159.9 22.1 %collective-permute-start.21 = (bf16[4,512,128]{2,1,0:T(8,128)(2,1)}, bf16[4,512,128]{2,1,0:T(8,128)(2,1)}, u32[]{:S(2)}, u32[]{:S(2)}) collective-permute-start(bf16[4,512,128]{2,1,0:T(8,128)(2,1)} %collective-permute-done.17.refs_2_), channel_id=1, source_target_pairs={{0,4},{4,8},{8,12},{12,16},{16,20},{20,24},{24,28},{28,0},{1,5},{5... | collective-permute-start | bytes 1572872 | tf_op jit(solution)/shard_map/kb2_right/ppermute | solution.py:426
  160.8 31.1 %collective-permute-start.28 = (bf16[4,512,128]{2,1,0:T(8,128)(2,1)}, bf16[4,512,128]{2,1,0:T(8,128)(2,1)}, u32[]{:S(2)}, u32[]{:S(2)}) collective-permute-start(bf16[4,512,128]{2,1,0:T(8,128)(2,1)} %collective-permute-done.26.refs_2_), channel_id=1, source_target_pairs={{0,28},{4,0},{8,4},{12,8},{16,12},{20,16},{24,20},{28,24},{1,29},{... | collective-permute-start | bytes 1572872 | tf_op jit(solution)/shard_map/kb3_left/ppermute | solution.py:426
  175.7 20.6 %collective-permute-start.31 = (bf16[4,512,128]{2,1,0:T(8,128)(2,1)}, bf16[4,512,128]{2,1,0:T(8,128)(2,1)S(1)}, u32[]{:S(2)}, u32[]{:S(2)}) collective-permute-start(bf16[4,512,128]{2,1,0:T(8,128)(2,1)} %collective-permute-done.22.refs_3_), channel_id=1, source_target_pairs={{0,4},{4,8},{8,12},{12,16},{16,20},{20,24},{24,28},{28,0},{1,5},{5... | collective-permute-start | bytes 1572872 | tf_op jit(solution)/shard_map/vb3_right/ppermute | solution.py:426
  177.9 18.4 %collective-permute-start.32 = (bf16[4,512,128]{2,1,0:T(8,128)(2,1)S(1)}, bf16[4,512,128]{2,1,0:T(8,128)(2,1)S(1)}, u32[]{:S(2)}, u32[]{:S(2)}) collective-permute-start(bf16[4,512,128]{2,1,0:T(8,128)(2,1)S(1)} %collective-permute-done.29.refs_5_), channel_id=1, source_target_pairs={{0,28},{4,0},{8,4},{12,8},{16,12},{20,16},{24,20},{28,24},{1,29},{... | collective-permute-start | bytes 1572872 | tf_op jit(solution)/shard_map/vb4_left/ppermute | solution.py:426
  (26 other events, 238.0 us)

commit v8 on v7

--- a/solution.py
+++ b/solution.py
@@ -101,7 +101,7 @@
     )(angles.T, inv_freq, queries, keys)
 
 
-def attend_kernel(offsets, heads, first, last, meta, *refs):
+def attend_kernel(offsets, heads, first, last, rows, meta, *refs):
     count = len(offsets)
     given_q, refs = refs[0], refs[1:]
     k_refs, v_refs = refs[:count], refs[count : 2 * count]
@@ -111,10 +111,10 @@
     given = None
     if not first:
         given, rest = rest[:3], rest[3:]
-    r = pl.program_id(0)
+    r = pl.program_id(0) + rows[0]
     scale = HEAD**-0.5 * math.log2(math.e)
 
-    @pl.when(r == 0)
+    @pl.when(pl.program_id(0) == 0)
     def _():
         def hold(kb, carry):
             for at in range(count):
@@ -255,11 +255,13 @@
     if not last:
         leave(*rest)
     else:
-        packed_refs = rest[3:]
-
-        @pl.when(r == 0)
-        def _():
-            leave(*rest[:3])
+        packed_refs = rest
+        if 0 in rows:
+            packed_refs = rest[3:]
+
+            @pl.when(r == 0)
+            def _():
+                leave(*rest[:3])
 
         def send(packed_ref, lead):
             def pack(qb, carry):
@@ -289,18 +291,19 @@
                 pl.when(r == row + 1)(functools.partial(send, packed_ref, ()))
 
 
-def attend(meta, queries, chunk, offsets, keys, values, state, last):
+def attend(meta, queries, chunk, offsets, keys, values, state, last, rows=(0, 1, 2, 3), grant=VMEM_LIMIT):
     first_head, heads = chunk
     apart = first_head > 0
+    begin = rows[0]
     width = heads * HEAD
     first = state is None
-    acc_spec = pl.BlockSpec((4, width, BLOCK), lambda r, meta: (r, 0, 0))
-    run_spec = pl.BlockSpec((4, 8, BLOCK), lambda r, meta: (r, 0, 0))
+    acc_spec = pl.BlockSpec((4, width, BLOCK), lambda r, meta: (r + begin, 0, 0))
+    run_spec = pl.BlockSpec((4, 8, BLOCK), lambda r, meta: (r + begin, 0, 0))
     state_specs = [acc_spec, run_spec, run_spec]
     in_specs = [
         pl.BlockSpec(
             (1, 512, width),
-            lambda r, meta: (jnp.minimum(meta[16 * RING] + r, ROWS - 1), 0, first_head // heads),
+            lambda r, meta: (jnp.minimum(meta[16 * RING] + r + begin, ROWS - 1), 0, first_head // heads),
         )
     ]
     in_specs += [pl.BlockSpec((4, width, BLOCK), lambda r, meta: (0, 0, 0))] * (2 * len(offsets))
@@ -330,6 +333,9 @@
                 else [            pl.BlockSpec((1, 4, width + STAT, BLOCK), lambda r, meta: ((meta[16 * RING] + jnp.maximum(r, 1)) & 3, 0, 0, 0))]
             ),
         ]
+        if apart:
+            out_shape = out_shape[:3] if rows == (0,) else out_shape[3:]
+            out_specs = out_specs[:3] if rows == (0,) else out_specs[3:]
     else:
         out_shape = [
             jax.ShapeDtypeStruct((16, width, BLOCK), f32),
@@ -348,22 +354,22 @@
         pltpu.SMEM((80,), jnp.int32),
     ]
     return list(pl.pallas_call(
-        functools.partial(attend_kernel, offsets, heads, first, last),
+        functools.partial(attend_kernel, offsets, heads, first, last, rows),
         out_shape=out_shape,
         grid_spec=pltpu.PrefetchScalarGridSpec(
             num_scalar_prefetch=1,
-            grid=(ROWS,),
+            grid=(len(rows),),
             in_specs=in_specs,
             out_specs=out_specs,
             scratch_shapes=scratch,
         ),
-        compiler_params=pltpu.CompilerParams(vmem_limit_bytes=VMEM_LIMIT),
+        compiler_params=pltpu.CompilerParams(vmem_limit_bytes=grant),
         cost_estimate=pl.CostEstimate(
             flops=int((2 + 3 * len(offsets)) * 1.1e9),
             bytes_accessed=1 << 20,
             transcendentals=0,
         ),
-        name=f"attend_{first_head}_{'_'.join(str(o % RING) for o in offsets)}",
+        name=f"attend_{first_head}_{'_'.join(str(o % RING) for o in offsets)}_row{begin}",
     )(meta, *operands))
 
 
@@ -502,7 +508,7 @@
     meta = jnp.sum(jnp.where(hit, code, 0), axis=2).reshape(-1)
     meta = jnp.concatenate([meta, my_y.astype(jnp.int32)[None]])
 
-    def call(part, group, state, last):
+    def call(part, group, state, last, **more):
         offsets = []
         for distance in group:
             offsets += [distance] if distance in (0, 4) else [-distance, distance]
@@ -516,6 +522,7 @@
             [values[o] for o in offsets],
             state,
             last,
+            **more,
         )
 
     def pick(rows, step):
@@ -548,17 +555,19 @@
     right.send("vb", vb, 3, first_b[1])
     left.send("vb", vb, 4, first_b[1])
     right.send("kb", kb, 3)
-    second_b = call(1, GROUPS[1][1], first_b, False)
+    second_b = call(1, GROUPS[1][1], first_b, False, grant=60 << 20)
     left.send("kb", kb, 4, second_b[1])
     mine_a = state[:3]
     with jax.named_scope("partials_a"):
         parts_a = lax.all_to_all(state[3], "y", 0, 0, tiled=True)
     second_b[1] = after(second_b[1], parts_a)
-    state = call(1, GROUPS[1][2], second_b, True)
+    sends = call(1, GROUPS[1][2], second_b, True, rows=(1, 2, 3), grant=60 << 20)
     parts_b = []
     for s in (1, 2, 3):
         with jax.named_scope(f"partial_b{s}"):
-            parts_b.append(to_row(state[2 + s], s))
+            parts_b.append(to_row(sends[s - 1], s))
+    second_b[1] = after(second_b[1], sends[0])
+    state = call(1, GROUPS[1][2], second_b, True, rows=(0,), grant=60 << 20)
     parts_a = after(parts_a, state[1])
     out = join(CHUNKS[0], mine_a, [pick(parts_a, -s) for s in (1, 2, 3)], None)
     return join(CHUNKS[1], state[:3], parts_b, out)

time: 241 us -> 236 us (0.979)
  waiting for transfers between devices: 80.9 us -> 74.8 us
  Pallas kernels: 73.8 us -> 78.8 us
  local copies, waits for them, and re-layouts: 12.6 us -> 8.93 us
    pallas_call x5 -> x6, Pallas kernels: 61.4 us -> 67.9 us  [attend(): pl.pallas_call(functools.partial(attend_kernel, offsets, heads, first, la...]
    ppermute x3, waiting for transfers between devices: 6.72 us -> 2.82 us  [to_row(): return lax.ppermute(value, 'y', moves)]
    unnamed x24 -> x34, local copies, waits for them, and re-layouts: 8.67 us -> 4.94 us
  transfers between devices with their start and end apart: 38 -> 38, of which waited for: 15 -> 14; matrix products, arithmetic and copies ran while one was open for 2% -> 2% of each run, Pallas kernels for 21% -> 25%
where the time goes in v8:
time: 236 us; the launch traced here: 233 us
  Pallas kernels  78.8 us (33%)
  waiting for transfers between devices  74.8 us (32%)
  starting transfers between devices  67.2 us (28%)
  local copies, waits for them, and re-layouts  8.93 us (4%)
  other arithmetic  3.03 us (1%)
    pallas_call x6, Pallas kernels, attend(): pl.pallas_call(functools.partial(attend_kernel, offsets, heads, first, la...  67.9 us
    ppermute x28, waiting for transfers between devices, shift(): lax.ppermute(value, axis, [(i, (i + step) % size) for i in range(size)])  56.4 us
    ppermute x28, starting transfers between devices, shift(): lax.ppermute(value, axis, [(i, (i + step) % size) for i in range(size)])  46.9 us
    ppermute x5, waiting for transfers between devices, swap(): return lax.ppermute(value, axis, [(i, i ^ bit) for i in range(size)])  15.6 us
    pallas_call x1, Pallas kernels, rotate(): pl.pallas_call(rotate_kernel, out_shape=[jax.ShapeDtypeStruct((ROWS, *que...  7.03 us
    ppermute x5, starting transfers between devices, swap(): return lax.ppermute(value, axis, [(i, i ^ bit) for i in range(size)])  6.91 us
    all_to_all x1, starting transfers between devices, shards(): queries = lax.all_to_all(query_rot, 'y', 0, 0, tiled=True)  5 us
    unnamed x34, local copies, waits for them, and re-layouts  4.94 us
  transfers between devices with their start and end apart: 38, of which 14 were waited for; matrix products, arithmetic and copies ran while one was open for 2% of the time, Pallas kernels for 25%

profile of v8, /device:TPU:2, one launch (start us, length us, event | category | flops | bytes accessed | tf_op | source)
XLA Modules:
  0.0 233.1 jit_solution(17157613480461922146)
XLA Ops:
  1.7 5.9 %collective-permute-start.2 = (bf16[4,512,128]{2,1,0:T(8,128)(2,1)S(1)}, bf16[4,512,128]{2,1,0:T(8,128)(2,1)S(1)}, u32[]{:S(2)}, u32[]{:S(2)}) collective-permute-start(bf16[4,512,128]{2,1,0:T(8,128)(2,1)S(1)} %get-tuple-element.109.refs_6_), channel_id=1, source_target_pairs={{0,28},{4,0},{8,4},{12,8},{16,12},{20,16},{24,20},{28,24},{1,29},{... | collective-permute-start | bytes 1572872 | tf_op jit(solution)/shard_map/va1_left/ppermute | solution.py:432
  11.6 3.3 %collective-permute-start.1 = (f32[8,10]{0,1:T(8,128)S(1)}, f32[8,10]{0,1:T(8,128)S(1)}, u32[]{:S(2)}, u32[]{:S(2)}) collective-permute-start(f32[8,10]{0,1:T(8,128)S(1)} %pad_maximum_fusion), channel_id=1, source_target_pairs={{0,64},{32,96},{64,0},{96,32},{1,65},{33,97},{65,1},{97,33},{2,66}... | collective-permute-start | bytes 968 | tf_op jit(solution)/shard_map/prefix/ppermute | solution.py:442
  18.8 3.4 %collective-permute-done.3.refs_7_ = bf16[4,512,128]{2,1,0:T(8,128)(2,1)S(1)} collective-permute-done((bf16[4,512,128]{2,1,0:T(8,128)(2,1)S(1)}, bf16[4,512,128]{2,1,0:T(8,128)(2,1)S(1)}, u32[]{:S(2)}, u32[]{:S(2)}) %collective-permute-start.3) | collective-permute-done | bytes 524320 | tf_op jit(solution)/shard_map/va1_right/ppermute | solution.py:432
  22.4 3.5 %collective-permute-done.4 = f32[8,2]{0,1:T(2,128)S(1)} collective-permute-done((f32[8,2]{0,1:T(2,128)S(1)}, f32[8,2]{0,1:T(2,128)S(1)}, u32[]{:S(2)}, u32[]{:S(2)}) %collective-permute-start.4) | collective-permute-done | bytes 96 | tf_op jit(solution)/shard_map/prefix/ppermute | solution.py:442
  26.0 4.4 %collective-permute-done.5 = f32[8,2]{0,1:T(2,128)S(1)} collective-permute-done((f32[8,2]{0,1:T(2,128)S(1)}, f32[8,2]{0,1:T(2,128)S(1)}, u32[]{:S(2)}, u32[]{:S(2)}) %collective-permute-start.5) | collective-permute-done | bytes 96 | tf_op jit(solution)/shard_map/prefix/ppermute | solution.py:442
  32.3 5.8 %collective-permute-done.6 = f32[8,2]{0,1:T(2,128)S(1)} collective-permute-done((f32[8,2]{0,1:T(2,128)S(1)}, f32[8,2]{0,1:T(2,128)S(1)}, u32[]{:S(2)}, u32[]{:S(2)}) %collective-permute-start.6) | collective-permute-done | bytes 96 | tf_op jit(solution)/shard_map/prefix/ppermute | solution.py:442
  38.8 7.0 %rotate.1 = (bf16[4,512,1024]{2,1,0:T(8,128)(2,1)}, bf16[4,512,128]{2,1,0:T(8,128)(2,1)}, bf16[4,512,128]{2,1,0:T(8,128)(2,1)}) custom-call(f32[512,8]{1,0:T(8,128)} %bitcast.28, f32[1,128]{1,0:T(1,128)} %maximum_bitcast_fusion.freq_ref, bf16[512,1024]{1,0:T(8,128)(2,1)} %q_ref.1, bf16[512,1024]{1,0:T(8,128)(2,1)} %k_ref.1), custom_call_target="tpu_custom_call" | custom-call | flops 5000000000 | bytes 6291456 | tf_op jit(solution)/shard_map/rotate/pallas_call | solution.py:83
  45.8 5.0 %all-to-all-start = ((bf16[4,512,1024]{2,1,0:T(8,128)(2,1)}), bf16[4,512,1024]{2,1,0:T(8,128)(2,1)}, u32[]{:S(2)}, u32[]{:S(2)}) async-start(bf16[4,512,1024]{2,1,0:T(8,128)(2,1)} %get-tuple-element.56), calls=%async_computation | async-start | bytes 8388608 | tf_op jit(solution)/shard_map/queries/all_to_all | solution.py:496
  54.2 3.2 %collective-permute-start.13 = (bf16[4,512,128]{2,1,0:T(8,128)(2,1)S(1)}, bf16[4,512,128]{2,1,0:T(8,128)(2,1)}, u32[]{:S(2)}, u32[]{:S(2)}) collective-permute-start(bf16[4,512,128]{2,1,0:T(8,128)(2,1)S(1)} %copy-done.5), channel_id=1, source_target_pairs={{0,28},{4,0},{8,4},{12,8},{16,12},{20,16},{24,20},{28,24},{1,29},{... | collective-permute-start | bytes 1572872 | tf_op jit(solution)/shard_map/ka1_left/ppermute | solution.py:432
  57.6 9.3 %collective-permute-done.7.refs_9_ = bf16[4,512,128]{2,1,0:T(8,128)(2,1)} collective-permute-done((bf16[4,512,128]{2,1,0:T(8,128)(2,1)S(1)}, bf16[4,512,128]{2,1,0:T(8,128)(2,1)}, u32[]{:S(2)}, u32[]{:S(2)}) %collective-permute-start.7) | collective-permute-done | bytes 524320 | tf_op jit(solution)/shard_map/va2_right/ppermute | solution.py:432
  66.9 7.2 %collective-permute-done.8.refs_2_ = bf16[4,512,128]{2,1,0:T(8,128)(2,1)} collective-permute-done((bf16[4,512,128]{2,1,0:T(8,128)(2,1)S(1)}, bf16[4,512,128]{2,1,0:T(8,128)(2,1)}, u32[]{:S(2)}, u32[]{:S(2)}) %collective-permute-start.8) | collective-permute-done | bytes 524320 | tf_op jit(solution)/shard_map/ka1_right/ppermute | solution.py:432
  79.9 9.5 %collective-permute-done.9.refs_4_ = bf16[4,512,128]{2,1,0:T(8,128)(2,1)} collective-permute-done((bf16[4,512,128]{2,1,0:T(8,128)(2,1)}, bf16[4,512,128]{2,1,0:T(8,128)(2,1)}, u32[]{:S(2)}, u32[]{:S(2)}) %collective-permute-start.9) | collective-permute-done | bytes 524320 | tf_op jit(solution)/shard_map/va3_right/ppermute | solution.py:432
  89.4 8.0 %collective-permute-done.10.refs_4_ = bf16[4,512,128]{2,1,0:T(8,128)(2,1)} collective-permute-done((bf16[4,512,128]{2,1,0:T(8,128)(2,1)}, bf16[4,512,128]{2,1,0:T(8,128)(2,1)}, u32[]{:S(2)}, u32[]{:S(2)}) %collective-permute-start.10) | collective-permute-done | bytes 524320 | tf_op jit(solution)/shard_map/ka2_right/ppermute | solution.py:432
  103.5 17.1 %attend_0_0_7_1_6_2_row0.1 = (f32[16,512,128]{2,1,0:T(8,128)S(1)}, f32[16,8,128]{2,1,0:T(8,128)S(1)}, f32[16,8,128]{2,1,0:T(8,128)S(1)}) custom-call(s32[129]{0:T(256)S(1)} %pad_add_fusion.meta, bf16[4,512,1024]{2,1,0:T(8,128)(2,1)} %all-to-all-done.refs_0_, bf16[4,512,128]{2,1,0:T(8,128)(2,1)S(1)} %copy-done.5, ...), custom_call_target="tpu_custom_call" | custom-call | flops 18699999232 | bytes 1048576 | tf_op jit(solution)/shard_map/attend_0_0_7_1_6_2_row0/pallas_call | solution.py:356
  127.1 9.8 %collective-permute-done.16.refs_3_ = bf16[4,512,128]{2,1,0:T(8,128)(2,1)S(1)} collective-permute-done((bf16[4,512,128]{2,1,0:T(8,128)(2,1)}, bf16[4,512,128]{2,1,0:T(8,128)(2,1)S(1)}, u32[]{:S(2)}, u32[]{:S(2)}) %collective-permute-start.16) | collective-permute-done | bytes 524320 | tf_op jit(solution)/shard_map/ka4_right/ppermute | solution.py:432
  140.2 11.4 %attend_0_5_3_4_row0.1 = (f32[4,512,128]{2,1,0:T(8,128)S(1)}, f32[4,8,128]{2,1,0:T(8,128)S(1)}, f32[4,8,128]{2,1,0:T(8,128)S(1)}, bf16[4,4,560,128]{3,2,1,0:T(8,128)(2,1)}) custom-call(s32[129]{0:T(256)S(1)} %pad_add_fusion.meta, bf16[4,512,1024]{2,1,0:T(8,128)(2,1)} %all-to-all-done.refs_0_, bf16[4,512,128]{2,1,0:T(8,128)(2,1)} %collective-permute-done.12.refs_1_, ...), custom_call_target="tpu_custom_call" | custom-call | flops 12099999744 | bytes 1048576 | tf_op jit(solution)/shard_map/attend_0_5_3_4_row0/pallas_call | solution.py:356
  154.8 4.5 %all-to-all-start.1 = ((bf16[4,4,560,128]{3,2,1,0:T(8,128)(2,1)}), bf16[4,4,560,128]{3,2,1,0:T(8,128)(2,1)}, u32[]{:S(2)}, u32[]{:S(2)}) async-start(bf16[4,4,560,128]{3,2,1,0:T(8,128)(2,1)} %get-tuple-element.92), calls=%async_computation.1 | async-start | bytes 4587520 | tf_op jit(solution)/shard_map/partials_a/all_to_all | solution.py:562
  162.7 12.6 %attend_4_0_7_1_row0.1 = (f32[16,512,128]{2,1,0:T(8,128)S(1)}, f32[16,8,128]{2,1,0:T(8,128)S(1)}, f32[16,8,128]{2,1,0:T(8,128)S(1)}) custom-call(s32[129]{0:T(256)S(1)} %pad_add_fusion.meta, bf16[4,512,1024]{2,1,0:T(8,128)(2,1)} %all-to-all-done.refs_0_, bf16[4,512,128]{2,1,0:T(8,128)(2,1)S(1)} %copy-done.4, ...), custom_call_target="tpu_custom_call" | custom-call | flops 12099999744 | bytes 1048576 | tf_op jit(solution)/shard_map/attend_4_0_7_1_row0/pallas_call | solution.py:356
  178.6 3.2 %collective-permute-start.32 = (bf16[4,512,128]{2,1,0:T(8,128)(2,1)}, bf16[4,512,128]{2,1,0:T(8,128)(2,1)S(1)}, u32[]{:S(2)}, u32[]{:S(2)}) collective-permute-start(bf16[4,512,128]{2,1,0:T(8,128)(2,1)} %collective-permute-done.29.refs_5_), channel_id=1, source_target_pairs={{0,28},{4,0},{8,4},{12,8},{16,12},{20,16},{24,20},{28,24},{1,29},{... | collective-permute-start | bytes 1572872 | tf_op jit(solution)/shard_map/vb4_left/ppermute | solution.py:432
  181.9 9.7 %attend_4_6_2_row0.1 = (f32[16,512,128]{2,1,0:T(8,128)}, f32[16,8,128]{2,1,0:T(8,128)}, f32[16,8,128]{2,1,0:T(8,128)}) custom-call(s32[129]{0:T(256)} %copy-done.3, bf16[4,512,1024]{2,1,0:T(8,128)(2,1)} %all-to-all-done.refs_0_, bf16[4,512,128]{2,1,0:T(8,128)(2,1)} %collective-permute-done.21.refs_1_, bf16[4,512,128]{2,1,0:T(8,128)(2,1)} %collective-permute-done.26.refs_2_, ...), custom_call_target="tpu_custom_call" | custom-call | flops 8800000000 | bytes 1048576 | tf_op jit(solution)/shard_map/attend_4_6_2_row0/pallas_call | solution.py:356
  191.6 4.4 %collective-permute-start.30 = (bf16[4,512,128]{2,1,0:T(8,128)(2,1)}, bf16[4,512,128]{2,1,0:T(8,128)(2,1)S(1)}, u32[]{:S(2)}, u32[]{:S(2)}) collective-permute-start(bf16[4,512,128]{2,1,0:T(8,128)(2,1)} %collective-permute-done.28.refs_2_), channel_id=1, source_target_pairs={{0,28},{4,0},{8,4},{12,8},{16,12},{20,16},{24,20},{28,24},{1,29},{... | collective-permute-start | bytes 1572872 | tf_op jit(solution)/shard_map/kb4_left/ppermute | solution.py:432
  196.0 6.9 %collective-permute-done.30.refs_3_ = bf16[4,512,128]{2,1,0:T(8,128)(2,1)S(1)} collective-permute-done((bf16[4,512,128]{2,1,0:T(8,128)(2,1)}, bf16[4,512,128]{2,1,0:T(8,128)(2,1)S(1)}, u32[]{:S(2)}, u32[]{:S(2)}) %collective-permute-start.30) | collective-permute-done | bytes 524320 | tf_op jit(solution)/shard_map/kb4_left/ppermute | solution.py:432
  203.8 12.5 %attend_4_5_3_4_row1.1 = (bf16[4,560,128]{2,1,0:T(8,128)(2,1)}, bf16[4,560,128]{2,1,0:T(8,128)(2,1)}, bf16[4,560,128]{2,1,0:T(8,128)(2,1)}) custom-call(s32[129]{0:T(256)} %copy-done.3, bf16[4,512,1024]{2,1,0:T(8,128)(2,1)} %all-to-all-done.refs_0_, bf16[4,512,128]{2,1,0:T(8,128)(2,1)} %copy-done.15, bf16[4,512,128]{2,1,0:T(8,128)(2,1)} %collective-permute-done.28.refs_2_, ...), custom_call_target="tpu_custom_call" | custom-call | flops 12099999744 | bytes 1048576 | tf_op jit(solution)/shard_map/attend_4_5_3_4_row1/pallas_call | solution.py:356
  220.2 4.6 %attend_4_5_3_4_row0.1 = (f32[4,512,128]{2,1,0:T(8,128)}, f32[4,8,128]{2,1,0:T(8,128)}, f32[4,8,128]{2,1,0:T(8,128)}) custom-call(s32[129]{0:T(256)} %copy-done.3, bf16[4,512,1024]{2,1,0:T(8,128)(2,1)} %all-to-all-done.refs_0_, bf16[4,512,128]{2,1,0:T(8,128)(2,1)} %copy-done.15, bf16[4,512,128]{2,1,0:T(8,128)(2,1)} %collective-permute-done.28.refs_2_, ...), custom_call_target="tpu_custom_call" | custom-call | flops 12099999744 | bytes 1048576 | tf_op jit(solution)/shard_map/attend_4_5_3_4_row0/pallas_call | solution.py:356
  (140 shorter events, 60.4 us)
Async XLA Ops:
  1.7 17.1 %collective-permute-start.2 = (bf16[4,512,128]{2,1,0:T(8,128)(2,1)S(1)}, bf16[4,512,128]{2,1,0:T(8,128)(2,1)S(1)}, u32[]{:S(2)}, u32[]{:S(2)}) collective-permute-start(bf16[4,512,128]{2,1,0:T(8,128)(2,1)S(1)} %get-tuple-element.109.refs_6_), channel_id=1, source_target_pairs={{0,28},{4,0},{8,4},{12,8},{16,12},{20,16},{24,20},{28,24},{1,29},{... | collective-permute-start | bytes 1572872 | tf_op jit(solution)/shard_map/va1_left/ppermute | solution.py:432
  45.8 57.7 %all-to-all-start = ((bf16[4,512,1024]{2,1,0:T(8,128)(2,1)}), bf16[4,512,1024]{2,1,0:T(8,128)(2,1)}, u32[]{:S(2)}, u32[]{:S(2)}) async-start(bf16[4,512,1024]{2,1,0:T(8,128)(2,1)} %get-tuple-element.56), calls=%async_computation | async-start | bytes 8388608 | tf_op jit(solution)/shard_map/queries/all_to_all | solution.py:496
  51.0 26.4 %collective-permute-start.15 = (bf16[4,512,128]{2,1,0:T(8,128)(2,1)S(1)}, bf16[4,512,128]{2,1,0:T(8,128)(2,1)}, u32[]{:S(2)}, u32[]{:S(2)}) collective-permute-start(bf16[4,512,128]{2,1,0:T(8,128)(2,1)S(1)} %collective-permute-done.2.refs_8_), channel_id=1, source_target_pairs={{0,28},{4,0},{8,4},{12,8},{16,12},{20,16},{24,20},{28,24},{1,29},{... | collective-permute-start | bytes 1572872 | tf_op jit(solution)/shard_map/va2_left/ppermute | solution.py:432
  54.2 19.9 %collective-permute-start.8 = (bf16[4,512,128]{2,1,0:T(8,128)(2,1)S(1)}, bf16[4,512,128]{2,1,0:T(8,128)(2,1)}, u32[]{:S(2)}, u32[]{:S(2)}) collective-permute-start(bf16[4,512,128]{2,1,0:T(8,128)(2,1)S(1)} %copy-done.5), channel_id=1, source_target_pairs={{0,4},{4,8},{8,12},{12,16},{16,20},{20,24},{24,28},{28,0},{1,5},{5... | collective-permute-start | bytes 1572872 | tf_op jit(solution)/shard_map/ka1_right/ppermute | solution.py:432
  54.2 20.4 %collective-permute-start.13 = (bf16[4,512,128]{2,1,0:T(8,128)(2,1)S(1)}, bf16[4,512,128]{2,1,0:T(8,128)(2,1)}, u32[]{:S(2)}, u32[]{:S(2)}) collective-permute-start(bf16[4,512,128]{2,1,0:T(8,128)(2,1)S(1)} %copy-done.5), channel_id=1, source_target_pairs={{0,28},{4,0},{8,4},{12,8},{16,12},{20,16},{24,20},{28,24},{1,29},{... | collective-permute-start | bytes 1572872 | tf_op jit(solution)/shard_map/ka1_left/ppermute | solution.py:432
  74.1 23.3 %collective-permute-start.10 = (bf16[4,512,128]{2,1,0:T(8,128)(2,1)}, bf16[4,512,128]{2,1,0:T(8,128)(2,1)}, u32[]{:S(2)}, u32[]{:S(2)}) collective-permute-start(bf16[4,512,128]{2,1,0:T(8,128)(2,1)} %collective-permute-done.8.refs_2_), channel_id=1, source_target_pairs={{0,4},{4,8},{8,12},{12,16},{16,20},{20,24},{24,28},{28,0},{1,5},{5... | collective-permute-start | bytes 1572872 | tf_op jit(solution)/shard_map/ka2_right/ppermute | solution.py:432
  74.7 23.3 %collective-permute-start.14 = (bf16[4,512,128]{2,1,0:T(8,128)(2,1)}, bf16[4,512,128]{2,1,0:T(8,128)(2,1)}, u32[]{:S(2)}, u32[]{:S(2)}) collective-permute-start(bf16[4,512,128]{2,1,0:T(8,128)(2,1)} %collective-permute-done.13.refs_3_), channel_id=1, source_target_pairs={{0,28},{4,0},{8,4},{12,8},{16,12},{20,16},{24,20},{28,24},{1,29},{... | collective-permute-start | bytes 1572872 | tf_op jit(solution)/shard_map/ka2_left/ppermute | solution.py:432
  77.4 23.3 %collective-permute-start.19 = (bf16[4,512,128]{2,1,0:T(8,128)(2,1)}, bf16[4,512,128]{2,1,0:T(8,128)(2,1)S(1)}, u32[]{:S(2)}, u32[]{:S(2)}) collective-permute-start(bf16[4,512,128]{2,1,0:T(8,128)(2,1)} %collective-permute-done.15.refs_10_), channel_id=1, source_target_pairs={{0,28},{4,0},{8,4},{12,8},{16,12},{20,16},{24,20},{28,24},{1,29},{... | collective-permute-start | bytes 1572872 | tf_op jit(solution)/shard_map/va3_left/ppermute | solution.py:432
  97.4 26.5 %collective-permute-start.11 = (bf16[4,512,128]{2,1,0:T(8,128)(2,1)}, bf16[4,512,128]{2,1,0:T(8,128)(2,1)}, u32[]{:S(2)}, u32[]{:S(2)}) collective-permute-start(bf16[4,512,128]{2,1,0:T(8,128)(2,1)} %collective-permute-done.9.refs_4_), channel_id=1, source_target_pairs={{0,4},{4,8},{8,12},{12,16},{16,20},{20,24},{24,28},{28,0},{1,5},{5... | collective-permute-start | bytes 1572872 | tf_op jit(solution)/shard_map/va4_right/ppermute | solution.py:432
  97.4 23.2 %collective-permute-start.12 = (bf16[4,512,128]{2,1,0:T(8,128)(2,1)}, bf16[4,512,128]{2,1,0:T(8,128)(2,1)}, u32[]{:S(2)}, u32[]{:S(2)}) collective-permute-start(bf16[4,512,128]{2,1,0:T(8,128)(2,1)} %collective-permute-done.10.refs_4_), channel_id=1, source_target_pairs={{0,4},{4,8},{8,12},{12,16},{16,20},{20,24},{24,28},{28,0},{1,5},{5... | collective-permute-start | bytes 1572872 | tf_op jit(solution)/shard_map/ka3_right/ppermute | solution.py:432
  98.0 24.3 %collective-permute-start.18 = (bf16[4,512,128]{2,1,0:T(8,128)(2,1)}, bf16[4,512,128]{2,1,0:T(8,128)(2,1)}, u32[]{:S(2)}, u32[]{:S(2)}) collective-permute-start(bf16[4,512,128]{2,1,0:T(8,128)(2,1)} %collective-permute-done.14.refs_5_), channel_id=1, source_target_pairs={{0,28},{4,0},{8,4},{12,8},{16,12},{20,16},{24,20},{28,24},{1,29},{... | collective-permute-start | bytes 1572872 | tf_op jit(solution)/shard_map/ka3_left/ppermute | solution.py:432
  101.5 22.8 %collective-permute-start.25 = (bf16[4,512,128]{2,1,0:T(8,128)(2,1)S(1)}, bf16[4,512,128]{2,1,0:T(8,128)(2,1)}, u32[]{:S(2)}, u32[]{:S(2)}) collective-permute-start(bf16[4,512,128]{2,1,0:T(8,128)(2,1)S(1)} %get-tuple-element.79.refs_4_), channel_id=1, source_target_pairs={{0,28},{4,0},{8,4},{12,8},{16,12},{20,16},{24,20},{28,24},{1,29},{... | collective-permute-start | bytes 1572872 | tf_op jit(solution)/shard_map/vb1_left/ppermute | solution.py:432
  120.6 16.4 %collective-permute-start.16 = (bf16[4,512,128]{2,1,0:T(8,128)(2,1)}, bf16[4,512,128]{2,1,0:T(8,128)(2,1)S(1)}, u32[]{:S(2)}, u32[]{:S(2)}) collective-permute-start(bf16[4,512,128]{2,1,0:T(8,128)(2,1)} %collective-permute-done.12.refs_1_), channel_id=1, source_target_pairs={{0,4},{4,8},{8,12},{12,16},{16,20},{20,24},{24,28},{28,0},{1,5},{5... | collective-permute-start | bytes 1572872 | tf_op jit(solution)/shard_map/ka4_right/ppermute | solution.py:432
  123.9 27.7 %collective-permute-start.20 = (bf16[4,512,128]{2,1,0:T(8,128)(2,1)S(1)}, bf16[4,512,128]{2,1,0:T(8,128)(2,1)}, u32[]{:S(2)}, u32[]{:S(2)}) collective-permute-start(bf16[4,512,128]{2,1,0:T(8,128)(2,1)S(1)} %get-tuple-element.79.refs_4_), channel_id=1, source_target_pairs={{0,4},{4,8},{8,12},{12,16},{16,20},{20,24},{24,28},{28,0},{1,5},{5... | collective-permute-start | bytes 1572872 | tf_op jit(solution)/shard_map/vb1_right/ppermute | solution.py:432
  124.3 27.3 %collective-permute-start.27 = (bf16[4,512,128]{2,1,0:T(8,128)(2,1)}, bf16[4,512,128]{2,1,0:T(8,128)(2,1)}, u32[]{:S(2)}, u32[]{:S(2)}) collective-permute-start(bf16[4,512,128]{2,1,0:T(8,128)(2,1)} %collective-permute-done.25.refs_6_), channel_id=1, source_target_pairs={{0,28},{4,0},{8,4},{12,8},{16,12},{20,16},{24,20},{28,24},{1,29},{... | collective-permute-start | bytes 1572872 | tf_op jit(solution)/shard_map/vb2_left/ppermute | solution.py:432
  136.9 22.5 %collective-permute-start.17 = (bf16[4,512,128]{2,1,0:T(8,128)(2,1)S(1)}, bf16[4,512,128]{2,1,0:T(8,128)(2,1)S(1)}, u32[]{:S(2)}, u32[]{:S(2)}) collective-permute-start(bf16[4,512,128]{2,1,0:T(8,128)(2,1)S(1)} %copy-done.4), channel_id=1, source_target_pairs={{0,4},{4,8},{8,12},{12,16},{16,20},{20,24},{24,28},{28,0},{1,5},{5... | collective-permute-start | bytes 1572872 | tf_op jit(solution)/shard_map/kb1_right/ppermute | solution.py:432
  137.3 22.5 %collective-permute-start.26 = (bf16[4,512,128]{2,1,0:T(8,128)(2,1)S(1)}, bf16[4,512,128]{2,1,0:T(8,128)(2,1)}, u32[]{:S(2)}, u32[]{:S(2)}) collective-permute-start(bf16[4,512,128]{2,1,0:T(8,128)(2,1)S(1)} %collective-permute-done.24.refs_3_), channel_id=1, source_target_pairs={{0,28},{4,0},{8,4},{12,8},{16,12},{20,16},{24,20},{28,24},{1,29},{... | collective-permute-start | bytes 1572872 | tf_op jit(solution)/shard_map/kb2_left/ppermute | solution.py:432
  151.6 27.0 %collective-permute-start.22 = (bf16[4,512,128]{2,1,0:T(8,128)(2,1)}, bf16[4,512,128]{2,1,0:T(8,128)(2,1)}, u32[]{:S(2)}, u32[]{:S(2)}) collective-permute-start(bf16[4,512,128]{2,1,0:T(8,128)(2,1)} %collective-permute-done.20.refs_5_), channel_id=1, source_target_pairs={{0,4},{4,8},{8,12},{12,16},{16,20},{20,24},{24,28},{28,0},{1,5},{5... | collective-permute-start | bytes 1572872 | tf_op jit(solution)/shard_map/vb2_right/ppermute | solution.py:432
  151.6 27.0 %collective-permute-start.29 = (bf16[4,512,128]{2,1,0:T(8,128)(2,1)}, bf16[4,512,128]{2,1,0:T(8,128)(2,1)}, u32[]{:S(2)}, u32[]{:S(2)}) collective-permute-start(bf16[4,512,128]{2,1,0:T(8,128)(2,1)} %collective-permute-done.27.refs_4_), channel_id=1, source_target_pairs={{0,28},{4,0},{8,4},{12,8},{16,12},{20,16},{24,20},{28,24},{1,29},{... | collective-permute-start | bytes 1572872 | tf_op jit(solution)/shard_map/vb3_left/ppermute | solution.py:432
  154.8 41.1 %all-to-all-start.1 = ((bf16[4,4,560,128]{3,2,1,0:T(8,128)(2,1)}), bf16[4,4,560,128]{3,2,1,0:T(8,128)(2,1)}, u32[]{:S(2)}, u32[]{:S(2)}) async-start(bf16[4,4,560,128]{3,2,1,0:T(8,128)(2,1)} %get-tuple-element.92), calls=%async_computation.1 | async-start | bytes 4587520 | tf_op jit(solution)/shard_map/partials_a/all_to_all | solution.py:562
  159.4 22.4 %collective-permute-start.21 = (bf16[4,512,128]{2,1,0:T(8,128)(2,1)S(1)}, bf16[4,512,128]{2,1,0:T(8,128)(2,1)}, u32[]{:S(2)}, u32[]{:S(2)}) collective-permute-start(bf16[4,512,128]{2,1,0:T(8,128)(2,1)S(1)} %collective-permute-done.17.refs_2_), channel_id=1, source_target_pairs={{0,4},{4,8},{8,12},{12,16},{16,20},{20,24},{24,28},{28,0},{1,5},{5... | collective-permute-start | bytes 1572872 | tf_op jit(solution)/shard_map/kb2_right/ppermute | solution.py:432
  159.8 31.8 %collective-permute-start.28 = (bf16[4,512,128]{2,1,0:T(8,128)(2,1)}, bf16[4,512,128]{2,1,0:T(8,128)(2,1)}, u32[]{:S(2)}, u32[]{:S(2)}) collective-permute-start(bf16[4,512,128]{2,1,0:T(8,128)(2,1)} %collective-permute-done.26.refs_2_), channel_id=1, source_target_pairs={{0,28},{4,0},{8,4},{12,8},{16,12},{20,16},{24,20},{28,24},{1,29},{... | collective-permute-start | bytes 1572872 | tf_op jit(solution)/shard_map/kb3_left/ppermute | solution.py:432
  178.6 17.4 %collective-permute-start.31 = (bf16[4,512,128]{2,1,0:T(8,128)(2,1)}, bf16[4,512,128]{2,1,0:T(8,128)(2,1)S(1)}, u32[]{:S(2)}, u32[]{:S(2)}) collective-permute-start(bf16[4,512,128]{2,1,0:T(8,128)(2,1)} %collective-permute-done.22.refs_3_), channel_id=1, source_target_pairs={{0,4},{4,8},{8,12},{12,16},{16,20},{20,24},{24,28},{28,0},{1,5},{5... | collective-permute-start | bytes 1572872 | tf_op jit(solution)/shard_map/vb3_right/ppermute | solution.py:432
  178.6 17.4 %collective-permute-start.32 = (bf16[4,512,128]{2,1,0:T(8,128)(2,1)}, bf16[4,512,128]{2,1,0:T(8,128)(2,1)S(1)}, u32[]{:S(2)}, u32[]{:S(2)}) collective-permute-start(bf16[4,512,128]{2,1,0:T(8,128)(2,1)} %collective-permute-done.29.refs_5_), channel_id=1, source_target_pairs={{0,28},{4,0},{8,4},{12,8},{16,12},{20,16},{24,20},{28,24},{1,29},{... | collective-permute-start | bytes 1572872 | tf_op jit(solution)/shard_map/vb4_left/ppermute | solution.py:432
  (31 other events, 358.4 us)

commit v9 on v8

--- a/solution.py
+++ b/solution.py
@@ -551,7 +551,7 @@
     left.send("vb", vb, 3, state[1])
     right.send("kb", kb, 2, state[1])
     left.send("kb", kb, 3, state[1])
-    first_b = call(1, GROUPS[1][0], None, False)
+    first_b = call(1, GROUPS[1][0], None, False, grant=60 << 20)
     right.send("vb", vb, 3, first_b[1])
     left.send("vb", vb, 4, first_b[1])
     right.send("kb", kb, 3)

time: 236 us -> 235 us (level)
  local copies, waits for them, and re-layouts: 8.93 us -> 4.86 us
  waiting for transfers between devices: 74.8 us -> 78.2 us
    unnamed x34 -> x24, local copies, waits for them, and re-layouts: 4.94 us -> 0.05 us
    ppermute x28, waiting for transfers between devices: 56.4 us -> 59.7 us  [shift(): lax.ppermute(value, axis, [(i, (i + step) % size) for i in range(size)])]
  transfers between devices with their start and end apart: 38 -> 38, of which waited for: 14 -> 16; matrix products, arithmetic and copies ran while one was open for 2% -> 2% of each run, Pallas kernels for 25% -> 25%
where the time goes in v9:
time: 235 us; the launch traced here: 233 us
  Pallas kernels  79.9 us (34%)
  waiting for transfers between devices  78.2 us (33%)
  starting transfers between devices  66.7 us (28%)
  local copies, waits for them, and re-layouts  4.86 us (2%)
  other arithmetic  3.02 us (1%)
    pallas_call x6, Pallas kernels, attend(): pl.pallas_call(functools.partial(attend_kernel, offsets, heads, first, la...  69 us
    ppermute x28, waiting for transfers between devices, shift(): lax.ppermute(value, axis, [(i, (i + step) % size) for i in range(size)])  59.7 us
    ppermute x28, starting transfers between devices, shift(): lax.ppermute(value, axis, [(i, (i + step) % size) for i in range(size)])  46.4 us
    ppermute x5, waiting for transfers between devices, swap(): return lax.ppermute(value, axis, [(i, i ^ bit) for i in range(size)])  15.7 us
    pallas_call x1, Pallas kernels, rotate(): pl.pallas_call(rotate_kernel, out_shape=[jax.ShapeDtypeStruct((ROWS, *que...  7.03 us
    ppermute x5, starting transfers between devices, swap(): return lax.ppermute(value, axis, [(i, i ^ bit) for i in range(size)])  6.82 us
    all_to_all x1, starting transfers between devices, shards(): queries = lax.all_to_all(query_rot, 'y', 0, 0, tiled=True)  5 us
  transfers between devices with their start and end apart: 38, of which 16 were waited for; matrix products, arithmetic and copies ran while one was open for 2% of the time, Pallas kernels for 25%

profile of v9, /device:TPU:2, one launch (start us, length us, event | category | flops | bytes accessed | tf_op | source)
XLA Modules:
  0.0 233.1 jit_solution(740745784425525616)
XLA Ops:
  2.5 5.9 %collective-permute-start.2 = (bf16[4,512,128]{2,1,0:T(8,128)(2,1)S(1)}, bf16[4,512,128]{2,1,0:T(8,128)(2,1)S(1)}, u32[]{:S(2)}, u32[]{:S(2)}) collective-permute-start(bf16[4,512,128]{2,1,0:T(8,128)(2,1)S(1)} %get-tuple-element.109.refs_6_), channel_id=1, source_target_pairs={{0,28},{4,0},{8,4},{12,8},{16,12},{20,16},{24,20},{28,24},{1,29},{... | collective-permute-start | bytes 1572872 | tf_op jit(solution)/shard_map/va1_left/ppermute | solution.py:432
  12.3 3.3 %collective-permute-start.1 = (f32[8,10]{0,1:T(8,128)S(1)}, f32[8,10]{0,1:T(8,128)S(1)}, u32[]{:S(2)}, u32[]{:S(2)}) collective-permute-start(f32[8,10]{0,1:T(8,128)S(1)} %pad_maximum_fusion), channel_id=1, source_target_pairs={{0,64},{32,96},{64,0},{96,32},{1,65},{33,97},{65,1},{97,33},{2,66}... | collective-permute-start | bytes 968 | tf_op jit(solution)/shard_map/prefix/ppermute | solution.py:442
  19.6 3.4 %collective-permute-done.3.refs_7_ = bf16[4,512,128]{2,1,0:T(8,128)(2,1)S(1)} collective-permute-done((bf16[4,512,128]{2,1,0:T(8,128)(2,1)S(1)}, bf16[4,512,128]{2,1,0:T(8,128)(2,1)S(1)}, u32[]{:S(2)}, u32[]{:S(2)}) %collective-permute-start.3) | collective-permute-done | bytes 524320 | tf_op jit(solution)/shard_map/va1_right/ppermute | solution.py:432
  23.1 3.5 %collective-permute-done.4 = f32[8,2]{0,1:T(2,128)S(1)} collective-permute-done((f32[8,2]{0,1:T(2,128)S(1)}, f32[8,2]{0,1:T(2,128)S(1)}, u32[]{:S(2)}, u32[]{:S(2)}) %collective-permute-start.4) | collective-permute-done | bytes 96 | tf_op jit(solution)/shard_map/prefix/ppermute | solution.py:442
  26.8 4.4 %collective-permute-done.5 = f32[8,2]{0,1:T(2,128)S(1)} collective-permute-done((f32[8,2]{0,1:T(2,128)S(1)}, f32[8,2]{0,1:T(2,128)S(1)}, u32[]{:S(2)}, u32[]{:S(2)}) %collective-permute-start.5) | collective-permute-done | bytes 96 | tf_op jit(solution)/shard_map/prefix/ppermute | solution.py:442
  32.9 5.9 %collective-permute-done.6 = f32[8,2]{0,1:T(2,128)S(1)} collective-permute-done((f32[8,2]{0,1:T(2,128)S(1)}, f32[8,2]{0,1:T(2,128)S(1)}, u32[]{:S(2)}, u32[]{:S(2)}) %collective-permute-start.6) | collective-permute-done | bytes 96 | tf_op jit(solution)/shard_map/prefix/ppermute | solution.py:442
  39.5 7.0 %rotate.1 = (bf16[4,512,1024]{2,1,0:T(8,128)(2,1)}, bf16[4,512,128]{2,1,0:T(8,128)(2,1)}, bf16[4,512,128]{2,1,0:T(8,128)(2,1)}) custom-call(f32[512,8]{1,0:T(8,128)} %bitcast.28, f32[1,128]{1,0:T(1,128)} %maximum_bitcast_fusion.freq_ref, bf16[512,1024]{1,0:T(8,128)(2,1)} %q_ref.1, bf16[512,1024]{1,0:T(8,128)(2,1)} %k_ref.1), custom_call_target="tpu_custom_call" | custom-call | flops 5000000000 | bytes 6291456 | tf_op jit(solution)/shard_map/rotate/pallas_call | solution.py:83
  46.6 5.0 %all-to-all-start = ((bf16[4,512,1024]{2,1,0:T(8,128)(2,1)}), bf16[4,512,1024]{2,1,0:T(8,128)(2,1)}, u32[]{:S(2)}, u32[]{:S(2)}) async-start(bf16[4,512,1024]{2,1,0:T(8,128)(2,1)} %get-tuple-element.56), calls=%async_computation | async-start | bytes 8388608 | tf_op jit(solution)/shard_map/queries/all_to_all | solution.py:496
  51.7 3.2 %collective-permute-start.15 = (bf16[4,512,128]{2,1,0:T(8,128)(2,1)S(1)}, bf16[4,512,128]{2,1,0:T(8,128)(2,1)}, u32[]{:S(2)}, u32[]{:S(2)}) collective-permute-start(bf16[4,512,128]{2,1,0:T(8,128)(2,1)S(1)} %collective-permute-done.2.refs_8_), channel_id=1, source_target_pairs={{0,28},{4,0},{8,4},{12,8},{16,12},{20,16},{24,20},{28,24},{1,29},{... | collective-permute-start | bytes 1572872 | tf_op jit(solution)/shard_map/va2_left/ppermute | solution.py:432
  55.0 3.2 %collective-permute-start.13 = (bf16[4,512,128]{2,1,0:T(8,128)(2,1)S(1)}, bf16[4,512,128]{2,1,0:T(8,128)(2,1)}, u32[]{:S(2)}, u32[]{:S(2)}) collective-permute-start(bf16[4,512,128]{2,1,0:T(8,128)(2,1)S(1)} %copy-done.4), channel_id=1, source_target_pairs={{0,28},{4,0},{8,4},{12,8},{16,12},{20,16},{24,20},{28,24},{1,29},{... | collective-permute-start | bytes 1572872 | tf_op jit(solution)/shard_map/ka1_left/ppermute | solution.py:432
  58.3 9.3 %collective-permute-done.7.refs_9_ = bf16[4,512,128]{2,1,0:T(8,128)(2,1)} collective-permute-done((bf16[4,512,128]{2,1,0:T(8,128)(2,1)S(1)}, bf16[4,512,128]{2,1,0:T(8,128)(2,1)}, u32[]{:S(2)}, u32[]{:S(2)}) %collective-permute-start.7) | collective-permute-done | bytes 524320 | tf_op jit(solution)/shard_map/va2_right/ppermute | solution.py:432
  67.7 7.2 %collective-permute-done.8.refs_2_ = bf16[4,512,128]{2,1,0:T(8,128)(2,1)} collective-permute-done((bf16[4,512,128]{2,1,0:T(8,128)(2,1)S(1)}, bf16[4,512,128]{2,1,0:T(8,128)(2,1)}, u32[]{:S(2)}, u32[]{:S(2)}) %collective-permute-start.8) | collective-permute-done | bytes 524320 | tf_op jit(solution)/shard_map/ka1_right/ppermute | solution.py:432
  80.6 9.4 %collective-permute-done.9.refs_4_ = bf16[4,512,128]{2,1,0:T(8,128)(2,1)S(1)} collective-permute-done((bf16[4,512,128]{2,1,0:T(8,128)(2,1)}, bf16[4,512,128]{2,1,0:T(8,128)(2,1)S(1)}, u32[]{:S(2)}, u32[]{:S(2)}) %collective-permute-start.9) | collective-permute-done | bytes 524320 | tf_op jit(solution)/shard_map/va3_right/ppermute | solution.py:432
  90.0 8.3 %collective-permute-done.10.refs_4_ = bf16[4,512,128]{2,1,0:T(8,128)(2,1)} collective-permute-done((bf16[4,512,128]{2,1,0:T(8,128)(2,1)}, bf16[4,512,128]{2,1,0:T(8,128)(2,1)}, u32[]{:S(2)}, u32[]{:S(2)}) %collective-permute-start.10) | collective-permute-done | bytes 524320 | tf_op jit(solution)/shard_map/ka2_right/ppermute | solution.py:432
  103.6 16.5 %attend_0_0_7_1_6_2_row0.1 = (f32[16,512,128]{2,1,0:T(8,128)S(1)}, f32[16,8,128]{2,1,0:T(8,128)S(1)}, f32[16,8,128]{2,1,0:T(8,128)S(1)}) custom-call(s32[129]{0:T(256)S(1)} %pad_add_fusion.meta, bf16[4,512,1024]{2,1,0:T(8,128)(2,1)} %all-to-all-done.refs_0_, bf16[4,512,128]{2,1,0:T(8,128)(2,1)S(1)} %copy-done.4, ...), custom_call_target="tpu_custom_call" | custom-call | flops 18699999232 | bytes 1048576 | tf_op jit(solution)/shard_map/attend_0_0_7_1_6_2_row0/pallas_call | solution.py:356
  128.0 9.8 %collective-permute-done.16.refs_3_ = bf16[4,512,128]{2,1,0:T(8,128)(2,1)S(1)} collective-permute-done((bf16[4,512,128]{2,1,0:T(8,128)(2,1)}, bf16[4,512,128]{2,1,0:T(8,128)(2,1)S(1)}, u32[]{:S(2)}, u32[]{:S(2)}) %collective-permute-start.16) | collective-permute-done | bytes 524320 | tf_op jit(solution)/shard_map/ka4_right/ppermute | solution.py:432
  141.0 11.2 %attend_0_5_3_4_row0.1 = (f32[4,512,128]{2,1,0:T(8,128)S(1)}, f32[4,8,128]{2,1,0:T(8,128)S(1)}, f32[4,8,128]{2,1,0:T(8,128)S(1)}, bf16[4,4,560,128]{3,2,1,0:T(8,128)(2,1)}) custom-call(s32[129]{0:T(256)S(1)} %pad_add_fusion.meta, bf16[4,512,1024]{2,1,0:T(8,128)(2,1)} %all-to-all-done.refs_0_, bf16[4,512,128]{2,1,0:T(8,128)(2,1)} %collective-permute-done.12.refs_1_, ...), custom_call_target="tpu_custom_call" | custom-call | flops 12099999744 | bytes 1048576 | tf_op jit(solution)/shard_map/attend_0_5_3_4_row0/pallas_call | solution.py:356
  155.6 4.5 %all-to-all-start.1 = ((bf16[4,4,560,128]{3,2,1,0:T(8,128)(2,1)}), bf16[4,4,560,128]{3,2,1,0:T(8,128)(2,1)}, u32[]{:S(2)}, u32[]{:S(2)}) async-start(bf16[4,4,560,128]{3,2,1,0:T(8,128)(2,1)} %get-tuple-element.92), calls=%async_computation.1 | async-start | bytes 4587520 | tf_op jit(solution)/shard_map/partials_a/all_to_all | solution.py:562
  163.6 13.9 %attend_4_0_7_1_row0.1 = (f32[16,512,128]{2,1,0:T(8,128)}, f32[16,8,128]{2,1,0:T(8,128)}, f32[16,8,128]{2,1,0:T(8,128)}) custom-call(s32[129]{0:T(256)} %copy-done.3, bf16[4,512,1024]{2,1,0:T(8,128)(2,1)} %all-to-all-done.refs_0_, bf16[4,512,128]{2,1,0:T(8,128)(2,1)} %get-tuple-element.78.refs_1_, bf16[4,512,128]{2,1,0:T(8,128)(2,1)} %collective-permute-done.17.refs_2_, ...), custom_call_target="tpu_custom_call" | custom-call | flops 12099999744 | bytes 1048576 | tf_op jit(solution)/shard_map/attend_4_0_7_1_row0/pallas_call | solution.py:356
  182.8 10.2 %attend_4_6_2_row0.1 = (f32[16,512,128]{2,1,0:T(8,128)}, f32[16,8,128]{2,1,0:T(8,128)}, f32[16,8,128]{2,1,0:T(8,128)}) custom-call(s32[129]{0:T(256)} %copy-done.3, bf16[4,512,1024]{2,1,0:T(8,128)(2,1)} %all-to-all-done.refs_0_, bf16[4,512,128]{2,1,0:T(8,128)(2,1)} %collective-permute-done.21.refs_1_, bf16[4,512,128]{2,1,0:T(8,128)(2,1)} %collective-permute-done.26.refs_2_, ...), custom_call_target="tpu_custom_call" | custom-call | flops 8800000000 | bytes 1048576 | tf_op jit(solution)/shard_map/attend_4_6_2_row0/pallas_call | solution.py:356
  193.1 3.9 %collective-permute-start.30 = (bf16[4,512,128]{2,1,0:T(8,128)(2,1)S(1)}, bf16[4,512,128]{2,1,0:T(8,128)(2,1)}, u32[]{:S(2)}, u32[]{:S(2)}) collective-permute-start(bf16[4,512,128]{2,1,0:T(8,128)(2,1)S(1)} %collective-permute-done.28.refs_2_), channel_id=1, source_target_pairs={{0,28},{4,0},{8,4},{12,8},{16,12},{20,16},{24,20},{28,24},{1,29},{... | collective-permute-start | bytes 1572872 | tf_op jit(solution)/shard_map/kb4_left/ppermute | solution.py:432
  197.0 6.7 %collective-permute-done.30.refs_3_ = bf16[4,512,128]{2,1,0:T(8,128)(2,1)} collective-permute-done((bf16[4,512,128]{2,1,0:T(8,128)(2,1)S(1)}, bf16[4,512,128]{2,1,0:T(8,128)(2,1)}, u32[]{:S(2)}, u32[]{:S(2)}) %collective-permute-start.30) | collective-permute-done | bytes 524320 | tf_op jit(solution)/shard_map/kb4_left/ppermute | solution.py:432
  203.7 12.5 %attend_4_5_3_4_row1.1 = (bf16[4,560,128]{2,1,0:T(8,128)(2,1)}, bf16[4,560,128]{2,1,0:T(8,128)(2,1)}, bf16[4,560,128]{2,1,0:T(8,128)(2,1)}) custom-call(s32[129]{0:T(256)} %copy-done.3, bf16[4,512,1024]{2,1,0:T(8,128)(2,1)} %all-to-all-done.refs_0_, bf16[4,512,128]{2,1,0:T(8,128)(2,1)} %collective-permute-done.23.refs_1_, bf16[4,512,128]{2,1,0:T(8,128)(2,1)} %copy-done.9, ...), custom_call_target="tpu_custom_call" | custom-call | flops 12099999744 | bytes 1048576 | tf_op jit(solution)/shard_map/attend_4_5_3_4_row1/pallas_call | solution.py:356
  220.1 4.6 %attend_4_5_3_4_row0.1 = (f32[4,512,128]{2,1,0:T(8,128)}, f32[4,8,128]{2,1,0:T(8,128)}, f32[4,8,128]{2,1,0:T(8,128)}) custom-call(s32[129]{0:T(256)} %copy-done.3, bf16[4,512,1024]{2,1,0:T(8,128)(2,1)} %all-to-all-done.refs_0_, bf16[4,512,128]{2,1,0:T(8,128)(2,1)} %collective-permute-done.23.refs_1_, bf16[4,512,128]{2,1,0:T(8,128)(2,1)} %copy-done.9, ...), custom_call_target="tpu_custom_call" | custom-call | flops 12099999744 | bytes 1048576 | tf_op jit(solution)/shard_map/attend_4_5_3_4_row0/pallas_call | solution.py:356
  (130 shorter events, 59.7 us)
Async XLA Ops:
  2.5 17.0 %collective-permute-start.2 = (bf16[4,512,128]{2,1,0:T(8,128)(2,1)S(1)}, bf16[4,512,128]{2,1,0:T(8,128)(2,1)S(1)}, u32[]{:S(2)}, u32[]{:S(2)}) collective-permute-start(bf16[4,512,128]{2,1,0:T(8,128)(2,1)S(1)} %get-tuple-element.109.refs_6_), channel_id=1, source_target_pairs={{0,28},{4,0},{8,4},{12,8},{16,12},{20,16},{24,20},{28,24},{1,29},{... | collective-permute-start | bytes 1572872 | tf_op jit(solution)/shard_map/va1_left/ppermute | solution.py:432
  46.6 57.1 %all-to-all-start = ((bf16[4,512,1024]{2,1,0:T(8,128)(2,1)}), bf16[4,512,1024]{2,1,0:T(8,128)(2,1)}, u32[]{:S(2)}, u32[]{:S(2)}) async-start(bf16[4,512,1024]{2,1,0:T(8,128)(2,1)} %get-tuple-element.56), calls=%async_computation | async-start | bytes 8388608 | tf_op jit(solution)/shard_map/queries/all_to_all | solution.py:496
  51.7 26.4 %collective-permute-start.15 = (bf16[4,512,128]{2,1,0:T(8,128)(2,1)S(1)}, bf16[4,512,128]{2,1,0:T(8,128)(2,1)}, u32[]{:S(2)}, u32[]{:S(2)}) collective-permute-start(bf16[4,512,128]{2,1,0:T(8,128)(2,1)S(1)} %collective-permute-done.2.refs_8_), channel_id=1, source_target_pairs={{0,28},{4,0},{8,4},{12,8},{16,12},{20,16},{24,20},{28,24},{1,29},{... | collective-permute-start | bytes 1572872 | tf_op jit(solution)/shard_map/va2_left/ppermute | solution.py:432
  55.0 19.9 %collective-permute-start.8 = (bf16[4,512,128]{2,1,0:T(8,128)(2,1)S(1)}, bf16[4,512,128]{2,1,0:T(8,128)(2,1)}, u32[]{:S(2)}, u32[]{:S(2)}) collective-permute-start(bf16[4,512,128]{2,1,0:T(8,128)(2,1)S(1)} %copy-done.4), channel_id=1, source_target_pairs={{0,4},{4,8},{8,12},{12,16},{16,20},{20,24},{24,28},{28,0},{1,5},{5... | collective-permute-start | bytes 1572872 | tf_op jit(solution)/shard_map/ka1_right/ppermute | solution.py:432
  55.0 20.4 %collective-permute-start.13 = (bf16[4,512,128]{2,1,0:T(8,128)(2,1)S(1)}, bf16[4,512,128]{2,1,0:T(8,128)(2,1)}, u32[]{:S(2)}, u32[]{:S(2)}) collective-permute-start(bf16[4,512,128]{2,1,0:T(8,128)(2,1)S(1)} %copy-done.4), channel_id=1, source_target_pairs={{0,28},{4,0},{8,4},{12,8},{16,12},{20,16},{24,20},{28,24},{1,29},{... | collective-permute-start | bytes 1572872 | tf_op jit(solution)/shard_map/ka1_left/ppermute | solution.py:432
  74.8 23.5 %collective-permute-start.10 = (bf16[4,512,128]{2,1,0:T(8,128)(2,1)}, bf16[4,512,128]{2,1,0:T(8,128)(2,1)}, u32[]{:S(2)}, u32[]{:S(2)}) collective-permute-start(bf16[4,512,128]{2,1,0:T(8,128)(2,1)} %collective-permute-done.8.refs_2_), channel_id=1, source_target_pairs={{0,4},{4,8},{8,12},{12,16},{16,20},{20,24},{24,28},{28,0},{1,5},{5... | collective-permute-start | bytes 1572872 | tf_op jit(solution)/shard_map/ka2_right/ppermute | solution.py:432
  75.4 23.5 %collective-permute-start.14 = (bf16[4,512,128]{2,1,0:T(8,128)(2,1)}, bf16[4,512,128]{2,1,0:T(8,128)(2,1)}, u32[]{:S(2)}, u32[]{:S(2)}) collective-permute-start(bf16[4,512,128]{2,1,0:T(8,128)(2,1)} %collective-permute-done.13.refs_3_), channel_id=1, source_target_pairs={{0,28},{4,0},{8,4},{12,8},{16,12},{20,16},{24,20},{28,24},{1,29},{... | collective-permute-start | bytes 1572872 | tf_op jit(solution)/shard_map/ka2_left/ppermute | solution.py:432
  78.1 23.5 %collective-permute-start.19 = (bf16[4,512,128]{2,1,0:T(8,128)(2,1)}, bf16[4,512,128]{2,1,0:T(8,128)(2,1)S(1)}, u32[]{:S(2)}, u32[]{:S(2)}) collective-permute-start(bf16[4,512,128]{2,1,0:T(8,128)(2,1)} %collective-permute-done.15.refs_10_), channel_id=1, source_target_pairs={{0,28},{4,0},{8,4},{12,8},{16,12},{20,16},{24,20},{28,24},{1,29},{... | collective-permute-start | bytes 1572872 | tf_op jit(solution)/shard_map/va3_left/ppermute | solution.py:432
  98.4 26.4 %collective-permute-start.11 = (bf16[4,512,128]{2,1,0:T(8,128)(2,1)S(1)}, bf16[4,512,128]{2,1,0:T(8,128)(2,1)}, u32[]{:S(2)}, u32[]{:S(2)}) collective-permute-start(bf16[4,512,128]{2,1,0:T(8,128)(2,1)S(1)} %collective-permute-done.9.refs_4_), channel_id=1, source_target_pairs={{0,4},{4,8},{8,12},{12,16},{16,20},{20,24},{24,28},{28,0},{1,5},{5... | collective-permute-start | bytes 1572872 | tf_op jit(solution)/shard_map/va4_right/ppermute | solution.py:432
  98.4 23.1 %collective-permute-start.12 = (bf16[4,512,128]{2,1,0:T(8,128)(2,1)}, bf16[4,512,128]{2,1,0:T(8,128)(2,1)}, u32[]{:S(2)}, u32[]{:S(2)}) collective-permute-start(bf16[4,512,128]{2,1,0:T(8,128)(2,1)} %collective-permute-done.10.refs_4_), channel_id=1, source_target_pairs={{0,4},{4,8},{8,12},{12,16},{16,20},{20,24},{24,28},{28,0},{1,5},{5... | collective-permute-start | bytes 1572872 | tf_op jit(solution)/shard_map/ka3_right/ppermute | solution.py:432
  98.9 24.5 %collective-permute-start.18 = (bf16[4,512,128]{2,1,0:T(8,128)(2,1)}, bf16[4,512,128]{2,1,0:T(8,128)(2,1)}, u32[]{:S(2)}, u32[]{:S(2)}) collective-permute-start(bf16[4,512,128]{2,1,0:T(8,128)(2,1)} %collective-permute-done.14.refs_5_), channel_id=1, source_target_pairs={{0,28},{4,0},{8,4},{12,8},{16,12},{20,16},{24,20},{28,24},{1,29},{... | collective-permute-start | bytes 1572872 | tf_op jit(solution)/shard_map/ka3_left/ppermute | solution.py:432
  101.6 23.8 %collective-permute-start.25 = (bf16[4,512,128]{2,1,0:T(8,128)(2,1)}, bf16[4,512,128]{2,1,0:T(8,128)(2,1)}, u32[]{:S(2)}, u32[]{:S(2)}) collective-permute-start(bf16[4,512,128]{2,1,0:T(8,128)(2,1)} %get-tuple-element.79.refs_4_), channel_id=1, source_target_pairs={{0,28},{4,0},{8,4},{12,8},{16,12},{20,16},{24,20},{28,24},{1,29},{... | collective-permute-start | bytes 1572872 | tf_op jit(solution)/shard_map/vb1_left/ppermute | solution.py:432
  121.5 16.3 %collective-permute-start.16 = (bf16[4,512,128]{2,1,0:T(8,128)(2,1)}, bf16[4,512,128]{2,1,0:T(8,128)(2,1)S(1)}, u32[]{:S(2)}, u32[]{:S(2)}) collective-permute-start(bf16[4,512,128]{2,1,0:T(8,128)(2,1)} %collective-permute-done.12.refs_1_), channel_id=1, source_target_pairs={{0,4},{4,8},{8,12},{12,16},{16,20},{20,24},{24,28},{28,0},{1,5},{5... | collective-permute-start | bytes 1572872 | tf_op jit(solution)/shard_map/ka4_right/ppermute | solution.py:432
  124.7 27.5 %collective-permute-start.20 = (bf16[4,512,128]{2,1,0:T(8,128)(2,1)S(1)}, bf16[4,512,128]{2,1,0:T(8,128)(2,1)}, u32[]{:S(2)}, u32[]{:S(2)}) collective-permute-start(bf16[4,512,128]{2,1,0:T(8,128)(2,1)S(1)} %copy-done.5), channel_id=1, source_target_pairs={{0,4},{4,8},{8,12},{12,16},{16,20},{20,24},{24,28},{28,0},{1,5},{5... | collective-permute-start | bytes 1572872 | tf_op jit(solution)/shard_map/vb1_right/ppermute | solution.py:432
  125.5 26.9 %collective-permute-start.27 = (bf16[4,512,128]{2,1,0:T(8,128)(2,1)}, bf16[4,512,128]{2,1,0:T(8,128)(2,1)}, u32[]{:S(2)}, u32[]{:S(2)}) collective-permute-start(bf16[4,512,128]{2,1,0:T(8,128)(2,1)} %collective-permute-done.25.refs_6_), channel_id=1, source_target_pairs={{0,28},{4,0},{8,4},{12,8},{16,12},{20,16},{24,20},{28,24},{1,29},{... | collective-permute-start | bytes 1572872 | tf_op jit(solution)/shard_map/vb2_left/ppermute | solution.py:432
  137.8 22.6 %collective-permute-start.17 = (bf16[4,512,128]{2,1,0:T(8,128)(2,1)}, bf16[4,512,128]{2,1,0:T(8,128)(2,1)}, u32[]{:S(2)}, u32[]{:S(2)}) collective-permute-start(bf16[4,512,128]{2,1,0:T(8,128)(2,1)} %get-tuple-element.78.refs_1_), channel_id=1, source_target_pairs={{0,4},{4,8},{8,12},{12,16},{16,20},{20,24},{24,28},{28,0},{1,5},{5... | collective-permute-start | bytes 1572872 | tf_op jit(solution)/shard_map/kb1_right/ppermute | solution.py:432
  138.5 22.6 %collective-permute-start.26 = (bf16[4,512,128]{2,1,0:T(8,128)(2,1)S(1)}, bf16[4,512,128]{2,1,0:T(8,128)(2,1)}, u32[]{:S(2)}, u32[]{:S(2)}) collective-permute-start(bf16[4,512,128]{2,1,0:T(8,128)(2,1)S(1)} %collective-permute-done.24.refs_3_), channel_id=1, source_target_pairs={{0,28},{4,0},{8,4},{12,8},{16,12},{20,16},{24,20},{28,24},{1,29},{... | collective-permute-start | bytes 1572872 | tf_op jit(solution)/shard_map/kb2_left/ppermute | solution.py:432
  152.2 25.3 %collective-permute-start.22 = (bf16[4,512,128]{2,1,0:T(8,128)(2,1)}, bf16[4,512,128]{2,1,0:T(8,128)(2,1)S(1)}, u32[]{:S(2)}, u32[]{:S(2)}) collective-permute-start(bf16[4,512,128]{2,1,0:T(8,128)(2,1)} %collective-permute-done.20.refs_5_), channel_id=1, source_target_pairs={{0,4},{4,8},{8,12},{12,16},{16,20},{20,24},{24,28},{28,0},{1,5},{5... | collective-permute-start | bytes 1572872 | tf_op jit(solution)/shard_map/vb2_right/ppermute | solution.py:432
  152.3 27.4 %collective-permute-start.29 = (bf16[4,512,128]{2,1,0:T(8,128)(2,1)}, bf16[4,512,128]{2,1,0:T(8,128)(2,1)S(1)}, u32[]{:S(2)}, u32[]{:S(2)}) collective-permute-start(bf16[4,512,128]{2,1,0:T(8,128)(2,1)} %collective-permute-done.27.refs_4_), channel_id=1, source_target_pairs={{0,28},{4,0},{8,4},{12,8},{16,12},{20,16},{24,20},{28,24},{1,29},{... | collective-permute-start | bytes 1572872 | tf_op jit(solution)/shard_map/vb3_left/ppermute | solution.py:432
  155.6 41.4 %all-to-all-start.1 = ((bf16[4,4,560,128]{3,2,1,0:T(8,128)(2,1)}), bf16[4,4,560,128]{3,2,1,0:T(8,128)(2,1)}, u32[]{:S(2)}, u32[]{:S(2)}) async-start(bf16[4,4,560,128]{3,2,1,0:T(8,128)(2,1)} %get-tuple-element.92), calls=%async_computation.1 | async-start | bytes 4587520 | tf_op jit(solution)/shard_map/partials_a/all_to_all | solution.py:562
  160.3 22.5 %collective-permute-start.21 = (bf16[4,512,128]{2,1,0:T(8,128)(2,1)}, bf16[4,512,128]{2,1,0:T(8,128)(2,1)}, u32[]{:S(2)}, u32[]{:S(2)}) collective-permute-start(bf16[4,512,128]{2,1,0:T(8,128)(2,1)} %collective-permute-done.17.refs_2_), channel_id=1, source_target_pairs={{0,4},{4,8},{8,12},{12,16},{16,20},{20,24},{24,28},{28,0},{1,5},{5... | collective-permute-start | bytes 1572872 | tf_op jit(solution)/shard_map/kb2_right/ppermute | solution.py:432
  161.1 32.0 %collective-permute-start.28 = (bf16[4,512,128]{2,1,0:T(8,128)(2,1)}, bf16[4,512,128]{2,1,0:T(8,128)(2,1)S(1)}, u32[]{:S(2)}, u32[]{:S(2)}) collective-permute-start(bf16[4,512,128]{2,1,0:T(8,128)(2,1)} %collective-permute-done.26.refs_2_), channel_id=1, source_target_pairs={{0,28},{4,0},{8,4},{12,8},{16,12},{20,16},{24,20},{28,24},{1,29},{... | collective-permute-start | bytes 1572872 | tf_op jit(solution)/shard_map/kb3_left/ppermute | solution.py:432
  177.5 19.4 %collective-permute-start.31 = (bf16[4,512,128]{2,1,0:T(8,128)(2,1)S(1)}, bf16[4,512,128]{2,1,0:T(8,128)(2,1)}, u32[]{:S(2)}, u32[]{:S(2)}) collective-permute-start(bf16[4,512,128]{2,1,0:T(8,128)(2,1)S(1)} %collective-permute-done.22.refs_3_), channel_id=1, source_target_pairs={{0,4},{4,8},{8,12},{12,16},{16,20},{20,24},{24,28},{28,0},{1,5},{5... | collective-permute-start | bytes 1572872 | tf_op jit(solution)/shard_map/vb3_right/ppermute | solution.py:432
  179.7 17.2 %collective-permute-start.32 = (bf16[4,512,128]{2,1,0:T(8,128)(2,1)S(1)}, bf16[4,512,128]{2,1,0:T(8,128)(2,1)}, u32[]{:S(2)}, u32[]{:S(2)}) collective-permute-start(bf16[4,512,128]{2,1,0:T(8,128)(2,1)S(1)} %collective-permute-done.29.refs_5_), channel_id=1, source_target_pairs={{0,28},{4,0},{8,4},{12,8},{16,12},{20,16},{24,20},{28,24},{1,29},{... | collective-permute-start | bytes 1572872 | tf_op jit(solution)/shard_map/vb4_left/ppermute | solution.py:432
  (26 other events, 317.2 us)

commit v10 on v9

--- a/solution.py
+++ b/solution.py
@@ -552,9 +552,9 @@
     right.send("kb", kb, 2, state[1])
     left.send("kb", kb, 3, state[1])
     first_b = call(1, GROUPS[1][0], None, False, grant=60 << 20)
-    right.send("vb", vb, 3, first_b[1])
-    left.send("vb", vb, 4, first_b[1])
-    right.send("kb", kb, 3)
+    right.send("vb", vb, 3)
+    left.send("vb", vb, 4)
+    right.send("kb", kb, 3, first_b[1])
     second_b = call(1, GROUPS[1][1], first_b, False, grant=60 << 20)
     left.send("kb", kb, 4, second_b[1])
     mine_a = state[:3]

time: 235 us -> 241 us (1.026)
  waiting for transfers between devices: 78.2 us -> 98.2 us
  starting transfers between devices: 66.7 us -> 58.2 us
  Pallas kernels: 79.9 us -> 75 us
    ppermute x28, waiting for transfers between devices: 59.7 us -> 79.7 us  [shift(): lax.ppermute(value, axis, [(i, (i + step) % size) for i in range(size)])]
    ppermute x28, starting transfers between devices: 46.4 us -> 37.9 us  [shift(): lax.ppermute(value, axis, [(i, (i + step) % size) for i in range(size)])]
    pallas_call x6, Pallas kernels: 69 us -> 64.1 us  [attend(): pl.pallas_call(functools.partial(attend_kernel, offsets, heads, first, la...]
  transfers between devices with their start and end apart: 38 -> 38, of which waited for: 16 -> 18; matrix products, arithmetic and copies ran while one was open for 2% -> 2% of each run, Pallas kernels for 25% -> 23%
where the time goes in v10:
time: 241 us; the launch traced here: 240 us
  waiting for transfers between devices  98.2 us (41%)
  Pallas kernels  75 us (31%)
  starting transfers between devices  58.2 us (24%)
  local copies, waits for them, and re-layouts  4.81 us (2%)
  other arithmetic  3.05 us (1%)
    ppermute x28, waiting for transfers between devices, shift(): lax.ppermute(value, axis, [(i, (i + step) % size) for i in range(size)])  79.7 us
    pallas_call x6, Pallas kernels, attend(): pl.pallas_call(functools.partial(attend_kernel, offsets, heads, first, la...  64.1 us
    ppermute x28, starting transfers between devices, shift(): lax.ppermute(value, axis, [(i, (i + step) % size) for i in range(size)])  37.9 us
    ppermute x5, waiting for transfers between devices, swap(): return lax.ppermute(value, axis, [(i, i ^ bit) for i in range(size)])  15.7 us
    pallas_call x1, Pallas kernels, rotate(): pl.pallas_call(rotate_kernel, out_shape=[jax.ShapeDtypeStruct((ROWS, *que...  7.04 us
    ppermute x5, starting transfers between devices, swap(): return lax.ppermute(value, axis, [(i, i ^ bit) for i in range(size)])  6.82 us
    all_to_all x1, starting transfers between devices, shards(): queries = lax.all_to_all(query_rot, 'y', 0, 0, tiled=True)  4.99 us
  transfers between devices with their start and end apart: 38, of which 18 were waited for; matrix products, arithmetic and copies ran while one was open for 2% of the time, Pallas kernels for 23%

profile of v10, /device:TPU:2, one launch (start us, length us, event | category | flops | bytes accessed | tf_op | source)
XLA Modules:
  0.0 239.6 jit_solution(4464528790929861801)
XLA Ops:
  2.5 5.9 %collective-permute-start.2 = (bf16[4,512,128]{2,1,0:T(8,128)(2,1)S(1)}, bf16[4,512,128]{2,1,0:T(8,128)(2,1)S(1)}, u32[]{:S(2)}, u32[]{:S(2)}) collective-permute-start(bf16[4,512,128]{2,1,0:T(8,128)(2,1)S(1)} %get-tuple-element.109.refs_6_), channel_id=1, source_target_pairs={{0,28},{4,0},{8,4},{12,8},{16,12},{20,16},{24,20},{28,24},{1,29},{... | collective-permute-start | bytes 1572872 | tf_op jit(solution)/shard_map/va1_left/ppermute | solution.py:432
  12.3 3.3 %collective-permute-start.1 = (f32[8,10]{0,1:T(8,128)S(1)}, f32[8,10]{0,1:T(8,128)S(1)}, u32[]{:S(2)}, u32[]{:S(2)}) collective-permute-start(f32[8,10]{0,1:T(8,128)S(1)} %pad_maximum_fusion), channel_id=1, source_target_pairs={{0,64},{32,96},{64,0},{96,32},{1,65},{33,97},{65,1},{97,33},{2,66}... | collective-permute-start | bytes 968 | tf_op jit(solution)/shard_map/prefix/ppermute | solution.py:442
  19.5 3.4 %collective-permute-done.3.refs_7_ = bf16[4,512,128]{2,1,0:T(8,128)(2,1)S(1)} collective-permute-done((bf16[4,512,128]{2,1,0:T(8,128)(2,1)S(1)}, bf16[4,512,128]{2,1,0:T(8,128)(2,1)S(1)}, u32[]{:S(2)}, u32[]{:S(2)}) %collective-permute-start.3) | collective-permute-done | bytes 524320 | tf_op jit(solution)/shard_map/va1_right/ppermute | solution.py:432
  23.1 3.6 %collective-permute-done.4 = f32[8,2]{0,1:T(2,128)S(1)} collective-permute-done((f32[8,2]{0,1:T(2,128)S(1)}, f32[8,2]{0,1:T(2,128)S(1)}, u32[]{:S(2)}, u32[]{:S(2)}) %collective-permute-start.4) | collective-permute-done | bytes 96 | tf_op jit(solution)/shard_map/prefix/ppermute | solution.py:442
  26.7 4.4 %collective-permute-done.5 = f32[8,2]{0,1:T(2,128)S(1)} collective-permute-done((f32[8,2]{0,1:T(2,128)S(1)}, f32[8,2]{0,1:T(2,128)S(1)}, u32[]{:S(2)}, u32[]{:S(2)}) %collective-permute-start.5) | collective-permute-done | bytes 96 | tf_op jit(solution)/shard_map/prefix/ppermute | solution.py:442
  33.0 5.7 %collective-permute-done.6 = f32[8,2]{0,1:T(2,128)S(1)} collective-permute-done((f32[8,2]{0,1:T(2,128)S(1)}, f32[8,2]{0,1:T(2,128)S(1)}, u32[]{:S(2)}, u32[]{:S(2)}) %collective-permute-start.6) | collective-permute-done | bytes 96 | tf_op jit(solution)/shard_map/prefix/ppermute | solution.py:442
  39.5 7.0 %rotate.1 = (bf16[4,512,1024]{2,1,0:T(8,128)(2,1)}, bf16[4,512,128]{2,1,0:T(8,128)(2,1)}, bf16[4,512,128]{2,1,0:T(8,128)(2,1)}) custom-call(f32[512,8]{1,0:T(8,128)} %bitcast.28, f32[1,128]{1,0:T(1,128)} %maximum_bitcast_fusion.freq_ref, bf16[512,1024]{1,0:T(8,128)(2,1)} %q_ref.1, bf16[512,1024]{1,0:T(8,128)(2,1)} %k_ref.1), custom_call_target="tpu_custom_call" | custom-call | flops 5000000000 | bytes 6291456 | tf_op jit(solution)/shard_map/rotate/pallas_call | solution.py:83
  46.6 5.0 %all-to-all-start = ((bf16[4,512,1024]{2,1,0:T(8,128)(2,1)}), bf16[4,512,1024]{2,1,0:T(8,128)(2,1)}, u32[]{:S(2)}, u32[]{:S(2)}) async-start(bf16[4,512,1024]{2,1,0:T(8,128)(2,1)} %get-tuple-element.56), calls=%async_computation | async-start | bytes 8388608 | tf_op jit(solution)/shard_map/queries/all_to_all | solution.py:496
  55.9 10.6 %collective-permute-done.15.refs_10_ = bf16[4,512,128]{2,1,0:T(8,128)(2,1)} collective-permute-done((bf16[4,512,128]{2,1,0:T(8,128)(2,1)S(1)}, bf16[4,512,128]{2,1,0:T(8,128)(2,1)}, u32[]{:S(2)}, u32[]{:S(2)}) %collective-permute-start.15) | collective-permute-done | bytes 524320 | tf_op jit(solution)/shard_map/va2_left/ppermute | solution.py:432
  66.4 8.4 %collective-permute-done.13.refs_3_ = bf16[4,512,128]{2,1,0:T(8,128)(2,1)} collective-permute-done((bf16[4,512,128]{2,1,0:T(8,128)(2,1)S(1)}, bf16[4,512,128]{2,1,0:T(8,128)(2,1)}, u32[]{:S(2)}, u32[]{:S(2)}) %collective-permute-start.13) | collective-permute-done | bytes 524320 | tf_op jit(solution)/shard_map/ka1_left/ppermute | solution.py:432
  79.4 9.4 %collective-permute-done.19.refs_5_ = bf16[4,512,128]{2,1,0:T(8,128)(2,1)S(1)} collective-permute-done((bf16[4,512,128]{2,1,0:T(8,128)(2,1)}, bf16[4,512,128]{2,1,0:T(8,128)(2,1)S(1)}, u32[]{:S(2)}, u32[]{:S(2)}) %collective-permute-start.19) | collective-permute-done | bytes 524320 | tf_op jit(solution)/shard_map/va3_left/ppermute | solution.py:432
  88.8 9.3 %collective-permute-done.14.refs_5_ = bf16[4,512,128]{2,1,0:T(8,128)(2,1)} collective-permute-done((bf16[4,512,128]{2,1,0:T(8,128)(2,1)}, bf16[4,512,128]{2,1,0:T(8,128)(2,1)}, u32[]{:S(2)}, u32[]{:S(2)}) %collective-permute-start.14) | collective-permute-done | bytes 524320 | tf_op jit(solution)/shard_map/ka2_left/ppermute | solution.py:432
  102.2 15.5 %attend_0_0_7_1_6_2_row0.1 = (f32[16,512,128]{2,1,0:T(8,128)S(1)}, f32[16,8,128]{2,1,0:T(8,128)S(1)}, f32[16,8,128]{2,1,0:T(8,128)S(1)}) custom-call(s32[129]{0:T(256)S(1)} %pad_add_fusion.meta, bf16[4,512,1024]{2,1,0:T(8,128)(2,1)} %all-to-all-done.refs_0_, bf16[4,512,128]{2,1,0:T(8,128)(2,1)S(1)} %copy-done.4, ...), custom_call_target="tpu_custom_call" | custom-call | flops 18699999232 | bytes 1048576 | tf_op jit(solution)/shard_map/attend_0_0_7_1_6_2_row0/pallas_call | solution.py:356
  117.7 3.8 %collective-permute-done.18.refs_2_ = bf16[4,512,128]{2,1,0:T(8,128)(2,1)} collective-permute-done((bf16[4,512,128]{2,1,0:T(8,128)(2,1)}, bf16[4,512,128]{2,1,0:T(8,128)(2,1)}, u32[]{:S(2)}, u32[]{:S(2)}) %collective-permute-start.18) | collective-permute-done | bytes 524320 | tf_op jit(solution)/shard_map/ka3_left/ppermute | solution.py:432
  125.5 11.0 %collective-permute-done.22.refs_3_ = bf16[4,512,128]{2,1,0:T(8,128)(2,1)S(1)} collective-permute-done((bf16[4,512,128]{2,1,0:T(8,128)(2,1)}, bf16[4,512,128]{2,1,0:T(8,128)(2,1)S(1)}, u32[]{:S(2)}, u32[]{:S(2)}) %collective-permute-start.22) | collective-permute-done | bytes 524320 | tf_op jit(solution)/shard_map/kb1_left/ppermute | solution.py:432
  138.6 10.2 %attend_0_5_3_4_row0.1 = (f32[4,512,128]{2,1,0:T(8,128)S(1)}, f32[4,8,128]{2,1,0:T(8,128)S(1)}, f32[4,8,128]{2,1,0:T(8,128)S(1)}, bf16[4,4,560,128]{3,2,1,0:T(8,128)(2,1)}) custom-call(s32[129]{0:T(256)S(1)} %pad_add_fusion.meta, bf16[4,512,1024]{2,1,0:T(8,128)(2,1)} %all-to-all-done.refs_0_, bf16[4,512,128]{2,1,0:T(8,128)(2,1)} %collective-permute-done.12.refs_1_, ...), custom_call_target="tpu_custom_call" | custom-call | flops 12099999744 | bytes 1048576 | tf_op jit(solution)/shard_map/attend_0_5_3_4_row0/pallas_call | solution.py:356
  148.8 5.0 %collective-permute-start.29 = (bf16[4,512,128]{2,1,0:T(8,128)(2,1)}, bf16[4,512,128]{2,1,0:T(8,128)(2,1)S(1)}, u32[]{:S(2)}, u32[]{:S(2)}) collective-permute-start(bf16[4,512,128]{2,1,0:T(8,128)(2,1)} %collective-permute-done.27.refs_4_), channel_id=1, source_target_pairs={{0,28},{4,0},{8,4},{12,8},{16,12},{20,16},{24,20},{28,24},{1,29},{... | collective-permute-start | bytes 1572872 | tf_op jit(solution)/shard_map/vb3_left/ppermute | solution.py:432
  153.8 4.5 %all-to-all-start.1 = ((bf16[4,4,560,128]{3,2,1,0:T(8,128)(2,1)}), bf16[4,4,560,128]{3,2,1,0:T(8,128)(2,1)}, u32[]{:S(2)}, u32[]{:S(2)}) async-start(bf16[4,4,560,128]{3,2,1,0:T(8,128)(2,1)} %get-tuple-element.92), calls=%async_computation.1 | async-start | bytes 4587520 | tf_op jit(solution)/shard_map/partials_a/all_to_all | solution.py:562
  161.1 6.2 %collective-permute-done.29.refs_5_ = bf16[4,512,128]{2,1,0:T(8,128)(2,1)S(1)} collective-permute-done((bf16[4,512,128]{2,1,0:T(8,128)(2,1)}, bf16[4,512,128]{2,1,0:T(8,128)(2,1)S(1)}, u32[]{:S(2)}, u32[]{:S(2)}) %collective-permute-start.29) | collective-permute-done | bytes 524320 | tf_op jit(solution)/shard_map/vb3_left/ppermute | solution.py:432
  175.2 13.2 %attend_4_0_7_1_row0.1 = (f32[16,512,128]{2,1,0:T(8,128)}, f32[16,8,128]{2,1,0:T(8,128)}, f32[16,8,128]{2,1,0:T(8,128)}) custom-call(s32[129]{0:T(256)} %copy-done.3, bf16[4,512,1024]{2,1,0:T(8,128)(2,1)} %all-to-all-done.refs_0_, bf16[4,512,128]{2,1,0:T(8,128)(2,1)} %get-tuple-element.76.refs_1_, bf16[4,512,128]{2,1,0:T(8,128)(2,1)} %collective-permute-done.17.refs_2_, ...), custom_call_target="tpu_custom_call" | custom-call | flops 12099999744 | bytes 1048576 | tf_op jit(solution)/shard_map/attend_4_0_7_1_row0/pallas_call | solution.py:356
  188.4 9.1 %attend_4_6_2_row0.1 = (f32[16,512,128]{2,1,0:T(8,128)}, f32[16,8,128]{2,1,0:T(8,128)}, f32[16,8,128]{2,1,0:T(8,128)}) custom-call(s32[129]{0:T(256)} %copy-done.3, bf16[4,512,1024]{2,1,0:T(8,128)(2,1)} %all-to-all-done.refs_0_, bf16[4,512,128]{2,1,0:T(8,128)(2,1)} %collective-permute-done.21.refs_1_, bf16[4,512,128]{2,1,0:T(8,128)(2,1)} %collective-permute-done.26.refs_2_, ...), custom_call_target="tpu_custom_call" | custom-call | flops 8800000000 | bytes 1048576 | tf_op jit(solution)/shard_map/attend_4_6_2_row0/pallas_call | solution.py:356
  200.8 7.4 %collective-permute-done.30.refs_3_ = bf16[4,512,128]{2,1,0:T(8,128)(2,1)} collective-permute-done((bf16[4,512,128]{2,1,0:T(8,128)(2,1)}, bf16[4,512,128]{2,1,0:T(8,128)(2,1)}, u32[]{:S(2)}, u32[]{:S(2)}) %collective-permute-start.30) | collective-permute-done | bytes 524320 | tf_op jit(solution)/shard_map/kb4_left/ppermute | solution.py:432
  211.3 11.5 %attend_4_5_3_4_row1.1 = (bf16[4,560,128]{2,1,0:T(8,128)(2,1)}, bf16[4,560,128]{2,1,0:T(8,128)(2,1)}, bf16[4,560,128]{2,1,0:T(8,128)(2,1)}) custom-call(s32[129]{0:T(256)} %copy-done.3, bf16[4,512,1024]{2,1,0:T(8,128)(2,1)} %all-to-all-done.refs_0_, bf16[4,512,128]{2,1,0:T(8,128)(2,1)} %collective-permute-done.25.refs_1_, ...), custom_call_target="tpu_custom_call" | custom-call | flops 12099999744 | bytes 1048576 | tf_op jit(solution)/shard_map/attend_4_5_3_4_row1/pallas_call | solution.py:356
  226.7 4.6 %attend_4_5_3_4_row0.1 = (f32[4,512,128]{2,1,0:T(8,128)}, f32[4,8,128]{2,1,0:T(8,128)}, f32[4,8,128]{2,1,0:T(8,128)}) custom-call(s32[129]{0:T(256)} %copy-done.3, bf16[4,512,1024]{2,1,0:T(8,128)(2,1)} %all-to-all-done.refs_0_, bf16[4,512,128]{2,1,0:T(8,128)(2,1)} %collective-permute-done.25.refs_1_, bf16[4,512,128]{2,1,0:T(8,128)(2,1)} %collective-permute-done.28.refs_2_, ...), custom_call_target="tpu_custom_call" | custom-call | flops 12099999744 | bytes 1048576 | tf_op jit(solution)/shard_map/attend_4_5_3_4_row0/pallas_call | solution.py:356
  (130 shorter events, 61.4 us)
Async XLA Ops:
  2.5 17.0 %collective-permute-start.2 = (bf16[4,512,128]{2,1,0:T(8,128)(2,1)S(1)}, bf16[4,512,128]{2,1,0:T(8,128)(2,1)S(1)}, u32[]{:S(2)}, u32[]{:S(2)}) collective-permute-start(bf16[4,512,128]{2,1,0:T(8,128)(2,1)S(1)} %get-tuple-element.109.refs_6_), channel_id=1, source_target_pairs={{0,28},{4,0},{8,4},{12,8},{16,12},{20,16},{24,20},{28,24},{1,29},{... | collective-permute-start | bytes 1572872 | tf_op jit(solution)/shard_map/va1_left/ppermute | solution.py:432
  46.6 55.6 %all-to-all-start = ((bf16[4,512,1024]{2,1,0:T(8,128)(2,1)}), bf16[4,512,1024]{2,1,0:T(8,128)(2,1)}, u32[]{:S(2)}, u32[]{:S(2)}) async-start(bf16[4,512,1024]{2,1,0:T(8,128)(2,1)} %get-tuple-element.56), calls=%async_computation | async-start | bytes 8388608 | tf_op jit(solution)/shard_map/queries/all_to_all | solution.py:496
  52.0 25.1 %collective-permute-start.7 = (bf16[4,512,128]{2,1,0:T(8,128)(2,1)S(1)}, bf16[4,512,128]{2,1,0:T(8,128)(2,1)}, u32[]{:S(2)}, u32[]{:S(2)}) collective-permute-start(bf16[4,512,128]{2,1,0:T(8,128)(2,1)S(1)} %collective-permute-done.3.refs_7_), channel_id=1, source_target_pairs={{0,4},{4,8},{8,12},{12,16},{16,20},{20,24},{24,28},{28,0},{1,5},{5... | collective-permute-start | bytes 1572872 | tf_op jit(solution)/shard_map/va2_right/ppermute | solution.py:432
  53.7 21.1 %collective-permute-start.13 = (bf16[4,512,128]{2,1,0:T(8,128)(2,1)S(1)}, bf16[4,512,128]{2,1,0:T(8,128)(2,1)}, u32[]{:S(2)}, u32[]{:S(2)}) collective-permute-start(bf16[4,512,128]{2,1,0:T(8,128)(2,1)S(1)} %copy-done.4), channel_id=1, source_target_pairs={{0,28},{4,0},{8,4},{12,8},{16,12},{20,16},{24,20},{28,24},{1,29},{... | collective-permute-start | bytes 1572872 | tf_op jit(solution)/shard_map/ka1_left/ppermute | solution.py:432
  55.2 19.9 %collective-permute-start.8 = (bf16[4,512,128]{2,1,0:T(8,128)(2,1)S(1)}, bf16[4,512,128]{2,1,0:T(8,128)(2,1)}, u32[]{:S(2)}, u32[]{:S(2)}) collective-permute-start(bf16[4,512,128]{2,1,0:T(8,128)(2,1)S(1)} %copy-done.4), channel_id=1, source_target_pairs={{0,4},{4,8},{8,12},{12,16},{16,20},{20,24},{24,28},{28,0},{1,5},{5... | collective-permute-start | bytes 1572872 | tf_op jit(solution)/shard_map/ka1_right/ppermute | solution.py:432
  75.1 23.0 %collective-permute-start.14 = (bf16[4,512,128]{2,1,0:T(8,128)(2,1)}, bf16[4,512,128]{2,1,0:T(8,128)(2,1)}, u32[]{:S(2)}, u32[]{:S(2)}) collective-permute-start(bf16[4,512,128]{2,1,0:T(8,128)(2,1)} %collective-permute-done.13.refs_3_), channel_id=1, source_target_pairs={{0,28},{4,0},{8,4},{12,8},{16,12},{20,16},{24,20},{28,24},{1,29},{... | collective-permute-start | bytes 1572872 | tf_op jit(solution)/shard_map/ka2_left/ppermute | solution.py:432
  75.1 23.3 %collective-permute-start.10 = (bf16[4,512,128]{2,1,0:T(8,128)(2,1)}, bf16[4,512,128]{2,1,0:T(8,128)(2,1)}, u32[]{:S(2)}, u32[]{:S(2)}) collective-permute-start(bf16[4,512,128]{2,1,0:T(8,128)(2,1)} %collective-permute-done.8.refs_2_), channel_id=1, source_target_pairs={{0,4},{4,8},{8,12},{12,16},{16,20},{20,24},{24,28},{28,0},{1,5},{5... | collective-permute-start | bytes 1572872 | tf_op jit(solution)/shard_map/ka2_right/ppermute | solution.py:432
  77.1 23.3 %collective-permute-start.9 = (bf16[4,512,128]{2,1,0:T(8,128)(2,1)}, bf16[4,512,128]{2,1,0:T(8,128)(2,1)S(1)}, u32[]{:S(2)}, u32[]{:S(2)}) collective-permute-start(bf16[4,512,128]{2,1,0:T(8,128)(2,1)} %collective-permute-done.7.refs_9_), channel_id=1, source_target_pairs={{0,4},{4,8},{8,12},{12,16},{16,20},{20,24},{24,28},{28,0},{1,5},{5... | collective-permute-start | bytes 1572872 | tf_op jit(solution)/shard_map/va3_right/ppermute | solution.py:432
  98.1 25.4 %collective-permute-start.23 = (bf16[4,512,128]{2,1,0:T(8,128)(2,1)}, bf16[4,512,128]{2,1,0:T(8,128)(2,1)}, u32[]{:S(2)}, u32[]{:S(2)}) collective-permute-start(bf16[4,512,128]{2,1,0:T(8,128)(2,1)} %get-tuple-element.77.refs_4_), channel_id=1, source_target_pairs={{0,28},{4,0},{8,4},{12,8},{16,12},{20,16},{24,20},{28,24},{1,29},{... | collective-permute-start | bytes 1572872 | tf_op jit(solution)/shard_map/vb1_left/ppermute | solution.py:432
  98.4 23.0 %collective-permute-start.18 = (bf16[4,512,128]{2,1,0:T(8,128)(2,1)}, bf16[4,512,128]{2,1,0:T(8,128)(2,1)}, u32[]{:S(2)}, u32[]{:S(2)}) collective-permute-start(bf16[4,512,128]{2,1,0:T(8,128)(2,1)} %collective-permute-done.14.refs_5_), channel_id=1, source_target_pairs={{0,28},{4,0},{8,4},{12,8},{16,12},{20,16},{24,20},{28,24},{1,29},{... | collective-permute-start | bytes 1572872 | tf_op jit(solution)/shard_map/ka3_left/ppermute | solution.py:432
  98.5 23.4 %collective-permute-start.12 = (bf16[4,512,128]{2,1,0:T(8,128)(2,1)}, bf16[4,512,128]{2,1,0:T(8,128)(2,1)}, u32[]{:S(2)}, u32[]{:S(2)}) collective-permute-start(bf16[4,512,128]{2,1,0:T(8,128)(2,1)} %collective-permute-done.10.refs_4_), channel_id=1, source_target_pairs={{0,4},{4,8},{8,12},{12,16},{16,20},{20,24},{24,28},{28,0},{1,5},{5... | collective-permute-start | bytes 1572872 | tf_op jit(solution)/shard_map/ka3_right/ppermute | solution.py:432
  100.4 24.7 %collective-permute-start.11 = (bf16[4,512,128]{2,1,0:T(8,128)(2,1)S(1)}, bf16[4,512,128]{2,1,0:T(8,128)(2,1)}, u32[]{:S(2)}, u32[]{:S(2)}) collective-permute-start(bf16[4,512,128]{2,1,0:T(8,128)(2,1)S(1)} %collective-permute-done.9.refs_4_), channel_id=1, source_target_pairs={{0,4},{4,8},{8,12},{12,16},{16,20},{20,24},{24,28},{28,0},{1,5},{5... | collective-permute-start | bytes 1572872 | tf_op jit(solution)/shard_map/va4_right/ppermute | solution.py:432
  121.9 16.3 %collective-permute-start.16 = (bf16[4,512,128]{2,1,0:T(8,128)(2,1)}, bf16[4,512,128]{2,1,0:T(8,128)(2,1)S(1)}, u32[]{:S(2)}, u32[]{:S(2)}) collective-permute-start(bf16[4,512,128]{2,1,0:T(8,128)(2,1)} %collective-permute-done.12.refs_1_), channel_id=1, source_target_pairs={{0,4},{4,8},{8,12},{12,16},{16,20},{20,24},{24,28},{28,0},{1,5},{5... | collective-permute-start | bytes 1572872 | tf_op jit(solution)/shard_map/ka4_right/ppermute | solution.py:432
  123.5 25.3 %collective-permute-start.27 = (bf16[4,512,128]{2,1,0:T(8,128)(2,1)}, bf16[4,512,128]{2,1,0:T(8,128)(2,1)}, u32[]{:S(2)}, u32[]{:S(2)}) collective-permute-start(bf16[4,512,128]{2,1,0:T(8,128)(2,1)} %collective-permute-done.23.refs_6_), channel_id=1, source_target_pairs={{0,28},{4,0},{8,4},{12,8},{16,12},{20,16},{24,20},{28,24},{1,29},{... | collective-permute-start | bytes 1572872 | tf_op jit(solution)/shard_map/vb2_left/ppermute | solution.py:432
  125.1 28.6 %collective-permute-start.20 = (bf16[4,512,128]{2,1,0:T(8,128)(2,1)S(1)}, bf16[4,512,128]{2,1,0:T(8,128)(2,1)}, u32[]{:S(2)}, u32[]{:S(2)}) collective-permute-start(bf16[4,512,128]{2,1,0:T(8,128)(2,1)S(1)} %copy-done.5), channel_id=1, source_target_pairs={{0,4},{4,8},{8,12},{12,16},{16,20},{20,24},{24,28},{28,0},{1,5},{5... | collective-permute-start | bytes 1572872 | tf_op jit(solution)/shard_map/vb1_right/ppermute | solution.py:432
  136.5 24.6 %collective-permute-start.26 = (bf16[4,512,128]{2,1,0:T(8,128)(2,1)S(1)}, bf16[4,512,128]{2,1,0:T(8,128)(2,1)}, u32[]{:S(2)}, u32[]{:S(2)}) collective-permute-start(bf16[4,512,128]{2,1,0:T(8,128)(2,1)S(1)} %collective-permute-done.22.refs_3_), channel_id=1, source_target_pairs={{0,28},{4,0},{8,4},{12,8},{16,12},{20,16},{24,20},{28,24},{1,29},{... | collective-permute-start | bytes 1572872 | tf_op jit(solution)/shard_map/kb2_left/ppermute | solution.py:432
  138.2 22.6 %collective-permute-start.17 = (bf16[4,512,128]{2,1,0:T(8,128)(2,1)}, bf16[4,512,128]{2,1,0:T(8,128)(2,1)}, u32[]{:S(2)}, u32[]{:S(2)}) collective-permute-start(bf16[4,512,128]{2,1,0:T(8,128)(2,1)} %get-tuple-element.76.refs_1_), channel_id=1, source_target_pairs={{0,4},{4,8},{8,12},{12,16},{16,20},{20,24},{24,28},{28,0},{1,5},{5... | collective-permute-start | bytes 1572872 | tf_op jit(solution)/shard_map/kb1_right/ppermute | solution.py:432
  148.8 18.6 %collective-permute-start.29 = (bf16[4,512,128]{2,1,0:T(8,128)(2,1)}, bf16[4,512,128]{2,1,0:T(8,128)(2,1)S(1)}, u32[]{:S(2)}, u32[]{:S(2)}) collective-permute-start(bf16[4,512,128]{2,1,0:T(8,128)(2,1)} %collective-permute-done.27.refs_4_), channel_id=1, source_target_pairs={{0,28},{4,0},{8,4},{12,8},{16,12},{20,16},{24,20},{28,24},{1,29},{... | collective-permute-start | bytes 1572872 | tf_op jit(solution)/shard_map/vb3_left/ppermute | solution.py:432
  153.8 18.2 %collective-permute-start.24 = (bf16[4,512,128]{2,1,0:T(8,128)(2,1)}, bf16[4,512,128]{2,1,0:T(8,128)(2,1)}, u32[]{:S(2)}, u32[]{:S(2)}) collective-permute-start(bf16[4,512,128]{2,1,0:T(8,128)(2,1)} %collective-permute-done.20.refs_5_), channel_id=1, source_target_pairs={{0,4},{4,8},{8,12},{12,16},{16,20},{20,24},{24,28},{28,0},{1,5},{5... | collective-permute-start | bytes 1572872 | tf_op jit(solution)/shard_map/vb2_right/ppermute | solution.py:432
  153.8 47.0 %all-to-all-start.1 = ((bf16[4,4,560,128]{3,2,1,0:T(8,128)(2,1)}), bf16[4,4,560,128]{3,2,1,0:T(8,128)(2,1)}, u32[]{:S(2)}, u32[]{:S(2)}) async-start(bf16[4,4,560,128]{3,2,1,0:T(8,128)(2,1)} %get-tuple-element.92), calls=%async_computation.1 | async-start | bytes 4587520 | tf_op jit(solution)/shard_map/partials_a/all_to_all | solution.py:562
  160.7 27.7 %collective-permute-start.21 = (bf16[4,512,128]{2,1,0:T(8,128)(2,1)}, bf16[4,512,128]{2,1,0:T(8,128)(2,1)}, u32[]{:S(2)}, u32[]{:S(2)}) collective-permute-start(bf16[4,512,128]{2,1,0:T(8,128)(2,1)} %collective-permute-done.17.refs_2_), channel_id=1, source_target_pairs={{0,4},{4,8},{8,12},{12,16},{16,20},{20,24},{24,28},{28,0},{1,5},{5... | collective-permute-start | bytes 1572872 | tf_op jit(solution)/shard_map/kb2_right/ppermute | solution.py:432
  167.4 33.4 %collective-permute-start.32 = (bf16[4,512,128]{2,1,0:T(8,128)(2,1)S(1)}, bf16[4,512,128]{2,1,0:T(8,128)(2,1)S(1)}, u32[]{:S(2)}, u32[]{:S(2)}) collective-permute-start(bf16[4,512,128]{2,1,0:T(8,128)(2,1)S(1)} %collective-permute-done.29.refs_5_), channel_id=1, source_target_pairs={{0,28},{4,0},{8,4},{12,8},{16,12},{20,16},{24,20},{28,24},{1,29},{... | collective-permute-start | bytes 1572872 | tf_op jit(solution)/shard_map/vb4_left/ppermute | solution.py:432
  172.0 28.8 %collective-permute-start.31 = (bf16[4,512,128]{2,1,0:T(8,128)(2,1)}, bf16[4,512,128]{2,1,0:T(8,128)(2,1)S(1)}, u32[]{:S(2)}, u32[]{:S(2)}) collective-permute-start(bf16[4,512,128]{2,1,0:T(8,128)(2,1)} %collective-permute-done.24.refs_3_), channel_id=1, source_target_pairs={{0,4},{4,8},{8,12},{12,16},{16,20},{20,24},{24,28},{28,0},{1,5},{5... | collective-permute-start | bytes 1572872 | tf_op jit(solution)/shard_map/vb3_right/ppermute | solution.py:432
  172.4 25.2 %collective-permute-start.28 = (bf16[4,512,128]{2,1,0:T(8,128)(2,1)}, bf16[4,512,128]{2,1,0:T(8,128)(2,1)}, u32[]{:S(2)}, u32[]{:S(2)}) collective-permute-start(bf16[4,512,128]{2,1,0:T(8,128)(2,1)} %collective-permute-done.26.refs_2_), channel_id=1, source_target_pairs={{0,28},{4,0},{8,4},{12,8},{16,12},{20,16},{24,20},{28,24},{1,29},{... | collective-permute-start | bytes 1572872 | tf_op jit(solution)/shard_map/kb3_left/ppermute | solution.py:432
  (26 other events, 321.9 us)
